TPU v7x, 32 devices: a whole 2x2x4 slice. The times are simulated.
32 devices in a mesh: ht: 4 (over x, core), wt: 8 (over z, y).
Axes of the slice: x: 2, y: 2, z: 4, core: 2. Of those that a mesh axis runs over, the one named last changes fastest.
Arguments:
- queries: bfloat16 [64, 64, 1024], P('ht', 'wt'), may hold values from -30 to 30
- keys_new: bfloat16 [64, 64, 1024], P('ht', 'wt'), may hold values from -10 to 10, as said below
- values_new: bfloat16 [64, 64, 1024], P('ht', 'wt'), may hold values from -6 to 6
- keys_cache: bfloat16 [1, 64, 64, 1024], P(None, 'ht', 'wt'), may hold values from -10 to 10, as said below
- values_cache: bfloat16 [1, 64, 64, 1024], P(None, 'ht', 'wt'), may hold values from -6 to 6
- conv_weight: float32 [3, 3, 1024], replicated, may hold values from -2 to 2
- conv_bias: float32 [1024], replicated, may hold values from -2.5 to 2.5
Outputs:
- block_out: bfloat16 [64, 64, 1024], P('ht', 'wt')
Inputs may be any that keep to these rules, and one draw needn't show every extreme that they name: `keys_new`: key features. `keys_cache`: key features.
All inputs are finite; a program needn't handle non-finite values.
Results may differ from a plain program's by a relative error of at most 0.003.
Values may be sent and summed in bfloat16 or wider, within the bound.
No kernel may reach another device: no remote copies, remote signals or barrier semaphores. Data moves between devices by JAX's collectives and lax.ppermute only.
A program may use at most 64 MiB of HBM per device.

v0:
```python
import jax
import jax.numpy as jnp
from jax import lax
from jax.sharding import PartitionSpec as P

HD = 128
WIN = 32


def with_halo(block, sides, width):
    for axis, dim in sides:
        count = lax.axis_size(axis)
        forward = [(i, i + 1) for i in range(count - 1)]
        backward = [(target, source) for source, target in forward]
        low = lax.ppermute(
            lax.slice_in_dim(block, block.shape[dim] - width, None, axis=dim), axis, forward
        )
        high = lax.ppermute(lax.slice_in_dim(block, 0, width, axis=dim), axis, backward)
        block = jnp.concatenate([low, block, high], axis=dim)
    return block


def window_allowed(row_start, col_start, frame_rows, frame_cols, tile_rows, tile_cols, half_win):
    ext_rows = jnp.arange(tile_rows + 2 * half_win, dtype=jnp.int32) - half_win
    ext_cols = jnp.arange(tile_cols + 2 * half_win, dtype=jnp.int32) - half_win
    query_rows = jnp.arange(tile_rows, dtype=jnp.int32)
    query_cols = jnp.arange(tile_cols, dtype=jnp.int32)
    row_delta = ext_rows[None, :] - query_rows[:, None]
    col_delta = ext_cols[None, :] - query_cols[:, None]
    global_rows = row_start + ext_rows
    global_cols = col_start + ext_cols
    row_valid = (
        (row_delta >= -half_win)
        & (row_delta < half_win)
        & ((global_rows >= 0) & (global_rows < frame_rows))[None, :]
    )
    col_valid = (
        (col_delta >= -half_win)
        & (col_delta < half_win)
        & ((global_cols >= 0) & (global_cols < frame_cols))[None, :]
    )
    allowed = row_valid[:, None, :, None] & col_valid[None, :, None, :]
    return allowed.reshape(
        tile_rows * tile_cols, (tile_rows + 2 * half_win) * (tile_cols + 2 * half_win)
    )


def attend(query_rows, keys_flat, values_flat, allowed, heads, head_dim):
    score_scale = head_dim ** (-0.5)

    def one_head(head_index):
        scores = (
            jnp.einsum("qd,kd->qk", query_rows, keys_flat, preferred_element_type=jnp.float32)
            * score_scale
        )
        scores = jnp.where(allowed, scores, -1e30)
        row_top = jnp.max(scores, axis=1, keepdims=True)
        weights_f = jnp.exp(scores - row_top)
        denominator = jnp.sum(weights_f, axis=1, keepdims=True)
        numerator = jnp.dot(
            weights_f.astype(jnp.bfloat16), values_flat, preferred_element_type=jnp.float32
        )
        return numerator / denominator

    outputs = lax.map(one_head, jnp.arange(heads, dtype=jnp.int32))
    return outputs.transpose(1, 0, 2).reshape(query_rows.shape[0], heads * head_dim)


def local_conv(padded, conv_weight, conv_bias, tile_rows, tile_cols):
    enhanced = jnp.zeros((tile_rows, tile_cols, padded.shape[2]), jnp.float32) + conv_bias
    for row_shift in range(3):
        for col_shift in range(3):
            enhanced = (
                enhanced
                + padded[
                    row_shift : row_shift + tile_rows, col_shift : col_shift + tile_cols
                ].astype(jnp.float32)
                * conv_weight[row_shift, col_shift]
            )
    return enhanced


def cycle_conv(values_new, conv_weight, conv_bias):
    tile_rows, tile_cols, channels = values_new.shape
    padded = with_halo(values_new, (("ht", 0), ("wt", 1)), 1)
    return local_conv(padded, conv_weight, conv_bias, tile_rows, tile_cols)


def shards(queries, keys_new, values_new, keys_cache, values_cache, conv_weight, conv_bias):
    tile_rows, tile_cols, channels = queries.shape
    frames = keys_cache.shape[0] + 1
    half_win = WIN // 2
    stacked = jnp.concatenate([keys_cache, keys_new[None], values_cache, values_new[None]], axis=0)
    row_start = lax.axis_index("ht") * tile_rows
    frame_rows = tile_rows * lax.axis_size("ht")
    frame_cols = tile_cols * lax.axis_size("wt")
    heads = channels // HD
    copies = lax.axis_size("wt") // heads
    bundle = jnp.concatenate([stacked, queries[None]], axis=0)
    members = bundle.shape[0]
    spread = bundle.reshape(members, tile_rows, tile_cols, 1, heads, HD)
    spread = jnp.broadcast_to(spread, (members, tile_rows, tile_cols, copies, heads, HD))
    spread = spread.reshape(members, tile_rows, tile_cols, copies * heads, HD)
    strips = lax.all_to_all(spread, "wt", split_axis=3, concat_axis=2, tiled=True)
    strips = strips.reshape(members, tile_rows, frame_cols, HD)
    device_index = lax.axis_index("wt")
    my_group = device_index // heads
    block_width = tile_cols * heads
    block_start = my_group * block_width
    padded_cols = jnp.pad(strips, ((0, 0), (0, 0), (half_win, half_win), (0, 0)))
    window = lax.dynamic_slice_in_dim(padded_cols, block_start, block_width + 2 * half_win, 2)
    query_part = window[2 * frames, :, half_win : half_win + block_width]
    region = with_halo(window[: 2 * frames], (("ht", 1),), half_win)

    def one_block(step):
        offset = step * tile_cols
        query_block = lax.dynamic_slice_in_dim(query_part, offset, tile_cols, 1).reshape(
            tile_rows * tile_cols, HD
        )
        sub = lax.dynamic_slice_in_dim(region, offset, tile_cols + 2 * half_win, 2)
        keys_flat = sub[:frames].reshape(-1, HD)
        values_flat = sub[frames:].reshape(-1, HD)
        allowed = window_allowed(
            row_start, block_start + offset, frame_rows, frame_cols, tile_rows, tile_cols, half_win
        )
        allowed = jnp.tile(allowed, (1, frames))
        result = attend(query_block, keys_flat, values_flat, allowed, 1, HD)
        return result.reshape(tile_rows, tile_cols, HD)

    blocks = lax.map(one_block, jnp.arange(heads, dtype=jnp.int32))
    payload = blocks.transpose(1, 0, 2, 3)
    payload = jnp.broadcast_to(payload[:, None], (tile_rows, copies, heads, tile_cols, HD))
    payload = payload.reshape(tile_rows, copies * heads, tile_cols, HD)
    returned = lax.all_to_all(
        payload.astype(jnp.bfloat16), "wt", split_axis=1, concat_axis=1, tiled=True
    ).astype(payload.dtype)
    own = lax.dynamic_slice_in_dim(returned, my_group * heads, heads, 1)
    combined = own.transpose(0, 2, 1, 3).reshape(tile_rows, tile_cols, channels)
    combined = combined + cycle_conv(values_new, conv_weight, conv_bias)
    return combined.astype(jnp.bfloat16)


def solution(mesh):
    placed = (
        P("ht", "wt", None),
        P("ht", "wt", None),
        P("ht", "wt", None),
        P(None, "ht", "wt", None),
        P(None, "ht", "wt", None),
        P(),
        P(),
    )
    return jax.shard_map(
        shards, mesh=mesh, in_specs=placed, out_specs=P("ht", "wt", None), check_vma=False
    )
```

profile of v0, /device:TPU:6, one launch (start us, length us, event | category | flops | bytes accessed | tf_op | source)
XLA Modules:
  0.0 164.7 jit_solution(13249952250339896658)
XLA Ops:
  3.6 36.9 %all_to_all.20 = bf16[5,16,8,8,128]{4,2,1,0,3:T(8,128)(2,1)S(1)} all-to-all(bf16[5,16,8,8,128]{4,2,1,0,3:T(8,128)(2,1)S(1)} %copy.17), channel_id=1, replica_groups=mesh['ht'=4,'wt'=8] {'wt'}, dimensions={3} | all-to-all | bytes 2621440 | tf_op jit(solution)/shard_map/all_to_all | solution.py:104
  41.1 1.9 %collective-permute-start.1 = (bf16[4,16,96,128]{3,2,1,0:T(8,128)(2,1)S(1)}, bf16[4,16,96,128]{3,2,1,0:T(8,128)(2,1)}, u32[]{:S(2)}, u32[]{:S(2)}) collective-permute-start(bf16[4,16,96,128]{3,2,1,0:T(8,128)(2,1)S(1)} %pad_slice_fusion), channel_id=1, source_target_pairs={{8,0},{16,8},{24,16},{9,1},{17,9},{25,17},{10,2},{18,10},{26,18},{... | collective-permute-start | bytes 4718600 | tf_op jit(solution)/shard_map/ppermute | solution.py:18
  43.0 3.6 %collective-permute-start = (bf16[4,16,96,128]{3,2,1,0:T(8,128)(2,1)S(1)}, bf16[4,16,96,128]{3,2,1,0:T(8,128)(2,1)}, u32[]{:S(2)}, u32[]{:S(2)}) collective-permute-start(bf16[4,16,96,128]{3,2,1,0:T(8,128)(2,1)S(1)} %pad_slice_fusion), channel_id=1, source_target_pairs={{0,8},{8,16},{16,24},{1,9},{9,17},{17,25},{2,10},{10,18},{18,26},{... | collective-permute-start | bytes 4718600 | tf_op jit(solution)/shard_map/ppermute | solution.py:15
  46.6 1.9 %collective-permute-start.2 = (bf16[1,8,1024]{2,1,0:T(8,128)(2,1)S(1)}, bf16[1,8,1024]{2,1,0:T(8,128)(2,1)S(1)}, u32[]{:S(2)}, u32[]{:S(2)}) collective-permute-start(bf16[1,8,1024]{2,1,0:T(8,128)(2,1)S(1)} %get-tuple-element.156), channel_id=1, source_target_pairs={{0,8},{8,16},{16,24},{1,9},{9,17},{17,25},{2,10},{10,18},{18,26},{... | collective-permute-start | bytes 49160 | tf_op jit(solution)/shard_map/ppermute | solution.py:15
  48.5 3.6 %collective-permute-start.3 = (bf16[1,8,1024]{2,1,0:T(8,128)(2,1)S(1)}, bf16[1,8,1024]{2,1,0:T(8,128)(2,1)S(1)}, u32[]{:S(2)}, u32[]{:S(2)}) collective-permute-start(bf16[1,8,1024]{2,1,0:T(8,128)(2,1)S(1)} %get-tuple-element.155), channel_id=1, source_target_pairs={{8,0},{16,8},{24,16},{9,1},{17,9},{25,17},{10,2},{18,10},{26,18},{... | collective-permute-start | bytes 49160 | tf_op jit(solution)/shard_map/ppermute | solution.py:18
  52.2 12.7 %collective-permute-done.2 = bf16[1,8,1024]{2,1,0:T(8,128)(2,1)S(1)} collective-permute-done((bf16[1,8,1024]{2,1,0:T(8,128)(2,1)S(1)}, bf16[1,8,1024]{2,1,0:T(8,128)(2,1)S(1)}, u32[]{:S(2)}, u32[]{:S(2)}) %collective-permute-start.2) | collective-permute-done | bytes 16416 | tf_op jit(solution)/shard_map/ppermute | solution.py:15
  65.7 3.8 %pad_maximum_fusion = bf16[4,48,96,128]{3,2,1,0:T(8,128)(2,1)} fusion(bf16[4,16,96,128]{3,2,1,0:T(8,128)(2,1)} %collective-permute-done.1, bf16[4,16,96,128]{3,2,1,0:T(8,128)(2,1)S(1)} %pad_slice_fusion, bf16[4,16,96,128]{3,2,1,0:T(8,128)(2,1)} %collective-permute-done), kind=kLoop, calls=%fused_computation.29 | loop fusion | flops 4718592 | bytes 9437184 | tf_op jit(solution)/shard_map/concatenate | solution.py:19
  69.5 78.8 %while.17 = (s32[]{:T(128)}, bf16[8,16,8,128]{3,2,1,0:T(8,128)(2,1)}, s32[]{:T(128)}, s32[8]{0:T(128)S(1)}, s32[]{:T(128)}, /*index=5*/bf16[16,64,128]{2,1,0:T(8...) while((s32[]{:T(128)}, ...), condition=%wide.region_3.4_spmd, body=%wide.region_0.3_spmd.sunk | while | flops 255366752 | bytes 15341304 | solution.py:130
  71.4 2.0 %and.148 = pred[128,1920]{1,0:T(8,128)(4,1)S(1)} reshape(pred[16,8,48,40]{3,2,1,0:T(8,128)(4,1)S(1)} %broadcast_and_fusion.2) | data formatting | bytes 491520 | tf_op jit(solution)/shard_map/while/body/eval_jaxpr/and | solution.py:42
  74.5 1.9 %constant_dynamic-slice_fusion.3 = (bf16[2,48,40,128]{3,2,1,0:T(8,128)(2,1)S(1)}, bf16[2,48,40,128]{3,2,1,0:T(8,128)(2,1)S(1)}) fusion(bf16[4,48,96,128]{3,2,1,0:T(8,128)(2,1)} %get-tuple-element.249, s32[]{:T(128)S(6)} %select_n.34, s32[]{:T(128)S(6)} %add.172), kind=kLoop, calls=%fused_computation.24.clone.1 | loop fusion | bytes 3932168 | tf_op jit(solution)/shard_map/while/body/eval_jaxpr/slice | solution.py:121
  81.2 2.0 %and.148 = pred[128,1920]{1,0:T(8,128)(4,1)S(1)} reshape(pred[16,8,48,40]{3,2,1,0:T(8,128)(4,1)S(1)} %broadcast_and_fusion.2) | data formatting | bytes 491520 | tf_op jit(solution)/shard_map/while/body/eval_jaxpr/and | solution.py:42
  84.4 1.9 %constant_dynamic-slice_fusion.3 = (bf16[2,48,40,128]{3,2,1,0:T(8,128)(2,1)S(1)}, bf16[2,48,40,128]{3,2,1,0:T(8,128)(2,1)S(1)}) fusion(bf16[4,48,96,128]{3,2,1,0:T(8,128)(2,1)} %get-tuple-element.249, s32[]{:T(128)S(6)} %select_n.34, s32[]{:T(128)S(6)} %add.172), kind=kLoop, calls=%fused_computation.24.clone.1 | loop fusion | bytes 3932168 | tf_op jit(solution)/shard_map/while/body/eval_jaxpr/slice | solution.py:121
  86.2 1.3 fusion.42
  91.1 2.0 %and.148 = pred[128,1920]{1,0:T(8,128)(4,1)S(1)} reshape(pred[16,8,48,40]{3,2,1,0:T(8,128)(4,1)S(1)} %broadcast_and_fusion.2) | data formatting | bytes 491520 | tf_op jit(solution)/shard_map/while/body/eval_jaxpr/and | solution.py:42
  94.2 1.9 %constant_dynamic-slice_fusion.3 = (bf16[2,48,40,128]{3,2,1,0:T(8,128)(2,1)S(1)}, bf16[2,48,40,128]{3,2,1,0:T(8,128)(2,1)S(1)}) fusion(bf16[4,48,96,128]{3,2,1,0:T(8,128)(2,1)} %get-tuple-element.249, s32[]{:T(128)S(6)} %select_n.34, s32[]{:T(128)S(6)} %add.172), kind=kLoop, calls=%fused_computation.24.clone.1 | loop fusion | bytes 3932168 | tf_op jit(solution)/shard_map/while/body/eval_jaxpr/slice | solution.py:121
  100.9 2.0 %and.148 = pred[128,1920]{1,0:T(8,128)(4,1)S(1)} reshape(pred[16,8,48,40]{3,2,1,0:T(8,128)(4,1)S(1)} %broadcast_and_fusion.2) | data formatting | bytes 491520 | tf_op jit(solution)/shard_map/while/body/eval_jaxpr/and | solution.py:42
  104.1 1.9 %constant_dynamic-slice_fusion.3 = (bf16[2,48,40,128]{3,2,1,0:T(8,128)(2,1)S(1)}, bf16[2,48,40,128]{3,2,1,0:T(8,128)(2,1)S(1)}) fusion(bf16[4,48,96,128]{3,2,1,0:T(8,128)(2,1)} %get-tuple-element.249, s32[]{:T(128)S(6)} %select_n.34, s32[]{:T(128)S(6)} %add.172), kind=kLoop, calls=%fused_computation.24.clone.1 | loop fusion | bytes 3932168 | tf_op jit(solution)/shard_map/while/body/eval_jaxpr/slice | solution.py:121
  105.9 1.3 fusion.42
  110.7 2.0 %and.148 = pred[128,1920]{1,0:T(8,128)(4,1)S(1)} reshape(pred[16,8,48,40]{3,2,1,0:T(8,128)(4,1)S(1)} %broadcast_and_fusion.2) | data formatting | bytes 491520 | tf_op jit(solution)/shard_map/while/body/eval_jaxpr/and | solution.py:42
  113.9 1.9 %constant_dynamic-slice_fusion.3 = (bf16[2,48,40,128]{3,2,1,0:T(8,128)(2,1)S(1)}, bf16[2,48,40,128]{3,2,1,0:T(8,128)(2,1)S(1)}) fusion(bf16[4,48,96,128]{3,2,1,0:T(8,128)(2,1)} %get-tuple-element.249, s32[]{:T(128)S(6)} %select_n.34, s32[]{:T(128)S(6)} %add.172), kind=kLoop, calls=%fused_computation.24.clone.1 | loop fusion | bytes 3932168 | tf_op jit(solution)/shard_map/while/body/eval_jaxpr/slice | solution.py:121
  120.6 2.0 %and.148 = pred[128,1920]{1,0:T(8,128)(4,1)S(1)} reshape(pred[16,8,48,40]{3,2,1,0:T(8,128)(4,1)S(1)} %broadcast_and_fusion.2) | data formatting | bytes 491520 | tf_op jit(solution)/shard_map/while/body/eval_jaxpr/and | solution.py:42
  123.8 1.9 %constant_dynamic-slice_fusion.3 = (bf16[2,48,40,128]{3,2,1,0:T(8,128)(2,1)S(1)}, bf16[2,48,40,128]{3,2,1,0:T(8,128)(2,1)S(1)}) fusion(bf16[4,48,96,128]{3,2,1,0:T(8,128)(2,1)} %get-tuple-element.249, s32[]{:T(128)S(6)} %select_n.34, s32[]{:T(128)S(6)} %add.172), kind=kLoop, calls=%fused_computation.24.clone.1 | loop fusion | bytes 3932168 | tf_op jit(solution)/shard_map/while/body/eval_jaxpr/slice | solution.py:121
  125.6 1.3 fusion.42
  130.4 2.0 %and.148 = pred[128,1920]{1,0:T(8,128)(4,1)S(1)} reshape(pred[16,8,48,40]{3,2,1,0:T(8,128)(4,1)S(1)} %broadcast_and_fusion.2) | data formatting | bytes 491520 | tf_op jit(solution)/shard_map/while/body/eval_jaxpr/and | solution.py:42
  133.6 1.9 %constant_dynamic-slice_fusion.3 = (bf16[2,48,40,128]{3,2,1,0:T(8,128)(2,1)S(1)}, bf16[2,48,40,128]{3,2,1,0:T(8,128)(2,1)S(1)}) fusion(bf16[4,48,96,128]{3,2,1,0:T(8,128)(2,1)} %get-tuple-element.249, s32[]{:T(128)S(6)} %select_n.34, s32[]{:T(128)S(6)} %add.172), kind=kLoop, calls=%fused_computation.24.clone.1 | loop fusion | bytes 3932168 | tf_op jit(solution)/shard_map/while/body/eval_jaxpr/slice | solution.py:121
  140.3 2.0 %and.148 = pred[128,1920]{1,0:T(8,128)(4,1)S(1)} reshape(pred[16,8,48,40]{3,2,1,0:T(8,128)(4,1)S(1)} %broadcast_and_fusion.2) | data formatting | bytes 491520 | tf_op jit(solution)/shard_map/while/body/eval_jaxpr/and | solution.py:42
  143.4 1.9 %constant_dynamic-slice_fusion.3 = (bf16[2,48,40,128]{3,2,1,0:T(8,128)(2,1)S(1)}, bf16[2,48,40,128]{3,2,1,0:T(8,128)(2,1)S(1)}) fusion(bf16[4,48,96,128]{3,2,1,0:T(8,128)(2,1)} %get-tuple-element.249, s32[]{:T(128)S(6)} %select_n.34, s32[]{:T(128)S(6)} %add.172), kind=kLoop, calls=%fused_computation.24.clone.1 | loop fusion | bytes 3932168 | tf_op jit(solution)/shard_map/while/body/eval_jaxpr/slice | solution.py:121
  148.2 4.2 %all-to-all-start.1 = ((bf16[16,8,8,128]{3,2,0,1:T(8,128)(2,1)}), bf16[16,8,8,128]{3,2,0,1:T(8,128)(2,1)S(1)}, u32[]{:S(2)}, u32[]{:S(2)}) async-start(bf16[16,8,8,128]{3,2,0,1:T(8,128)(2,1)} %bitcast.66), calls=%async_computation.1 | async-start | bytes 524288 | tf_op jit(solution)/shard_map/all_to_all | solution.py:134
  152.5 3.4 %collective-permute-start.4 = (bf16[18,1,1024]{2,1,0:T(2,128)(2,1)S(1)}, bf16[18,1,1024]{2,1,0:T(2,128)(2,1)S(1)}, u32[]{:S(2)}, u32[]{:S(2)}) collective-permute-start(bf16[18,1,1024]{2,1,0:T(2,128)(2,1)S(1)} %get-tuple-element.153), channel_id=1, source_target_pairs={{0,1},{1,2},{2,3},{3,4},{4,5},{5,6},{6,7},{8,9},{9,10},{10,11},{11... | collective-permute-start | bytes 110600 | tf_op jit(solution)/shard_map/ppermute | solution.py:15
  155.9 2.5 %collective-permute-start.5 = (bf16[18,1,1024]{2,1,0:T(2,128)(2,1)S(1)}, bf16[18,1,1024]{2,1,0:T(2,128)(2,1)S(1)}, u32[]{:S(2)}, u32[]{:S(2)}) collective-permute-start(bf16[18,1,1024]{2,1,0:T(2,128)(2,1)S(1)} %get-tuple-element.154), channel_id=1, source_target_pairs={{1,0},{2,1},{3,2},{4,3},{5,4},{6,5},{7,6},{9,8},{10,9},{11,10},{12... | collective-permute-start | bytes 110600 | tf_op jit(solution)/shard_map/ppermute | solution.py:18
  159.0 4.0 %collective-permute-done.5 = bf16[18,1,1024]{2,1,0:T(2,128)(2,1)S(1)} collective-permute-done((bf16[18,1,1024]{2,1,0:T(2,128)(2,1)S(1)}, bf16[18,1,1024]{2,1,0:T(2,128)(2,1)S(1)}, u32[]{:S(2)}, u32[]{:S(2)}) %collective-permute-start.5) | collective-permute-done | bytes 36896 | tf_op jit(solution)/shard_map/ppermute | solution.py:18
  163.1 1.6 fusion.18
  (139 shorter events, 43.3 us)
Async XLA Ops:
  0.0 3.1 %copy-start = (bf16[16,8,1024]{2,1,0:T(8,128)(2,1)S(1)}, bf16[16,8,1024]{2,1,0:T(8,128)(2,1)}, u32[]{:S(2)}) copy-start(bf16[16,8,1024]{2,1,0:T(8,128)(2,1)} %param.11) | copy-start | bytes 786436
  0.0 3.2 %copy-start.1 = (bf16[16,8,1024]{2,1,0:T(8,128)(2,1)S(1)}, bf16[16,8,1024]{2,1,0:T(8,128)(2,1)}, u32[]{:S(2)}) copy-start(bf16[16,8,1024]{2,1,0:T(8,128)(2,1)} %param.9) | copy-start | bytes 786436
  41.1 24.6 %collective-permute-start.1 = (bf16[4,16,96,128]{3,2,1,0:T(8,128)(2,1)S(1)}, bf16[4,16,96,128]{3,2,1,0:T(8,128)(2,1)}, u32[]{:S(2)}, u32[]{:S(2)}) collective-permute-start(bf16[4,16,96,128]{3,2,1,0:T(8,128)(2,1)S(1)} %pad_slice_fusion), channel_id=1, source_target_pairs={{8,0},{16,8},{24,16},{9,1},{17,9},{25,17},{10,2},{18,10},{26,18},{... | collective-permute-start | bytes 4718600 | tf_op jit(solution)/shard_map/ppermute | solution.py:18
  43.0 22.7 %collective-permute-start = (bf16[4,16,96,128]{3,2,1,0:T(8,128)(2,1)S(1)}, bf16[4,16,96,128]{3,2,1,0:T(8,128)(2,1)}, u32[]{:S(2)}, u32[]{:S(2)}) collective-permute-start(bf16[4,16,96,128]{3,2,1,0:T(8,128)(2,1)S(1)} %pad_slice_fusion), channel_id=1, source_target_pairs={{0,8},{8,16},{16,24},{1,9},{9,17},{17,25},{2,10},{10,18},{18,26},{... | collective-permute-start | bytes 4718600 | tf_op jit(solution)/shard_map/ppermute | solution.py:15
  46.6 18.3 %collective-permute-start.2 = (bf16[1,8,1024]{2,1,0:T(8,128)(2,1)S(1)}, bf16[1,8,1024]{2,1,0:T(8,128)(2,1)S(1)}, u32[]{:S(2)}, u32[]{:S(2)}) collective-permute-start(bf16[1,8,1024]{2,1,0:T(8,128)(2,1)S(1)} %get-tuple-element.156), channel_id=1, source_target_pairs={{0,8},{8,16},{16,24},{1,9},{9,17},{17,25},{2,10},{10,18},{18,26},{... | collective-permute-start | bytes 49160 | tf_op jit(solution)/shard_map/ppermute | solution.py:15
  48.5 16.4 %collective-permute-start.3 = (bf16[1,8,1024]{2,1,0:T(8,128)(2,1)S(1)}, bf16[1,8,1024]{2,1,0:T(8,128)(2,1)S(1)}, u32[]{:S(2)}, u32[]{:S(2)}) collective-permute-start(bf16[1,8,1024]{2,1,0:T(8,128)(2,1)S(1)} %get-tuple-element.155), channel_id=1, source_target_pairs={{8,0},{16,8},{24,16},{9,1},{17,9},{25,17},{10,2},{18,10},{26,18},{... | collective-permute-start | bytes 49160 | tf_op jit(solution)/shard_map/ppermute | solution.py:18
  69.5 88.9 %copy-start.2 = (f32[3,3,1024]{2,1,0:T(4,128)S(1)}, f32[3,3,1024]{2,1,0:T(4,128)}, u32[]{:S(2)}) copy-start(f32[3,3,1024]{2,1,0:T(4,128)} %param.14) | copy-start | bytes 110596
  69.5 93.6 %copy-start.3 = (f32[1024]{0:T(1024)S(1)}, f32[1024]{0:T(1024)}, u32[]{:S(2)}) copy-start(f32[1024]{0:T(1024)} %param.15) | copy-start | bytes 12292
  148.2 14.8 %all-to-all-start.1 = ((bf16[16,8,8,128]{3,2,0,1:T(8,128)(2,1)}), bf16[16,8,8,128]{3,2,0,1:T(8,128)(2,1)S(1)}, u32[]{:S(2)}, u32[]{:S(2)}) async-start(bf16[16,8,8,128]{3,2,0,1:T(8,128)(2,1)} %bitcast.66), calls=%async_computation.1 | async-start | bytes 524288 | tf_op jit(solution)/shard_map/all_to_all | solution.py:134
  152.5 6.5 %collective-permute-start.4 = (bf16[18,1,1024]{2,1,0:T(2,128)(2,1)S(1)}, bf16[18,1,1024]{2,1,0:T(2,128)(2,1)S(1)}, u32[]{:S(2)}, u32[]{:S(2)}) collective-permute-start(bf16[18,1,1024]{2,1,0:T(2,128)(2,1)S(1)} %get-tuple-element.153), channel_id=1, source_target_pairs={{0,1},{1,2},{2,3},{3,4},{4,5},{5,6},{6,7},{8,9},{9,10},{10,11},{11... | collective-permute-start | bytes 110600 | tf_op jit(solution)/shard_map/ppermute | solution.py:15
  155.9 7.1 %collective-permute-start.5 = (bf16[18,1,1024]{2,1,0:T(2,128)(2,1)S(1)}, bf16[18,1,1024]{2,1,0:T(2,128)(2,1)S(1)}, u32[]{:S(2)}, u32[]{:S(2)}) collective-permute-start(bf16[18,1,1024]{2,1,0:T(2,128)(2,1)S(1)} %get-tuple-element.154), channel_id=1, source_target_pairs={{1,0},{2,1},{3,2},{4,3},{5,4},{6,5},{7,6},{9,8},{10,9},{11,10},{12... | collective-permute-start | bytes 110600 | tf_op jit(solution)/shard_map/ppermute | solution.py:18
where the time goes:
time: 166 us; the launch traced here: 165 us
  local copies, waits for them, and re-layouts  50.3 us (30%)
  blocking collectives  36.9 us (22%)
  starting transfers between devices  21.1 us (13%)
  matrix products  20 us (12%)
  waiting for transfers between devices  17.4 us (10%)
  other arithmetic  12.6 us (8%)
  loops' own time  6.24 us (4%)
    all_to_all x1, blocking collectives, shards(): lax.all_to_all(spread, 'wt', split_axis=3, concat_axis=2, tiled=True)  36.9 us
    and x16, local copies, waits for them, and re-layouts, window_allowed(): allowed = row_valid[:, None, :, None] & col_valid[None, :, None, :]  19.4 us
    slice x8, local copies, waits for them, and re-layouts, one_block(): keys_flat = sub[:frames].reshape(-1, HD)  14.9 us
    ppermute x3, waiting for transfers between devices, with_halo(): lax.ppermute(lax.slice_in_dim(block, block.shape[dim] - width, None, axis...  13.3 us
    dot_general x8, matrix products, one_head(): jnp.einsum('qd,kd->qk', query_rows, keys_flat, preferred_element_type=jnp...  10.8 us
    dot_general x8, matrix products, one_head(): jnp.dot(weights_f.astype(jnp.bfloat16), values_flat, preferred_element_ty...  9.19 us
    ppermute x3, starting transfers between devices, with_halo(): lax.ppermute(lax.slice_in_dim(block, block.shape[dim] - width, None, axis...  8.85 us
    ppermute x3, starting transfers between devices, with_halo(): lax.ppermute(lax.slice_in_dim(block, 0, width, axis=dim), axis, backward)  8.03 us
  transfers between devices with their start and end apart: 7, of which 3 were waited for; matrix products, arithmetic and copies ran while one was open for 1% of the time, Pallas kernels for 0%

commit v1 on v0

--- a/solution.py
+++ b/solution.py
@@ -1,7 +1,11 @@
+import functools
+
 import jax
 import jax.numpy as jnp
 from jax import lax
-from jax.sharding import PartitionSpec as P
+from jax.experimental import pallas as pl
+from jax.experimental.pallas import tpu as pltpu
+from jax.sharding import Mesh, PartitionSpec as P
 
 HD = 128
 WIN = 32
@@ -140,16 +144,227 @@
     return combined.astype(jnp.bfloat16)
 
 
+LOG2E = 1.4426950408889634
+NEG = -1e30
+VMEM = pl.BlockSpec(memory_space=pltpu.VMEM)
+SMEM = pl.BlockSpec(memory_space=pltpu.SMEM)
+
+
+def index_of(position, shape, dim):
+    return lax.broadcasted_iota(jnp.int32, shape, dim) if position is None else position
+
+
+def tile_masks(tile_rows, tile_cols):
+    size = tile_rows * tile_cols
+    query = lax.broadcasted_iota(jnp.int32, (size, size), 0)
+    key = lax.broadcasted_iota(jnp.int32, (size, size), 1)
+    upper = key // tile_cols >= query // tile_cols
+    left = key % tile_cols >= query % tile_cols
+    return upper, left
+
+
+def attend_kernel(grid_rows, grid_cols, tile_rows, tile_cols, info_ref, weight_ref, bias_ref, q_ref, *refs):
+    out_ref = refs[-1]
+    frames = [refs[3 * f : 3 * f + 3] for f in range((len(refs) - 1) // 3)]
+    size = tile_rows * tile_cols
+    scale = HD ** (-0.5) * LOG2E
+    bias_left = jnp.where(info_ref[0] > 0, 0.0, NEG).astype(jnp.float32)
+    bias_right = jnp.where(info_ref[1] > 0, 0.0, NEG).astype(jnp.float32)
+    upper, left = tile_masks(tile_rows, tile_cols)
+    upper_one = upper.astype(jnp.float32).astype(jnp.bfloat16)
+    left_one = left.astype(jnp.float32).astype(jnp.bfloat16)
+    lower_one = 1 - upper_one
+    right_one = 1 - left_one
+    ones = jnp.ones((size, HD), jnp.bfloat16)
+
+    def slot(row, col):
+        return info_ref[2 + row * grid_cols + col]
+
+    def tile(frame, part, row, col):
+        side = 1 if col < 0 else (2 if col >= grid_cols else 0)
+        return frames[frame][side][slot(row, col % grid_cols), part].reshape(size, HD)
+
+    def piece(row, col):
+        query = q_ref[slot(row, col)].reshape(size, HD)
+
+        def score(frame, key_row, key_col):
+            raw = lax.dot_general(
+                query, tile(frame, 0, key_row, key_col), (((1,), (1,)), ((), ())),
+                preferred_element_type=jnp.float32,
+            )
+            if key_col < 0:
+                raw = raw + bias_left
+            elif key_col >= grid_cols:
+                raw = raw + bias_right
+            return raw
+
+        up, down = row > 0, row + 1 < grid_rows
+
+        def beside(frame, key_col):
+            if up and down:
+                return jnp.where(upper, score(frame, row - 1, key_col), score(frame, row + 1, key_col))
+            if down:
+                return jnp.where(upper, NEG, score(frame, row + 1, key_col))
+            return jnp.where(upper, score(frame, row - 1, key_col), NEG)
+
+        blocks = []
+        for frame in range(len(frames)):
+            for step in (-1, 0, 1):
+                blocks.append((frame, False, step, score(frame, row, col + step)))
+                blocks.append((frame, True, step, beside(frame, col + step)))
+            blocks.append((frame, False, 2, jnp.where(left, score(frame, row, col - 2), score(frame, row, col + 2))))
+            blocks.append((frame, True, 2, jnp.where(left, beside(frame, col - 2), beside(frame, col + 2))))
+        top = blocks[0][3]
+        for entry in blocks[1:]:
+            top = jnp.maximum(top, entry[3])
+        top = jnp.max(top, axis=1, keepdims=True)
+        total = jnp.zeros((size, 2 * HD), jnp.float32)
+        for frame, off_row, step, raw in blocks:
+            weights = jnp.exp2((raw - top) * scale).astype(jnp.bfloat16)
+            if off_row and up and down:
+                by_row = [(row - 1, weights * upper_one), (row + 1, weights * lower_one)]
+            elif off_row:
+                by_row = [(row + 1 if down else row - 1, weights)]
+            else:
+                by_row = [(row, weights)]
+            parts = []
+            for key_row, part in by_row:
+                if step == 2:
+                    parts.append((key_row, col - 2, part * left_one))
+                    parts.append((key_row, col + 2, part * right_one))
+                else:
+                    parts.append((key_row, col + step, part))
+            for key_row, key_col, part in parts:
+                wide = jnp.concatenate([tile(frame, 1, key_row, key_col), ones], axis=1)
+                total = total + jnp.dot(part, wide, preferred_element_type=jnp.float32)
+        return total[:, :HD] / total[:, HD:]
+
+    last = len(frames) - 1
+    sub = lax.broadcasted_iota(jnp.int32, (tile_cols, HD), 0)
+    taps = [[weight_ref[a, pl.ds(b, 1), :] for b in range(3)] for a in range(3)]
+
+    def enhanced(row, col):
+        lines = []
+        for key_row in range(row * tile_rows - 1, (row + 1) * tile_rows + 1):
+            tile_row, line = key_row // tile_rows, key_row % tile_rows
+            if tile_row < 0 or tile_row >= grid_rows:
+                lines.append(None)
+                continue
+
+            def values(key_col):
+                side = 1 if key_col < 0 else (2 if key_col >= grid_cols else 0)
+                return frames[last][side][slot(tile_row, key_col % grid_cols), 1, line].astype(jnp.float32)
+
+            here, before, after = values(col), values(col - 1), values(col + 1)
+            low = jnp.where(sub == 0, pltpu.roll(before, 1, 0), pltpu.roll(here, 1, 0))
+            high = jnp.where(sub == tile_cols - 1, pltpu.roll(after, tile_cols - 1, 0), pltpu.roll(here, tile_cols - 1, 0))
+            lines.append((low, here, high))
+        sums = []
+        for line in range(tile_rows):
+            total = jnp.broadcast_to(bias_ref[...], (tile_cols, HD))
+            for a in range(3):
+                if lines[line + a] is not None:
+                    for b in range(3):
+                        total = total + lines[line + a][b] * taps[a][b]
+            sums.append(total)
+        return jnp.stack(sums, axis=0)
+
+    for row in range(grid_rows):
+        for col in range(grid_cols):
+            attended = piece(row, col).reshape(tile_rows, tile_cols, HD)
+            out_ref[slot(row, col)] = (attended + enhanced(row, col)).astype(jnp.bfloat16)
+
+
+def pack_kernel(heads, q_ref, kn_ref, vn_ref, kc_ref, vc_ref, first_ref, second_ref):
+    for head in range(heads):
+        lanes = pl.ds(head * HD, HD)
+        first_ref[head, 0] = kc_ref[0, :, :, lanes]
+        first_ref[head, 1] = vc_ref[0, :, :, lanes]
+        second_ref[head, 0] = kn_ref[:, :, lanes]
+        second_ref[head, 1] = vn_ref[:, :, lanes]
+        second_ref[head, 2] = q_ref[:, :, lanes]
+
+
+def head_shards(shape, queries, keys_new, values_new, keys_cache, values_cache, conv_weight, conv_bias):
+    group_rows, group_cols, far = shape
+    tile_rows, tile_cols, channels = queries.shape
+    heads = channels // HD
+    group = ("ht", "near")
+    block = (tile_rows, tile_cols, HD)
+    first, second = pl.pallas_call(
+        functools.partial(pack_kernel, heads),
+        out_shape=(
+            jax.ShapeDtypeStruct((heads, 2) + block, jnp.bfloat16),
+            jax.ShapeDtypeStruct((heads, 3) + block, jnp.bfloat16),
+        ),
+        in_specs=[VMEM] * 5,
+        out_specs=(VMEM, VMEM),
+    )(queries, keys_new, values_new, keys_cache, values_cache)
+
+    def exchange(x):
+        return lax.all_to_all(x, group, split_axis=0, concat_axis=0, tiled=True)
+
+    up = [(i, i + 1) for i in range(far - 1)]
+    down = [(i + 1, i) for i in range(far - 1)]
+
+    def halo(x):
+        return lax.ppermute(x, "far", up), lax.ppermute(x, "far", down)
+
+    cached = exchange(first)
+    cached_left, cached_right = halo(cached)
+    second, _ = lax.optimization_barrier((second, cached))
+    current = exchange(second)
+    new, query = current[:, :2], current[:, 2]
+    new_left, new_right = halo(new)
+    far_index = lax.axis_index("far")
+    head = lax.axis_index("ht") * group_cols + lax.axis_index("near")
+    info = jnp.concatenate(
+        [
+            jnp.stack([far_index > 0, far_index < far - 1]).astype(jnp.int32),
+            jnp.arange(heads, dtype=jnp.int32),
+        ]
+    )
+    weight = lax.dynamic_slice_in_dim(conv_weight, head * HD, HD, 2)
+    bias = lax.dynamic_slice_in_dim(conv_bias.reshape(1, channels), head * HD, HD, 1)
+    result = pl.pallas_call(
+        functools.partial(attend_kernel, group_rows, group_cols, tile_rows, tile_cols),
+        out_shape=jax.ShapeDtypeStruct((heads,) + block, jnp.bfloat16),
+        in_specs=[SMEM] + [VMEM] * 9,
+        out_specs=VMEM,
+        compiler_params=pltpu.CompilerParams(vmem_limit_bytes=48 * 1024 * 1024),
+    )(info, weight, bias, query, cached, cached_left, cached_right, new, new_left, new_right)
+    returned = exchange(result)
+    return returned.transpose(1, 2, 0, 3).reshape(tile_rows, tile_cols, channels)
+
+
+def grouping(mesh, heads):
+    rows, cols = mesh.shape["ht"], mesh.shape["wt"]
+    group_rows = rows
+    group_cols = heads // group_rows if heads % group_rows == 0 else 0
+    if group_cols != 2 or cols % group_cols:
+        return None
+    return group_rows, group_cols, cols // group_cols
+
+
 def solution(mesh):
-    placed = (
-        P("ht", "wt", None),
-        P("ht", "wt", None),
-        P("ht", "wt", None),
-        P(None, "ht", "wt", None),
-        P(None, "ht", "wt", None),
-        P(),
-        P(),
-    )
-    return jax.shard_map(
-        shards, mesh=mesh, in_specs=placed, out_specs=P("ht", "wt", None), check_vma=False
-    )
+    def program(queries, *rest):
+        heads = queries.shape[2] // HD
+        shape = grouping(mesh, heads)
+        if shape is None or queries.shape[0] != mesh.shape["ht"] * (WIN // 2) or queries.shape[1] != mesh.shape["wt"] * (WIN // 4):
+            placed = (P("ht", "wt", None),) * 3 + (P(None, "ht", "wt", None),) * 2 + (P(), P())
+            return jax.shard_map(
+                shards, mesh=mesh, in_specs=placed, out_specs=P("ht", "wt", None), check_vma=False
+            )(queries, *rest)
+        devices = mesh.devices.reshape(shape[0], shape[2], shape[1])
+        split = Mesh(devices, ("ht", "far", "near"))
+        tile = P("ht", ("far", "near"), None)
+        past = P(None, "ht", ("far", "near"), None)
+        return jax.shard_map(
+            functools.partial(head_shards, shape),
+            mesh=split,
+            in_specs=(tile, tile, tile, past, past, P(), P()),
+            out_specs=tile,
+            check_vma=False,
+        )(queries, *rest)
+
+    return program

time: 166 us -> 70 us (0.42)
  the two profiles are of different devices: /device:TPU:6 before, /device:TPU:0 now
where the time goes in v1:
time: 70 us; the launch traced here: 69.5 us
  blocking collectives  23.6 us (34%)
  waiting for transfers between devices  15.8 us (23%)
  starting transfers between devices  15.3 us (22%)
  Pallas kernels  13 us (19%)
  local copies, waits for them, and re-layouts  1.57 us (2%)
    all_to_all x2, blocking collectives, exchange(): return lax.all_to_all(x, group, split_axis=0, concat_axis=0, tiled=True)  23.6 us
    ppermute x4, starting transfers between devices, halo(): return (lax.ppermute(x, 'far', up), lax.ppermute(x, 'far', down))  11.7 us
    pallas_call x1, Pallas kernels, head_shards(): pl.pallas_call(functools.partial(attend_kernel, group_rows, group_cols, t...  10.4 us
    ppermute x4, waiting for transfers between devices, halo(): return (lax.ppermute(x, 'far', up), lax.ppermute(x, 'far', down))  10.2 us
    all_to_all x1, waiting for transfers between devices, exchange(): return lax.all_to_all(x, group, split_axis=0, concat_axis=0, tiled=True)  5.68 us
    all_to_all x1, starting transfers between devices, exchange(): return lax.all_to_all(x, group, split_axis=0, concat_axis=0, tiled=True)  3.55 us
    pallas_call x1, Pallas kernels, head_shards(): pl.pallas_call(functools.partial(pack_kernel, heads), out_shape=(jax.Shap...  2.56 us
  transfers between devices with their start and end apart: 5, of which 3 were waited for; matrix products, arithmetic and copies ran while one was open for 1% of the time, Pallas kernels for 0%

profile of v1, /device:TPU:0, one launch (start us, length us, event | category | flops | bytes accessed | tf_op | source)
XLA Modules:
  0.0 69.5 jit_solution(12386668252627582522)
XLA Ops:
  0.0 0.0 copy-start
  0.0 2.6 %shard_map.73 = (bf16[8,2,16,8,128]{4,3,2,1,0:T(8,128)(2,1)}, bf16[8,3,16,8,128]{4,3,2,1,0:T(8,128)(2,1)}) custom-call(bf16[16,8,1024]{2,1,0:T(8,128)(2,1)} %q_ref.1, bf16[16,8,1024]{2,1,0:T(8,128)(2,1)} %kn_ref.1, bf16[16,8,1024]{2,1,0:T(8,128)(2,1)} %vn_ref.1, bf16[1,16,8,1024]{3,2,1,0:T(8,128)(2,1)} %kc_ref.1, bf16[1,16,8,1024]{3,2,1,0:T(8,128)(2,1)} %vc_ref.1), custom_call_target="tpu_custom_call" | custom-call | tf_op jit(solution)/shard_map/pallas_call | solution.py:294
  2.6 14.0 %all_to_all.15.refs_0_ = bf16[8,2,16,8,128]{4,3,2,1,0:T(8,128)(2,1)S(1)} all-to-all(bf16[8,2,16,8,128]{4,3,2,1,0:T(8,128)(2,1)} %get-tuple-element.9), channel_id=1, replica_groups=mesh['ht'=4,'far'=4,'near'=2] {'ht','near'}, dimensions={0} | all-to-all | bytes 1048576 | tf_op jit(solution)/shard_map/all_to_all | solution.py:305
  16.6 3.5 %all-to-all-start.1 = ((bf16[8,3,16,8,128]{4,3,2,1,0:T(8,128)(2,1)}), bf16[8,3,16,8,128]{4,3,2,1,0:T(8,128)(2,1)S(1)}, u32[]{:S(2)}, u32[]{:S(2)}) async-start(bf16[8,3,16,8,128]{4,3,2,1,0:T(8,128)(2,1)} %get-tuple-element.10), calls=%async_computation.1 | async-start | bytes 1572864 | tf_op jit(solution)/shard_map/all_to_all | solution.py:305
  20.1 0.1 add_convert_fusion
  20.2 1.3 %collective-permute-start.1 = (bf16[8,2,16,8,128]{4,3,2,1,0:T(8,128)(2,1)S(1)}, bf16[8,2,16,8,128]{4,3,2,1,0:T(8,128)(2,1)S(1)}, u32[]{:S(2)}, u32[]{:S(2)}) collective-permute-start(bf16[8,2,16,8,128]{4,3,2,1,0:T(8,128)(2,1)S(1)} %all_to_all.15.refs_0_), channel_id=1, source_target_pairs={{2,0},{4,2},{6,4},{3,1},{5,3},{7,5},{10,8},{12,10},{14,12},{11,9},... | collective-permute-start | bytes 1572872 | tf_op jit(solution)/shard_map/ppermute | solution.py:311
  21.5 4.6 %collective-permute-start = (bf16[8,2,16,8,128]{4,3,2,1,0:T(8,128)(2,1)S(1)}, bf16[8,2,16,8,128]{4,3,2,1,0:T(8,128)(2,1)S(1)}, u32[]{:S(2)}, u32[]{:S(2)}) collective-permute-start(bf16[8,2,16,8,128]{4,3,2,1,0:T(8,128)(2,1)S(1)} %all_to_all.15.refs_0_), channel_id=1, source_target_pairs={{0,2},{2,4},{4,6},{1,3},{3,5},{5,7},{8,10},{10,12},{12,14},{9,11},... | collective-permute-start | bytes 1572872 | tf_op jit(solution)/shard_map/ppermute | solution.py:311
  26.1 5.7 %all-to-all-done.1 = bf16[8,3,16,8,128]{4,3,2,1,0:T(8,128)(2,1)S(1)} async-done(((bf16[8,3,16,8,128]{4,3,2,1,0:T(8,128)(2,1)}), bf16[8,3,16,8,128]{4,3,2,1,0:T(8,128)(2,1)S(1)}, u32[]{:S(2)}, u32[]{:S(2)}) %all-to-all-start.1) | async-done | bytes 786464 | tf_op jit(solution)/shard_map/all_to_all | solution.py:305
  31.8 1.3 %collective-permute-start.3 = (bf16[8,2,16,8,128]{4,3,2,1,0:T(8,128)(2,1)S(1)}, bf16[8,2,16,8,128]{4,3,2,1,0:T(8,128)(2,1)S(1)}, u32[]{:S(2)}, u32[]{:S(2)}) collective-permute-start(bf16[8,2,16,8,128]{4,3,2,1,0:T(8,128)(2,1)S(1)} %slice.9.refs_3_), channel_id=1, source_target_pairs={{2,0},{4,2},{6,4},{3,1},{5,3},{7,5},{10,8},{12,10},{14,12},{11,9},... | collective-permute-start | bytes 1572872 | tf_op jit(solution)/shard_map/ppermute | solution.py:311
  33.1 4.6 %collective-permute-start.2 = (bf16[8,2,16,8,128]{4,3,2,1,0:T(8,128)(2,1)S(1)}, bf16[8,2,16,8,128]{4,3,2,1,0:T(8,128)(2,1)S(1)}, u32[]{:S(2)}, u32[]{:S(2)}) collective-permute-start(bf16[8,2,16,8,128]{4,3,2,1,0:T(8,128)(2,1)S(1)} %slice.9.refs_3_), channel_id=1, source_target_pairs={{0,2},{2,4},{4,6},{1,3},{3,5},{5,7},{8,10},{10,12},{12,14},{9,11},... | collective-permute-start | bytes 1572872 | tf_op jit(solution)/shard_map/ppermute | solution.py:311
  37.7 0.8 %dynamic-slice_bitcast_fusion.bias_ref = f32[1,128]{1,0:T(1,128)S(1)} fusion(f32[1024]{0:T(1024)} %param.13, s32[]{:T(128)S(6)} %select_n.4), kind=kLoop, calls=%fused_computation.4 | loop fusion | bytes 1028 | tf_op jit(solution)/shard_map/dynamic_slice | solution.py:328
  38.5 0.1 pad_add_fusion.info_ref
  38.5 0.0 copy-done
  38.6 0.0 collective-permute-done.1.refs_2_
  38.6 0.0 collective-permute-done.refs_1_
  38.6 9.0 %collective-permute-done.3.refs_5_ = bf16[8,2,16,8,128]{4,3,2,1,0:T(8,128)(2,1)S(1)} collective-permute-done((bf16[8,2,16,8,128]{4,3,2,1,0:T(8,128)(2,1)S(1)}, bf16[8,2,16,8,128]{4,3,2,1,0:T(8,128)(2,1)S(1)}, u32[]{:S(2)}, u32[]{:S(2)}) %collective-permute-start.3) | collective-permute-done | bytes 524320 | tf_op jit(solution)/shard_map/ppermute | solution.py:311
  47.6 1.2 %collective-permute-done.2.refs_4_ = bf16[8,2,16,8,128]{4,3,2,1,0:T(8,128)(2,1)S(1)} collective-permute-done((bf16[8,2,16,8,128]{4,3,2,1,0:T(8,128)(2,1)S(1)}, bf16[8,2,16,8,128]{4,3,2,1,0:T(8,128)(2,1)S(1)}, u32[]{:S(2)}, u32[]{:S(2)}) %collective-permute-start.2) | collective-permute-done | bytes 524320 | tf_op jit(solution)/shard_map/ppermute | solution.py:311
  48.7 10.4 %shard_map.74 = bf16[8,16,8,128]{3,2,1,0:T(8,128)(2,1)S(1)} custom-call(s32[10]{0:T(128)S(1)} %pad_add_fusion.info_ref, f32[3,3,128]{2,1,0:T(4,128)S(1)} %constant_dynamic-slice_fusion.weight_ref, f32[1,128]{1,0:T(1,128)S(1)} %dynamic-slice_bitcast_fusion.bias_ref, bf16[8,16,8,128]{3,2,1,0:T(8,128)(2,1)S(1)} %slice_bitcast_fusion.q_ref, ...), custom_call_target="tpu_custom_call" | custom-call | tf_op jit(solution)/shard_map/pallas_call | solution.py:329
  59.2 9.6 %all_to_all.16 = bf16[8,16,8,128]{3,2,1,0:T(8,128)(2,1)S(1)} all-to-all(bf16[8,16,8,128]{3,2,1,0:T(8,128)(2,1)S(1)} %shard_map.74), channel_id=1, replica_groups=mesh['ht'=4,'far'=4,'near'=2] {'ht','near'}, dimensions={0} | all-to-all | bytes 524288 | tf_op jit(solution)/shard_map/all_to_all | solution.py:305
  68.8 0.7 %copy_bitcast_fusion = bf16[16,8,1024]{2,1,0:T(8,128)(2,1)} fusion(bf16[8,16,8,128]{3,2,1,0:T(8,128)(2,1)S(1)} %all_to_all.16), kind=kLoop, calls=%fused_computation | loop fusion | bytes 524288 | tf_op jit(solution)/shard_map/reshape | solution.py:337
  (4 shorter events, 0.1 us)
Async XLA Ops:
  0.0 38.5 %copy-start = (f32[3,3,1024]{2,1,0:T(4,128)S(1)}, f32[3,3,1024]{2,1,0:T(4,128)}, u32[]{:S(2)}) copy-start(f32[3,3,1024]{2,1,0:T(4,128)} %param.12) | copy-start | bytes 110596
  16.6 15.2 %all-to-all-start.1 = ((bf16[8,3,16,8,128]{4,3,2,1,0:T(8,128)(2,1)}), bf16[8,3,16,8,128]{4,3,2,1,0:T(8,128)(2,1)S(1)}, u32[]{:S(2)}, u32[]{:S(2)}) async-start(bf16[8,3,16,8,128]{4,3,2,1,0:T(8,128)(2,1)} %get-tuple-element.10), calls=%async_computation.1 | async-start | bytes 1572864 | tf_op jit(solution)/shard_map/all_to_all | solution.py:305
  20.2 18.4 %collective-permute-start.1 = (bf16[8,2,16,8,128]{4,3,2,1,0:T(8,128)(2,1)S(1)}, bf16[8,2,16,8,128]{4,3,2,1,0:T(8,128)(2,1)S(1)}, u32[]{:S(2)}, u32[]{:S(2)}) collective-permute-start(bf16[8,2,16,8,128]{4,3,2,1,0:T(8,128)(2,1)S(1)} %all_to_all.15.refs_0_), channel_id=1, source_target_pairs={{2,0},{4,2},{6,4},{3,1},{5,3},{7,5},{10,8},{12,10},{14,12},{11,9},... | collective-permute-start | bytes 1572872 | tf_op jit(solution)/shard_map/ppermute | solution.py:311
  21.5 17.1 %collective-permute-start = (bf16[8,2,16,8,128]{4,3,2,1,0:T(8,128)(2,1)S(1)}, bf16[8,2,16,8,128]{4,3,2,1,0:T(8,128)(2,1)S(1)}, u32[]{:S(2)}, u32[]{:S(2)}) collective-permute-start(bf16[8,2,16,8,128]{4,3,2,1,0:T(8,128)(2,1)S(1)} %all_to_all.15.refs_0_), channel_id=1, source_target_pairs={{0,2},{2,4},{4,6},{1,3},{3,5},{5,7},{8,10},{10,12},{12,14},{9,11},... | collective-permute-start | bytes 1572872 | tf_op jit(solution)/shard_map/ppermute | solution.py:311
  31.8 15.8 %collective-permute-start.3 = (bf16[8,2,16,8,128]{4,3,2,1,0:T(8,128)(2,1)S(1)}, bf16[8,2,16,8,128]{4,3,2,1,0:T(8,128)(2,1)S(1)}, u32[]{:S(2)}, u32[]{:S(2)}) collective-permute-start(bf16[8,2,16,8,128]{4,3,2,1,0:T(8,128)(2,1)S(1)} %slice.9.refs_3_), channel_id=1, source_target_pairs={{2,0},{4,2},{6,4},{3,1},{5,3},{7,5},{10,8},{12,10},{14,12},{11,9},... | collective-permute-start | bytes 1572872 | tf_op jit(solution)/shard_map/ppermute | solution.py:311
  33.1 15.6 %collective-permute-start.2 = (bf16[8,2,16,8,128]{4,3,2,1,0:T(8,128)(2,1)S(1)}, bf16[8,2,16,8,128]{4,3,2,1,0:T(8,128)(2,1)S(1)}, u32[]{:S(2)}, u32[]{:S(2)}) collective-permute-start(bf16[8,2,16,8,128]{4,3,2,1,0:T(8,128)(2,1)S(1)} %slice.9.refs_3_), channel_id=1, source_target_pairs={{0,2},{2,4},{4,6},{1,3},{3,5},{5,7},{8,10},{10,12},{12,14},{9,11},... | collective-permute-start | bytes 1572872 | tf_op jit(solution)/shard_map/ppermute | solution.py:311

commit v2 on v1

--- a/solution.py
+++ b/solution.py
@@ -6,6 +6,7 @@
 from jax.experimental import pallas as pl
 from jax.experimental.pallas import tpu as pltpu
 from jax.sharding import Mesh, PartitionSpec as P
+
 
 HD = 128
 WIN = 32
@@ -85,7 +86,7 @@
 
 
 def cycle_conv(values_new, conv_weight, conv_bias):
-    tile_rows, tile_cols, channels = values_new.shape
+    tile_rows, tile_cols, _ = values_new.shape
     padded = with_halo(values_new, (("ht", 0), ("wt", 1)), 1)
     return local_conv(padded, conv_weight, conv_bias, tile_rows, tile_cols)
 
@@ -148,10 +149,7 @@
 NEG = -1e30
 VMEM = pl.BlockSpec(memory_space=pltpu.VMEM)
 SMEM = pl.BlockSpec(memory_space=pltpu.SMEM)
-
-
-def index_of(position, shape, dim):
-    return lax.broadcasted_iota(jnp.int32, shape, dim) if position is None else position
+LIMIT = pltpu.CompilerParams(vmem_limit_bytes=48 * 1024 * 1024)
 
 
 def tile_masks(tile_rows, tile_cols):
@@ -163,83 +161,114 @@
     return upper, left
 
 
-def attend_kernel(grid_rows, grid_cols, tile_rows, tile_cols, info_ref, weight_ref, bias_ref, q_ref, *refs):
-    out_ref = refs[-1]
-    frames = [refs[3 * f : 3 * f + 3] for f in range((len(refs) - 1) // 3)]
-    size = tile_rows * tile_cols
-    scale = HD ** (-0.5) * LOG2E
-    bias_left = jnp.where(info_ref[0] > 0, 0.0, NEG).astype(jnp.float32)
-    bias_right = jnp.where(info_ref[1] > 0, 0.0, NEG).astype(jnp.float32)
-    upper, left = tile_masks(tile_rows, tile_cols)
-    upper_one = upper.astype(jnp.float32).astype(jnp.bfloat16)
-    left_one = left.astype(jnp.float32).astype(jnp.bfloat16)
-    lower_one = 1 - upper_one
-    right_one = 1 - left_one
-    ones = jnp.ones((size, HD), jnp.bfloat16)
-
-    def slot(row, col):
-        return info_ref[2 + row * grid_cols + col]
-
-    def tile(frame, part, row, col):
-        side = 1 if col < 0 else (2 if col >= grid_cols else 0)
-        return frames[frame][side][slot(row, col % grid_cols), part].reshape(size, HD)
-
-    def piece(row, col):
-        query = q_ref[slot(row, col)].reshape(size, HD)
-
-        def score(frame, key_row, key_col):
-            raw = lax.dot_general(
-                query, tile(frame, 0, key_row, key_col), (((1,), (1,)), ((), ())),
-                preferred_element_type=jnp.float32,
-            )
-            if key_col < 0:
-                raw = raw + bias_left
-            elif key_col >= grid_cols:
-                raw = raw + bias_right
-            return raw
-
-        up, down = row > 0, row + 1 < grid_rows
+class Window:
+    def __init__(self, grid, tile, info_ref, q_ref, sides):
+        self.grid_rows, self.grid_cols = grid
+        self.tile_rows, self.tile_cols = tile
+        self.size = self.tile_rows * self.tile_cols
+        self.info, self.q, self.sides = info_ref, q_ref, sides
+        self.scale = HD ** (-0.5) * LOG2E
+        self.bias_left = jnp.where(info_ref[0] > 0, 0.0, NEG).astype(jnp.float32)
+        self.bias_right = jnp.where(info_ref[1] > 0, 0.0, NEG).astype(jnp.float32)
+        self.upper, self.left = tile_masks(self.tile_rows, self.tile_cols)
+        self.upper_one = self.upper.astype(jnp.float32).astype(jnp.bfloat16)
+        self.left_one = self.left.astype(jnp.float32).astype(jnp.bfloat16)
+        self.ones = jnp.ones((self.size, HD), jnp.bfloat16)
+
+    def slot(self, row, col):
+        return self.info[2 + row * self.grid_cols + col]
+
+    def side(self, col):
+        return 1 if col < 0 else (2 if col >= self.grid_cols else 0)
+
+    def tile(self, frame, part, row, col):
+        ref = self.sides[frame][self.side(col)]
+        return ref[self.slot(row, col % self.grid_cols), part].reshape(self.size, HD)
+
+    def score(self, query, frame, row, col):
+        raw = lax.dot_general(
+            query, self.tile(frame, 0, row, col), (((1,), (1,)), ((), ())),
+            preferred_element_type=jnp.float32,
+        )
+        if self.side(col) == 1:
+            raw = raw + self.bias_left
+        elif self.side(col) == 2:
+            raw = raw + self.bias_right
+        return raw
+
+    def attend(self, row, col, wanted):
+        query = self.q[self.slot(row, col)].reshape(self.size, HD)
+        up, down = row > 0, row + 1 < self.grid_rows
 
         def beside(frame, key_col):
             if up and down:
-                return jnp.where(upper, score(frame, row - 1, key_col), score(frame, row + 1, key_col))
+                above = self.score(query, frame, row - 1, key_col)
+                return jnp.where(self.upper, above, self.score(query, frame, row + 1, key_col))
             if down:
-                return jnp.where(upper, NEG, score(frame, row + 1, key_col))
-            return jnp.where(upper, score(frame, row - 1, key_col), NEG)
+                return jnp.where(self.upper, NEG, self.score(query, frame, row + 1, key_col))
+            return jnp.where(self.upper, self.score(query, frame, row - 1, key_col), NEG)
+
+        def level(frame, key_col):
+            return self.score(query, frame, row, key_col)
 
         blocks = []
-        for frame in range(len(frames)):
-            for step in (-1, 0, 1):
-                blocks.append((frame, False, step, score(frame, row, col + step)))
-                blocks.append((frame, True, step, beside(frame, col + step)))
-            blocks.append((frame, False, 2, jnp.where(left, score(frame, row, col - 2), score(frame, row, col + 2))))
-            blocks.append((frame, True, 2, jnp.where(left, beside(frame, col - 2), beside(frame, col + 2))))
+        for frame, step in wanted:
+            for off_row, make in ((False, level), (True, beside)):
+                if off_row and not (up or down):
+                    continue
+                if step == 2:
+                    raw = jnp.where(self.left, make(frame, col - 2), make(frame, col + 2))
+                else:
+                    raw = make(frame, col + step)
+                blocks.append((frame, off_row, step, raw))
         top = blocks[0][3]
         for entry in blocks[1:]:
             top = jnp.maximum(top, entry[3])
-        top = jnp.max(top, axis=1, keepdims=True)
-        total = jnp.zeros((size, 2 * HD), jnp.float32)
+        return blocks, jnp.max(top, axis=1, keepdims=True)
+
+    def weigh(self, row, col, blocks, top):
+        up, down = row > 0, row + 1 < self.grid_rows
+        total = jnp.zeros((self.size, 2 * HD), jnp.float32)
         for frame, off_row, step, raw in blocks:
-            weights = jnp.exp2((raw - top) * scale).astype(jnp.bfloat16)
+            weights = jnp.exp2((raw - top) * self.scale).astype(jnp.bfloat16)
             if off_row and up and down:
-                by_row = [(row - 1, weights * upper_one), (row + 1, weights * lower_one)]
+                by_row = [(row - 1, weights * self.upper_one), (row + 1, weights * (1 - self.upper_one))]
             elif off_row:
                 by_row = [(row + 1 if down else row - 1, weights)]
             else:
                 by_row = [(row, weights)]
-            parts = []
             for key_row, part in by_row:
                 if step == 2:
-                    parts.append((key_row, col - 2, part * left_one))
-                    parts.append((key_row, col + 2, part * right_one))
+                    pair = [(col - 2, part * self.left_one), (col + 2, part * (1 - self.left_one))]
                 else:
-                    parts.append((key_row, col + step, part))
-            for key_row, key_col, part in parts:
-                wide = jnp.concatenate([tile(frame, 1, key_row, key_col), ones], axis=1)
-                total = total + jnp.dot(part, wide, preferred_element_type=jnp.float32)
-        return total[:, :HD] / total[:, HD:]
-
-    last = len(frames) - 1
+                    pair = [(col + step, part)]
+                for key_col, one in pair:
+                    wide = jnp.concatenate([self.tile(frame, 1, key_row, key_col), self.ones], axis=1)
+                    total = total + jnp.dot(one, wide, preferred_element_type=jnp.float32)
+        return total
+
+    def inner_steps(self, col):
+        near = [step for step in (-1, 0, 1) if 0 <= col + step < self.grid_cols]
+        return near, [step for step in (-1, 0, 1, 2) if step not in near]
+
+
+def early_kernel(grid, tile, info_ref, q_ref, c_ref, cl_ref, cr_ref, n_ref, sum_ref, top_ref):
+    window = Window(grid, tile, info_ref, q_ref, [[c_ref, cl_ref, cr_ref], [n_ref, None, None]])
+    for row in range(grid[0]):
+        for col in range(grid[1]):
+            near, _ = window.inner_steps(col)
+            wanted = [(0, step) for step in (-1, 0, 1, 2)] + [(1, step) for step in near]
+            blocks, top = window.attend(row, col, wanted)
+            sum_ref[row * grid[1] + col] = window.weigh(row, col, blocks, top)
+            top_ref[row * grid[1] + col] = jnp.broadcast_to(top, (window.size, HD))
+
+
+def late_kernel(
+    grid, tile, info_ref, weight_ref, bias_ref, q_ref, n_ref, nl_ref, nr_ref, sum_ref, top_ref, out_ref
+):
+    window = Window(grid, tile, info_ref, q_ref, [None, [n_ref, nl_ref, nr_ref]])
+    grid_rows, grid_cols = grid
+    tile_rows, tile_cols = tile
     sub = lax.broadcasted_iota(jnp.int32, (tile_cols, HD), 0)
     taps = [[weight_ref[a, pl.ds(b, 1), :] for b in range(3)] for a in range(3)]
 
@@ -252,12 +281,14 @@
                 continue
 
             def values(key_col):
-                side = 1 if key_col < 0 else (2 if key_col >= grid_cols else 0)
-                return frames[last][side][slot(tile_row, key_col % grid_cols), 1, line].astype(jnp.float32)
+                ref = window.sides[1][window.side(key_col)]
+                return ref[window.slot(tile_row, key_col % grid_cols), 1, line].astype(jnp.float32)
 
             here, before, after = values(col), values(col - 1), values(col + 1)
             low = jnp.where(sub == 0, pltpu.roll(before, 1, 0), pltpu.roll(here, 1, 0))
-            high = jnp.where(sub == tile_cols - 1, pltpu.roll(after, tile_cols - 1, 0), pltpu.roll(here, tile_cols - 1, 0))
+            high = jnp.where(
+                sub == tile_cols - 1, pltpu.roll(after, tile_cols - 1, 0), pltpu.roll(here, tile_cols - 1, 0)
+            )
             lines.append((low, here, high))
         sums = []
         for line in range(tile_rows):
@@ -271,38 +302,67 @@
 
     for row in range(grid_rows):
         for col in range(grid_cols):
-            attended = piece(row, col).reshape(tile_rows, tile_cols, HD)
-            out_ref[slot(row, col)] = (attended + enhanced(row, col)).astype(jnp.bfloat16)
-
-
-def pack_kernel(heads, q_ref, kn_ref, vn_ref, kc_ref, vc_ref, first_ref, second_ref):
-    for head in range(heads):
-        lanes = pl.ds(head * HD, HD)
-        first_ref[head, 0] = kc_ref[0, :, :, lanes]
-        first_ref[head, 1] = vc_ref[0, :, :, lanes]
-        second_ref[head, 0] = kn_ref[:, :, lanes]
-        second_ref[head, 1] = vn_ref[:, :, lanes]
-        second_ref[head, 2] = q_ref[:, :, lanes]
-
-
-def head_shards(shape, queries, keys_new, values_new, keys_cache, values_cache, conv_weight, conv_bias):
+            _, wanted = window.inner_steps(col)
+            blocks, top = window.attend(row, col, [(1, step) for step in wanted])
+            before = top_ref[row * grid_cols + col][:, :1]
+            best = jnp.maximum(top, before)
+            total = window.weigh(row, col, blocks, best)
+            total = total + sum_ref[row * grid_cols + col] * jnp.exp2((before - best) * window.scale)
+            attended = (total[:, :HD] / total[:, HD:]).reshape(tile_rows, tile_cols, HD)
+            place = info_ref[2 + grid_rows * grid_cols + row * grid_cols + col]
+            out_ref[place // 2, place % 2] = (attended + enhanced(row, col)).astype(jnp.bfloat16)
+
+
+def lanes(head):
+    return pl.ds(pl.multiple_of(head * HD, HD), HD)
+
+
+def pack_kernel(members, flips, side, me_ref, *refs):
+    sources, buffers = refs[:members], refs[members:]
+    for buffer, flip in zip(buffers, flips):
+        for other in range(2):
+            head = me_ref[0] ^ (flip ^ (side if other else 0))
+            for member, source in enumerate(sources):
+                buffer[other, member] = source[:, :, lanes(head)]
+
+
+def unpack_kernel(flips, side, me_ref, *refs):
+    out_ref, beside_ref = refs[-1], refs[-2]
+    for i, flip in enumerate(flips):
+        out_ref[:, :, lanes(me_ref[0] ^ flip)] = refs[i][0]
+        out_ref[:, :, lanes(me_ref[0] ^ (flip ^ side))] = beside_ref[i]
+
+
+def head_step(shape, queries, keys_new, values_new, keys_cache, values_cache, conv_weight, conv_bias):
     group_rows, group_cols, far = shape
     tile_rows, tile_cols, channels = queries.shape
     heads = channels // HD
-    group = ("ht", "near")
+    grid, tile = (group_rows, group_cols), (tile_rows, tile_cols)
+    axes = ("ht", "near")
     block = (tile_rows, tile_cols, HD)
-    first, second = pl.pallas_call(
-        functools.partial(pack_kernel, heads),
-        out_shape=(
-            jax.ShapeDtypeStruct((heads, 2) + block, jnp.bfloat16),
-            jax.ShapeDtypeStruct((heads, 3) + block, jnp.bfloat16),
-        ),
-        in_specs=[VMEM] * 5,
-        out_specs=(VMEM, VMEM),
-    )(queries, keys_new, values_new, keys_cache, values_cache)
-
-    def exchange(x):
-        return lax.all_to_all(x, group, split_axis=0, concat_axis=0, tiled=True)
+    side = group_cols
+    flips = [flip for flip in range(heads) if not flip & side]
+    me = lax.axis_index("ht") * group_cols + lax.axis_index("near")
+    me = me.astype(jnp.int32)
+    me_ref = me.reshape(1)
+
+    def swap(x, flip):
+        return lax.ppermute(x, axes, [(s, s ^ flip) for s in range(heads)])
+
+    def pack(*arrays):
+        return pl.pallas_call(
+            functools.partial(pack_kernel, len(arrays), flips, side),
+            out_shape=[jax.ShapeDtypeStruct((2, len(arrays)) + block, jnp.bfloat16)] * len(flips),
+            in_specs=[SMEM] + [VMEM] * len(arrays),
+            out_specs=[VMEM] * len(flips),
+            cost_estimate=pl.CostEstimate(flops=0, bytes_accessed=len(arrays) << 20, transcendentals=0),
+        )(me_ref, *arrays)
+
+    def gather(buffers):
+        got = [buffers[0]] + [swap(b, flip) for b, flip in zip(buffers[1:], flips[1:])]
+        forward = jnp.stack([b[1] for b in got])
+        beside = swap(forward, side)
+        return jnp.concatenate([jnp.stack([b[0] for b in got]), beside], axis=0)
 
     up = [(i, i + 1) for i in range(far - 1)]
     down = [(i + 1, i) for i in range(far - 1)]
@@ -310,31 +370,54 @@
     def halo(x):
         return lax.ppermute(x, "far", up), lax.ppermute(x, "far", down)
 
-    cached = exchange(first)
+    packed_cached = pack(keys_cache[0], values_cache[0])
+    packed_current = pack(keys_new, values_new, queries)
+    cached = gather(packed_cached)
     cached_left, cached_right = halo(cached)
-    second, _ = lax.optimization_barrier((second, cached))
-    current = exchange(second)
+    current = gather(packed_current)
     new, query = current[:, :2], current[:, 2]
     new_left, new_right = halo(new)
     far_index = lax.axis_index("far")
-    head = lax.axis_index("ht") * group_cols + lax.axis_index("near")
+    flip = me ^ jnp.arange(heads, dtype=jnp.int32)
+    beside = (flip // side) % 2
+    order = flip % side + flip // (2 * side) * side
     info = jnp.concatenate(
         [
             jnp.stack([far_index > 0, far_index < far - 1]).astype(jnp.int32),
-            jnp.arange(heads, dtype=jnp.int32),
+            beside * len(flips) + order,
+            order * 2 + beside,
         ]
     )
-    weight = lax.dynamic_slice_in_dim(conv_weight, head * HD, HD, 2)
-    bias = lax.dynamic_slice_in_dim(conv_bias.reshape(1, channels), head * HD, HD, 1)
+    weight = lax.dynamic_slice_in_dim(conv_weight, me * HD, HD, 2)
+    bias = lax.dynamic_slice_in_dim(conv_bias.reshape(1, channels), me * HD, HD, 1)
+    size = tile_rows * tile_cols
+    sums, tops = pl.pallas_call(
+        functools.partial(early_kernel, grid, tile),
+        out_shape=(
+            jax.ShapeDtypeStruct((heads, size, 2 * HD), jnp.float32),
+            jax.ShapeDtypeStruct((heads, size, HD), jnp.float32),
+        ),
+        in_specs=[SMEM] + [VMEM] * 5,
+        out_specs=(VMEM, VMEM),
+        compiler_params=LIMIT,
+        cost_estimate=pl.CostEstimate(flops=2**32, bytes_accessed=2**22, transcendentals=2**21),
+    )(info, query, cached, cached_left, cached_right, new)
     result = pl.pallas_call(
-        functools.partial(attend_kernel, group_rows, group_cols, tile_rows, tile_cols),
-        out_shape=jax.ShapeDtypeStruct((heads,) + block, jnp.bfloat16),
-        in_specs=[SMEM] + [VMEM] * 9,
+        functools.partial(late_kernel, grid, tile),
+        out_shape=jax.ShapeDtypeStruct((len(flips), 2) + block, jnp.bfloat16),
+        in_specs=[SMEM] + [VMEM] * 8,
         out_specs=VMEM,
-        compiler_params=pltpu.CompilerParams(vmem_limit_bytes=48 * 1024 * 1024),
-    )(info, weight, bias, query, cached, cached_left, cached_right, new, new_left, new_right)
-    returned = exchange(result)
-    return returned.transpose(1, 2, 0, 3).reshape(tile_rows, tile_cols, channels)
+        compiler_params=LIMIT,
+        cost_estimate=pl.CostEstimate(flops=2**30, bytes_accessed=2**22, transcendentals=2**19),
+    )(info, weight, bias, query, new, new_left, new_right, sums, tops)
+    got = [result[0]] + [swap(result[i], flips[i]) for i in range(1, len(flips))]
+    other = swap(jnp.stack([b[1] for b in got]), side)
+    return pl.pallas_call(
+        functools.partial(unpack_kernel, flips, side),
+        out_shape=jax.ShapeDtypeStruct(queries.shape, jnp.bfloat16),
+        in_specs=[SMEM] + [VMEM] * (len(flips) + 1),
+        out_specs=VMEM,
+    )(me_ref, *got, other)
 
 
 def grouping(mesh, heads):
@@ -359,12 +442,13 @@
         split = Mesh(devices, ("ht", "far", "near"))
         tile = P("ht", ("far", "near"), None)
         past = P(None, "ht", ("far", "near"), None)
-        return jax.shard_map(
-            functools.partial(head_shards, shape),
+        step = jax.shard_map(
+            functools.partial(head_step, shape),
             mesh=split,
             in_specs=(tile, tile, tile, past, past, P(), P()),
             out_specs=tile,
             check_vma=False,
-        )(queries, *rest)
+        )
+        return step(queries, *rest)
 
     return program

time: 70 us -> 71.6 us (1.023)
  blocking collectives: 23.6 us -> 0 us
  waiting for transfers between devices: 15.8 us -> 24.5 us
  starting transfers between devices: 15.3 us -> 22.9 us
  Pallas kernels: 13 us -> 18 us
  local copies, waits for them, and re-layouts: 1.57 us -> 5.16 us
    all_to_all x2 -> x0, blocking collectives: 23.6 us -> none  [exchange(): return lax.all_to_all(x, group, split_axis=0, concat_axis=0, tiled=True)]
    ppermute x0 -> x12, waiting for transfers between devices: none -> 12.2 us  [swap(): return lax.ppermute(x, axes, [(s, s ^ flip) for s in range(heads)])]
    ppermute x0 -> x12, starting transfers between devices: none -> 12 us  [swap(): return lax.ppermute(x, axes, [(s, s ^ flip) for s in range(heads)])]
    all_to_all x1 -> x0, waiting for transfers between devices: 5.68 us -> none  [exchange(): return lax.all_to_all(x, group, split_axis=0, concat_axis=0, tiled=True)]
    pallas_call x2 -> x5, Pallas kernels: 13 us -> 18 us  [the longest x1 7.42 us: head_step(): pl.pallas_call(functools.partial(early_kernel, grid, tile), out_shape=(ja...]
    all_to_all x1 -> x0, starting transfers between devices: 3.55 us -> none  [exchange(): return lax.all_to_all(x, group, split_axis=0, concat_axis=0, tiled=True)]
    unnamed x2 -> x16, local copies, waits for them, and re-layouts: 0.01 us -> 2.71 us
    ppermute x4, waiting for transfers between devices: 10.2 us -> 12.3 us  [halo(): return (lax.ppermute(x, 'far', up), lax.ppermute(x, 'far', down))]
  transfers between devices with their start and end apart: 5 -> 16, of which waited for: 3 -> 10; matrix products, arithmetic and copies ran while one was open for 1% -> 2% of each run, Pallas kernels for 0% -> 14%
where the time goes in v2:
time: 71.6 us; the launch traced here: 71.1 us
  waiting for transfers between devices  24.5 us (34%)
  starting transfers between devices  22.9 us (32%)
  Pallas kernels  18 us (25%)
  local copies, waits for them, and re-layouts  5.16 us (7%)
    ppermute x4, waiting for transfers between devices, halo(): return (lax.ppermute(x, 'far', up), lax.ppermute(x, 'far', down))  12.3 us
    ppermute x12, waiting for transfers between devices, swap(): return lax.ppermute(x, axes, [(s, s ^ flip) for s in range(heads)])  12.2 us
    ppermute x12, starting transfers between devices, swap(): return lax.ppermute(x, axes, [(s, s ^ flip) for s in range(heads)])  12 us
    ppermute x4, starting transfers between devices, halo(): return (lax.ppermute(x, 'far', up), lax.ppermute(x, 'far', down))  10.9 us
    pallas_call x1, Pallas kernels, head_step(): pl.pallas_call(functools.partial(early_kernel, grid, tile), out_shape=(ja...  7.42 us
    pallas_call x1, Pallas kernels, head_step(): pl.pallas_call(functools.partial(late_kernel, grid, tile), out_shape=jax....  4.61 us
    pallas_call x2, Pallas kernels, pack(): pl.pallas_call(functools.partial(pack_kernel, len(arrays), flips, side),...  4.21 us
    unnamed x16, local copies, waits for them, and re-layouts  2.71 us
  transfers between devices with their start and end apart: 16, of which 10 were waited for; matrix products, arithmetic and copies ran while one was open for 2% of the time, Pallas kernels for 14%

profile of v2, /device:TPU:0, one launch (start us, length us, event | category | flops | bytes accessed | tf_op | source)
XLA Modules:
  0.0 71.1 jit_solution(6227664792860959867)
XLA Ops:
  0.0 2.0 %shard_map.74 = (bf16[2,2,16,8,128]{4,3,2,1,0:T(8,128)(2,1)}, bf16[2,2,16,8,128]{4,3,2,1,0:T(8,128)(2,1)}, bf16[2,2,16,8,128]{4,3,2,1,0:T(8,128)(2,1)}, bf16[2,2,16,8,128]{4,3,2,1,0:T(8,128)(2,1)}) custom-call(s32[1]{0:T(128)} %bitcast.me_ref, bf16[16,8,1024]{2,1,0:T(8,128)(2,1)} %bitcast.19, bf16[16,8,1024]{2,1,0:T(8,128)(2,1)} %bitcast.20), custom_call_target="tpu_custom_call" | custom-call | bytes 2097152 | tf_op jit(solution)/shard_map/pallas_call | solution.py:353
  2.0 3.0 %collective-permute-start.6 = (bf16[2,2,16,8,128]{4,3,2,1,0:T(8,128)(2,1)}, bf16[2,2,16,8,128]{4,3,2,1,0:T(8,128)(2,1)S(1)}, u32[]{:S(2)}, u32[]{:S(2)}) collective-permute-start(bf16[2,2,16,8,128]{4,3,2,1,0:T(8,128)(2,1)} %get-tuple-element.20), channel_id=1, source_target_pairs={{0,1},{1,0},{8,9},{9,8},{16,17},{17,16},{24,25},{25,24},{2,3},{3,2... | collective-permute-start | bytes 393224 | tf_op jit(solution)/shard_map/ppermute | solution.py:350
  5.0 1.5 %collective-permute-start.7 = (bf16[2,2,16,8,128]{4,3,2,1,0:T(8,128)(2,1)}, bf16[2,2,16,8,128]{4,3,2,1,0:T(8,128)(2,1)S(1)}, u32[]{:S(2)}, u32[]{:S(2)}) collective-permute-start(bf16[2,2,16,8,128]{4,3,2,1,0:T(8,128)(2,1)} %get-tuple-element.21), channel_id=1, source_target_pairs={{0,16},{1,17},{8,24},{9,25},{16,0},{17,1},{24,8},{25,9},{2,18},{3,... | collective-permute-start | bytes 393224 | tf_op jit(solution)/shard_map/ppermute | solution.py:350
  6.5 2.2 %shard_map.73 = (bf16[2,3,16,8,128]{4,3,2,1,0:T(8,128)(2,1)}, bf16[2,3,16,8,128]{4,3,2,1,0:T(8,128)(2,1)}, bf16[2,3,16,8,128]{4,3,2,1,0:T(8,128)(2,1)}, bf16[2,3,16,8,128]{4,3,2,1,0:T(8,128)(2,1)}) custom-call(s32[1]{0:T(128)} %bitcast.me_ref, bf16[16,8,1024]{2,1,0:T(8,128)(2,1)} %refs_0_.1, bf16[16,8,1024]{2,1,0:T(8,128)(2,1)} %refs_1_.1, ...), custom_call_target="tpu_custom_call" | custom-call | bytes 3145728 | tf_op jit(solution)/shard_map/pallas_call | solution.py:353
  8.7 2.0 %collective-permute-start = (bf16[2,3,16,8,128]{4,3,2,1,0:T(8,128)(2,1)}, bf16[2,3,16,8,128]{4,3,2,1,0:T(8,128)(2,1)S(1)}, u32[]{:S(2)}, u32[]{:S(2)}) collective-permute-start(bf16[2,3,16,8,128]{4,3,2,1,0:T(8,128)(2,1)} %get-tuple-element.16), channel_id=1, source_target_pairs={{0,1},{1,0},{8,9},{9,8},{16,17},{17,16},{24,25},{25,24},{2,3},{3,2... | collective-permute-start | bytes 589832 | tf_op jit(solution)/shard_map/ppermute | solution.py:350
  10.7 1.5 %collective-permute-start.1 = (bf16[2,3,16,8,128]{4,3,2,1,0:T(8,128)(2,1)}, bf16[2,3,16,8,128]{4,3,2,1,0:T(8,128)(2,1)S(1)}, u32[]{:S(2)}, u32[]{:S(2)}) collective-permute-start(bf16[2,3,16,8,128]{4,3,2,1,0:T(8,128)(2,1)} %get-tuple-element.17), channel_id=1, source_target_pairs={{0,16},{1,17},{8,24},{9,25},{16,0},{17,1},{24,8},{25,9},{2,18},{3,... | collective-permute-start | bytes 589832 | tf_op jit(solution)/shard_map/ppermute | solution.py:350
  12.3 0.8 %copy-done.7 = bf16[2,3,16,8,128]{4,3,2,1,0:T(8,128)(2,1)S(1)} copy-done((bf16[2,3,16,8,128]{4,3,2,1,0:T(8,128)(2,1)S(1)}, bf16[2,3,16,8,128]{4,3,2,1,0:T(8,128)(2,1)}, u32[]{:S(2)}) %copy-start.7) | copy-done | bytes 196632
  13.7 4.5 %collective-permute-done = bf16[2,3,16,8,128]{4,3,2,1,0:T(8,128)(2,1)S(1)} collective-permute-done((bf16[2,3,16,8,128]{4,3,2,1,0:T(8,128)(2,1)}, bf16[2,3,16,8,128]{4,3,2,1,0:T(8,128)(2,1)S(1)}, u32[]{:S(2)}, u32[]{:S(2)}) %collective-permute-start) | collective-permute-done | bytes 196640 | tf_op jit(solution)/shard_map/ppermute | solution.py:350
  18.7 2.4 %collective-permute-done.2 = bf16[2,3,16,8,128]{4,3,2,1,0:T(8,128)(2,1)S(1)} collective-permute-done((bf16[2,3,16,8,128]{4,3,2,1,0:T(8,128)(2,1)S(1)}, bf16[2,3,16,8,128]{4,3,2,1,0:T(8,128)(2,1)S(1)}, u32[]{:S(2)}, u32[]{:S(2)}) %collective-permute-start.2) | collective-permute-done | bytes 196640 | tf_op jit(solution)/shard_map/ppermute | solution.py:350
  21.3 0.8 %dynamic-slice_bitcast_fusion.bias_ref = f32[1,128]{1,0:T(1,128)S(1)} fusion(f32[1024]{0:T(1024)} %param.13, s32[]{:T(128)S(6)} %select_n.27), kind=kLoop, calls=%fused_computation.34 | loop fusion | bytes 1028 | tf_op jit(solution)/shard_map/dynamic_slice | solution.py:392
  22.1 3.7 %collective-permute-start.10 = (bf16[8,2,16,8,128]{4,3,2,1,0:T(8,128)(2,1)S(1)}, bf16[8,2,16,8,128]{4,3,2,1,0:T(8,128)(2,1)S(1)}, u32[]{:S(2)}, u32[]{:S(2)}) collective-permute-start(bf16[8,2,16,8,128]{4,3,2,1,0:T(8,128)(2,1)S(1)} %constant_dynamic-update-slice_fusion.1.c_ref), channel_id=1, source_target_pairs={{0,2},{2,4},{4,6},{1,3},{3,5},{5,7},{8,10},{10,12},{12,14},{9,11},... | collective-permute-start | bytes 1572872 | tf_op jit(solution)/shard_map/ppermute | solution.py:371
  25.8 1.3 %collective-permute-start.11 = (bf16[8,2,16,8,128]{4,3,2,1,0:T(8,128)(2,1)S(1)}, bf16[8,2,16,8,128]{4,3,2,1,0:T(8,128)(2,1)S(1)}, u32[]{:S(2)}, u32[]{:S(2)}) collective-permute-start(bf16[8,2,16,8,128]{4,3,2,1,0:T(8,128)(2,1)S(1)} %constant_dynamic-update-slice_fusion.1.c_ref), channel_id=1, source_target_pairs={{2,0},{4,2},{6,4},{3,1},{5,3},{7,5},{10,8},{12,10},{14,12},{11,9},... | collective-permute-start | bytes 1572872 | tf_op jit(solution)/shard_map/ppermute | solution.py:371
  27.3 4.6 %collective-permute-start.4 = (bf16[8,2,16,8,128]{4,3,2,1,0:T(8,128)(2,1)S(1)}, bf16[8,2,16,8,128]{4,3,2,1,0:T(8,128)(2,1)S(1)}, u32[]{:S(2)}, u32[]{:S(2)}) collective-permute-start(bf16[8,2,16,8,128]{4,3,2,1,0:T(8,128)(2,1)S(1)} %slice.116.n_ref), channel_id=1, source_target_pairs={{0,2},{2,4},{4,6},{1,3},{3,5},{5,7},{8,10},{10,12},{12,14},{9,11},... | collective-permute-start | bytes 1572872 | tf_op jit(solution)/shard_map/ppermute | solution.py:371
  31.9 1.3 %collective-permute-start.5 = (bf16[8,2,16,8,128]{4,3,2,1,0:T(8,128)(2,1)S(1)}, bf16[8,2,16,8,128]{4,3,2,1,0:T(8,128)(2,1)S(1)}, u32[]{:S(2)}, u32[]{:S(2)}) collective-permute-start(bf16[8,2,16,8,128]{4,3,2,1,0:T(8,128)(2,1)S(1)} %slice.116.n_ref), channel_id=1, source_target_pairs={{2,0},{4,2},{6,4},{3,1},{5,3},{7,5},{10,8},{12,10},{14,12},{11,9},... | collective-permute-start | bytes 1572872 | tf_op jit(solution)/shard_map/ppermute | solution.py:371
  33.3 4.8 %collective-permute-done.10.cl_ref = bf16[8,2,16,8,128]{4,3,2,1,0:T(8,128)(2,1)S(1)} collective-permute-done((bf16[8,2,16,8,128]{4,3,2,1,0:T(8,128)(2,1)S(1)}, bf16[8,2,16,8,128]{4,3,2,1,0:T(8,128)(2,1)S(1)}, u32[]{:S(2)}, u32[]{:S(2)}) %collective-permute-start.10) | collective-permute-done | bytes 524320 | tf_op jit(solution)/shard_map/ppermute | solution.py:371
  38.1 4.4 %collective-permute-done.11.cr_ref = bf16[8,2,16,8,128]{4,3,2,1,0:T(8,128)(2,1)S(1)} collective-permute-done((bf16[8,2,16,8,128]{4,3,2,1,0:T(8,128)(2,1)S(1)}, bf16[8,2,16,8,128]{4,3,2,1,0:T(8,128)(2,1)S(1)}, u32[]{:S(2)}, u32[]{:S(2)}) %collective-permute-start.11) | collective-permute-done | bytes 524320 | tf_op jit(solution)/shard_map/ppermute | solution.py:371
  42.5 7.4 %shard_map.75 = (f32[8,128,256]{2,1,0:T(8,128)S(1)}, f32[8,128,128]{2,1,0:T(8,128)S(1)}) custom-call(s32[18]{0:T(128)S(1)} %pad_add_fusion.info_ref, bf16[8,16,8,128]{3,2,1,0:T(8,128)(2,1)S(1)} %slice_bitcast_fusion.q_ref, bf16[8,2,16,8,128]{4,3,2,1,0:T(8,128)(2,1)S(1)} %constant_dynamic-update-slice_fusion.1.c_ref, ...), custom_call_target="tpu_custom_call" | custom-call | flops 4294967296 | bytes 4194304 | tf_op jit(solution)/shard_map/pallas_call | solution.py:394
  50.0 3.0 %collective-permute-done.5.nr_ref = bf16[8,2,16,8,128]{4,3,2,1,0:T(8,128)(2,1)S(1)} collective-permute-done((bf16[8,2,16,8,128]{4,3,2,1,0:T(8,128)(2,1)S(1)}, bf16[8,2,16,8,128]{4,3,2,1,0:T(8,128)(2,1)S(1)}, u32[]{:S(2)}, u32[]{:S(2)}) %collective-permute-start.5) | collective-permute-done | bytes 524320 | tf_op jit(solution)/shard_map/ppermute | solution.py:371
  53.0 4.6 %shard_map.76 = bf16[4,2,16,8,128]{4,3,2,1,0:T(8,128)(2,1)S(1)} custom-call(s32[18]{0:T(128)S(1)} %pad_add_fusion.info_ref, f32[3,3,128]{2,1,0:T(4,128)S(1)} %constant_dynamic-slice_fusion.weight_ref, f32[1,128]{1,0:T(1,128)S(1)} %dynamic-slice_bitcast_fusion.bias_ref, bf16[8,16,8,128]{3,2,1,0:T(8,128)(2,1)S(1)} %slice_bitcast_fusion.q_ref, ...), custom_call_target="tpu_custom_call" | custom-call | flops 1073741824 | bytes 4194304 | tf_op jit(solution)/shard_map/pallas_call | solution.py:405
  57.6 0.6 slice_bitcast_fusion.1
  58.3 1.5 %collective-permute-start.12 = (bf16[2,16,8,128]{3,2,1,0:T(8,128)(2,1)S(1)}, bf16[2,16,8,128]{3,2,1,0:T(8,128)(2,1)S(1)}, u32[]{:S(2)}, u32[]{:S(2)}) collective-permute-start(bf16[2,16,8,128]{3,2,1,0:T(8,128)(2,1)S(1)} %get-tuple-element.27), channel_id=1, source_target_pairs={{0,1},{1,0},{8,9},{9,8},{16,17},{17,16},{24,25},{25,24},{2,3},{3,2... | collective-permute-start | bytes 196616 | tf_op jit(solution)/shard_map/ppermute | solution.py:350
  59.8 1.5 %collective-permute-start.13 = (bf16[2,16,8,128]{3,2,1,0:T(8,128)(2,1)S(1)}, bf16[2,16,8,128]{3,2,1,0:T(8,128)(2,1)S(1)}, u32[]{:S(2)}, u32[]{:S(2)}) collective-permute-start(bf16[2,16,8,128]{3,2,1,0:T(8,128)(2,1)S(1)} %get-tuple-element.26), channel_id=1, source_target_pairs={{0,16},{1,17},{8,24},{9,25},{16,0},{17,1},{24,8},{25,9},{2,18},{3,... | collective-permute-start | bytes 196616 | tf_op jit(solution)/shard_map/ppermute | solution.py:350
  61.3 0.5 collective-permute-start.14
  61.8 0.8 %collective-permute-done.12.refs_1_ = bf16[2,16,8,128]{3,2,1,0:T(8,128)(2,1)S(1)} collective-permute-done((bf16[2,16,8,128]{3,2,1,0:T(8,128)(2,1)S(1)}, bf16[2,16,8,128]{3,2,1,0:T(8,128)(2,1)S(1)}, u32[]{:S(2)}, u32[]{:S(2)}) %collective-permute-start.12) | collective-permute-done | bytes 65568 | tf_op jit(solution)/shard_map/ppermute | solution.py:350
  62.5 0.6 copy-done.2
  63.2 0.9 %collective-permute-done.13.refs_2_ = bf16[2,16,8,128]{3,2,1,0:T(8,128)(2,1)S(1)} collective-permute-done((bf16[2,16,8,128]{3,2,1,0:T(8,128)(2,1)S(1)}, bf16[2,16,8,128]{3,2,1,0:T(8,128)(2,1)S(1)}, u32[]{:S(2)}, u32[]{:S(2)}) %collective-permute-start.13) | collective-permute-done | bytes 65568 | tf_op jit(solution)/shard_map/ppermute | solution.py:350
  64.0 0.6 copy-done.3
  64.7 1.8 %collective-permute-done.14.refs_3_ = bf16[2,16,8,128]{3,2,1,0:T(8,128)(2,1)S(1)} collective-permute-done((bf16[2,16,8,128]{3,2,1,0:T(8,128)(2,1)S(1)}, bf16[2,16,8,128]{3,2,1,0:T(8,128)(2,1)S(1)}, u32[]{:S(2)}, u32[]{:S(2)}) %collective-permute-start.14) | collective-permute-done | bytes 65568 | tf_op jit(solution)/shard_map/ppermute | solution.py:350
  66.5 0.7 %slice-done.1 = bf16[1,16,8,128]{3,2,1,0:T(8,128)(2,1)S(1)} async-done(((bf16[2,16,8,128]{3,2,1,0:T(8,128)(2,1)}), bf16[1,16,8,128]{3,2,1,0:T(8,128)(2,1)S(1)}, s32[]{:S(2)}) %slice-start.1) | async-done | bytes 32792 | tf_op jit(solution)/shard_map/slice | solution.py:414
  67.3 1.3 %collective-permute-done.15.refs_4_ = bf16[4,16,8,128]{3,2,1,0:T(8,128)(2,1)S(1)} collective-permute-done((bf16[4,16,8,128]{3,2,1,0:T(8,128)(2,1)S(1)}, bf16[4,16,8,128]{3,2,1,0:T(8,128)(2,1)S(1)}, u32[]{:S(2)}, u32[]{:S(2)}) %collective-permute-start.15) | collective-permute-done | bytes 131104 | tf_op jit(solution)/shard_map/ppermute | solution.py:350
  68.6 0.7 copy-done.6
  69.3 1.8 %shard_map.77 = bf16[16,8,1024]{2,1,0:T(8,128)(2,1)} custom-call(s32[1]{0:T(128)} %bitcast.me_ref, bf16[2,16,8,128]{3,2,1,0:T(8,128)(2,1)} %get-tuple-element.28.refs_0_, bf16[2,16,8,128]{3,2,1,0:T(8,128)(2,1)} %copy-done.2, bf16[2,16,8,128]{3,2,1,0:T(8,128)(2,1)} %copy-done.3, bf16[2,16,8,128]{3,2,1,0:T(8,128)(2,1)} %copy-done.4, ...), custom_call_target="tpu_custom_call" | custom-call | tf_op jit(solution)/shard_map/pallas_call | solution.py:415
  (48 shorter events, 1.6 us)
Async XLA Ops:
  0.0 27.2 %copy-start = (f32[3,3,1024]{2,1,0:T(4,128)S(1)}, f32[3,3,1024]{2,1,0:T(4,128)}, u32[]{:S(2)}) copy-start(f32[3,3,1024]{2,1,0:T(4,128)} %param.12) | copy-start | bytes 110596
  2.0 10.3 %collective-permute-start.6 = (bf16[2,2,16,8,128]{4,3,2,1,0:T(8,128)(2,1)}, bf16[2,2,16,8,128]{4,3,2,1,0:T(8,128)(2,1)S(1)}, u32[]{:S(2)}, u32[]{:S(2)}) collective-permute-start(bf16[2,2,16,8,128]{4,3,2,1,0:T(8,128)(2,1)} %get-tuple-element.20), channel_id=1, source_target_pairs={{0,1},{1,0},{8,9},{9,8},{16,17},{17,16},{24,25},{25,24},{2,3},{3,2... | collective-permute-start | bytes 393224 | tf_op jit(solution)/shard_map/ppermute | solution.py:350
  5.0 8.5 %collective-permute-start.7 = (bf16[2,2,16,8,128]{4,3,2,1,0:T(8,128)(2,1)}, bf16[2,2,16,8,128]{4,3,2,1,0:T(8,128)(2,1)S(1)}, u32[]{:S(2)}, u32[]{:S(2)}) collective-permute-start(bf16[2,2,16,8,128]{4,3,2,1,0:T(8,128)(2,1)} %get-tuple-element.21), channel_id=1, source_target_pairs={{0,16},{1,17},{8,24},{9,25},{16,0},{17,1},{24,8},{25,9},{2,18},{3,... | collective-permute-start | bytes 393224 | tf_op jit(solution)/shard_map/ppermute | solution.py:350
  6.5 5.7 %copy-start.5 = (bf16[2,2,16,8,128]{4,3,2,1,0:T(8,128)(2,1)S(1)}, bf16[2,2,16,8,128]{4,3,2,1,0:T(8,128)(2,1)}, u32[]{:S(2)}) copy-start(bf16[2,2,16,8,128]{4,3,2,1,0:T(8,128)(2,1)} %get-tuple-element.19) | copy-start | bytes 393220
  6.5 7.0 %collective-permute-start.8 = (bf16[2,2,16,8,128]{4,3,2,1,0:T(8,128)(2,1)}, bf16[2,2,16,8,128]{4,3,2,1,0:T(8,128)(2,1)S(1)}, u32[]{:S(2)}, u32[]{:S(2)}) collective-permute-start(bf16[2,2,16,8,128]{4,3,2,1,0:T(8,128)(2,1)} %get-tuple-element.22), channel_id=1, source_target_pairs={{0,17},{1,16},{8,25},{9,24},{16,1},{17,0},{24,9},{25,8},{2,19},{3,... | collective-permute-start | bytes 393224 | tf_op jit(solution)/shard_map/ppermute | solution.py:350
  8.7 3.5 %copy-start.1 = (bf16[2,3,16,8,128]{4,3,2,1,0:T(8,128)(2,1)S(1)}, bf16[2,3,16,8,128]{4,3,2,1,0:T(8,128)(2,1)}, u32[]{:S(2)}) copy-start(bf16[2,3,16,8,128]{4,3,2,1,0:T(8,128)(2,1)} %get-tuple-element.15) | copy-start | bytes 589828
  8.7 9.4 %collective-permute-start = (bf16[2,3,16,8,128]{4,3,2,1,0:T(8,128)(2,1)}, bf16[2,3,16,8,128]{4,3,2,1,0:T(8,128)(2,1)S(1)}, u32[]{:S(2)}, u32[]{:S(2)}) collective-permute-start(bf16[2,3,16,8,128]{4,3,2,1,0:T(8,128)(2,1)} %get-tuple-element.16), channel_id=1, source_target_pairs={{0,1},{1,0},{8,9},{9,8},{16,17},{17,16},{24,25},{25,24},{2,3},{3,2... | collective-permute-start | bytes 589832 | tf_op jit(solution)/shard_map/ppermute | solution.py:350
  10.7 8.0 %collective-permute-start.1 = (bf16[2,3,16,8,128]{4,3,2,1,0:T(8,128)(2,1)}, bf16[2,3,16,8,128]{4,3,2,1,0:T(8,128)(2,1)S(1)}, u32[]{:S(2)}, u32[]{:S(2)}) collective-permute-start(bf16[2,3,16,8,128]{4,3,2,1,0:T(8,128)(2,1)} %get-tuple-element.17), channel_id=1, source_target_pairs={{0,16},{1,17},{8,24},{9,25},{16,0},{17,1},{24,8},{25,9},{2,18},{3,... | collective-permute-start | bytes 589832 | tf_op jit(solution)/shard_map/ppermute | solution.py:350
  12.2 0.9 %copy-start.7 = (bf16[2,3,16,8,128]{4,3,2,1,0:T(8,128)(2,1)S(1)}, bf16[2,3,16,8,128]{4,3,2,1,0:T(8,128)(2,1)}, u32[]{:S(2)}) copy-start(bf16[2,3,16,8,128]{4,3,2,1,0:T(8,128)(2,1)} %get-tuple-element.18) | copy-start | bytes 589828
  13.1 8.0 %collective-permute-start.2 = (bf16[2,3,16,8,128]{4,3,2,1,0:T(8,128)(2,1)S(1)}, bf16[2,3,16,8,128]{4,3,2,1,0:T(8,128)(2,1)S(1)}, u32[]{:S(2)}, u32[]{:S(2)}) collective-permute-start(bf16[2,3,16,8,128]{4,3,2,1,0:T(8,128)(2,1)S(1)} %copy-done.7), channel_id=1, source_target_pairs={{0,17},{1,16},{8,25},{9,24},{16,1},{17,0},{24,9},{25,8},{2,19},{3,... | collective-permute-start | bytes 589832 | tf_op jit(solution)/shard_map/ppermute | solution.py:350
  13.6 8.5 %collective-permute-start.9 = (bf16[4,2,16,8,128]{4,3,2,1,0:T(8,128)(2,1)S(1)}, bf16[4,2,16,8,128]{4,3,2,1,0:T(8,128)(2,1)S(1)}, u32[]{:S(2)}, u32[]{:S(2)}) collective-permute-start(bf16[4,2,16,8,128]{4,3,2,1,0:T(8,128)(2,1)S(1)} %pad_maximum_fusion.1), channel_id=1, source_target_pairs={{0,8},{1,9},{8,0},{9,1},{16,24},{17,25},{24,16},{25,17},{2,10},{3,... | collective-permute-start | bytes 786440 | tf_op jit(solution)/shard_map/ppermute | solution.py:350
  21.2 6.0 %collective-permute-start.3 = (bf16[4,3,16,8,128]{4,3,2,1,0:T(8,128)(2,1)S(1)}, bf16[4,3,16,8,128]{4,3,2,1,0:T(8,128)(2,1)S(1)}, u32[]{:S(2)}, u32[]{:S(2)}) collective-permute-start(bf16[4,3,16,8,128]{4,3,2,1,0:T(8,128)(2,1)S(1)} %pad_maximum_fusion), channel_id=1, source_target_pairs={{0,8},{1,9},{8,0},{9,1},{16,24},{17,25},{24,16},{25,17},{2,10},{3,... | collective-permute-start | bytes 1179656 | tf_op jit(solution)/shard_map/ppermute | solution.py:350
  22.1 16.0 %collective-permute-start.10 = (bf16[8,2,16,8,128]{4,3,2,1,0:T(8,128)(2,1)S(1)}, bf16[8,2,16,8,128]{4,3,2,1,0:T(8,128)(2,1)S(1)}, u32[]{:S(2)}, u32[]{:S(2)}) collective-permute-start(bf16[8,2,16,8,128]{4,3,2,1,0:T(8,128)(2,1)S(1)} %constant_dynamic-update-slice_fusion.1.c_ref), channel_id=1, source_target_pairs={{0,2},{2,4},{4,6},{1,3},{3,5},{5,7},{8,10},{10,12},{12,14},{9,11},... | collective-permute-start | bytes 1572872 | tf_op jit(solution)/shard_map/ppermute | solution.py:371
  25.8 16.7 %collective-permute-start.11 = (bf16[8,2,16,8,128]{4,3,2,1,0:T(8,128)(2,1)S(1)}, bf16[8,2,16,8,128]{4,3,2,1,0:T(8,128)(2,1)S(1)}, u32[]{:S(2)}, u32[]{:S(2)}) collective-permute-start(bf16[8,2,16,8,128]{4,3,2,1,0:T(8,128)(2,1)S(1)} %constant_dynamic-update-slice_fusion.1.c_ref), channel_id=1, source_target_pairs={{2,0},{4,2},{6,4},{3,1},{5,3},{7,5},{10,8},{12,10},{14,12},{11,9},... | collective-permute-start | bytes 1572872 | tf_op jit(solution)/shard_map/ppermute | solution.py:371
  27.3 22.6 %collective-permute-start.4 = (bf16[8,2,16,8,128]{4,3,2,1,0:T(8,128)(2,1)S(1)}, bf16[8,2,16,8,128]{4,3,2,1,0:T(8,128)(2,1)S(1)}, u32[]{:S(2)}, u32[]{:S(2)}) collective-permute-start(bf16[8,2,16,8,128]{4,3,2,1,0:T(8,128)(2,1)S(1)} %slice.116.n_ref), channel_id=1, source_target_pairs={{0,2},{2,4},{4,6},{1,3},{3,5},{5,7},{8,10},{10,12},{12,14},{9,11},... | collective-permute-start | bytes 1572872 | tf_op jit(solution)/shard_map/ppermute | solution.py:371
  31.9 21.1 %collective-permute-start.5 = (bf16[8,2,16,8,128]{4,3,2,1,0:T(8,128)(2,1)S(1)}, bf16[8,2,16,8,128]{4,3,2,1,0:T(8,128)(2,1)S(1)}, u32[]{:S(2)}, u32[]{:S(2)}) collective-permute-start(bf16[8,2,16,8,128]{4,3,2,1,0:T(8,128)(2,1)S(1)} %slice.116.n_ref), channel_id=1, source_target_pairs={{2,0},{4,2},{6,4},{3,1},{5,3},{7,5},{10,8},{12,10},{14,12},{11,9},... | collective-permute-start | bytes 1572872 | tf_op jit(solution)/shard_map/ppermute | solution.py:371
  58.3 4.3 %collective-permute-start.12 = (bf16[2,16,8,128]{3,2,1,0:T(8,128)(2,1)S(1)}, bf16[2,16,8,128]{3,2,1,0:T(8,128)(2,1)S(1)}, u32[]{:S(2)}, u32[]{:S(2)}) collective-permute-start(bf16[2,16,8,128]{3,2,1,0:T(8,128)(2,1)S(1)} %get-tuple-element.27), channel_id=1, source_target_pairs={{0,1},{1,0},{8,9},{9,8},{16,17},{17,16},{24,25},{25,24},{2,3},{3,2... | collective-permute-start | bytes 196616 | tf_op jit(solution)/shard_map/ppermute | solution.py:350
  59.8 4.3 %collective-permute-start.13 = (bf16[2,16,8,128]{3,2,1,0:T(8,128)(2,1)S(1)}, bf16[2,16,8,128]{3,2,1,0:T(8,128)(2,1)S(1)}, u32[]{:S(2)}, u32[]{:S(2)}) collective-permute-start(bf16[2,16,8,128]{3,2,1,0:T(8,128)(2,1)S(1)} %get-tuple-element.26), channel_id=1, source_target_pairs={{0,16},{1,17},{8,24},{9,25},{16,0},{17,1},{24,8},{25,9},{2,18},{3,... | collective-permute-start | bytes 196616 | tf_op jit(solution)/shard_map/ppermute | solution.py:350
  61.3 5.2 %collective-permute-start.14 = (bf16[2,16,8,128]{3,2,1,0:T(8,128)(2,1)S(1)}, bf16[2,16,8,128]{3,2,1,0:T(8,128)(2,1)S(1)}, u32[]{:S(2)}, u32[]{:S(2)}) collective-permute-start(bf16[2,16,8,128]{3,2,1,0:T(8,128)(2,1)S(1)} %get-tuple-element.25), channel_id=1, source_target_pairs={{0,17},{1,16},{8,25},{9,24},{16,1},{17,0},{24,9},{25,8},{2,19},{3,... | collective-permute-start | bytes 196616 | tf_op jit(solution)/shard_map/ppermute | solution.py:350
  62.5 0.6 copy-start.2
  64.0 0.6 copy-start.3
  64.7 1.8 %slice-start = ((bf16[2,16,8,128]{3,2,1,0:T(8,128)(2,1)}), bf16[1,16,8,128]{3,2,1,0:T(8,128)(2,1)S(1)}, s32[]{:S(2)}) async-start(bf16[2,16,8,128]{3,2,1,0:T(8,128)(2,1)} %copy-done.2), calls=%async_computation | async-start | bytes 65536 | tf_op jit(solution)/shard_map/slice | solution.py:414
  66.4 0.8 %copy-start.4 = (bf16[2,16,8,128]{3,2,1,0:T(8,128)(2,1)}, bf16[2,16,8,128]{3,2,1,0:T(8,128)(2,1)S(1)}, u32[]{:S(2)}) copy-start(bf16[2,16,8,128]{3,2,1,0:T(8,128)(2,1)S(1)} %collective-permute-done.14.refs_3_) | copy-start | bytes 196612
  66.4 0.8 %slice-start.1 = ((bf16[2,16,8,128]{3,2,1,0:T(8,128)(2,1)}), bf16[1,16,8,128]{3,2,1,0:T(8,128)(2,1)S(1)}, s32[]{:S(2)}) async-start(bf16[2,16,8,128]{3,2,1,0:T(8,128)(2,1)} %copy-done.3), calls=%async_computation.1 | async-start | bytes 65536 | tf_op jit(solution)/shard_map/slice | solution.py:414
  67.2 1.4 %collective-permute-start.15 = (bf16[4,16,8,128]{3,2,1,0:T(8,128)(2,1)S(1)}, bf16[4,16,8,128]{3,2,1,0:T(8,128)(2,1)S(1)}, u32[]{:S(2)}, u32[]{:S(2)}) collective-permute-start(bf16[4,16,8,128]{3,2,1,0:T(8,128)(2,1)S(1)} %pad_maximum_fusion.2), channel_id=1, source_target_pairs={{0,8},{1,9},{8,0},{9,1},{16,24},{17,25},{24,16},{25,17},{2,10},{3,... | collective-permute-start | bytes 393224 | tf_op jit(solution)/shard_map/ppermute | solution.py:350
  68.6 0.7 copy-start.6

commit v3 on v2

--- a/solution.py
+++ b/solution.py
@@ -149,31 +149,25 @@
 NEG = -1e30
 VMEM = pl.BlockSpec(memory_space=pltpu.VMEM)
 SMEM = pl.BlockSpec(memory_space=pltpu.SMEM)
-LIMIT = pltpu.CompilerParams(vmem_limit_bytes=48 * 1024 * 1024)
-
-
-def tile_masks(tile_rows, tile_cols):
-    size = tile_rows * tile_cols
-    query = lax.broadcasted_iota(jnp.int32, (size, size), 0)
-    key = lax.broadcasted_iota(jnp.int32, (size, size), 1)
-    upper = key // tile_cols >= query // tile_cols
-    left = key % tile_cols >= query % tile_cols
-    return upper, left
+LIMIT = pltpu.CompilerParams(vmem_limit_bytes=8 * 1024 * 1024)
+SMALL = pltpu.CompilerParams(vmem_limit_bytes=4 * 1024 * 1024)
 
 
 class Window:
-    def __init__(self, grid, tile, info_ref, q_ref, sides):
+    def __init__(self, grid, tile, info_ref, current_ref, sides):
         self.grid_rows, self.grid_cols = grid
         self.tile_rows, self.tile_cols = tile
         self.size = self.tile_rows * self.tile_cols
-        self.info, self.q, self.sides = info_ref, q_ref, sides
+        self.info, self.current, self.sides = info_ref, current_ref, sides
         self.scale = HD ** (-0.5) * LOG2E
         self.bias_left = jnp.where(info_ref[0] > 0, 0.0, NEG).astype(jnp.float32)
         self.bias_right = jnp.where(info_ref[1] > 0, 0.0, NEG).astype(jnp.float32)
-        self.upper, self.left = tile_masks(self.tile_rows, self.tile_cols)
+        query = lax.broadcasted_iota(jnp.int32, (self.size, self.size), 0)
+        key = lax.broadcasted_iota(jnp.int32, (self.size, self.size), 1)
+        self.upper = key // self.tile_cols >= query // self.tile_cols
+        self.left = key % self.tile_cols >= query % self.tile_cols
         self.upper_one = self.upper.astype(jnp.float32).astype(jnp.bfloat16)
         self.left_one = self.left.astype(jnp.float32).astype(jnp.bfloat16)
-        self.ones = jnp.ones((self.size, HD), jnp.bfloat16)
 
     def slot(self, row, col):
         return self.info[2 + row * self.grid_cols + col]
@@ -182,34 +176,38 @@
         return 1 if col < 0 else (2 if col >= self.grid_cols else 0)
 
     def tile(self, frame, part, row, col):
-        ref = self.sides[frame][self.side(col)]
-        return ref[self.slot(row, col % self.grid_cols), part].reshape(self.size, HD)
-
-    def score(self, query, frame, row, col):
-        raw = lax.dot_general(
-            query, self.tile(frame, 0, row, col), (((1,), (1,)), ((), ())),
-            preferred_element_type=jnp.float32,
-        )
-        if self.side(col) == 1:
-            raw = raw + self.bias_left
-        elif self.side(col) == 2:
-            raw = raw + self.bias_right
-        return raw
-
-    def attend(self, row, col, wanted):
-        query = self.q[self.slot(row, col)].reshape(self.size, HD)
+        ref, base = self.sides[frame][self.side(col)]
+        return ref[self.slot(row, col % self.grid_cols), base + part].reshape(self.size, HD)
+
+    def steps(self, col, inner):
+        near = [step for step in (-1, 0, 1) if 0 <= col + step < self.grid_cols]
+        return near if inner else [step for step in (-1, 0, 1, 2) if step not in near]
+
+    def attend(self, row, col, wanted, before):
+        query = self.current[self.slot(row, col), 2].reshape(self.size, HD)
+        rows = [r for r in (row - 1, row, row + 1) if 0 <= r < self.grid_rows]
+        needed = []
+        for frame, step in wanted:
+            for key_col in (col - 2, col + 2) if step == 2 else (col + step,):
+                needed += [(frame, r, key_col) for r in rows]
+        keys = jnp.concatenate([self.tile(frame, 0, r, c) for frame, r, c in needed], axis=0)
+        raw = lax.dot_general(query, keys, (((1,), (1,)), ((), ())), preferred_element_type=jnp.float32)
+        scores = {}
+        for i, (frame, r, c) in enumerate(needed):
+            score = raw[:, i * self.size : (i + 1) * self.size]
+            if self.side(c) == 1:
+                score = score + self.bias_left
+            elif self.side(c) == 2:
+                score = score + self.bias_right
+            scores[frame, r, c] = score
         up, down = row > 0, row + 1 < self.grid_rows
 
-        def beside(frame, key_col):
-            if up and down:
-                above = self.score(query, frame, row - 1, key_col)
-                return jnp.where(self.upper, above, self.score(query, frame, row + 1, key_col))
-            if down:
-                return jnp.where(self.upper, NEG, self.score(query, frame, row + 1, key_col))
-            return jnp.where(self.upper, self.score(query, frame, row - 1, key_col), NEG)
-
-        def level(frame, key_col):
-            return self.score(query, frame, row, key_col)
+        def level(frame, c):
+            return scores[frame, row, c]
+
+        def beside(frame, c):
+            above = scores[frame, row - 1, c] if up else NEG
+            return jnp.where(self.upper, above, scores[frame, row + 1, c] if down else NEG)
 
         blocks = []
         for frame, step in wanted:
@@ -217,82 +215,62 @@
                 if off_row and not (up or down):
                     continue
                 if step == 2:
-                    raw = jnp.where(self.left, make(frame, col - 2), make(frame, col + 2))
+                    block = jnp.where(self.left, make(frame, col - 2), make(frame, col + 2))
                 else:
-                    raw = make(frame, col + step)
-                blocks.append((frame, off_row, step, raw))
+                    block = make(frame, col + step)
+                blocks.append((frame, off_row, step, block))
         top = blocks[0][3]
         for entry in blocks[1:]:
             top = jnp.maximum(top, entry[3])
-        return blocks, jnp.max(top, axis=1, keepdims=True)
-
-    def weigh(self, row, col, blocks, top):
-        up, down = row > 0, row + 1 < self.grid_rows
-        total = jnp.zeros((self.size, 2 * HD), jnp.float32)
-        for frame, off_row, step, raw in blocks:
-            weights = jnp.exp2((raw - top) * self.scale).astype(jnp.bfloat16)
+        top = jnp.max(top, axis=1, keepdims=True)
+        if before is not None:
+            top = jnp.maximum(top, before[0])
+        parts = []
+        for frame, off_row, step, block in blocks:
+            weights = jnp.exp2((block - top) * self.scale).astype(jnp.bfloat16)
             if off_row and up and down:
                 by_row = [(row - 1, weights * self.upper_one), (row + 1, weights * (1 - self.upper_one))]
             elif off_row:
                 by_row = [(row + 1 if down else row - 1, weights)]
             else:
                 by_row = [(row, weights)]
-            for key_row, part in by_row:
+            for r, part in by_row:
                 if step == 2:
-                    pair = [(col - 2, part * self.left_one), (col + 2, part * (1 - self.left_one))]
+                    parts.append((frame, r, col - 2, part * self.left_one))
+                    parts.append((frame, r, col + 2, part * (1 - self.left_one)))
                 else:
-                    pair = [(col + step, part)]
-                for key_col, one in pair:
-                    wide = jnp.concatenate([self.tile(frame, 1, key_row, key_col), self.ones], axis=1)
-                    total = total + jnp.dot(one, wide, preferred_element_type=jnp.float32)
-        return total
-
-    def inner_steps(self, col):
-        near = [step for step in (-1, 0, 1) if 0 <= col + step < self.grid_cols]
-        return near, [step for step in (-1, 0, 1, 2) if step not in near]
-
-
-def early_kernel(grid, tile, info_ref, q_ref, c_ref, cl_ref, cr_ref, n_ref, sum_ref, top_ref):
-    window = Window(grid, tile, info_ref, q_ref, [[c_ref, cl_ref, cr_ref], [n_ref, None, None]])
-    for row in range(grid[0]):
-        for col in range(grid[1]):
-            near, _ = window.inner_steps(col)
-            wanted = [(0, step) for step in (-1, 0, 1, 2)] + [(1, step) for step in near]
-            blocks, top = window.attend(row, col, wanted)
-            sum_ref[row * grid[1] + col] = window.weigh(row, col, blocks, top)
-            top_ref[row * grid[1] + col] = jnp.broadcast_to(top, (window.size, HD))
-
-
-def late_kernel(
-    grid, tile, info_ref, weight_ref, bias_ref, q_ref, n_ref, nl_ref, nr_ref, sum_ref, top_ref, out_ref
-):
-    window = Window(grid, tile, info_ref, q_ref, [None, [n_ref, nl_ref, nr_ref]])
-    grid_rows, grid_cols = grid
-    tile_rows, tile_cols = tile
-    sub = lax.broadcasted_iota(jnp.int32, (tile_cols, HD), 0)
-    taps = [[weight_ref[a, pl.ds(b, 1), :] for b in range(3)] for a in range(3)]
-
-    def enhanced(row, col):
+                    parts.append((frame, r, col + step, part))
+        values = jnp.concatenate([self.tile(frame, 1, r, c) for frame, r, c, _ in parts], axis=0)
+        values = jnp.concatenate([values, jnp.ones_like(values)], axis=1)
+        weights = jnp.concatenate([part for _, _, _, part in parts], axis=1)
+        total = jnp.dot(weights, values, preferred_element_type=jnp.float32)
+        if before is not None:
+            total = total + before[1] * jnp.exp2((before[0] - top) * self.scale)
+        return top, total
+
+    def enhanced(self, row, col, weight_ref, bias_ref):
+        shape = (self.tile_cols, HD)
+        sub = lax.broadcasted_iota(jnp.int32, shape, 0)
+        taps = [[weight_ref[a, pl.ds(b, 1), :] for b in range(3)] for a in range(3)]
+        last = self.tile_cols - 1
         lines = []
-        for key_row in range(row * tile_rows - 1, (row + 1) * tile_rows + 1):
-            tile_row, line = key_row // tile_rows, key_row % tile_rows
-            if tile_row < 0 or tile_row >= grid_rows:
+        for key_row in range(row * self.tile_rows - 1, (row + 1) * self.tile_rows + 1):
+            tile_row, line = key_row // self.tile_rows, key_row % self.tile_rows
+            if tile_row < 0 or tile_row >= self.grid_rows:
                 lines.append(None)
                 continue
 
-            def values(key_col):
-                ref = window.sides[1][window.side(key_col)]
-                return ref[window.slot(tile_row, key_col % grid_cols), 1, line].astype(jnp.float32)
+            def values(c):
+                ref, base = self.sides[1][self.side(c)]
+                return ref[self.slot(tile_row, c % self.grid_cols), base + 1, line].astype(jnp.float32)
 
             here, before, after = values(col), values(col - 1), values(col + 1)
             low = jnp.where(sub == 0, pltpu.roll(before, 1, 0), pltpu.roll(here, 1, 0))
-            high = jnp.where(
-                sub == tile_cols - 1, pltpu.roll(after, tile_cols - 1, 0), pltpu.roll(here, tile_cols - 1, 0)
-            )
+            high = jnp.where(sub == last, pltpu.roll(after, last, 0), pltpu.roll(here, last, 0))
             lines.append((low, here, high))
         sums = []
-        for line in range(tile_rows):
-            total = jnp.broadcast_to(bias_ref[...], (tile_cols, HD))
+        for line in range(self.tile_rows):
+            total = jnp.broadcast_to(bias_ref[...], shape)
             for a in range(3):
                 if lines[line + a] is not None:
                     for b in range(3):
@@ -300,37 +278,75 @@
             sums.append(total)
         return jnp.stack(sums, axis=0)
 
-    for row in range(grid_rows):
-        for col in range(grid_cols):
-            _, wanted = window.inner_steps(col)
-            blocks, top = window.attend(row, col, [(1, step) for step in wanted])
-            before = top_ref[row * grid_cols + col][:, :1]
-            best = jnp.maximum(top, before)
-            total = window.weigh(row, col, blocks, best)
-            total = total + sum_ref[row * grid_cols + col] * jnp.exp2((before - best) * window.scale)
-            attended = (total[:, :HD] / total[:, HD:]).reshape(tile_rows, tile_cols, HD)
-            place = info_ref[2 + grid_rows * grid_cols + row * grid_cols + col]
-            out_ref[place // 2, place % 2] = (attended + enhanced(row, col)).astype(jnp.bfloat16)
+
+def running(top_ref, sum_ref, index):
+    return top_ref[index][:, :1], sum_ref[index]
+
+
+def own_kernel(grid, tile, info_ref, current_ref, cached_ref, sum_ref, top_ref):
+    window = Window(grid, tile, info_ref, current_ref, [[(cached_ref, 0)], [(current_ref, 0)]])
+    for row in range(grid[0]):
+        for col in range(grid[1]):
+            wanted = [(frame, step) for frame in (0, 1) for step in window.steps(col, True)]
+            top, total = window.attend(row, col, wanted, None)
+            sum_ref[row * grid[1] + col] = total
+            top_ref[row * grid[1] + col] = jnp.broadcast_to(top, (window.size, HD))
+
+
+def cached_kernel(grid, tile, info_ref, current_ref, left_ref, right_ref, sum_in, top_in, sum_ref, top_ref):
+    window = Window(grid, tile, info_ref, current_ref, [[None, (left_ref, 0), (right_ref, 0)]])
+    for row in range(grid[0]):
+        for col in range(grid[1]):
+            index = row * grid[1] + col
+            wanted = [(0, step) for step in window.steps(col, False)]
+            top, total = window.attend(row, col, wanted, running(top_in, sum_in, index))
+            sum_ref[index] = total
+            top_ref[index] = jnp.broadcast_to(top, (window.size, HD))
+
+
+def last_kernel(
+    grid, tile, info_ref, weight_ref, bias_ref, current_ref, halo_ref, sum_in, top_in, same_ref, beside_ref
+):
+    window = Window(grid, tile, info_ref, current_ref, [None, [(current_ref, 0), (halo_ref, 0), (halo_ref, 2)]])
+    count = grid[0] * grid[1]
+    for row in range(grid[0]):
+        for col in range(grid[1]):
+            index = row * grid[1] + col
+            wanted = [(1, step) for step in window.steps(col, False)]
+            _, total = window.attend(row, col, wanted, running(top_in, sum_in, index))
+            attended = (total[:, :HD] / total[:, HD:]).reshape(tile + (HD,))
+            out = (attended + window.enhanced(row, col, weight_ref, bias_ref)).astype(jnp.bfloat16)
+            place = info_ref[2 + index]
+
+            @pl.when(place < count // 2)
+            def _():
+                same_ref[place] = out
+
+            @pl.when(place >= count // 2)
+            def _():
+                beside_ref[place - count // 2] = out
 
 
 def lanes(head):
     return pl.ds(pl.multiple_of(head * HD, HD), HD)
 
 
-def pack_kernel(members, flips, side, me_ref, *refs):
-    sources, buffers = refs[:members], refs[members:]
+def pack_kernel(flips, side, members, me_ref, *refs):
+    buffers = refs[len(refs) - len(flips) :]
     for buffer, flip in zip(buffers, flips):
         for other in range(2):
             head = me_ref[0] ^ (flip ^ (side if other else 0))
-            for member, source in enumerate(sources):
-                buffer[other, member] = source[:, :, lanes(head)]
-
-
-def unpack_kernel(flips, side, me_ref, *refs):
-    out_ref, beside_ref = refs[-1], refs[-2]
-    for i, flip in enumerate(flips):
+            for member, (source, lead) in enumerate(members):
+                buffer[other, member] = refs[source][lead, :, :, lanes(head)]
+
+
+def unpack_kernel(flips, side, me_ref, same_ref, beside_ref, *refs):
+    out_ref = refs[-1]
+    out_ref[:, :, lanes(me_ref[0])] = same_ref[0]
+    out_ref[:, :, lanes(me_ref[0] ^ side)] = beside_ref[0]
+    for i, flip in enumerate(flips[1:]):
         out_ref[:, :, lanes(me_ref[0] ^ flip)] = refs[i][0]
-        out_ref[:, :, lanes(me_ref[0] ^ (flip ^ side))] = beside_ref[i]
+        out_ref[:, :, lanes(me_ref[0] ^ (flip ^ side))] = refs[i][1]
 
 
 def head_step(shape, queries, keys_new, values_new, keys_cache, values_cache, conv_weight, conv_bias):
@@ -350,12 +366,14 @@
         return lax.ppermute(x, axes, [(s, s ^ flip) for s in range(heads)])
 
     def pack(*arrays):
+        members = [(i, lead) for i, array in enumerate(arrays) for lead in range(array.shape[0])]
         return pl.pallas_call(
-            functools.partial(pack_kernel, len(arrays), flips, side),
-            out_shape=[jax.ShapeDtypeStruct((2, len(arrays)) + block, jnp.bfloat16)] * len(flips),
+            functools.partial(pack_kernel, flips, side, members),
+            out_shape=[jax.ShapeDtypeStruct((2, len(members)) + block, jnp.bfloat16)] * len(flips),
             in_specs=[SMEM] + [VMEM] * len(arrays),
             out_specs=[VMEM] * len(flips),
-            cost_estimate=pl.CostEstimate(flops=0, bytes_accessed=len(arrays) << 20, transcendentals=0),
+            compiler_params=SMALL,
+            cost_estimate=pl.CostEstimate(flops=0, bytes_accessed=len(members) << 20, transcendentals=0),
         )(me_ref, *arrays)
 
     def gather(buffers):
@@ -370,13 +388,15 @@
     def halo(x):
         return lax.ppermute(x, "far", up), lax.ppermute(x, "far", down)
 
-    packed_cached = pack(keys_cache[0], values_cache[0])
-    packed_current = pack(keys_new, values_new, queries)
+    pair = jnp.stack([keys_new, values_new])
+    new_left, new_right = halo(pair)
+    packed_cached = pack(keys_cache, values_cache)
     cached = gather(packed_cached)
+    packed_current = pack(keys_new[None], values_new[None], queries[None])
+    current = gather(packed_current)
     cached_left, cached_right = halo(cached)
-    current = gather(packed_current)
-    new, query = current[:, :2], current[:, 2]
-    new_left, new_right = halo(new)
+    packed_beyond = pack(new_left, new_right)
+    beyond = gather(packed_beyond)
     far_index = lax.axis_index("far")
     flip = me ^ jnp.arange(heads, dtype=jnp.int32)
     beside = (flip // side) % 2
@@ -385,39 +405,40 @@
         [
             jnp.stack([far_index > 0, far_index < far - 1]).astype(jnp.int32),
             beside * len(flips) + order,
-            order * 2 + beside,
         ]
     )
     weight = lax.dynamic_slice_in_dim(conv_weight, me * HD, HD, 2)
     bias = lax.dynamic_slice_in_dim(conv_bias.reshape(1, channels), me * HD, HD, 1)
     size = tile_rows * tile_cols
-    sums, tops = pl.pallas_call(
-        functools.partial(early_kernel, grid, tile),
-        out_shape=(
-            jax.ShapeDtypeStruct((heads, size, 2 * HD), jnp.float32),
-            jax.ShapeDtypeStruct((heads, size, HD), jnp.float32),
-        ),
-        in_specs=[SMEM] + [VMEM] * 5,
-        out_specs=(VMEM, VMEM),
-        compiler_params=LIMIT,
-        cost_estimate=pl.CostEstimate(flops=2**32, bytes_accessed=2**22, transcendentals=2**21),
-    )(info, query, cached, cached_left, cached_right, new)
-    result = pl.pallas_call(
-        functools.partial(late_kernel, grid, tile),
-        out_shape=jax.ShapeDtypeStruct((len(flips), 2) + block, jnp.bfloat16),
-        in_specs=[SMEM] + [VMEM] * 8,
-        out_specs=VMEM,
-        compiler_params=LIMIT,
-        cost_estimate=pl.CostEstimate(flops=2**30, bytes_accessed=2**22, transcendentals=2**19),
-    )(info, weight, bias, query, new, new_left, new_right, sums, tops)
-    got = [result[0]] + [swap(result[i], flips[i]) for i in range(1, len(flips))]
-    other = swap(jnp.stack([b[1] for b in got]), side)
+    state = (
+        jax.ShapeDtypeStruct((heads, size, 2 * HD), jnp.float32),
+        jax.ShapeDtypeStruct((heads, size, HD), jnp.float32),
+    )
+
+    def attention(kernel, out_shape, *operands):
+        return pl.pallas_call(
+            functools.partial(kernel, grid, tile),
+            out_shape=out_shape,
+            in_specs=[SMEM] + [VMEM] * len(operands),
+            out_specs=(VMEM, VMEM),
+            compiler_params=LIMIT,
+            cost_estimate=pl.CostEstimate(flops=2**31, bytes_accessed=2**22, transcendentals=2**20),
+        )(info, *operands)
+
+    sums, tops = attention(own_kernel, state, current, cached)
+    sums, tops = attention(cached_kernel, state, current, cached_left, cached_right, sums, tops)
+    half = jax.ShapeDtypeStruct((len(flips),) + block, jnp.bfloat16)
+    same, other = attention(last_kernel, (half, half), weight, bias, current, beyond, sums, tops)
+    received = swap(other, side)
+    pairs = [jnp.stack([same[i], received[i]]) for i in range(1, len(flips))]
+    got = [swap(pair, flip) for pair, flip in zip(pairs, flips[1:])]
     return pl.pallas_call(
         functools.partial(unpack_kernel, flips, side),
         out_shape=jax.ShapeDtypeStruct(queries.shape, jnp.bfloat16),
         in_specs=[SMEM] + [VMEM] * (len(flips) + 1),
         out_specs=VMEM,
-    )(me_ref, *got, other)
+        compiler_params=SMALL,
+    )(me_ref, same, received, *got)
 
 
 def grouping(mesh, heads):

time: 71.6 us -> 70.7 us (0.987)
  starting transfers between devices: 22.9 us -> 28.4 us
  Pallas kernels: 18 us -> 13.6 us
  waiting for transfers between devices: 24.5 us -> 20.6 us
  other arithmetic: 0.28 us -> 2.29 us
    ppermute x4, waiting for transfers between devices: 12.3 us -> 0.01 us  [halo(): return (lax.ppermute(x, 'far', up), lax.ppermute(x, 'far', down))]
    ppermute x12 -> x16, waiting for transfers between devices: 12.2 us -> 20.5 us  [swap(): return lax.ppermute(x, axes, [(s, s ^ flip) for s in range(heads)])]
    ppermute x12 -> x16, starting transfers between devices: 12 us -> 16.5 us  [swap(): return lax.ppermute(x, axes, [(s, s ^ flip) for s in range(heads)])]
    pallas_call x4 -> x6, Pallas kernels: 16.2 us -> 12.9 us  [the longest x3 11.5 us: attention(): pl.pallas_call(functools.partial(kernel, grid, tile), out_shape=out_shape...]
    slice x8 -> x12, local copies, waits for them, and re-layouts: 0.13 us -> 3.51 us  [gather(): forward = jnp.stack([b[1] for b in got])]
    unnamed x16 -> x18, local copies, waits for them, and re-layouts: 2.71 us -> 0.71 us
    another operation x1 -> x4, other arithmetic: 0.02 us -> 1.96 us  [the longest x1 1.94 us: head_step(): pair = jnp.stack([keys_new, values_new])]
    pallas_call x1, Pallas kernels: 1.81 us -> 0.77 us  [head_step(): pl.pallas_call(functools.partial(unpack_kernel, flips, side), out_shape=j...]
  transfers between devices with their start and end apart: 16 -> 20, of which waited for: 10 -> 10; matrix products, arithmetic and copies ran while one was open for 2% -> 7% of each run, Pallas kernels for 14% -> 10%
where the time goes in v3:
time: 70.7 us; the launch traced here: 70.3 us
  starting transfers between devices  28.4 us (40%)
  waiting for transfers between devices  20.6 us (29%)
  Pallas kernels  13.6 us (19%)
  local copies, waits for them, and re-layouts  5.15 us (7%)
  other arithmetic  2.29 us (3%)
    ppermute x16, waiting for transfers between devices, swap(): return lax.ppermute(x, axes, [(s, s ^ flip) for s in range(heads)])  20.5 us
    ppermute x16, starting transfers between devices, swap(): return lax.ppermute(x, axes, [(s, s ^ flip) for s in range(heads)])  16.5 us
    ppermute x4, starting transfers between devices, halo(): return (lax.ppermute(x, 'far', up), lax.ppermute(x, 'far', down))  11.9 us
    pallas_call x3, Pallas kernels, attention(): pl.pallas_call(functools.partial(kernel, grid, tile), out_shape=out_shape...  11.5 us
    slice x12, local copies, waits for them, and re-layouts, gather(): forward = jnp.stack([b[1] for b in got])  3.51 us
    another operation x1, other arithmetic, head_step(): pair = jnp.stack([keys_new, values_new])  1.94 us
  transfers between devices with their start and end apart: 20, of which 10 were waited for; matrix products, arithmetic and copies ran while one was open for 7% of the time, Pallas kernels for 10%

profile of v3, /device:TPU:0, one launch (start us, length us, event | category | flops | bytes accessed | tf_op | source)
XLA Modules:
  0.0 70.3 jit_solution(12382764829910869621)
XLA Ops:
  0.0 1.9 %pad_maximum_fusion = bf16[2,16,8,1024]{3,2,1,0:T(8,128)(2,1)} fusion(bf16[1,16,8,1024]{3,2,1,0:T(8,128)(2,1)} %bitcast.10, bf16[1,16,8,1024]{3,2,1,0:T(8,128)(2,1)} %bitcast.8), kind=kLoop, calls=%fused_computation | loop fusion | flops 262144 | bytes 1048576 | tf_op jit(solution)/shard_map/stack | solution.py:391
  1.9 5.0 %collective-permute-start.4 = (bf16[2,16,8,1024]{3,2,1,0:T(8,128)(2,1)}, bf16[2,16,8,1024]{3,2,1,0:T(8,128)(2,1)S(1)}, u32[]{:S(2)}, u32[]{:S(2)}) collective-permute-start(bf16[2,16,8,1024]{3,2,1,0:T(8,128)(2,1)} %pad_maximum_fusion), channel_id=1, source_target_pairs={{0,2},{2,4},{4,6},{1,3},{3,5},{5,7},{8,10},{10,12},{12,14},{9,11},... | collective-permute-start | bytes 1572872 | tf_op jit(solution)/shard_map/ppermute | solution.py:389
  6.9 1.3 %collective-permute-start.5 = (bf16[2,16,8,1024]{3,2,1,0:T(8,128)(2,1)}, bf16[2,16,8,1024]{3,2,1,0:T(8,128)(2,1)S(1)}, u32[]{:S(2)}, u32[]{:S(2)}) collective-permute-start(bf16[2,16,8,1024]{3,2,1,0:T(8,128)(2,1)} %pad_maximum_fusion), channel_id=1, source_target_pairs={{2,0},{4,2},{6,4},{3,1},{5,3},{7,5},{10,8},{12,10},{14,12},{11,9},... | collective-permute-start | bytes 1572872 | tf_op jit(solution)/shard_map/ppermute | solution.py:389
  8.3 0.9 %shard_map.75 = (bf16[2,2,16,8,128]{4,3,2,1,0:T(8,128)(2,1)S(1)}, bf16[2,2,16,8,128]{4,3,2,1,0:T(8,128)(2,1)}, bf16[2,2,16,8,128]{4,3,2,1,0:T(8,128)(2,1)}, bf16[2,2,16,8,128]{4,3,2,1,0:T(8,128)(2,1)}) custom-call(s32[1]{0:T(128)} %bitcast.me_ref, bf16[1,16,8,1024]{3,2,1,0:T(8,128)(2,1)S(1)} %copy-done.3, bf16[1,16,8,1024]{3,2,1,0:T(8,128)(2,1)S(1)} %copy-done.4), custom_call_target="tpu_custom_call" | custom-call | bytes 2097152 | tf_op jit(solution)/shard_map/pallas_call | solution.py:370
  9.2 1.5 %collective-permute-start.10 = (bf16[2,2,16,8,128]{4,3,2,1,0:T(8,128)(2,1)}, bf16[2,2,16,8,128]{4,3,2,1,0:T(8,128)(2,1)}, u32[]{:S(2)}, u32[]{:S(2)}) collective-permute-start(bf16[2,2,16,8,128]{4,3,2,1,0:T(8,128)(2,1)} %get-tuple-element.32), channel_id=1, source_target_pairs={{0,1},{1,0},{8,9},{9,8},{16,17},{17,16},{24,25},{25,24},{2,3},{3,2... | collective-permute-start | bytes 393224 | tf_op jit(solution)/shard_map/ppermute | solution.py:366
  10.7 1.5 %collective-permute-start.11 = (bf16[2,2,16,8,128]{4,3,2,1,0:T(8,128)(2,1)}, bf16[2,2,16,8,128]{4,3,2,1,0:T(8,128)(2,1)}, u32[]{:S(2)}, u32[]{:S(2)}) collective-permute-start(bf16[2,2,16,8,128]{4,3,2,1,0:T(8,128)(2,1)} %get-tuple-element.33), channel_id=1, source_target_pairs={{0,16},{1,17},{8,24},{9,25},{16,0},{17,1},{24,8},{25,9},{2,18},{3,... | collective-permute-start | bytes 393224 | tf_op jit(solution)/shard_map/ppermute | solution.py:366
  13.5 0.7 copy-done.6
  14.4 0.8 %dynamic-slice_bitcast_fusion.bias_ref = f32[1,128]{1,0:T(1,128)S(1)} fusion(f32[1024]{0:T(1024)} %param.13, s32[]{:T(128)S(6)} %select_n.27), kind=kLoop, calls=%fused_computation.39 | loop fusion | bytes 1028 | tf_op jit(solution)/shard_map/dynamic_slice | solution.py:411
  15.2 1.6 %collective-permute-start = (bf16[2,3,16,8,128]{4,3,2,1,0:T(8,128)(2,1)S(1)}, bf16[2,3,16,8,128]{4,3,2,1,0:T(8,128)(2,1)S(1)}, u32[]{:S(2)}, u32[]{:S(2)}) collective-permute-start(bf16[2,3,16,8,128]{4,3,2,1,0:T(8,128)(2,1)S(1)} %copy-done.7), channel_id=1, source_target_pairs={{0,1},{1,0},{8,9},{9,8},{16,17},{17,16},{24,25},{25,24},{2,3},{3,2... | collective-permute-start | bytes 589832 | tf_op jit(solution)/shard_map/ppermute | solution.py:366
  16.8 0.9 %fusion.15 = (bf16[1,2,16,8,128]{4,3,2,1,0:T(8,128)(2,1)S(1)}, bf16[8,2,16,8,128]{4,3,2,1,0:T(8,128)(2,1)S(1)}) fusion(bf16[2,2,16,8,128]{4,3,2,1,0:T(8,128)(2,1)} %collective-permute-done.10, bf16[8,2,16,8,128]{4,3,2,1,0:T(8,128)(2,1)S(1)} %get-tuple-element.64), kind=kLoop, calls=%fused_computation.52 | loop fusion | bytes 262144 | tf_op jit(solution)/shard_map/slice | solution.py:381
  17.7 1.6 %collective-permute-start.1 = (bf16[2,3,16,8,128]{4,3,2,1,0:T(8,128)(2,1)S(1)}, bf16[2,3,16,8,128]{4,3,2,1,0:T(8,128)(2,1)S(1)}, u32[]{:S(2)}, u32[]{:S(2)}) collective-permute-start(bf16[2,3,16,8,128]{4,3,2,1,0:T(8,128)(2,1)S(1)} %get-tuple-element.25), channel_id=1, source_target_pairs={{0,16},{1,17},{8,24},{9,25},{16,0},{17,1},{24,8},{25,9},{2,18},{3,... | collective-permute-start | bytes 589832 | tf_op jit(solution)/shard_map/ppermute | solution.py:366
  19.2 0.9 %fusion.16 = (bf16[1,2,16,8,128]{4,3,2,1,0:T(8,128)(2,1)S(1)}, bf16[8,2,16,8,128]{4,3,2,1,0:T(8,128)(2,1)S(1)}) fusion(bf16[2,2,16,8,128]{4,3,2,1,0:T(8,128)(2,1)} %collective-permute-done.11, bf16[8,2,16,8,128]{4,3,2,1,0:T(8,128)(2,1)S(1)} %get-tuple-element.66), kind=kLoop, calls=%fused_computation.53 | loop fusion | bytes 262144 | tf_op jit(solution)/shard_map/slice | solution.py:381
  20.1 0.8 %collective-permute-start.2 = (bf16[2,3,16,8,128]{4,3,2,1,0:T(8,128)(2,1)S(1)}, bf16[2,3,16,8,128]{4,3,2,1,0:T(8,128)(2,1)S(1)}, u32[]{:S(2)}, u32[]{:S(2)}) collective-permute-start(bf16[2,3,16,8,128]{4,3,2,1,0:T(8,128)(2,1)S(1)} %get-tuple-element.26), channel_id=1, source_target_pairs={{0,17},{1,16},{8,25},{9,24},{16,1},{17,0},{24,9},{25,8},{2,19},{3,... | collective-permute-start | bytes 589832 | tf_op jit(solution)/shard_map/ppermute | solution.py:366
  20.9 0.9 %fusion.17 = (bf16[1,2,16,8,128]{4,3,2,1,0:T(8,128)(2,1)S(1)}, bf16[8,2,16,8,128]{4,3,2,1,0:T(8,128)(2,1)S(1)}) fusion(bf16[2,2,16,8,128]{4,3,2,1,0:T(8,128)(2,1)} %collective-permute-done.12, bf16[8,2,16,8,128]{4,3,2,1,0:T(8,128)(2,1)S(1)} %get-tuple-element.68), kind=kLoop, calls=%fused_computation.54 | loop fusion | bytes 262144 | tf_op jit(solution)/shard_map/slice | solution.py:381
  21.8 1.8 %collective-permute-done = bf16[2,3,16,8,128]{4,3,2,1,0:T(8,128)(2,1)S(1)} collective-permute-done((bf16[2,3,16,8,128]{4,3,2,1,0:T(8,128)(2,1)S(1)}, bf16[2,3,16,8,128]{4,3,2,1,0:T(8,128)(2,1)S(1)}, u32[]{:S(2)}, u32[]{:S(2)}) %collective-permute-start) | collective-permute-done | bytes 196640 | tf_op jit(solution)/shard_map/ppermute | solution.py:366
  23.7 1.4 %collective-permute-done.1 = bf16[2,3,16,8,128]{4,3,2,1,0:T(8,128)(2,1)S(1)} collective-permute-done((bf16[2,3,16,8,128]{4,3,2,1,0:T(8,128)(2,1)S(1)}, bf16[2,3,16,8,128]{4,3,2,1,0:T(8,128)(2,1)S(1)}, u32[]{:S(2)}, u32[]{:S(2)}) %collective-permute-start.1) | collective-permute-done | bytes 196640 | tf_op jit(solution)/shard_map/ppermute | solution.py:366
  25.1 2.4 %collective-permute-done.2 = bf16[2,3,16,8,128]{4,3,2,1,0:T(8,128)(2,1)S(1)} collective-permute-done((bf16[2,3,16,8,128]{4,3,2,1,0:T(8,128)(2,1)S(1)}, bf16[2,3,16,8,128]{4,3,2,1,0:T(8,128)(2,1)S(1)}, u32[]{:S(2)}, u32[]{:S(2)}) %collective-permute-start.2) | collective-permute-done | bytes 196640 | tf_op jit(solution)/shard_map/ppermute | solution.py:366
  28.0 1.2 %collective-permute-start.6 = (bf16[2,4,16,8,128]{4,3,2,1,0:T(8,128)(2,1)S(1)}, bf16[2,4,16,8,128]{4,3,2,1,0:T(8,128)(2,1)S(1)}, u32[]{:S(2)}, u32[]{:S(2)}) collective-permute-start(bf16[2,4,16,8,128]{4,3,2,1,0:T(8,128)(2,1)S(1)} %get-tuple-element.28), channel_id=1, source_target_pairs={{0,1},{1,0},{8,9},{9,8},{16,17},{17,16},{24,25},{25,24},{2,3},{3,2... | collective-permute-start | bytes 786440 | tf_op jit(solution)/shard_map/ppermute | solution.py:366
  29.2 4.3 %collective-permute-start.14 = (bf16[8,2,16,8,128]{4,3,2,1,0:T(8,128)(2,1)S(1)}, bf16[8,2,16,8,128]{4,3,2,1,0:T(8,128)(2,1)S(1)}, u32[]{:S(2)}, u32[]{:S(2)}) collective-permute-start(bf16[8,2,16,8,128]{4,3,2,1,0:T(8,128)(2,1)S(1)} %constant_dynamic-update-slice_fusion.2.cached_ref), channel_id=1, source_target_pairs={{0,2},{2,4},{4,6},{1,3},{3,5},{5,7},{8,10},{10,12},{12,14},{9,11},... | collective-permute-start | bytes 1572872 | tf_op jit(solution)/shard_map/ppermute | solution.py:389
  33.6 1.3 %collective-permute-start.15 = (bf16[8,2,16,8,128]{4,3,2,1,0:T(8,128)(2,1)S(1)}, bf16[8,2,16,8,128]{4,3,2,1,0:T(8,128)(2,1)S(1)}, u32[]{:S(2)}, u32[]{:S(2)}) collective-permute-start(bf16[8,2,16,8,128]{4,3,2,1,0:T(8,128)(2,1)S(1)} %constant_dynamic-update-slice_fusion.2.cached_ref), channel_id=1, source_target_pairs={{2,0},{4,2},{6,4},{3,1},{5,3},{7,5},{10,8},{12,10},{14,12},{11,9},... | collective-permute-start | bytes 1572872 | tf_op jit(solution)/shard_map/ppermute | solution.py:389
  34.9 1.5 %collective-permute-start.7 = (bf16[2,4,16,8,128]{4,3,2,1,0:T(8,128)(2,1)S(1)}, bf16[2,4,16,8,128]{4,3,2,1,0:T(8,128)(2,1)S(1)}, u32[]{:S(2)}, u32[]{:S(2)}) collective-permute-start(bf16[2,4,16,8,128]{4,3,2,1,0:T(8,128)(2,1)S(1)} %get-tuple-element.29), channel_id=1, source_target_pairs={{0,16},{1,17},{8,24},{9,25},{16,0},{17,1},{24,8},{25,9},{2,18},{3,... | collective-permute-start | bytes 786440 | tf_op jit(solution)/shard_map/ppermute | solution.py:366
  36.8 2.0 %collective-permute-start.8 = (bf16[2,4,16,8,128]{4,3,2,1,0:T(8,128)(2,1)S(1)}, bf16[2,4,16,8,128]{4,3,2,1,0:T(8,128)(2,1)S(1)}, u32[]{:S(2)}, u32[]{:S(2)}) collective-permute-start(bf16[2,4,16,8,128]{4,3,2,1,0:T(8,128)(2,1)S(1)} %get-tuple-element.30), channel_id=1, source_target_pairs={{0,17},{1,16},{8,25},{9,24},{16,1},{17,0},{24,9},{25,8},{2,19},{3,... | collective-permute-start | bytes 786440 | tf_op jit(solution)/shard_map/ppermute | solution.py:366
  38.8 5.3 %collective-permute-done.7 = bf16[2,4,16,8,128]{4,3,2,1,0:T(8,128)(2,1)S(1)} collective-permute-done((bf16[2,4,16,8,128]{4,3,2,1,0:T(8,128)(2,1)S(1)}, bf16[2,4,16,8,128]{4,3,2,1,0:T(8,128)(2,1)S(1)}, u32[]{:S(2)}, u32[]{:S(2)}) %collective-permute-start.7) | collective-permute-done | bytes 262176 | tf_op jit(solution)/shard_map/ppermute | solution.py:366
  44.1 5.1 %collective-permute-done.8 = bf16[2,4,16,8,128]{4,3,2,1,0:T(8,128)(2,1)S(1)} collective-permute-done((bf16[2,4,16,8,128]{4,3,2,1,0:T(8,128)(2,1)S(1)}, bf16[2,4,16,8,128]{4,3,2,1,0:T(8,128)(2,1)S(1)}, u32[]{:S(2)}, u32[]{:S(2)}) %collective-permute-start.8) | collective-permute-done | bytes 262176 | tf_op jit(solution)/shard_map/ppermute | solution.py:366
  49.5 2.8 %shard_map.76 = (f32[8,128,256]{2,1,0:T(8,128)S(1)}, f32[8,128,128]{2,1,0:T(8,128)S(1)}) custom-call(s32[10]{0:T(128)S(1)} %pad_add_fusion.info_ref, bf16[8,3,16,8,128]{4,3,2,1,0:T(8,128)(2,1)S(1)} %constant_dynamic-update-slice_fusion.current_ref, bf16[8,2,16,8,128]{4,3,2,1,0:T(8,128)(2,1)S(1)} %constant_dynamic-update-slice_fusion.2.cached_ref), custom_call_target="tpu_custom_call" | custom-call | flops 2147483648 | bytes 4194304 | tf_op jit(solution)/shard_map/pallas_call | solution.py:419
  52.3 2.8 %shard_map.77 = (f32[8,128,256]{2,1,0:T(8,128)S(1)}, f32[8,128,128]{2,1,0:T(8,128)S(1)}) custom-call(s32[10]{0:T(128)S(1)} %pad_add_fusion.info_ref, bf16[8,3,16,8,128]{4,3,2,1,0:T(8,128)(2,1)S(1)} %constant_dynamic-update-slice_fusion.current_ref, bf16[8,2,16,8,128]{4,3,2,1,0:T(8,128)(2,1)S(1)} %collective-permute-done.14.left_ref, ...), custom_call_target="tpu_custom_call" | custom-call | flops 2147483648 | bytes 4194304 | tf_op jit(solution)/shard_map/pallas_call | solution.py:419
  55.2 6.0 %shard_map.78 = (bf16[4,16,8,128]{3,2,1,0:T(8,128)(2,1)S(1)}, bf16[4,16,8,128]{3,2,1,0:T(8,128)(2,1)S(1)}) custom-call(s32[10]{0:T(128)S(1)} %pad_add_fusion.info_ref, f32[3,3,128]{2,1,0:T(4,128)S(1)} %constant_dynamic-slice_fusion.weight_ref, f32[1,128]{1,0:T(1,128)S(1)} %dynamic-slice_bitcast_fusion.bias_ref, ...), custom_call_target="tpu_custom_call" | custom-call | flops 2147483648 | bytes 4194304 | tf_op jit(solution)/shard_map/pallas_call | solution.py:419
  61.7 1.0 %collective-permute-done.16.beside_ref = bf16[4,16,8,128]{3,2,1,0:T(8,128)(2,1)S(1)} collective-permute-done((bf16[4,16,8,128]{3,2,1,0:T(8,128)(2,1)S(1)}, bf16[4,16,8,128]{3,2,1,0:T(8,128)(2,1)S(1)}, u32[]{:S(2)}, u32[]{:S(2)}) %collective-permute-start.16) | collective-permute-done | bytes 131104 | tf_op jit(solution)/shard_map/ppermute | solution.py:366
  62.7 1.8 %collective-permute-start.19 = (bf16[2,16,8,128]{3,2,1,0:T(8,128)(2,1)S(1)}, bf16[2,16,8,128]{3,2,1,0:T(8,128)(2,1)S(1)}, u32[]{:S(2)}, u32[]{:S(2)}) collective-permute-start(bf16[2,16,8,128]{3,2,1,0:T(8,128)(2,1)S(1)} %pad_maximum_fusion.6), channel_id=1, source_target_pairs={{0,17},{1,16},{8,25},{9,24},{16,1},{17,0},{24,9},{25,8},{2,19},{3,... | collective-permute-start | bytes 196616 | tf_op jit(solution)/shard_map/ppermute | solution.py:366
  65.2 1.2 %collective-permute-start.17 = (bf16[2,16,8,128]{3,2,1,0:T(8,128)(2,1)S(1)}, bf16[2,16,8,128]{3,2,1,0:T(8,128)(2,1)S(1)}, u32[]{:S(2)}, u32[]{:S(2)}) collective-permute-start(bf16[2,16,8,128]{3,2,1,0:T(8,128)(2,1)S(1)} %pad_maximum_fusion.4), channel_id=1, source_target_pairs={{0,1},{1,0},{8,9},{9,8},{16,17},{17,16},{24,25},{25,24},{2,3},{3,2... | collective-permute-start | bytes 196616 | tf_op jit(solution)/shard_map/ppermute | solution.py:366
  66.4 2.2 %collective-permute-done.19.refs_2_ = bf16[2,16,8,128]{3,2,1,0:T(8,128)(2,1)S(1)} collective-permute-done((bf16[2,16,8,128]{3,2,1,0:T(8,128)(2,1)S(1)}, bf16[2,16,8,128]{3,2,1,0:T(8,128)(2,1)S(1)}, u32[]{:S(2)}, u32[]{:S(2)}) %collective-permute-start.19) | collective-permute-done | bytes 65568 | tf_op jit(solution)/shard_map/ppermute | solution.py:366
  69.6 0.8 %shard_map.79 = bf16[16,8,1024]{2,1,0:T(8,128)(2,1)} custom-call(s32[1]{0:T(128)} %bitcast.me_ref, bf16[4,16,8,128]{3,2,1,0:T(8,128)(2,1)S(1)} %get-tuple-element.39.same_ref, bf16[4,16,8,128]{3,2,1,0:T(8,128)(2,1)S(1)} %collective-permute-done.16.beside_ref, bf16[2,16,8,128]{3,2,1,0:T(8,128)(2,1)S(1)} %collective-permute-done.17.refs_0_, ...), custom_call_target="tpu_custom_call" | custom-call | tf_op jit(solution)/shard_map/pallas_call | solution.py:435
  (62 shorter events, 4.9 us)
Async XLA Ops:
  0.0 15.1 %copy-start = (f32[3,3,1024]{2,1,0:T(4,128)S(1)}, f32[3,3,1024]{2,1,0:T(4,128)}, u32[]{:S(2)}) copy-start(f32[3,3,1024]{2,1,0:T(4,128)} %param.12) | copy-start | bytes 110596
  0.0 8.2 %copy-start.3 = (bf16[1,16,8,1024]{3,2,1,0:T(8,128)(2,1)S(1)}, bf16[1,16,8,1024]{3,2,1,0:T(8,128)(2,1)}, u32[]{:S(2)}) copy-start(bf16[1,16,8,1024]{3,2,1,0:T(8,128)(2,1)} %refs_0_.1) | copy-start | bytes 786436
  0.0 8.2 %copy-start.4 = (bf16[1,16,8,1024]{3,2,1,0:T(8,128)(2,1)S(1)}, bf16[1,16,8,1024]{3,2,1,0:T(8,128)(2,1)}, u32[]{:S(2)}) copy-start(bf16[1,16,8,1024]{3,2,1,0:T(8,128)(2,1)} %refs_1_.1) | copy-start | bytes 786436
  1.9 25.8 %collective-permute-start.4 = (bf16[2,16,8,1024]{3,2,1,0:T(8,128)(2,1)}, bf16[2,16,8,1024]{3,2,1,0:T(8,128)(2,1)S(1)}, u32[]{:S(2)}, u32[]{:S(2)}) collective-permute-start(bf16[2,16,8,1024]{3,2,1,0:T(8,128)(2,1)} %pad_maximum_fusion), channel_id=1, source_target_pairs={{0,2},{2,4},{4,6},{1,3},{3,5},{5,7},{8,10},{10,12},{12,14},{9,11},... | collective-permute-start | bytes 1572872 | tf_op jit(solution)/shard_map/ppermute | solution.py:389
  6.9 20.8 %collective-permute-start.5 = (bf16[2,16,8,1024]{3,2,1,0:T(8,128)(2,1)}, bf16[2,16,8,1024]{3,2,1,0:T(8,128)(2,1)S(1)}, u32[]{:S(2)}, u32[]{:S(2)}) collective-permute-start(bf16[2,16,8,1024]{3,2,1,0:T(8,128)(2,1)} %pad_maximum_fusion), channel_id=1, source_target_pairs={{2,0},{4,2},{6,4},{3,1},{5,3},{7,5},{10,8},{12,10},{14,12},{11,9},... | collective-permute-start | bytes 1572872 | tf_op jit(solution)/shard_map/ppermute | solution.py:389
  8.3 5.0 %copy-start.2 = (bf16[16,8,1024]{2,1,0:T(8,128)(2,1)S(1)}, bf16[16,8,1024]{2,1,0:T(8,128)(2,1)}, u32[]{:S(2)}) copy-start(bf16[16,8,1024]{2,1,0:T(8,128)(2,1)} %param.9) | copy-start | bytes 786436
  8.3 5.0 %copy-start.5 = (bf16[16,8,1024]{2,1,0:T(8,128)(2,1)S(1)}, bf16[16,8,1024]{2,1,0:T(8,128)(2,1)}, u32[]{:S(2)}) copy-start(bf16[16,8,1024]{2,1,0:T(8,128)(2,1)} %param.7) | copy-start | bytes 786436
  9.2 4.2 %copy-start.1 = (bf16[16,8,1024]{2,1,0:T(8,128)(2,1)S(1)}, bf16[16,8,1024]{2,1,0:T(8,128)(2,1)}, u32[]{:S(2)}) copy-start(bf16[16,8,1024]{2,1,0:T(8,128)(2,1)} %param.8) | copy-start | bytes 786436
  9.2 6.0 %collective-permute-start.10 = (bf16[2,2,16,8,128]{4,3,2,1,0:T(8,128)(2,1)}, bf16[2,2,16,8,128]{4,3,2,1,0:T(8,128)(2,1)}, u32[]{:S(2)}, u32[]{:S(2)}) collective-permute-start(bf16[2,2,16,8,128]{4,3,2,1,0:T(8,128)(2,1)} %get-tuple-element.32), channel_id=1, source_target_pairs={{0,1},{1,0},{8,9},{9,8},{16,17},{17,16},{24,25},{25,24},{2,3},{3,2... | collective-permute-start | bytes 393224 | tf_op jit(solution)/shard_map/ppermute | solution.py:366
  10.7 7.0 %collective-permute-start.11 = (bf16[2,2,16,8,128]{4,3,2,1,0:T(8,128)(2,1)}, bf16[2,2,16,8,128]{4,3,2,1,0:T(8,128)(2,1)}, u32[]{:S(2)}, u32[]{:S(2)}) collective-permute-start(bf16[2,2,16,8,128]{4,3,2,1,0:T(8,128)(2,1)} %get-tuple-element.33), channel_id=1, source_target_pairs={{0,16},{1,17},{8,24},{9,25},{16,0},{17,1},{24,8},{25,9},{2,18},{3,... | collective-permute-start | bytes 393224 | tf_op jit(solution)/shard_map/ppermute | solution.py:366
  12.2 7.9 %collective-permute-start.12 = (bf16[2,2,16,8,128]{4,3,2,1,0:T(8,128)(2,1)}, bf16[2,2,16,8,128]{4,3,2,1,0:T(8,128)(2,1)}, u32[]{:S(2)}, u32[]{:S(2)}) collective-permute-start(bf16[2,2,16,8,128]{4,3,2,1,0:T(8,128)(2,1)} %get-tuple-element.34), channel_id=1, source_target_pairs={{0,17},{1,16},{8,25},{9,24},{16,1},{17,0},{24,9},{25,8},{2,19},{3,... | collective-permute-start | bytes 393224 | tf_op jit(solution)/shard_map/ppermute | solution.py:366
  13.5 0.7 copy-start.6
  14.2 1.0 %copy-start.7 = (bf16[2,3,16,8,128]{4,3,2,1,0:T(8,128)(2,1)S(1)}, bf16[2,3,16,8,128]{4,3,2,1,0:T(8,128)(2,1)}, u32[]{:S(2)}) copy-start(bf16[2,3,16,8,128]{4,3,2,1,0:T(8,128)(2,1)} %copy-done.6) | copy-start | bytes 589828
  15.2 8.5 %collective-permute-start = (bf16[2,3,16,8,128]{4,3,2,1,0:T(8,128)(2,1)S(1)}, bf16[2,3,16,8,128]{4,3,2,1,0:T(8,128)(2,1)S(1)}, u32[]{:S(2)}, u32[]{:S(2)}) collective-permute-start(bf16[2,3,16,8,128]{4,3,2,1,0:T(8,128)(2,1)S(1)} %copy-done.7), channel_id=1, source_target_pairs={{0,1},{1,0},{8,9},{9,8},{16,17},{17,16},{24,25},{25,24},{2,3},{3,2... | collective-permute-start | bytes 589832 | tf_op jit(solution)/shard_map/ppermute | solution.py:366
  17.7 7.4 %collective-permute-start.1 = (bf16[2,3,16,8,128]{4,3,2,1,0:T(8,128)(2,1)S(1)}, bf16[2,3,16,8,128]{4,3,2,1,0:T(8,128)(2,1)S(1)}, u32[]{:S(2)}, u32[]{:S(2)}) collective-permute-start(bf16[2,3,16,8,128]{4,3,2,1,0:T(8,128)(2,1)S(1)} %get-tuple-element.25), channel_id=1, source_target_pairs={{0,16},{1,17},{8,24},{9,25},{16,0},{17,1},{24,8},{25,9},{2,18},{3,... | collective-permute-start | bytes 589832 | tf_op jit(solution)/shard_map/ppermute | solution.py:366
  20.1 7.4 %collective-permute-start.2 = (bf16[2,3,16,8,128]{4,3,2,1,0:T(8,128)(2,1)S(1)}, bf16[2,3,16,8,128]{4,3,2,1,0:T(8,128)(2,1)S(1)}, u32[]{:S(2)}, u32[]{:S(2)}) collective-permute-start(bf16[2,3,16,8,128]{4,3,2,1,0:T(8,128)(2,1)S(1)} %get-tuple-element.26), channel_id=1, source_target_pairs={{0,17},{1,16},{8,25},{9,24},{16,1},{17,0},{24,9},{25,8},{2,19},{3,... | collective-permute-start | bytes 589832 | tf_op jit(solution)/shard_map/ppermute | solution.py:366
  20.9 0.9 %copy-start.8 = (bf16[1,2,16,8,128]{4,3,2,1,0:T(8,128)(2,1)S(1)}, bf16[1,2,16,8,128]{4,3,2,1,0:T(8,128)(2,1)}, u32[]{:S(2)}) copy-start(bf16[1,2,16,8,128]{4,3,2,1,0:T(8,128)(2,1)} %get-tuple-element.63) | copy-start | bytes 196612
  23.6 5.6 %collective-permute-start.13 = (bf16[4,2,16,8,128]{4,3,2,1,0:T(8,128)(2,1)S(1)}, bf16[4,2,16,8,128]{4,3,2,1,0:T(8,128)(2,1)S(1)}, u32[]{:S(2)}, u32[]{:S(2)}) collective-permute-start(bf16[4,2,16,8,128]{4,3,2,1,0:T(8,128)(2,1)S(1)} %pad_maximum_fusion.3), channel_id=1, source_target_pairs={{0,8},{1,9},{8,0},{9,1},{16,24},{17,25},{24,16},{25,17},{2,10},{3,... | collective-permute-start | bytes 786440 | tf_op jit(solution)/shard_map/ppermute | solution.py:366
  27.6 21.8 %collective-permute-start.3 = (bf16[4,3,16,8,128]{4,3,2,1,0:T(8,128)(2,1)S(1)}, bf16[4,3,16,8,128]{4,3,2,1,0:T(8,128)(2,1)S(1)}, u32[]{:S(2)}, u32[]{:S(2)}) collective-permute-start(bf16[4,3,16,8,128]{4,3,2,1,0:T(8,128)(2,1)S(1)} %pad_maximum_fusion.2), channel_id=1, source_target_pairs={{0,8},{1,9},{8,0},{9,1},{16,24},{17,25},{24,16},{25,17},{2,10},{3,... | collective-permute-start | bytes 1179656 | tf_op jit(solution)/shard_map/ppermute | solution.py:366
  28.0 8.7 %collective-permute-start.6 = (bf16[2,4,16,8,128]{4,3,2,1,0:T(8,128)(2,1)S(1)}, bf16[2,4,16,8,128]{4,3,2,1,0:T(8,128)(2,1)S(1)}, u32[]{:S(2)}, u32[]{:S(2)}) collective-permute-start(bf16[2,4,16,8,128]{4,3,2,1,0:T(8,128)(2,1)S(1)} %get-tuple-element.28), channel_id=1, source_target_pairs={{0,1},{1,0},{8,9},{9,8},{16,17},{17,16},{24,25},{25,24},{2,3},{3,2... | collective-permute-start | bytes 786440 | tf_op jit(solution)/shard_map/ppermute | solution.py:366
  29.2 23.1 %collective-permute-start.14 = (bf16[8,2,16,8,128]{4,3,2,1,0:T(8,128)(2,1)S(1)}, bf16[8,2,16,8,128]{4,3,2,1,0:T(8,128)(2,1)S(1)}, u32[]{:S(2)}, u32[]{:S(2)}) collective-permute-start(bf16[8,2,16,8,128]{4,3,2,1,0:T(8,128)(2,1)S(1)} %constant_dynamic-update-slice_fusion.2.cached_ref), channel_id=1, source_target_pairs={{0,2},{2,4},{4,6},{1,3},{3,5},{5,7},{8,10},{10,12},{12,14},{9,11},... | collective-permute-start | bytes 1572872 | tf_op jit(solution)/shard_map/ppermute | solution.py:389
  33.6 18.7 %collective-permute-start.15 = (bf16[8,2,16,8,128]{4,3,2,1,0:T(8,128)(2,1)S(1)}, bf16[8,2,16,8,128]{4,3,2,1,0:T(8,128)(2,1)S(1)}, u32[]{:S(2)}, u32[]{:S(2)}) collective-permute-start(bf16[8,2,16,8,128]{4,3,2,1,0:T(8,128)(2,1)S(1)} %constant_dynamic-update-slice_fusion.2.cached_ref), channel_id=1, source_target_pairs={{2,0},{4,2},{6,4},{3,1},{5,3},{7,5},{10,8},{12,10},{14,12},{11,9},... | collective-permute-start | bytes 1572872 | tf_op jit(solution)/shard_map/ppermute | solution.py:389
  34.9 9.2 %collective-permute-start.7 = (bf16[2,4,16,8,128]{4,3,2,1,0:T(8,128)(2,1)S(1)}, bf16[2,4,16,8,128]{4,3,2,1,0:T(8,128)(2,1)S(1)}, u32[]{:S(2)}, u32[]{:S(2)}) collective-permute-start(bf16[2,4,16,8,128]{4,3,2,1,0:T(8,128)(2,1)S(1)} %get-tuple-element.29), channel_id=1, source_target_pairs={{0,16},{1,17},{8,24},{9,25},{16,0},{17,1},{24,8},{25,9},{2,18},{3,... | collective-permute-start | bytes 786440 | tf_op jit(solution)/shard_map/ppermute | solution.py:366
  36.8 12.5 %collective-permute-start.8 = (bf16[2,4,16,8,128]{4,3,2,1,0:T(8,128)(2,1)S(1)}, bf16[2,4,16,8,128]{4,3,2,1,0:T(8,128)(2,1)S(1)}, u32[]{:S(2)}, u32[]{:S(2)}) collective-permute-start(bf16[2,4,16,8,128]{4,3,2,1,0:T(8,128)(2,1)S(1)} %get-tuple-element.30), channel_id=1, source_target_pairs={{0,17},{1,16},{8,25},{9,24},{16,1},{17,0},{24,9},{25,8},{2,19},{3,... | collective-permute-start | bytes 786440 | tf_op jit(solution)/shard_map/ppermute | solution.py:366
  49.4 5.7 %collective-permute-start.9 = (bf16[4,4,16,8,128]{4,3,2,1,0:T(8,128)(2,1)S(1)}, bf16[4,4,16,8,128]{4,3,2,1,0:T(8,128)(2,1)S(1)}, u32[]{:S(2)}, u32[]{:S(2)}) collective-permute-start(bf16[4,4,16,8,128]{4,3,2,1,0:T(8,128)(2,1)S(1)} %pad_maximum_fusion.1), channel_id=1, source_target_pairs={{0,8},{1,9},{8,0},{9,1},{16,24},{17,25},{24,16},{25,17},{2,10},{3,... | collective-permute-start | bytes 1572872 | tf_op jit(solution)/shard_map/ppermute | solution.py:366
  61.2 1.5 %collective-permute-start.16 = (bf16[4,16,8,128]{3,2,1,0:T(8,128)(2,1)S(1)}, bf16[4,16,8,128]{3,2,1,0:T(8,128)(2,1)S(1)}, u32[]{:S(2)}, u32[]{:S(2)}) collective-permute-start(bf16[4,16,8,128]{3,2,1,0:T(8,128)(2,1)S(1)} %get-tuple-element.40), channel_id=1, source_target_pairs={{0,8},{1,9},{8,0},{9,1},{16,24},{17,25},{24,16},{25,17},{2,10},{3,... | collective-permute-start | bytes 393224 | tf_op jit(solution)/shard_map/ppermute | solution.py:366
  62.7 5.9 %collective-permute-start.19 = (bf16[2,16,8,128]{3,2,1,0:T(8,128)(2,1)S(1)}, bf16[2,16,8,128]{3,2,1,0:T(8,128)(2,1)S(1)}, u32[]{:S(2)}, u32[]{:S(2)}) collective-permute-start(bf16[2,16,8,128]{3,2,1,0:T(8,128)(2,1)S(1)} %pad_maximum_fusion.6), channel_id=1, source_target_pairs={{0,17},{1,16},{8,25},{9,24},{16,1},{17,0},{24,9},{25,8},{2,19},{3,... | collective-permute-start | bytes 196616 | tf_op jit(solution)/shard_map/ppermute | solution.py:366
  64.6 4.3 %collective-permute-start.18 = (bf16[2,16,8,128]{3,2,1,0:T(8,128)(2,1)S(1)}, bf16[2,16,8,128]{3,2,1,0:T(8,128)(2,1)S(1)}, u32[]{:S(2)}, u32[]{:S(2)}) collective-permute-start(bf16[2,16,8,128]{3,2,1,0:T(8,128)(2,1)S(1)} %pad_maximum_fusion.5), channel_id=1, source_target_pairs={{0,16},{1,17},{8,24},{9,25},{16,0},{17,1},{24,8},{25,9},{2,18},{3,... | collective-permute-start | bytes 196616 | tf_op jit(solution)/shard_map/ppermute | solution.py:366
  65.2 4.4 %collective-permute-start.17 = (bf16[2,16,8,128]{3,2,1,0:T(8,128)(2,1)S(1)}, bf16[2,16,8,128]{3,2,1,0:T(8,128)(2,1)S(1)}, u32[]{:S(2)}, u32[]{:S(2)}) collective-permute-start(bf16[2,16,8,128]{3,2,1,0:T(8,128)(2,1)S(1)} %pad_maximum_fusion.4), channel_id=1, source_target_pairs={{0,1},{1,0},{8,9},{9,8},{16,17},{17,16},{24,25},{25,24},{2,3},{3,2... | collective-permute-start | bytes 196616 | tf_op jit(solution)/shard_map/ppermute | solution.py:366

commit v4 on v3

--- a/solution.py
+++ b/solution.py
@@ -154,105 +154,73 @@
 
 
 class Window:
-    def __init__(self, grid, tile, info_ref, current_ref, sides):
+    def __init__(self, grid, tile, info_ref, query_ref, pairs_ref):
         self.grid_rows, self.grid_cols = grid
         self.tile_rows, self.tile_cols = tile
         self.size = self.tile_rows * self.tile_cols
-        self.info, self.current, self.sides = info_ref, current_ref, sides
+        self.info, self.query, self.pairs = info_ref, query_ref, pairs_ref
         self.scale = HD ** (-0.5) * LOG2E
-        self.bias_left = jnp.where(info_ref[0] > 0, 0.0, NEG).astype(jnp.float32)
-        self.bias_right = jnp.where(info_ref[1] > 0, 0.0, NEG).astype(jnp.float32)
         query = lax.broadcasted_iota(jnp.int32, (self.size, self.size), 0)
         key = lax.broadcasted_iota(jnp.int32, (self.size, self.size), 1)
         self.upper = key // self.tile_cols >= query // self.tile_cols
         self.left = key % self.tile_cols >= query % self.tile_cols
         self.upper_one = self.upper.astype(jnp.float32).astype(jnp.bfloat16)
-        self.left_one = self.left.astype(jnp.float32).astype(jnp.bfloat16)
 
     def slot(self, row, col):
-        return self.info[2 + row * self.grid_cols + col]
-
-    def side(self, col):
-        return 1 if col < 0 else (2 if col >= self.grid_cols else 0)
-
-    def tile(self, frame, part, row, col):
-        ref, base = self.sides[frame][self.side(col)]
-        return ref[self.slot(row, col % self.grid_cols), base + part].reshape(self.size, HD)
-
-    def steps(self, col, inner):
-        near = [step for step in (-1, 0, 1) if 0 <= col + step < self.grid_cols]
-        return near if inner else [step for step in (-1, 0, 1, 2) if step not in near]
-
-    def attend(self, row, col, wanted, before):
-        query = self.current[self.slot(row, col), 2].reshape(self.size, HD)
+        return self.info[2 + row * self.grid_cols + col % self.grid_cols]
+
+    def tile(self, member, row, col):
+        return self.pairs[self.slot(row, col), member].reshape(self.size, HD)
+
+    def attend(self, row, col):
+        query = self.query[self.slot(row, col), pl.ds(0, self.tile_rows)].reshape(self.size, HD)
+        frames = range(self.pairs.shape[1] // 2)
+        cols = [c for c in range(self.grid_cols) if abs(c - col) <= 2]
+        up, down = row > 0, row + 1 < self.grid_rows
         rows = [r for r in (row - 1, row, row + 1) if 0 <= r < self.grid_rows]
-        needed = []
-        for frame, step in wanted:
-            for key_col in (col - 2, col + 2) if step == 2 else (col + step,):
-                needed += [(frame, r, key_col) for r in rows]
-        keys = jnp.concatenate([self.tile(frame, 0, r, c) for frame, r, c in needed], axis=0)
+        needed = [(f, r, c) for f in frames for c in cols for r in rows]
+        keys = jnp.concatenate([self.tile(2 * f, r, c) for f, r, c in needed], axis=0)
         raw = lax.dot_general(query, keys, (((1,), (1,)), ((), ())), preferred_element_type=jnp.float32)
-        scores = {}
-        for i, (frame, r, c) in enumerate(needed):
-            score = raw[:, i * self.size : (i + 1) * self.size]
-            if self.side(c) == 1:
-                score = score + self.bias_left
-            elif self.side(c) == 2:
-                score = score + self.bias_right
-            scores[frame, r, c] = score
-        up, down = row > 0, row + 1 < self.grid_rows
-
-        def level(frame, c):
-            return scores[frame, row, c]
-
-        def beside(frame, c):
-            above = scores[frame, row - 1, c] if up else NEG
-            return jnp.where(self.upper, above, scores[frame, row + 1, c] if down else NEG)
-
+        scores = {key: raw[:, i * self.size : (i + 1) * self.size] for i, key in enumerate(needed)}
         blocks = []
-        for frame, step in wanted:
-            for off_row, make in ((False, level), (True, beside)):
-                if off_row and not (up or down):
-                    continue
-                if step == 2:
-                    block = jnp.where(self.left, make(frame, col - 2), make(frame, col + 2))
-                else:
-                    block = make(frame, col + step)
-                blocks.append((frame, off_row, step, block))
+        for f in frames:
+            for c in cols:
+                found = [(False, scores[f, row, c])]
+                if up or down:
+                    above = scores[f, row - 1, c] if up else NEG
+                    found.append((True, jnp.where(self.upper, above, scores[f, row + 1, c] if down else NEG)))
+                for off_row, block in found:
+                    if c - col == 2:
+                        block = jnp.where(self.left, NEG, block)
+                    elif c - col == -2:
+                        block = jnp.where(self.left, block, NEG)
+                    blocks.append((f, off_row, c, block))
         top = blocks[0][3]
         for entry in blocks[1:]:
             top = jnp.maximum(top, entry[3])
         top = jnp.max(top, axis=1, keepdims=True)
-        if before is not None:
-            top = jnp.maximum(top, before[0])
         parts = []
-        for frame, off_row, step, block in blocks:
+        for f, off_row, c, block in blocks:
             weights = jnp.exp2((block - top) * self.scale).astype(jnp.bfloat16)
             if off_row and up and down:
-                by_row = [(row - 1, weights * self.upper_one), (row + 1, weights * (1 - self.upper_one))]
+                parts.append((f, row - 1, c, weights * self.upper_one))
+                parts.append((f, row + 1, c, weights * (1 - self.upper_one)))
             elif off_row:
-                by_row = [(row + 1 if down else row - 1, weights)]
+                parts.append((f, row + 1 if down else row - 1, c, weights))
             else:
-                by_row = [(row, weights)]
-            for r, part in by_row:
-                if step == 2:
-                    parts.append((frame, r, col - 2, part * self.left_one))
-                    parts.append((frame, r, col + 2, part * (1 - self.left_one)))
-                else:
-                    parts.append((frame, r, col + step, part))
-        values = jnp.concatenate([self.tile(frame, 1, r, c) for frame, r, c, _ in parts], axis=0)
+                parts.append((f, row, c, weights))
+        values = jnp.concatenate([self.tile(2 * f + 1, r, c) for f, r, c, _ in parts], axis=0)
         values = jnp.concatenate([values, jnp.ones_like(values)], axis=1)
         weights = jnp.concatenate([part for _, _, _, part in parts], axis=1)
         total = jnp.dot(weights, values, preferred_element_type=jnp.float32)
-        if before is not None:
-            total = total + before[1] * jnp.exp2((before[0] - top) * self.scale)
-        return top, total
-
-    def enhanced(self, row, col, weight_ref, bias_ref):
+        return total[:, :HD] / total[:, HD:], top * self.scale + jnp.log2(total[:, HD:])
+
+    def enhanced(self, row, col, weight_ref, bias_ref, before_ref, after_ref):
         shape = (self.tile_cols, HD)
         sub = lax.broadcasted_iota(jnp.int32, shape, 0)
         taps = [[weight_ref[a, pl.ds(b, 1), :] for b in range(3)] for a in range(3)]
         last = self.tile_cols - 1
+        member = self.pairs.shape[1] - 1
         lines = []
         for key_row in range(row * self.tile_rows - 1, (row + 1) * self.tile_rows + 1):
             tile_row, line = key_row // self.tile_rows, key_row % self.tile_rows
@@ -261,12 +229,17 @@
                 continue
 
             def values(c):
-                ref, base = self.sides[1][self.side(c)]
-                return ref[self.slot(tile_row, c % self.grid_cols), base + 1, line].astype(jnp.float32)
-
-            here, before, after = values(col), values(col - 1), values(col + 1)
-            low = jnp.where(sub == 0, pltpu.roll(before, 1, 0), pltpu.roll(here, 1, 0))
-            high = jnp.where(sub == last, pltpu.roll(after, last, 0), pltpu.roll(here, last, 0))
+                return self.pairs[self.slot(tile_row, c), member, line].astype(jnp.float32)
+
+            def edge(ref, c):
+                packed = ref[self.slot(tile_row, c), self.tile_rows + line // self.tile_cols].astype(jnp.float32)
+                return jnp.broadcast_to(packed[line % self.tile_cols : line % self.tile_cols + 1], shape)
+
+            here = values(col)
+            before = pltpu.roll(values(col - 1), 1, 0) if col > 0 else edge(before_ref, self.grid_cols - 1)
+            after = pltpu.roll(values(col + 1), last, 0) if col + 1 < self.grid_cols else edge(after_ref, 0)
+            low = jnp.where(sub == 0, before, pltpu.roll(here, 1, 0))
+            high = jnp.where(sub == last, after, pltpu.roll(here, last, 0))
             lines.append((low, here, high))
         sums = []
         for line in range(self.tile_rows):
@@ -279,65 +252,90 @@
         return jnp.stack(sums, axis=0)
 
 
-def running(top_ref, sum_ref, index):
-    return top_ref[index][:, :1], sum_ref[index]
-
-
-def own_kernel(grid, tile, info_ref, current_ref, cached_ref, sum_ref, top_ref):
-    window = Window(grid, tile, info_ref, current_ref, [[(cached_ref, 0)], [(current_ref, 0)]])
-    for row in range(grid[0]):
-        for col in range(grid[1]):
-            wanted = [(frame, step) for frame in (0, 1) for step in window.steps(col, True)]
-            top, total = window.attend(row, col, wanted, None)
-            sum_ref[row * grid[1] + col] = total
-            top_ref[row * grid[1] + col] = jnp.broadcast_to(top, (window.size, HD))
-
-
-def cached_kernel(grid, tile, info_ref, current_ref, left_ref, right_ref, sum_in, top_in, sum_ref, top_ref):
-    window = Window(grid, tile, info_ref, current_ref, [[None, (left_ref, 0), (right_ref, 0)]])
+def visit_kernel(grid, tile, first_col, info_ref, query_ref, pairs_ref, out_ref):
+    window = Window(grid, tile, info_ref, query_ref, pairs_ref)
+    size, count = window.size, grid[0] * grid[1]
+    lane = lax.broadcasted_iota(jnp.int32, (size, HD), 1)
+    packed = jnp.zeros((size, HD), jnp.float32)
     for row in range(grid[0]):
         for col in range(grid[1]):
             index = row * grid[1] + col
-            wanted = [(0, step) for step in window.steps(col, False)]
-            top, total = window.attend(row, col, wanted, running(top_in, sum_in, index))
-            sum_ref[index] = total
-            top_ref[index] = jnp.broadcast_to(top, (window.size, HD))
-
-
-def last_kernel(
-    grid, tile, info_ref, weight_ref, bias_ref, current_ref, halo_ref, sum_in, top_in, same_ref, beside_ref
+            part, level = window.attend(row, first_col + col)
+            out_ref[window.slot(row, col)] = part.reshape(tile + (HD,)).astype(jnp.bfloat16)
+            high = level.astype(jnp.bfloat16).astype(jnp.float32)
+            middle = (level - high).astype(jnp.bfloat16).astype(jnp.float32)
+            for i, piece in enumerate((high, middle, level - high - middle)):
+                packed = jnp.where(lane == i * count + index, piece, packed)
+    out_ref[count] = packed.reshape(tile + (HD,)).astype(jnp.bfloat16)
+
+
+def own_kernel(
+    grid, tile, info_ref, weight_ref, bias_ref, query_ref, pairs_ref, before_ref, after_ref, part_ref, level_ref, conv_ref
 ):
-    window = Window(grid, tile, info_ref, current_ref, [None, [(current_ref, 0), (halo_ref, 0), (halo_ref, 2)]])
-    count = grid[0] * grid[1]
+    window = Window(grid, tile, info_ref, query_ref, pairs_ref)
     for row in range(grid[0]):
         for col in range(grid[1]):
             index = row * grid[1] + col
-            wanted = [(1, step) for step in window.steps(col, False)]
-            _, total = window.attend(row, col, wanted, running(top_in, sum_in, index))
-            attended = (total[:, :HD] / total[:, HD:]).reshape(tile + (HD,))
-            out = (attended + window.enhanced(row, col, weight_ref, bias_ref)).astype(jnp.bfloat16)
-            place = info_ref[2 + index]
-
-            @pl.when(place < count // 2)
-            def _():
-                same_ref[place] = out
-
-            @pl.when(place >= count // 2)
-            def _():
-                beside_ref[place - count // 2] = out
+            part_ref[index], level_ref[index] = window.attend(row, col)
+            conv = window.enhanced(row, col, weight_ref, bias_ref, before_ref, after_ref)
+            conv_ref[index] = conv.reshape(window.size, HD)
+
+
+def join_kernel(grid, tile, info_ref, part_ref, level_ref, conv_ref, left_ref, right_ref, same_ref, beside_ref):
+    size, count = tile[0] * tile[1], grid[0] * grid[1]
+    present = [info_ref[0] > 0, info_ref[1] > 0]
+    visits = (left_ref, right_ref)
+    packed = [ref[count].reshape(size, HD).astype(jnp.float32) for ref in visits]
+    for index in range(count):
+        place = info_ref[2 + index]
+        parts, levels = [part_ref[index]], [level_ref[index]]
+        for ref, there, pack in zip(visits, present, packed):
+            parts.append(ref[place].reshape(size, HD).astype(jnp.float32))
+            level = pack[:, index : index + 1]
+            for i in (1, 2):
+                level = level + pack[:, i * count + index : i * count + index + 1]
+            levels.append(jnp.broadcast_to(jnp.where(there, level, NEG), (size, HD)))
+        top = jnp.maximum(jnp.maximum(levels[0], levels[1]), levels[2])
+        shares = [jnp.exp2(level - top) for level in levels]
+        mixed = sum(share * part for share, part in zip(shares, parts)) / sum(shares)
+        out = (mixed + conv_ref[index]).reshape(tile + (HD,)).astype(jnp.bfloat16)
+
+        @pl.when(place < count // 2)
+        def _():
+            same_ref[place] = out
+
+        @pl.when(place >= count // 2)
+        def _():
+            beside_ref[place - count // 2] = out
 
 
 def lanes(head):
     return pl.ds(pl.multiple_of(head * HD, HD), HD)
 
 
-def pack_kernel(flips, side, members, me_ref, *refs):
-    buffers = refs[len(refs) - len(flips) :]
+def pack_kernel(flips, side, me_ref, *refs):
+    sources, buffers = refs[: len(refs) - len(flips)], refs[len(refs) - len(flips) :]
     for buffer, flip in zip(buffers, flips):
         for other in range(2):
             head = me_ref[0] ^ (flip ^ (side if other else 0))
-            for member, (source, lead) in enumerate(members):
-                buffer[other, member] = refs[source][lead, :, :, lanes(head)]
+            for member, source in enumerate(sources):
+                buffer[other, member] = source[:, :, lanes(head)]
+
+
+def query_kernel(flips, side, me_ref, query_ref, values_ref, *buffers):
+    tile_rows, tile_cols, _ = query_ref.shape
+    sub = lax.broadcasted_iota(jnp.int32, (tile_cols, HD), 0)
+    for buffer, flip in zip(buffers, flips):
+        for other in range(2):
+            head = me_ref[0] ^ (flip ^ (side if other else 0))
+            buffer[other, pl.ds(0, tile_rows)] = query_ref[:, :, lanes(head)]
+            for start in range(0, tile_rows, tile_cols):
+                packed = jnp.zeros((tile_cols, HD), jnp.float32)
+                for line in range(tile_cols):
+                    values = values_ref[start + line, :, lanes(head)].astype(jnp.float32)
+                    edge = jnp.where(me_ref[1] == 0, values[:1], values[tile_cols - 1 :])
+                    packed = jnp.where(sub == line, edge, packed)
+                buffer[other, tile_rows + start // tile_cols] = packed.astype(jnp.bfloat16)
 
 
 def unpack_kernel(flips, side, me_ref, same_ref, beside_ref, *refs):
@@ -354,27 +352,27 @@
     tile_rows, tile_cols, channels = queries.shape
     heads = channels // HD
     grid, tile = (group_rows, group_cols), (tile_rows, tile_cols)
+    size = tile_rows * tile_cols
     axes = ("ht", "near")
     block = (tile_rows, tile_cols, HD)
     side = group_cols
     flips = [flip for flip in range(heads) if not flip & side]
-    me = lax.axis_index("ht") * group_cols + lax.axis_index("near")
-    me = me.astype(jnp.int32)
-    me_ref = me.reshape(1)
+    near = lax.axis_index("near").astype(jnp.int32)
+    me = lax.axis_index("ht").astype(jnp.int32) * group_cols + near
+    me_ref = jnp.stack([me, near])
 
     def swap(x, flip):
         return lax.ppermute(x, axes, [(s, s ^ flip) for s in range(heads)])
 
-    def pack(*arrays):
-        members = [(i, lead) for i, array in enumerate(arrays) for lead in range(array.shape[0])]
+    def call(kernel, out_shape, params, cost, *operands):
         return pl.pallas_call(
-            functools.partial(pack_kernel, flips, side, members),
-            out_shape=[jax.ShapeDtypeStruct((2, len(members)) + block, jnp.bfloat16)] * len(flips),
-            in_specs=[SMEM] + [VMEM] * len(arrays),
-            out_specs=[VMEM] * len(flips),
-            compiler_params=SMALL,
-            cost_estimate=pl.CostEstimate(flops=0, bytes_accessed=len(members) << 20, transcendentals=0),
-        )(me_ref, *arrays)
+            kernel,
+            out_shape=out_shape,
+            in_specs=[SMEM] + [VMEM] * (len(operands) - 1),
+            out_specs=jax.tree.map(lambda _: VMEM, out_shape),
+            compiler_params=params,
+            cost_estimate=pl.CostEstimate(flops=cost << 30, bytes_accessed=1 << 20, transcendentals=0),
+        )(*operands)
 
     def gather(buffers):
         got = [buffers[0]] + [swap(b, flip) for b, flip in zip(buffers[1:], flips[1:])]
@@ -384,19 +382,18 @@
 
     up = [(i, i + 1) for i in range(far - 1)]
     down = [(i + 1, i) for i in range(far - 1)]
-
-    def halo(x):
-        return lax.ppermute(x, "far", up), lax.ppermute(x, "far", down)
-
-    pair = jnp.stack([keys_new, values_new])
-    new_left, new_right = halo(pair)
-    packed_cached = pack(keys_cache, values_cache)
-    cached = gather(packed_cached)
-    packed_current = pack(keys_new[None], values_new[None], queries[None])
-    current = gather(packed_current)
-    cached_left, cached_right = halo(cached)
-    packed_beyond = pack(new_left, new_right)
-    beyond = gather(packed_beyond)
+    edges = -(-tile_rows // tile_cols)
+    buffer = jax.ShapeDtypeStruct((2, tile_rows + edges, tile_cols, HD), jnp.bfloat16)
+    packed_query = call(
+        functools.partial(query_kernel, flips, side), [buffer] * len(flips), SMALL, 0, me_ref, queries, values_new
+    )
+    query = gather(packed_query)
+    sources = (keys_cache[0], values_cache[0], keys_new, values_new)
+    buffer = jax.ShapeDtypeStruct((2, len(sources)) + block, jnp.bfloat16)
+    packed_pairs = call(functools.partial(pack_kernel, flips, side), [buffer] * len(flips), SMALL, 0, me_ref, *sources)
+    pairs = gather(packed_pairs)
+    query_left = lax.ppermute(query, "far", up)
+    query_right = lax.ppermute(query, "far", down)
     far_index = lax.axis_index("far")
     flip = me ^ jnp.arange(heads, dtype=jnp.int32)
     beside = (flip // side) % 2
@@ -409,36 +406,33 @@
     )
     weight = lax.dynamic_slice_in_dim(conv_weight, me * HD, HD, 2)
     bias = lax.dynamic_slice_in_dim(conv_bias.reshape(1, channels), me * HD, HD, 1)
-    size = tile_rows * tile_cols
-    state = (
-        jax.ShapeDtypeStruct((heads, size, 2 * HD), jnp.float32),
-        jax.ShapeDtypeStruct((heads, size, HD), jnp.float32),
-    )
-
-    def attention(kernel, out_shape, *operands):
-        return pl.pallas_call(
-            functools.partial(kernel, grid, tile),
-            out_shape=out_shape,
-            in_specs=[SMEM] + [VMEM] * len(operands),
-            out_specs=(VMEM, VMEM),
-            compiler_params=LIMIT,
-            cost_estimate=pl.CostEstimate(flops=2**31, bytes_accessed=2**22, transcendentals=2**20),
-        )(info, *operands)
-
-    sums, tops = attention(own_kernel, state, current, cached)
-    sums, tops = attention(cached_kernel, state, current, cached_left, cached_right, sums, tops)
+
+    def visit(queries, first_col):
+        kernel = functools.partial(visit_kernel, grid, tile, first_col)
+        return call(kernel, jax.ShapeDtypeStruct((heads + 1,) + block, jnp.bfloat16), LIMIT, 4, info, queries, pairs)
+
+    left_part = visit(query_left, -group_cols)
+    from_right = lax.ppermute(left_part, "far", down)
+    right_part = visit(query_right, group_cols)
+    from_left = lax.ppermute(right_part, "far", up)
+    part = jax.ShapeDtypeStruct((heads, size, HD), jnp.float32)
+    kernel = functools.partial(own_kernel, grid, tile)
+    own = call(kernel, [part] * 3, LIMIT, 4, info, weight, bias, query, pairs, query_left, query_right)
     half = jax.ShapeDtypeStruct((len(flips),) + block, jnp.bfloat16)
-    same, other = attention(last_kernel, (half, half), weight, bias, current, beyond, sums, tops)
+    kernel = functools.partial(join_kernel, grid, tile)
+    same, other = call(kernel, [half, half], LIMIT, 1, info, *own, from_left, from_right)
     received = swap(other, side)
-    pairs = [jnp.stack([same[i], received[i]]) for i in range(1, len(flips))]
-    got = [swap(pair, flip) for pair, flip in zip(pairs, flips[1:])]
-    return pl.pallas_call(
+    got = [swap(jnp.stack([same[i], received[i]]), flips[i]) for i in range(1, len(flips))]
+    return call(
         functools.partial(unpack_kernel, flips, side),
-        out_shape=jax.ShapeDtypeStruct(queries.shape, jnp.bfloat16),
-        in_specs=[SMEM] + [VMEM] * (len(flips) + 1),
-        out_specs=VMEM,
-        compiler_params=SMALL,
-    )(me_ref, same, received, *got)
+        jax.ShapeDtypeStruct(queries.shape, jnp.bfloat16),
+        SMALL,
+        0,
+        me_ref,
+        same,
+        received,
+        *got,
+    )
 
 
 def grouping(mesh, heads):

time: 70.7 us -> 68.2 us (0.965)
  waiting for transfers between devices: 20.6 us -> 26.6 us
  starting transfers between devices: 28.4 us -> 22.8 us
  other arithmetic: 2.29 us -> 0.37 us
    ppermute x4, waiting for transfers between devices: 0.01 us -> 10.2 us  [the longest x1 5.66 us: head_step(): from_right = lax.ppermute(left_part, 'far', down)]
    ppermute x16 -> x12, starting transfers between devices: 16.5 us -> 12.1 us  [swap(): return lax.ppermute(x, axes, [(s, s ^ flip) for s in range(heads)])]
    ppermute x16 -> x12, waiting for transfers between devices: 20.5 us -> 16.4 us  [swap(): return lax.ppermute(x, axes, [(s, s ^ flip) for s in range(heads)])]
    slice x12 -> x8, local copies, waits for them, and re-layouts: 3.51 us -> 0.15 us  [gather(): forward = jnp.stack([b[1] for b in got])]
    unnamed x18 -> x14, local copies, waits for them, and re-layouts: 0.71 us -> 3.81 us
    another operation x4, other arithmetic: 1.96 us -> 0.1 us  [the longest x1 0.07 us: head_step(): me_ref = jnp.stack([me, near])]
    ppermute x4, starting transfers between devices: 11.9 us -> 10.6 us  [the longest x1 4.55 us: head_step(): query_left = lax.ppermute(query, 'far', up)]
  transfers between devices with their start and end apart: 20 -> 16, of which waited for: 10 -> 8; matrix products, arithmetic and copies ran while one was open for 7% -> 2% of each run, Pallas kernels for 10% -> 14%
where the time goes in v4:
time: 68.2 us; the launch traced here: 67.9 us
  waiting for transfers between devices  26.6 us (39%)
  starting transfers between devices  22.8 us (33%)
  Pallas kernels  13 us (19%)
  local copies, waits for them, and re-layouts  4.84 us (7%)
    ppermute x12, waiting for transfers between devices, swap(): return lax.ppermute(x, axes, [(s, s ^ flip) for s in range(heads)])  16.4 us
    pallas_call x7, Pallas kernels, call(): pl.pallas_call(kernel, out_shape=out_shape, in_specs=[SMEM] + [VMEM] * (l...  13 us
    ppermute x12, starting transfers between devices, swap(): return lax.ppermute(x, axes, [(s, s ^ flip) for s in range(heads)])  12.1 us
    ppermute x1, waiting for transfers between devices, head_step(): from_right = lax.ppermute(left_part, 'far', down)  5.66 us
    ppermute x1, waiting for transfers between devices, head_step(): query_right = lax.ppermute(query, 'far', down)  4.58 us
    ppermute x1, starting transfers between devices, head_step(): query_left = lax.ppermute(query, 'far', up)  4.55 us
    unnamed x14, local copies, waits for them, and re-layouts  3.81 us
    ppermute x1, starting transfers between devices, head_step(): from_left = lax.ppermute(right_part, 'far', up)  3.5 us
  transfers between devices with their start and end apart: 16, of which 8 were waited for; matrix products, arithmetic and copies ran while one was open for 2% of the time, Pallas kernels for 14%

profile of v4, /device:TPU:0, one launch (start us, length us, event | category | flops | bytes accessed | tf_op | source)
XLA Modules:
  0.0 67.9 jit_solution(9639278908467755510)
XLA Ops:
  0.1 0.9 %copy-done.1 = bf16[16,8,1024]{2,1,0:T(8,128)(2,1)S(1)} copy-done((bf16[16,8,1024]{2,1,0:T(8,128)(2,1)S(1)}, bf16[16,8,1024]{2,1,0:T(8,128)(2,1)}, u32[]{:S(2)}) %copy-start.1) | copy-done | bytes 262168
  1.0 0.9 %copy-done.3 = bf16[16,8,1024]{2,1,0:T(8,128)(2,1)S(1)} copy-done((bf16[16,8,1024]{2,1,0:T(8,128)(2,1)S(1)}, bf16[16,8,1024]{2,1,0:T(8,128)(2,1)}, u32[]{:S(2)}) %copy-start.3) | copy-done | bytes 262168
  2.0 0.7 %shard_map.73 = (bf16[2,18,8,128]{3,2,1,0:T(8,128)(2,1)S(1)}, bf16[2,18,8,128]{3,2,1,0:T(8,128)(2,1)S(1)}, bf16[2,18,8,128]{3,2,1,0:T(8,128)(2,1)S(1)}, bf16[2,18,8,128]{3,2,1,0:T(8,128)(2,1)S(1)}) custom-call(s32[2]{0:T(128)S(1)} %pad_add_fusion.me_ref, bf16[16,8,1024]{2,1,0:T(8,128)(2,1)S(1)} %copy-done.3, bf16[16,8,1024]{2,1,0:T(8,128)(2,1)S(1)} %copy-done.1), custom_call_target="tpu_custom_call" | custom-call | bytes 1048576 | tf_op jit(solution)/shard_map/pallas_call | solution.py:368
  2.7 4.0 %collective-permute-start.2 = (bf16[2,18,8,128]{3,2,1,0:T(8,128)(2,1)S(1)}, bf16[2,18,8,128]{3,2,1,0:T(8,128)(2,1)S(1)}, u32[]{:S(2)}, u32[]{:S(2)}) collective-permute-start(bf16[2,18,8,128]{3,2,1,0:T(8,128)(2,1)S(1)} %get-tuple-element.21), channel_id=1, source_target_pairs={{0,17},{1,16},{8,25},{9,24},{16,1},{17,0},{24,9},{25,8},{2,19},{3,... | collective-permute-start | bytes 221192 | tf_op jit(solution)/shard_map/ppermute | solution.py:365
  6.7 0.5 collective-permute-start.1
  7.3 0.9 %copy-done.5 = bf16[1,16,8,1024]{3,2,1,0:T(8,128)(2,1)S(1)} copy-done((bf16[1,16,8,1024]{3,2,1,0:T(8,128)(2,1)S(1)}, bf16[1,16,8,1024]{3,2,1,0:T(8,128)(2,1)}, u32[]{:S(2)}) %copy-start.5) | copy-done | bytes 262168
  8.3 0.9 %copy-done.6 = bf16[16,8,1024]{2,1,0:T(8,128)(2,1)S(1)} copy-done((bf16[16,8,1024]{2,1,0:T(8,128)(2,1)S(1)}, bf16[16,8,1024]{2,1,0:T(8,128)(2,1)}, u32[]{:S(2)}) %copy-start.6) | copy-done | bytes 262168
  9.2 0.8 %shard_map.74 = (bf16[2,4,16,8,128]{4,3,2,1,0:T(8,128)(2,1)S(1)}, bf16[2,4,16,8,128]{4,3,2,1,0:T(8,128)(2,1)S(1)}, bf16[2,4,16,8,128]{4,3,2,1,0:T(8,128)(2,1)S(1)}, bf16[2,4,16,8,128]{4,3,2,1,0:T(8,128)(2,1)S(1)}) custom-call(s32[2]{0:T(128)S(1)} %pad_add_fusion.me_ref, bf16[16,8,1024]{2,1,0:T(8,128)(2,1)S(1)} %bitcast.8, bf16[16,8,1024]{2,1,0:T(8,128)(2,1)S(1)} %bitcast.9, ...), custom_call_target="tpu_custom_call" | custom-call | bytes 1048576 | tf_op jit(solution)/shard_map/pallas_call | solution.py:368
  10.0 2.9 %collective-permute-start.6 = (bf16[2,4,16,8,128]{4,3,2,1,0:T(8,128)(2,1)S(1)}, bf16[2,4,16,8,128]{4,3,2,1,0:T(8,128)(2,1)S(1)}, u32[]{:S(2)}, u32[]{:S(2)}) collective-permute-start(bf16[2,4,16,8,128]{4,3,2,1,0:T(8,128)(2,1)S(1)} %get-tuple-element.25), channel_id=1, source_target_pairs={{0,17},{1,16},{8,25},{9,24},{16,1},{17,0},{24,9},{25,8},{2,19},{3,... | collective-permute-start | bytes 786440 | tf_op jit(solution)/shard_map/ppermute | solution.py:365
  13.0 0.5 collective-permute-start.5
  13.5 0.2 collective-permute-start.4
  13.9 10.2 %collective-permute-done.4 = bf16[2,4,16,8,128]{4,3,2,1,0:T(8,128)(2,1)S(1)} collective-permute-done((bf16[2,4,16,8,128]{4,3,2,1,0:T(8,128)(2,1)S(1)}, bf16[2,4,16,8,128]{4,3,2,1,0:T(8,128)(2,1)S(1)}, u32[]{:S(2)}, u32[]{:S(2)}) %collective-permute-start.4) | collective-permute-done | bytes 262176 | tf_op jit(solution)/shard_map/ppermute | solution.py:365
  24.1 0.2 collective-permute-done.5
  24.7 1.3 %collective-permute-start.9 = (bf16[8,18,8,128]{3,2,1,0:T(8,128)(2,1)S(1)}, bf16[8,18,8,128]{3,2,1,0:T(8,128)(2,1)S(1)}, u32[]{:S(2)}, u32[]{:S(2)}) collective-permute-start(bf16[8,18,8,128]{3,2,1,0:T(8,128)(2,1)S(1)} %constant_dynamic-update-slice_fusion.query_ref), channel_id=1, source_target_pairs={{2,0},{4,2},{6,4},{3,1},{5,3},{7,5},{10,8},{12,10},{14,12},{11,9},... | collective-permute-start | bytes 884744 | tf_op jit(solution)/shard_map/ppermute | solution.py:396
  26.0 0.8 %dynamic-slice_bitcast_fusion.bias_ref = f32[1,128]{1,0:T(1,128)S(1)} fusion(f32[1024]{0:T(1024)} %param.13, s32[]{:T(128)S(6)} %select_n.27), kind=kLoop, calls=%fused_computation.33 | loop fusion | bytes 1028 | tf_op jit(solution)/shard_map/dynamic_slice | solution.py:408
  26.8 4.6 %collective-permute-start.8 = (bf16[8,18,8,128]{3,2,1,0:T(8,128)(2,1)S(1)}, bf16[8,18,8,128]{3,2,1,0:T(8,128)(2,1)S(1)}, u32[]{:S(2)}, u32[]{:S(2)}) collective-permute-start(bf16[8,18,8,128]{3,2,1,0:T(8,128)(2,1)S(1)} %constant_dynamic-update-slice_fusion.query_ref), channel_id=1, source_target_pairs={{0,2},{2,4},{4,6},{1,3},{3,5},{5,7},{8,10},{10,12},{12,14},{9,11},... | collective-permute-start | bytes 884744 | tf_op jit(solution)/shard_map/ppermute | solution.py:395
  31.5 4.6 %collective-permute-done.9.after_ref.query_ref = bf16[8,18,8,128]{3,2,1,0:T(8,128)(2,1)S(1)} collective-permute-done((bf16[8,18,8,128]{3,2,1,0:T(8,128)(2,1)S(1)}, bf16[8,18,8,128]{3,2,1,0:T(8,128)(2,1)S(1)}, u32[]{:S(2)}, u32[]{:S(2)}) %collective-permute-start.9) | collective-permute-done | bytes 294944 | tf_op jit(solution)/shard_map/ppermute | solution.py:396
  36.0 2.5 %shard_map.76 = bf16[9,16,8,128]{3,2,1,0:T(8,128)(2,1)S(1)} custom-call(s32[10]{0:T(128)S(1)} %pad_add_fusion.1.info_ref, bf16[8,18,8,128]{3,2,1,0:T(8,128)(2,1)S(1)} %collective-permute-done.9.after_ref.query_ref, bf16[8,4,16,8,128]{4,3,2,1,0:T(8,128)(2,1)S(1)} %constant_dynamic-update-slice_fusion.1.pairs_ref), custom_call_target="tpu_custom_call" | custom-call | flops 4294967296 | bytes 1048576 | tf_op jit(solution)/shard_map/pallas_call | solution.py:368
  38.6 3.5 %collective-permute-start.10 = (bf16[9,16,8,128]{3,2,1,0:T(8,128)(2,1)S(1)}, bf16[9,16,8,128]{3,2,1,0:T(8,128)(2,1)S(1)}, u32[]{:S(2)}, u32[]{:S(2)}) collective-permute-start(bf16[9,16,8,128]{3,2,1,0:T(8,128)(2,1)S(1)} %shard_map.76), channel_id=1, source_target_pairs={{0,2},{2,4},{4,6},{1,3},{3,5},{5,7},{8,10},{10,12},{12,14},{9,11},... | collective-permute-start | bytes 884744 | tf_op jit(solution)/shard_map/ppermute | solution.py:417
  42.1 2.8 %shard_map.77 = bf16[9,16,8,128]{3,2,1,0:T(8,128)(2,1)S(1)} custom-call(s32[10]{0:T(128)S(1)} %pad_add_fusion.1.info_ref, bf16[8,18,8,128]{3,2,1,0:T(8,128)(2,1)S(1)} %collective-permute-done.8.before_ref.query_ref, bf16[8,4,16,8,128]{4,3,2,1,0:T(8,128)(2,1)S(1)} %constant_dynamic-update-slice_fusion.1.pairs_ref), custom_call_target="tpu_custom_call" | custom-call | flops 4294967296 | bytes 1048576 | tf_op jit(solution)/shard_map/pallas_call | solution.py:368
  44.9 1.3 %collective-permute-start.11 = (bf16[9,16,8,128]{3,2,1,0:T(8,128)(2,1)S(1)}, bf16[9,16,8,128]{3,2,1,0:T(8,128)(2,1)S(1)}, u32[]{:S(2)}, u32[]{:S(2)}) collective-permute-start(bf16[9,16,8,128]{3,2,1,0:T(8,128)(2,1)S(1)} %shard_map.77), channel_id=1, source_target_pairs={{2,0},{4,2},{6,4},{3,1},{5,3},{7,5},{10,8},{12,10},{14,12},{11,9},... | collective-permute-start | bytes 884744 | tf_op jit(solution)/shard_map/ppermute | solution.py:415
  46.2 3.2 %shard_map.75 = (f32[8,128,128]{2,1,0:T(8,128)S(1)}, f32[8,128,128]{2,1,0:T(8,128)S(1)}, f32[8,128,128]{2,1,0:T(8,128)S(1)}) custom-call(s32[10]{0:T(128)S(1)} %pad_add_fusion.1.info_ref, f32[3,3,128]{2,1,0:T(4,128)S(1)} %constant_dynamic-slice_fusion.weight_ref, f32[1,128]{1,0:T(1,128)S(1)} %dynamic-slice_bitcast_fusion.bias_ref, ...), custom_call_target="tpu_custom_call" | custom-call | flops 4294967296 | bytes 1048576 | tf_op jit(solution)/shard_map/pallas_call | solution.py:368
  49.4 5.7 %collective-permute-done.11.right_ref = bf16[9,16,8,128]{3,2,1,0:T(8,128)(2,1)S(1)} collective-permute-done((bf16[9,16,8,128]{3,2,1,0:T(8,128)(2,1)S(1)}, bf16[9,16,8,128]{3,2,1,0:T(8,128)(2,1)S(1)}, u32[]{:S(2)}, u32[]{:S(2)}) %collective-permute-start.11) | collective-permute-done | bytes 294944 | tf_op jit(solution)/shard_map/ppermute | solution.py:415
  55.1 1.7 %shard_map.78 = (bf16[4,16,8,128]{3,2,1,0:T(8,128)(2,1)S(1)}, bf16[4,16,8,128]{3,2,1,0:T(8,128)(2,1)S(1)}) custom-call(s32[10]{0:T(128)S(1)} %pad_add_fusion.1.info_ref, f32[8,128,128]{2,1,0:T(8,128)S(1)} %get-tuple-element.26.part_ref, f32[8,128,128]{2,1,0:T(8,128)S(1)} %get-tuple-element.27.level_ref, f32[8,128,128]{2,1,0:T(8,128)S(1)} %get-tuple-element.28.conv_ref, ...), custom_call_target="tpu_custom_call" | custom-call | flops 1073741824 | bytes 1048576 | tf_op jit(solution)/shard_map/pallas_call | solution.py:368
  56.9 1.3 %collective-permute-done.12.beside_ref = bf16[4,16,8,128]{3,2,1,0:T(8,128)(2,1)S(1)} collective-permute-done((bf16[4,16,8,128]{3,2,1,0:T(8,128)(2,1)S(1)}, bf16[4,16,8,128]{3,2,1,0:T(8,128)(2,1)S(1)}, u32[]{:S(2)}, u32[]{:S(2)}) %collective-permute-start.12) | collective-permute-done | bytes 131104 | tf_op jit(solution)/shard_map/ppermute | solution.py:365
  58.2 1.5 %collective-permute-start.13 = (bf16[2,16,8,128]{3,2,1,0:T(8,128)(2,1)S(1)}, bf16[2,16,8,128]{3,2,1,0:T(8,128)(2,1)S(1)}, u32[]{:S(2)}, u32[]{:S(2)}) collective-permute-start(bf16[2,16,8,128]{3,2,1,0:T(8,128)(2,1)S(1)} %pad_maximum_fusion.2), channel_id=1, source_target_pairs={{0,1},{1,0},{8,9},{9,8},{16,17},{17,16},{24,25},{25,24},{2,3},{3,2... | collective-permute-start | bytes 196616 | tf_op jit(solution)/shard_map/ppermute | solution.py:365
  59.8 1.5 %collective-permute-start.14 = (bf16[2,16,8,128]{3,2,1,0:T(8,128)(2,1)S(1)}, bf16[2,16,8,128]{3,2,1,0:T(8,128)(2,1)S(1)}, u32[]{:S(2)}, u32[]{:S(2)}) collective-permute-start(bf16[2,16,8,128]{3,2,1,0:T(8,128)(2,1)S(1)} %pad_maximum_fusion.3), channel_id=1, source_target_pairs={{0,16},{1,17},{8,24},{9,25},{16,0},{17,1},{24,8},{25,9},{2,18},{3,... | collective-permute-start | bytes 196616 | tf_op jit(solution)/shard_map/ppermute | solution.py:365
  61.3 0.6 collective-permute-start.15
  61.9 0.6 collective-permute-done.13.refs_0_
  62.6 2.1 %collective-permute-done.14.refs_1_ = bf16[2,16,8,128]{3,2,1,0:T(8,128)(2,1)S(1)} collective-permute-done((bf16[2,16,8,128]{3,2,1,0:T(8,128)(2,1)S(1)}, bf16[2,16,8,128]{3,2,1,0:T(8,128)(2,1)S(1)}, u32[]{:S(2)}, u32[]{:S(2)}) %collective-permute-start.14) | collective-permute-done | bytes 65568 | tf_op jit(solution)/shard_map/ppermute | solution.py:365
  64.6 1.9 %collective-permute-done.15.refs_2_ = bf16[2,16,8,128]{3,2,1,0:T(8,128)(2,1)S(1)} collective-permute-done((bf16[2,16,8,128]{3,2,1,0:T(8,128)(2,1)S(1)}, bf16[2,16,8,128]{3,2,1,0:T(8,128)(2,1)S(1)}, u32[]{:S(2)}, u32[]{:S(2)}) %collective-permute-start.15) | collective-permute-done | bytes 65568 | tf_op jit(solution)/shard_map/ppermute | solution.py:365
  66.6 1.3 %shard_map.79 = bf16[16,8,1024]{2,1,0:T(8,128)(2,1)} custom-call(s32[2]{0:T(128)S(1)} %pad_add_fusion.me_ref, bf16[4,16,8,128]{3,2,1,0:T(8,128)(2,1)S(1)} %get-tuple-element.29.same_ref, bf16[4,16,8,128]{3,2,1,0:T(8,128)(2,1)S(1)} %collective-permute-done.12.beside_ref, bf16[2,16,8,128]{3,2,1,0:T(8,128)(2,1)S(1)} %collective-permute-done.13.refs_0_, ...), custom_call_target="tpu_custom_call" | custom-call | bytes 1048576 | tf_op jit(solution)/shard_map/pallas_call | solution.py:368
  (44 shorter events, 1.0 us)
Async XLA Ops:
  0.0 26.8 %copy-start = (f32[3,3,1024]{2,1,0:T(4,128)S(1)}, f32[3,3,1024]{2,1,0:T(4,128)}, u32[]{:S(2)}) copy-start(f32[3,3,1024]{2,1,0:T(4,128)} %param.12) | copy-start | bytes 110596
  0.1 0.9 %copy-start.1 = (bf16[16,8,1024]{2,1,0:T(8,128)(2,1)S(1)}, bf16[16,8,1024]{2,1,0:T(8,128)(2,1)}, u32[]{:S(2)}) copy-start(bf16[16,8,1024]{2,1,0:T(8,128)(2,1)} %refs_3_.1) | copy-start | bytes 786436
  1.0 0.9 %copy-start.3 = (bf16[16,8,1024]{2,1,0:T(8,128)(2,1)S(1)}, bf16[16,8,1024]{2,1,0:T(8,128)(2,1)}, u32[]{:S(2)}) copy-start(bf16[16,8,1024]{2,1,0:T(8,128)(2,1)} %query_ref.1) | copy-start | bytes 786436
  2.0 5.3 %copy-start.2 = (bf16[16,8,1024]{2,1,0:T(8,128)(2,1)S(1)}, bf16[16,8,1024]{2,1,0:T(8,128)(2,1)}, u32[]{:S(2)}) copy-start(bf16[16,8,1024]{2,1,0:T(8,128)(2,1)} %refs_3_.1) | copy-start | bytes 786436
  2.0 5.3 %copy-start.4 = (bf16[1,16,8,1024]{3,2,1,0:T(8,128)(2,1)S(1)}, bf16[1,16,8,1024]{3,2,1,0:T(8,128)(2,1)}, u32[]{:S(2)}) copy-start(bf16[1,16,8,1024]{3,2,1,0:T(8,128)(2,1)} %param.10) | copy-start | bytes 786436
  2.7 11.1 %collective-permute-start.2 = (bf16[2,18,8,128]{3,2,1,0:T(8,128)(2,1)S(1)}, bf16[2,18,8,128]{3,2,1,0:T(8,128)(2,1)S(1)}, u32[]{:S(2)}, u32[]{:S(2)}) collective-permute-start(bf16[2,18,8,128]{3,2,1,0:T(8,128)(2,1)S(1)} %get-tuple-element.21), channel_id=1, source_target_pairs={{0,17},{1,16},{8,25},{9,24},{16,1},{17,0},{24,9},{25,8},{2,19},{3,... | collective-permute-start | bytes 221192 | tf_op jit(solution)/shard_map/ppermute | solution.py:365
  6.7 7.1 %collective-permute-start.1 = (bf16[2,18,8,128]{3,2,1,0:T(8,128)(2,1)S(1)}, bf16[2,18,8,128]{3,2,1,0:T(8,128)(2,1)S(1)}, u32[]{:S(2)}, u32[]{:S(2)}) collective-permute-start(bf16[2,18,8,128]{3,2,1,0:T(8,128)(2,1)S(1)} %get-tuple-element.20), channel_id=1, source_target_pairs={{0,16},{1,17},{8,24},{9,25},{16,0},{17,1},{24,8},{25,9},{2,18},{3,... | collective-permute-start | bytes 221192 | tf_op jit(solution)/shard_map/ppermute | solution.py:365
  7.2 6.3 %collective-permute-start = (bf16[2,18,8,128]{3,2,1,0:T(8,128)(2,1)S(1)}, bf16[2,18,8,128]{3,2,1,0:T(8,128)(2,1)S(1)}, u32[]{:S(2)}, u32[]{:S(2)}) collective-permute-start(bf16[2,18,8,128]{3,2,1,0:T(8,128)(2,1)S(1)} %get-tuple-element.19), channel_id=1, source_target_pairs={{0,1},{1,0},{8,9},{9,8},{16,17},{17,16},{24,25},{25,24},{2,3},{3,2... | collective-permute-start | bytes 221192 | tf_op jit(solution)/shard_map/ppermute | solution.py:365
  7.3 1.0 %copy-start.5 = (bf16[1,16,8,1024]{3,2,1,0:T(8,128)(2,1)S(1)}, bf16[1,16,8,1024]{3,2,1,0:T(8,128)(2,1)}, u32[]{:S(2)}) copy-start(bf16[1,16,8,1024]{3,2,1,0:T(8,128)(2,1)} %param.11) | copy-start | bytes 786436
  8.3 0.9 %copy-start.6 = (bf16[16,8,1024]{2,1,0:T(8,128)(2,1)S(1)}, bf16[16,8,1024]{2,1,0:T(8,128)(2,1)}, u32[]{:S(2)}) copy-start(bf16[16,8,1024]{2,1,0:T(8,128)(2,1)} %refs_2_.1) | copy-start | bytes 786436
  10.0 14.3 %collective-permute-start.6 = (bf16[2,4,16,8,128]{4,3,2,1,0:T(8,128)(2,1)S(1)}, bf16[2,4,16,8,128]{4,3,2,1,0:T(8,128)(2,1)S(1)}, u32[]{:S(2)}, u32[]{:S(2)}) collective-permute-start(bf16[2,4,16,8,128]{4,3,2,1,0:T(8,128)(2,1)S(1)} %get-tuple-element.25), channel_id=1, source_target_pairs={{0,17},{1,16},{8,25},{9,24},{16,1},{17,0},{24,9},{25,8},{2,19},{3,... | collective-permute-start | bytes 786440 | tf_op jit(solution)/shard_map/ppermute | solution.py:365
  13.0 11.4 %collective-permute-start.5 = (bf16[2,4,16,8,128]{4,3,2,1,0:T(8,128)(2,1)S(1)}, bf16[2,4,16,8,128]{4,3,2,1,0:T(8,128)(2,1)S(1)}, u32[]{:S(2)}, u32[]{:S(2)}) collective-permute-start(bf16[2,4,16,8,128]{4,3,2,1,0:T(8,128)(2,1)S(1)} %get-tuple-element.24), channel_id=1, source_target_pairs={{0,16},{1,17},{8,24},{9,25},{16,0},{17,1},{24,8},{25,9},{2,18},{3,... | collective-permute-start | bytes 786440 | tf_op jit(solution)/shard_map/ppermute | solution.py:365
  13.5 10.6 %collective-permute-start.4 = (bf16[2,4,16,8,128]{4,3,2,1,0:T(8,128)(2,1)S(1)}, bf16[2,4,16,8,128]{4,3,2,1,0:T(8,128)(2,1)S(1)}, u32[]{:S(2)}, u32[]{:S(2)}) collective-permute-start(bf16[2,4,16,8,128]{4,3,2,1,0:T(8,128)(2,1)S(1)} %get-tuple-element.23), channel_id=1, source_target_pairs={{0,1},{1,0},{8,9},{9,8},{16,17},{17,16},{24,25},{25,24},{2,3},{3,2... | collective-permute-start | bytes 786440 | tf_op jit(solution)/shard_map/ppermute | solution.py:365
  13.8 10.9 %collective-permute-start.3 = (bf16[4,18,8,128]{3,2,1,0:T(8,128)(2,1)S(1)}, bf16[4,18,8,128]{3,2,1,0:T(8,128)(2,1)S(1)}, u32[]{:S(2)}, u32[]{:S(2)}) collective-permute-start(bf16[4,18,8,128]{3,2,1,0:T(8,128)(2,1)S(1)} %pad_maximum_fusion.1), channel_id=1, source_target_pairs={{0,8},{1,9},{8,0},{9,1},{16,24},{17,25},{24,16},{25,17},{2,10},{3,... | collective-permute-start | bytes 442376 | tf_op jit(solution)/shard_map/ppermute | solution.py:365
  24.5 6.9 %collective-permute-start.7 = (bf16[4,4,16,8,128]{4,3,2,1,0:T(8,128)(2,1)S(1)}, bf16[4,4,16,8,128]{4,3,2,1,0:T(8,128)(2,1)S(1)}, u32[]{:S(2)}, u32[]{:S(2)}) collective-permute-start(bf16[4,4,16,8,128]{4,3,2,1,0:T(8,128)(2,1)S(1)} %pad_maximum_fusion), channel_id=1, source_target_pairs={{0,8},{1,9},{8,0},{9,1},{16,24},{17,25},{24,16},{25,17},{2,10},{3,... | collective-permute-start | bytes 1572872 | tf_op jit(solution)/shard_map/ppermute | solution.py:365
  24.7 11.3 %collective-permute-start.9 = (bf16[8,18,8,128]{3,2,1,0:T(8,128)(2,1)S(1)}, bf16[8,18,8,128]{3,2,1,0:T(8,128)(2,1)S(1)}, u32[]{:S(2)}, u32[]{:S(2)}) collective-permute-start(bf16[8,18,8,128]{3,2,1,0:T(8,128)(2,1)S(1)} %constant_dynamic-update-slice_fusion.query_ref), channel_id=1, source_target_pairs={{2,0},{4,2},{6,4},{3,1},{5,3},{7,5},{10,8},{12,10},{14,12},{11,9},... | collective-permute-start | bytes 884744 | tf_op jit(solution)/shard_map/ppermute | solution.py:396
  26.8 15.3 %collective-permute-start.8 = (bf16[8,18,8,128]{3,2,1,0:T(8,128)(2,1)S(1)}, bf16[8,18,8,128]{3,2,1,0:T(8,128)(2,1)S(1)}, u32[]{:S(2)}, u32[]{:S(2)}) collective-permute-start(bf16[8,18,8,128]{3,2,1,0:T(8,128)(2,1)S(1)} %constant_dynamic-update-slice_fusion.query_ref), channel_id=1, source_target_pairs={{0,2},{2,4},{4,6},{1,3},{3,5},{5,7},{8,10},{10,12},{12,14},{9,11},... | collective-permute-start | bytes 884744 | tf_op jit(solution)/shard_map/ppermute | solution.py:395
  38.6 10.8 %collective-permute-start.10 = (bf16[9,16,8,128]{3,2,1,0:T(8,128)(2,1)S(1)}, bf16[9,16,8,128]{3,2,1,0:T(8,128)(2,1)S(1)}, u32[]{:S(2)}, u32[]{:S(2)}) collective-permute-start(bf16[9,16,8,128]{3,2,1,0:T(8,128)(2,1)S(1)} %shard_map.76), channel_id=1, source_target_pairs={{0,2},{2,4},{4,6},{1,3},{3,5},{5,7},{8,10},{10,12},{12,14},{9,11},... | collective-permute-start | bytes 884744 | tf_op jit(solution)/shard_map/ppermute | solution.py:417
  44.9 10.2 %collective-permute-start.11 = (bf16[9,16,8,128]{3,2,1,0:T(8,128)(2,1)S(1)}, bf16[9,16,8,128]{3,2,1,0:T(8,128)(2,1)S(1)}, u32[]{:S(2)}, u32[]{:S(2)}) collective-permute-start(bf16[9,16,8,128]{3,2,1,0:T(8,128)(2,1)S(1)} %shard_map.77), channel_id=1, source_target_pairs={{2,0},{4,2},{6,4},{3,1},{5,3},{7,5},{10,8},{12,10},{14,12},{11,9},... | collective-permute-start | bytes 884744 | tf_op jit(solution)/shard_map/ppermute | solution.py:415
  56.8 1.4 %collective-permute-start.12 = (bf16[4,16,8,128]{3,2,1,0:T(8,128)(2,1)S(1)}, bf16[4,16,8,128]{3,2,1,0:T(8,128)(2,1)S(1)}, u32[]{:S(2)}, u32[]{:S(2)}) collective-permute-start(bf16[4,16,8,128]{3,2,1,0:T(8,128)(2,1)S(1)} %get-tuple-element.30), channel_id=1, source_target_pairs={{0,8},{1,9},{8,0},{9,1},{16,24},{17,25},{24,16},{25,17},{2,10},{3,... | collective-permute-start | bytes 393224 | tf_op jit(solution)/shard_map/ppermute | solution.py:365
  58.2 4.3 %collective-permute-start.13 = (bf16[2,16,8,128]{3,2,1,0:T(8,128)(2,1)S(1)}, bf16[2,16,8,128]{3,2,1,0:T(8,128)(2,1)S(1)}, u32[]{:S(2)}, u32[]{:S(2)}) collective-permute-start(bf16[2,16,8,128]{3,2,1,0:T(8,128)(2,1)S(1)} %pad_maximum_fusion.2), channel_id=1, source_target_pairs={{0,1},{1,0},{8,9},{9,8},{16,17},{17,16},{24,25},{25,24},{2,3},{3,2... | collective-permute-start | bytes 196616 | tf_op jit(solution)/shard_map/ppermute | solution.py:365
  59.8 4.9 %collective-permute-start.14 = (bf16[2,16,8,128]{3,2,1,0:T(8,128)(2,1)S(1)}, bf16[2,16,8,128]{3,2,1,0:T(8,128)(2,1)S(1)}, u32[]{:S(2)}, u32[]{:S(2)}) collective-permute-start(bf16[2,16,8,128]{3,2,1,0:T(8,128)(2,1)S(1)} %pad_maximum_fusion.3), channel_id=1, source_target_pairs={{0,16},{1,17},{8,24},{9,25},{16,0},{17,1},{24,8},{25,9},{2,18},{3,... | collective-permute-start | bytes 196616 | tf_op jit(solution)/shard_map/ppermute | solution.py:365
  61.3 5.2 %collective-permute-start.15 = (bf16[2,16,8,128]{3,2,1,0:T(8,128)(2,1)S(1)}, bf16[2,16,8,128]{3,2,1,0:T(8,128)(2,1)S(1)}, u32[]{:S(2)}, u32[]{:S(2)}) collective-permute-start(bf16[2,16,8,128]{3,2,1,0:T(8,128)(2,1)S(1)} %pad_maximum_fusion.4), channel_id=1, source_target_pairs={{0,17},{1,16},{8,25},{9,24},{16,1},{17,0},{24,9},{25,8},{2,19},{3,... | collective-permute-start | bytes 196616 | tf_op jit(solution)/shard_map/ppermute | solution.py:365

commit v5 on v4

--- a/solution.py
+++ b/solution.py
@@ -149,6 +149,7 @@
 NEG = -1e30
 VMEM = pl.BlockSpec(memory_space=pltpu.VMEM)
 SMEM = pl.BlockSpec(memory_space=pltpu.SMEM)
+FAR = pl.BlockSpec(memory_space=pltpu.HBM)
 LIMIT = pltpu.CompilerParams(vmem_limit_bytes=8 * 1024 * 1024)
 SMALL = pltpu.CompilerParams(vmem_limit_bytes=4 * 1024 * 1024)
 
@@ -256,16 +257,16 @@
     window = Window(grid, tile, info_ref, query_ref, pairs_ref)
     size, count = window.size, grid[0] * grid[1]
     lane = lax.broadcasted_iota(jnp.int32, (size, HD), 1)
-    packed = jnp.zeros((size, HD), jnp.float32)
+    levels = jnp.zeros((size, HD), jnp.float32)
     for row in range(grid[0]):
         for col in range(grid[1]):
             index = row * grid[1] + col
             part, level = window.attend(row, first_col + col)
-            out_ref[window.slot(row, col)] = part.reshape(tile + (HD,)).astype(jnp.bfloat16)
-            high = level.astype(jnp.bfloat16).astype(jnp.float32)
-            middle = (level - high).astype(jnp.bfloat16).astype(jnp.float32)
-            for i, piece in enumerate((high, middle, level - high - middle)):
-                packed = jnp.where(lane == i * count + index, piece, packed)
+            out_ref[index] = part.reshape(tile + (HD,)).astype(jnp.bfloat16)
+            levels = jnp.where(lane == index, level, levels)
+    high = levels.astype(jnp.bfloat16).astype(jnp.float32)
+    middle = (levels - high).astype(jnp.bfloat16).astype(jnp.float32)
+    packed = high + pltpu.roll(middle, count, 1) + pltpu.roll(levels - high - middle, 2 * count, 1)
     out_ref[count] = packed.reshape(tile + (HD,)).astype(jnp.bfloat16)
 
 
@@ -290,7 +291,7 @@
         place = info_ref[2 + index]
         parts, levels = [part_ref[index]], [level_ref[index]]
         for ref, there, pack in zip(visits, present, packed):
-            parts.append(ref[place].reshape(size, HD).astype(jnp.float32))
+            parts.append(ref[index].reshape(size, HD).astype(jnp.float32))
             level = pack[:, index : index + 1]
             for i in (1, 2):
                 level = level + pack[:, i * count + index : i * count + index + 1]
@@ -313,38 +314,53 @@
     return pl.ds(pl.multiple_of(head * HD, HD), HD)
 
 
+def move(copies, sems):
+    started = [pltpu.make_async_copy(source, target, sems.at[i]) for i, (source, target) in enumerate(copies)]
+    for copy in started:
+        copy.start()
+    for copy in started:
+        copy.wait()
+
+
 def pack_kernel(flips, side, me_ref, *refs):
-    sources, buffers = refs[: len(refs) - len(flips)], refs[len(refs) - len(flips) :]
+    sources, buffers, sems = refs[: -len(flips) - 1], refs[-len(flips) - 1 : -1], refs[-1]
+    copies = []
     for buffer, flip in zip(buffers, flips):
         for other in range(2):
-            head = me_ref[0] ^ (flip ^ (side if other else 0))
+            head = lanes(me_ref[0] ^ (flip ^ (side if other else 0)))
             for member, source in enumerate(sources):
-                buffer[other, member] = source[:, :, lanes(head)]
-
-
-def query_kernel(flips, side, me_ref, query_ref, values_ref, *buffers):
+                copies.append((source.at[:, :, head], buffer.at[other, member]))
+    move(copies, sems)
+
+
+def query_kernel(flips, side, me_ref, query_ref, values_ref, *refs):
+    buffers, held_ref, sems = refs[:-2], refs[-2], refs[-1]
     tile_rows, tile_cols, _ = query_ref.shape
+    places = [(buffer, flip, other) for buffer, flip in zip(buffers, flips) for other in range(2)]
+    heads = [lanes(me_ref[0] ^ (flip ^ (side if other else 0))) for _, flip, other in places]
+    copies = [(values_ref, held_ref)]
+    for (buffer, _, other), head in zip(places, heads):
+        copies.append((query_ref.at[:, :, head], buffer.at[other, pl.ds(0, tile_rows)]))
+    move(copies, sems)
     sub = lax.broadcasted_iota(jnp.int32, (tile_cols, HD), 0)
-    for buffer, flip in zip(buffers, flips):
-        for other in range(2):
-            head = me_ref[0] ^ (flip ^ (side if other else 0))
-            buffer[other, pl.ds(0, tile_rows)] = query_ref[:, :, lanes(head)]
-            for start in range(0, tile_rows, tile_cols):
-                packed = jnp.zeros((tile_cols, HD), jnp.float32)
-                for line in range(tile_cols):
-                    values = values_ref[start + line, :, lanes(head)].astype(jnp.float32)
-                    edge = jnp.where(me_ref[1] == 0, values[:1], values[tile_cols - 1 :])
-                    packed = jnp.where(sub == line, edge, packed)
-                buffer[other, tile_rows + start // tile_cols] = packed.astype(jnp.bfloat16)
+    for (buffer, _, other), head in zip(places, heads):
+        for start in range(0, tile_rows, tile_cols):
+            packed = jnp.zeros((tile_cols, HD), jnp.float32)
+            for line in range(tile_cols):
+                values = held_ref[start + line, :, head].astype(jnp.float32)
+                edge = jnp.where(me_ref[1] == 0, values[:1], values[tile_cols - 1 :])
+                packed = jnp.where(sub == line, edge, packed)
+            buffer[other, tile_rows + start // tile_cols] = packed.astype(jnp.bfloat16)
 
 
 def unpack_kernel(flips, side, me_ref, same_ref, beside_ref, *refs):
-    out_ref = refs[-1]
-    out_ref[:, :, lanes(me_ref[0])] = same_ref[0]
-    out_ref[:, :, lanes(me_ref[0] ^ side)] = beside_ref[0]
-    for i, flip in enumerate(flips[1:]):
-        out_ref[:, :, lanes(me_ref[0] ^ flip)] = refs[i][0]
-        out_ref[:, :, lanes(me_ref[0] ^ (flip ^ side))] = refs[i][1]
+    out_ref, sems = refs[-2], refs[-1]
+    copies = []
+    for i, flip in enumerate(flips):
+        one, two = (refs[i - 1].at[0], refs[i - 1].at[1]) if i else (same_ref.at[0], beside_ref.at[0])
+        copies.append((one, out_ref.at[:, :, lanes(me_ref[0] ^ flip)]))
+        copies.append((two, out_ref.at[:, :, lanes(me_ref[0] ^ (flip ^ side))]))
+    move(copies, sems)
 
 
 def head_step(shape, queries, keys_new, values_new, keys_cache, values_cache, conv_weight, conv_bias):
@@ -364,15 +380,19 @@
     def swap(x, flip):
         return lax.ppermute(x, axes, [(s, s ^ flip) for s in range(heads)])
 
-    def call(kernel, out_shape, params, cost, *operands):
+    def call(kernel, out_shape, params, cost, *operands, space=(VMEM, VMEM), scratch=()):
         return pl.pallas_call(
             kernel,
             out_shape=out_shape,
-            in_specs=[SMEM] + [VMEM] * (len(operands) - 1),
-            out_specs=jax.tree.map(lambda _: VMEM, out_shape),
+            in_specs=[SMEM] + [space[0]] * (len(operands) - 1),
+            out_specs=jax.tree.map(lambda _: space[1], out_shape),
+            scratch_shapes=scratch,
             compiler_params=params,
             cost_estimate=pl.CostEstimate(flops=cost << 30, bytes_accessed=1 << 20, transcendentals=0),
         )(*operands)
+
+    def stay(x):
+        return pltpu.with_memory_space_constraint(x, pltpu.HBM)
 
     def gather(buffers):
         got = [buffers[0]] + [swap(b, flip) for b, flip in zip(buffers[1:], flips[1:])]
@@ -385,12 +405,29 @@
     edges = -(-tile_rows // tile_cols)
     buffer = jax.ShapeDtypeStruct((2, tile_rows + edges, tile_cols, HD), jnp.bfloat16)
     packed_query = call(
-        functools.partial(query_kernel, flips, side), [buffer] * len(flips), SMALL, 0, me_ref, queries, values_new
+        functools.partial(query_kernel, flips, side),
+        [buffer] * len(flips),
+        SMALL,
+        0,
+        me_ref,
+        stay(queries),
+        stay(values_new),
+        space=(FAR, VMEM),
+        scratch=[pltpu.VMEM(values_new.shape, jnp.bfloat16), pltpu.SemaphoreType.DMA((heads + 1,))],
     )
     query = gather(packed_query)
     sources = (keys_cache[0], values_cache[0], keys_new, values_new)
     buffer = jax.ShapeDtypeStruct((2, len(sources)) + block, jnp.bfloat16)
-    packed_pairs = call(functools.partial(pack_kernel, flips, side), [buffer] * len(flips), SMALL, 0, me_ref, *sources)
+    packed_pairs = call(
+        functools.partial(pack_kernel, flips, side),
+        [buffer] * len(flips),
+        SMALL,
+        0,
+        me_ref,
+        *map(stay, sources),
+        space=(FAR, VMEM),
+        scratch=[pltpu.SemaphoreType.DMA((heads * len(sources),))],
+    )
     pairs = gather(packed_pairs)
     query_left = lax.ppermute(query, "far", up)
     query_right = lax.ppermute(query, "far", down)
@@ -422,7 +459,9 @@
     kernel = functools.partial(join_kernel, grid, tile)
     same, other = call(kernel, [half, half], LIMIT, 1, info, *own, from_left, from_right)
     received = swap(other, side)
-    got = [swap(jnp.stack([same[i], received[i]]), flips[i]) for i in range(1, len(flips))]
+    got = []
+    for i in range(1, len(flips)):
+        got.append(swap(jnp.stack([same[i], received[i]]), flips[i]))
     return call(
         functools.partial(unpack_kernel, flips, side),
         jax.ShapeDtypeStruct(queries.shape, jnp.bfloat16),
@@ -432,6 +471,8 @@
         same,
         received,
         *got,
+        space=(VMEM, FAR),
+        scratch=[pltpu.SemaphoreType.DMA((heads,))],
     )
 
 

time: 68.2 us -> 66.7 us (0.978)
  local copies, waits for them, and re-layouts: 4.84 us -> 1.03 us
  Pallas kernels: 13 us -> 15.3 us
    unnamed x14 -> x2, local copies, waits for them, and re-layouts: 3.81 us -> 0.01 us
    pallas_call x7, Pallas kernels: 13 us -> 15.3 us  [call(): pl.pallas_call(kernel, out_shape=out_shape, in_specs=[SMEM] + [space[0]]...]
  transfers between devices with their start and end apart: 16 -> 16, of which waited for: 8 -> 8; matrix products, arithmetic and copies ran while one was open for 2% -> 2% of each run, Pallas kernels for 14% -> 16%
where the time goes in v5:
time: 66.7 us; the launch traced here: 66.4 us
  waiting for transfers between devices  26.6 us (40%)
  starting transfers between devices  22.8 us (34%)
  Pallas kernels  15.3 us (23%)
  local copies, waits for them, and re-layouts  1.03 us (2%)
    ppermute x12, waiting for transfers between devices, swap(): return lax.ppermute(x, axes, [(s, s ^ flip) for s in range(heads)])  16.4 us
    pallas_call x7, Pallas kernels, call(): pl.pallas_call(kernel, out_shape=out_shape, in_specs=[SMEM] + [space[0]]...  15.3 us
    ppermute x12, starting transfers between devices, swap(): return lax.ppermute(x, axes, [(s, s ^ flip) for s in range(heads)])  12.1 us
    ppermute x1, waiting for transfers between devices, head_step(): from_right = lax.ppermute(left_part, 'far', down)  5.66 us
    ppermute x1, waiting for transfers between devices, head_step(): query_right = lax.ppermute(query, 'far', down)  4.58 us
    ppermute x1, starting transfers between devices, head_step(): query_left = lax.ppermute(query, 'far', up)  4.55 us
    ppermute x1, starting transfers between devices, head_step(): from_left = lax.ppermute(right_part, 'far', up)  3.5 us
  transfers between devices with their start and end apart: 16, of which 8 were waited for; matrix products, arithmetic and copies ran while one was open for 2% of the time, Pallas kernels for 16%

profile of v5, /device:TPU:0, one launch (start us, length us, event | category | flops | bytes accessed | tf_op | source)
XLA Modules:
  0.0 66.4 jit_solution(12336655392094405607)
XLA Ops:
  0.0 0.1 pad_add_fusion.me_ref
  0.1 1.7 %shard_map.73 = (bf16[2,18,8,128]{3,2,1,0:T(8,128)(2,1)S(1)}, bf16[2,18,8,128]{3,2,1,0:T(8,128)(2,1)S(1)}, bf16[2,18,8,128]{3,2,1,0:T(8,128)(2,1)S(1)}, bf16[2,18,8,128]{3,2,1,0:T(8,128)(2,1)S(1)}) custom-call(s32[2]{0:T(128)S(1)} %pad_add_fusion.me_ref, bf16[16,8,1024]{2,1,0:T(8,128)(2,1)} %query_ref.1, bf16[16,8,1024]{2,1,0:T(8,128)(2,1)} %refs_3_.1), custom_call_target="tpu_custom_call" | custom-call | bytes 1048576 | tf_op jit(solution)/shard_map/pallas_call | solution.py:384
  1.8 4.0 %collective-permute-start.2 = (bf16[2,18,8,128]{3,2,1,0:T(8,128)(2,1)S(1)}, bf16[2,18,8,128]{3,2,1,0:T(8,128)(2,1)S(1)}, u32[]{:S(2)}, u32[]{:S(2)}) collective-permute-start(bf16[2,18,8,128]{3,2,1,0:T(8,128)(2,1)S(1)} %get-tuple-element.21), channel_id=1, source_target_pairs={{0,17},{1,16},{8,25},{9,24},{16,1},{17,0},{24,9},{25,8},{2,19},{3,... | collective-permute-start | bytes 221192 | tf_op jit(solution)/shard_map/ppermute | solution.py:381
  5.8 0.5 collective-permute-start.1
  6.3 0.1 collective-permute-start
  6.4 2.0 %shard_map.74 = (bf16[2,4,16,8,128]{4,3,2,1,0:T(8,128)(2,1)S(1)}, bf16[2,4,16,8,128]{4,3,2,1,0:T(8,128)(2,1)S(1)}, bf16[2,4,16,8,128]{4,3,2,1,0:T(8,128)(2,1)S(1)}, bf16[2,4,16,8,128]{4,3,2,1,0:T(8,128)(2,1)S(1)}) custom-call(s32[2]{0:T(128)S(1)} %pad_add_fusion.me_ref, bf16[16,8,1024]{2,1,0:T(8,128)(2,1)} %bitcast.8, bf16[16,8,1024]{2,1,0:T(8,128)(2,1)} %bitcast.9, ...), custom_call_target="tpu_custom_call" | custom-call | bytes 1048576 | tf_op jit(solution)/shard_map/pallas_call | solution.py:384
  8.4 2.9 %collective-permute-start.6 = (bf16[2,4,16,8,128]{4,3,2,1,0:T(8,128)(2,1)S(1)}, bf16[2,4,16,8,128]{4,3,2,1,0:T(8,128)(2,1)S(1)}, u32[]{:S(2)}, u32[]{:S(2)}) collective-permute-start(bf16[2,4,16,8,128]{4,3,2,1,0:T(8,128)(2,1)S(1)} %get-tuple-element.25), channel_id=1, source_target_pairs={{0,17},{1,16},{8,25},{9,24},{16,1},{17,0},{24,9},{25,8},{2,19},{3,... | collective-permute-start | bytes 786440 | tf_op jit(solution)/shard_map/ppermute | solution.py:381
  11.3 0.5 collective-permute-start.5
  11.9 0.2 collective-permute-start.4
  12.3 10.2 %collective-permute-done.4 = bf16[2,4,16,8,128]{4,3,2,1,0:T(8,128)(2,1)S(1)} collective-permute-done((bf16[2,4,16,8,128]{4,3,2,1,0:T(8,128)(2,1)S(1)}, bf16[2,4,16,8,128]{4,3,2,1,0:T(8,128)(2,1)S(1)}, u32[]{:S(2)}, u32[]{:S(2)}) %collective-permute-start.4) | collective-permute-done | bytes 262176 | tf_op jit(solution)/shard_map/ppermute | solution.py:381
  22.5 0.2 collective-permute-done.5
  22.9 0.1 add_convert_fusion
  23.0 0.1 pad_add_fusion.1.info_ref
  23.1 1.3 %collective-permute-start.9 = (bf16[8,18,8,128]{3,2,1,0:T(8,128)(2,1)S(1)}, bf16[8,18,8,128]{3,2,1,0:T(8,128)(2,1)S(1)}, u32[]{:S(2)}, u32[]{:S(2)}) collective-permute-start(bf16[8,18,8,128]{3,2,1,0:T(8,128)(2,1)S(1)} %constant_dynamic-update-slice_fusion.query_ref), channel_id=1, source_target_pairs={{2,0},{4,2},{6,4},{3,1},{5,3},{7,5},{10,8},{12,10},{14,12},{11,9},... | collective-permute-start | bytes 884744 | tf_op jit(solution)/shard_map/ppermute | solution.py:433
  24.4 0.8 %dynamic-slice_bitcast_fusion.bias_ref = f32[1,128]{1,0:T(1,128)S(1)} fusion(f32[1024]{0:T(1024)} %param.13, s32[]{:T(128)S(6)} %select_n.27), kind=kLoop, calls=%fused_computation.33 | loop fusion | bytes 1028 | tf_op jit(solution)/shard_map/dynamic_slice | solution.py:445
  25.2 4.6 %collective-permute-start.8 = (bf16[8,18,8,128]{3,2,1,0:T(8,128)(2,1)S(1)}, bf16[8,18,8,128]{3,2,1,0:T(8,128)(2,1)S(1)}, u32[]{:S(2)}, u32[]{:S(2)}) collective-permute-start(bf16[8,18,8,128]{3,2,1,0:T(8,128)(2,1)S(1)} %constant_dynamic-update-slice_fusion.query_ref), channel_id=1, source_target_pairs={{0,2},{2,4},{4,6},{1,3},{3,5},{5,7},{8,10},{10,12},{12,14},{9,11},... | collective-permute-start | bytes 884744 | tf_op jit(solution)/shard_map/ppermute | solution.py:432
  29.9 4.6 %collective-permute-done.9.after_ref.query_ref = bf16[8,18,8,128]{3,2,1,0:T(8,128)(2,1)S(1)} collective-permute-done((bf16[8,18,8,128]{3,2,1,0:T(8,128)(2,1)S(1)}, bf16[8,18,8,128]{3,2,1,0:T(8,128)(2,1)S(1)}, u32[]{:S(2)}, u32[]{:S(2)}) %collective-permute-start.9) | collective-permute-done | bytes 294944 | tf_op jit(solution)/shard_map/ppermute | solution.py:433
  34.4 2.6 %shard_map.76 = bf16[9,16,8,128]{3,2,1,0:T(8,128)(2,1)S(1)} custom-call(s32[10]{0:T(128)S(1)} %pad_add_fusion.1.info_ref, bf16[8,18,8,128]{3,2,1,0:T(8,128)(2,1)S(1)} %collective-permute-done.9.after_ref.query_ref, bf16[8,4,16,8,128]{4,3,2,1,0:T(8,128)(2,1)S(1)} %constant_dynamic-update-slice_fusion.1.pairs_ref), custom_call_target="tpu_custom_call" | custom-call | flops 4294967296 | bytes 1048576 | tf_op jit(solution)/shard_map/pallas_call | solution.py:384
  37.0 3.5 %collective-permute-start.10 = (bf16[9,16,8,128]{3,2,1,0:T(8,128)(2,1)S(1)}, bf16[9,16,8,128]{3,2,1,0:T(8,128)(2,1)S(1)}, u32[]{:S(2)}, u32[]{:S(2)}) collective-permute-start(bf16[9,16,8,128]{3,2,1,0:T(8,128)(2,1)S(1)} %shard_map.76), channel_id=1, source_target_pairs={{0,2},{2,4},{4,6},{1,3},{3,5},{5,7},{8,10},{10,12},{12,14},{9,11},... | collective-permute-start | bytes 884744 | tf_op jit(solution)/shard_map/ppermute | solution.py:454
  40.5 2.9 %shard_map.77 = bf16[9,16,8,128]{3,2,1,0:T(8,128)(2,1)S(1)} custom-call(s32[10]{0:T(128)S(1)} %pad_add_fusion.1.info_ref, bf16[8,18,8,128]{3,2,1,0:T(8,128)(2,1)S(1)} %collective-permute-done.8.before_ref.query_ref, bf16[8,4,16,8,128]{4,3,2,1,0:T(8,128)(2,1)S(1)} %constant_dynamic-update-slice_fusion.1.pairs_ref), custom_call_target="tpu_custom_call" | custom-call | flops 4294967296 | bytes 1048576 | tf_op jit(solution)/shard_map/pallas_call | solution.py:384
  43.4 1.3 %collective-permute-start.11 = (bf16[9,16,8,128]{3,2,1,0:T(8,128)(2,1)S(1)}, bf16[9,16,8,128]{3,2,1,0:T(8,128)(2,1)S(1)}, u32[]{:S(2)}, u32[]{:S(2)}) collective-permute-start(bf16[9,16,8,128]{3,2,1,0:T(8,128)(2,1)S(1)} %shard_map.77), channel_id=1, source_target_pairs={{2,0},{4,2},{6,4},{3,1},{5,3},{7,5},{10,8},{12,10},{14,12},{11,9},... | collective-permute-start | bytes 884744 | tf_op jit(solution)/shard_map/ppermute | solution.py:452
  44.7 3.2 %shard_map.75 = (f32[8,128,128]{2,1,0:T(8,128)S(1)}, f32[8,128,128]{2,1,0:T(8,128)S(1)}, f32[8,128,128]{2,1,0:T(8,128)S(1)}) custom-call(s32[10]{0:T(128)S(1)} %pad_add_fusion.1.info_ref, f32[3,3,128]{2,1,0:T(4,128)S(1)} %constant_dynamic-slice_fusion.weight_ref, f32[1,128]{1,0:T(1,128)S(1)} %dynamic-slice_bitcast_fusion.bias_ref, ...), custom_call_target="tpu_custom_call" | custom-call | flops 4294967296 | bytes 1048576 | tf_op jit(solution)/shard_map/pallas_call | solution.py:384
  47.9 5.7 %collective-permute-done.11.right_ref = bf16[9,16,8,128]{3,2,1,0:T(8,128)(2,1)S(1)} collective-permute-done((bf16[9,16,8,128]{3,2,1,0:T(8,128)(2,1)S(1)}, bf16[9,16,8,128]{3,2,1,0:T(8,128)(2,1)S(1)}, u32[]{:S(2)}, u32[]{:S(2)}) %collective-permute-start.11) | collective-permute-done | bytes 294944 | tf_op jit(solution)/shard_map/ppermute | solution.py:452
  53.5 1.7 %shard_map.78 = (bf16[4,16,8,128]{3,2,1,0:T(8,128)(2,1)S(1)}, bf16[4,16,8,128]{3,2,1,0:T(8,128)(2,1)S(1)}) custom-call(s32[10]{0:T(128)S(1)} %pad_add_fusion.1.info_ref, f32[8,128,128]{2,1,0:T(8,128)S(1)} %get-tuple-element.26.part_ref, f32[8,128,128]{2,1,0:T(8,128)S(1)} %get-tuple-element.27.level_ref, f32[8,128,128]{2,1,0:T(8,128)S(1)} %get-tuple-element.28.conv_ref, ...), custom_call_target="tpu_custom_call" | custom-call | flops 1073741824 | bytes 1048576 | tf_op jit(solution)/shard_map/pallas_call | solution.py:384
  55.4 1.3 %collective-permute-done.12.beside_ref = bf16[4,16,8,128]{3,2,1,0:T(8,128)(2,1)S(1)} collective-permute-done((bf16[4,16,8,128]{3,2,1,0:T(8,128)(2,1)S(1)}, bf16[4,16,8,128]{3,2,1,0:T(8,128)(2,1)S(1)}, u32[]{:S(2)}, u32[]{:S(2)}) %collective-permute-start.12) | collective-permute-done | bytes 131104 | tf_op jit(solution)/shard_map/ppermute | solution.py:381
  56.7 1.5 %collective-permute-start.13 = (bf16[2,16,8,128]{3,2,1,0:T(8,128)(2,1)S(1)}, bf16[2,16,8,128]{3,2,1,0:T(8,128)(2,1)S(1)}, u32[]{:S(2)}, u32[]{:S(2)}) collective-permute-start(bf16[2,16,8,128]{3,2,1,0:T(8,128)(2,1)S(1)} %pad_maximum_fusion.2), channel_id=1, source_target_pairs={{0,1},{1,0},{8,9},{9,8},{16,17},{17,16},{24,25},{25,24},{2,3},{3,2... | collective-permute-start | bytes 196616 | tf_op jit(solution)/shard_map/ppermute | solution.py:381
  58.3 1.5 %collective-permute-start.14 = (bf16[2,16,8,128]{3,2,1,0:T(8,128)(2,1)S(1)}, bf16[2,16,8,128]{3,2,1,0:T(8,128)(2,1)S(1)}, u32[]{:S(2)}, u32[]{:S(2)}) collective-permute-start(bf16[2,16,8,128]{3,2,1,0:T(8,128)(2,1)S(1)} %pad_maximum_fusion.3), channel_id=1, source_target_pairs={{0,16},{1,17},{8,24},{9,25},{16,0},{17,1},{24,8},{25,9},{2,18},{3,... | collective-permute-start | bytes 196616 | tf_op jit(solution)/shard_map/ppermute | solution.py:381
  59.8 0.6 collective-permute-start.15
  60.4 0.6 collective-permute-done.13.refs_0_
  61.1 2.1 %collective-permute-done.14.refs_1_ = bf16[2,16,8,128]{3,2,1,0:T(8,128)(2,1)S(1)} collective-permute-done((bf16[2,16,8,128]{3,2,1,0:T(8,128)(2,1)S(1)}, bf16[2,16,8,128]{3,2,1,0:T(8,128)(2,1)S(1)}, u32[]{:S(2)}, u32[]{:S(2)}) %collective-permute-start.14) | collective-permute-done | bytes 65568 | tf_op jit(solution)/shard_map/ppermute | solution.py:381
  63.1 1.9 %collective-permute-done.15.refs_2_ = bf16[2,16,8,128]{3,2,1,0:T(8,128)(2,1)S(1)} collective-permute-done((bf16[2,16,8,128]{3,2,1,0:T(8,128)(2,1)S(1)}, bf16[2,16,8,128]{3,2,1,0:T(8,128)(2,1)S(1)}, u32[]{:S(2)}, u32[]{:S(2)}) %collective-permute-start.15) | collective-permute-done | bytes 65568 | tf_op jit(solution)/shard_map/ppermute | solution.py:381
  65.0 1.3 %shard_map.79 = bf16[16,8,1024]{2,1,0:T(8,128)(2,1)} custom-call(s32[2]{0:T(128)S(1)} %pad_add_fusion.me_ref, bf16[4,16,8,128]{3,2,1,0:T(8,128)(2,1)S(1)} %get-tuple-element.29.same_ref, bf16[4,16,8,128]{3,2,1,0:T(8,128)(2,1)S(1)} %collective-permute-done.12.beside_ref, bf16[2,16,8,128]{3,2,1,0:T(8,128)(2,1)S(1)} %collective-permute-done.13.refs_0_, ...), custom_call_target="tpu_custom_call" | custom-call | bytes 1048576 | tf_op jit(solution)/shard_map/pallas_call | solution.py:384
  (32 shorter events, 0.6 us)
Async XLA Ops:
  0.0 25.2 %copy-start = (f32[3,3,1024]{2,1,0:T(4,128)S(1)}, f32[3,3,1024]{2,1,0:T(4,128)}, u32[]{:S(2)}) copy-start(f32[3,3,1024]{2,1,0:T(4,128)} %param.12) | copy-start | bytes 110596
  1.8 10.4 %collective-permute-start.2 = (bf16[2,18,8,128]{3,2,1,0:T(8,128)(2,1)S(1)}, bf16[2,18,8,128]{3,2,1,0:T(8,128)(2,1)S(1)}, u32[]{:S(2)}, u32[]{:S(2)}) collective-permute-start(bf16[2,18,8,128]{3,2,1,0:T(8,128)(2,1)S(1)} %get-tuple-element.21), channel_id=1, source_target_pairs={{0,17},{1,16},{8,25},{9,24},{16,1},{17,0},{24,9},{25,8},{2,19},{3,... | collective-permute-start | bytes 221192 | tf_op jit(solution)/shard_map/ppermute | solution.py:381
  5.8 6.4 %collective-permute-start.1 = (bf16[2,18,8,128]{3,2,1,0:T(8,128)(2,1)S(1)}, bf16[2,18,8,128]{3,2,1,0:T(8,128)(2,1)S(1)}, u32[]{:S(2)}, u32[]{:S(2)}) collective-permute-start(bf16[2,18,8,128]{3,2,1,0:T(8,128)(2,1)S(1)} %get-tuple-element.20), channel_id=1, source_target_pairs={{0,16},{1,17},{8,24},{9,25},{16,0},{17,1},{24,8},{25,9},{2,18},{3,... | collective-permute-start | bytes 221192 | tf_op jit(solution)/shard_map/ppermute | solution.py:381
  6.3 5.6 %collective-permute-start = (bf16[2,18,8,128]{3,2,1,0:T(8,128)(2,1)S(1)}, bf16[2,18,8,128]{3,2,1,0:T(8,128)(2,1)S(1)}, u32[]{:S(2)}, u32[]{:S(2)}) collective-permute-start(bf16[2,18,8,128]{3,2,1,0:T(8,128)(2,1)S(1)} %get-tuple-element.19), channel_id=1, source_target_pairs={{0,1},{1,0},{8,9},{9,8},{16,17},{17,16},{24,25},{25,24},{2,3},{3,2... | collective-permute-start | bytes 221192 | tf_op jit(solution)/shard_map/ppermute | solution.py:381
  8.4 14.3 %collective-permute-start.6 = (bf16[2,4,16,8,128]{4,3,2,1,0:T(8,128)(2,1)S(1)}, bf16[2,4,16,8,128]{4,3,2,1,0:T(8,128)(2,1)S(1)}, u32[]{:S(2)}, u32[]{:S(2)}) collective-permute-start(bf16[2,4,16,8,128]{4,3,2,1,0:T(8,128)(2,1)S(1)} %get-tuple-element.25), channel_id=1, source_target_pairs={{0,17},{1,16},{8,25},{9,24},{16,1},{17,0},{24,9},{25,8},{2,19},{3,... | collective-permute-start | bytes 786440 | tf_op jit(solution)/shard_map/ppermute | solution.py:381
  11.3 11.4 %collective-permute-start.5 = (bf16[2,4,16,8,128]{4,3,2,1,0:T(8,128)(2,1)S(1)}, bf16[2,4,16,8,128]{4,3,2,1,0:T(8,128)(2,1)S(1)}, u32[]{:S(2)}, u32[]{:S(2)}) collective-permute-start(bf16[2,4,16,8,128]{4,3,2,1,0:T(8,128)(2,1)S(1)} %get-tuple-element.24), channel_id=1, source_target_pairs={{0,16},{1,17},{8,24},{9,25},{16,0},{17,1},{24,8},{25,9},{2,18},{3,... | collective-permute-start | bytes 786440 | tf_op jit(solution)/shard_map/ppermute | solution.py:381
  11.9 10.6 %collective-permute-start.4 = (bf16[2,4,16,8,128]{4,3,2,1,0:T(8,128)(2,1)S(1)}, bf16[2,4,16,8,128]{4,3,2,1,0:T(8,128)(2,1)S(1)}, u32[]{:S(2)}, u32[]{:S(2)}) collective-permute-start(bf16[2,4,16,8,128]{4,3,2,1,0:T(8,128)(2,1)S(1)} %get-tuple-element.23), channel_id=1, source_target_pairs={{0,1},{1,0},{8,9},{9,8},{16,17},{17,16},{24,25},{25,24},{2,3},{3,2... | collective-permute-start | bytes 786440 | tf_op jit(solution)/shard_map/ppermute | solution.py:381
  12.2 10.9 %collective-permute-start.3 = (bf16[4,18,8,128]{3,2,1,0:T(8,128)(2,1)S(1)}, bf16[4,18,8,128]{3,2,1,0:T(8,128)(2,1)S(1)}, u32[]{:S(2)}, u32[]{:S(2)}) collective-permute-start(bf16[4,18,8,128]{3,2,1,0:T(8,128)(2,1)S(1)} %pad_maximum_fusion.1), channel_id=1, source_target_pairs={{0,8},{1,9},{8,0},{9,1},{16,24},{17,25},{24,16},{25,17},{2,10},{3,... | collective-permute-start | bytes 442376 | tf_op jit(solution)/shard_map/ppermute | solution.py:381
  22.9 6.9 %collective-permute-start.7 = (bf16[4,4,16,8,128]{4,3,2,1,0:T(8,128)(2,1)S(1)}, bf16[4,4,16,8,128]{4,3,2,1,0:T(8,128)(2,1)S(1)}, u32[]{:S(2)}, u32[]{:S(2)}) collective-permute-start(bf16[4,4,16,8,128]{4,3,2,1,0:T(8,128)(2,1)S(1)} %pad_maximum_fusion), channel_id=1, source_target_pairs={{0,8},{1,9},{8,0},{9,1},{16,24},{17,25},{24,16},{25,17},{2,10},{3,... | collective-permute-start | bytes 1572872 | tf_op jit(solution)/shard_map/ppermute | solution.py:381
  23.1 11.3 %collective-permute-start.9 = (bf16[8,18,8,128]{3,2,1,0:T(8,128)(2,1)S(1)}, bf16[8,18,8,128]{3,2,1,0:T(8,128)(2,1)S(1)}, u32[]{:S(2)}, u32[]{:S(2)}) collective-permute-start(bf16[8,18,8,128]{3,2,1,0:T(8,128)(2,1)S(1)} %constant_dynamic-update-slice_fusion.query_ref), channel_id=1, source_target_pairs={{2,0},{4,2},{6,4},{3,1},{5,3},{7,5},{10,8},{12,10},{14,12},{11,9},... | collective-permute-start | bytes 884744 | tf_op jit(solution)/shard_map/ppermute | solution.py:433
  25.2 15.3 %collective-permute-start.8 = (bf16[8,18,8,128]{3,2,1,0:T(8,128)(2,1)S(1)}, bf16[8,18,8,128]{3,2,1,0:T(8,128)(2,1)S(1)}, u32[]{:S(2)}, u32[]{:S(2)}) collective-permute-start(bf16[8,18,8,128]{3,2,1,0:T(8,128)(2,1)S(1)} %constant_dynamic-update-slice_fusion.query_ref), channel_id=1, source_target_pairs={{0,2},{2,4},{4,6},{1,3},{3,5},{5,7},{8,10},{10,12},{12,14},{9,11},... | collective-permute-start | bytes 884744 | tf_op jit(solution)/shard_map/ppermute | solution.py:432
  37.0 10.9 %collective-permute-start.10 = (bf16[9,16,8,128]{3,2,1,0:T(8,128)(2,1)S(1)}, bf16[9,16,8,128]{3,2,1,0:T(8,128)(2,1)S(1)}, u32[]{:S(2)}, u32[]{:S(2)}) collective-permute-start(bf16[9,16,8,128]{3,2,1,0:T(8,128)(2,1)S(1)} %shard_map.76), channel_id=1, source_target_pairs={{0,2},{2,4},{4,6},{1,3},{3,5},{5,7},{8,10},{10,12},{12,14},{9,11},... | collective-permute-start | bytes 884744 | tf_op jit(solution)/shard_map/ppermute | solution.py:454
  43.4 10.2 %collective-permute-start.11 = (bf16[9,16,8,128]{3,2,1,0:T(8,128)(2,1)S(1)}, bf16[9,16,8,128]{3,2,1,0:T(8,128)(2,1)S(1)}, u32[]{:S(2)}, u32[]{:S(2)}) collective-permute-start(bf16[9,16,8,128]{3,2,1,0:T(8,128)(2,1)S(1)} %shard_map.77), channel_id=1, source_target_pairs={{2,0},{4,2},{6,4},{3,1},{5,3},{7,5},{10,8},{12,10},{14,12},{11,9},... | collective-permute-start | bytes 884744 | tf_op jit(solution)/shard_map/ppermute | solution.py:452
  55.3 1.4 %collective-permute-start.12 = (bf16[4,16,8,128]{3,2,1,0:T(8,128)(2,1)S(1)}, bf16[4,16,8,128]{3,2,1,0:T(8,128)(2,1)S(1)}, u32[]{:S(2)}, u32[]{:S(2)}) collective-permute-start(bf16[4,16,8,128]{3,2,1,0:T(8,128)(2,1)S(1)} %get-tuple-element.30), channel_id=1, source_target_pairs={{0,8},{1,9},{8,0},{9,1},{16,24},{17,25},{24,16},{25,17},{2,10},{3,... | collective-permute-start | bytes 393224 | tf_op jit(solution)/shard_map/ppermute | solution.py:381
  56.7 4.3 %collective-permute-start.13 = (bf16[2,16,8,128]{3,2,1,0:T(8,128)(2,1)S(1)}, bf16[2,16,8,128]{3,2,1,0:T(8,128)(2,1)S(1)}, u32[]{:S(2)}, u32[]{:S(2)}) collective-permute-start(bf16[2,16,8,128]{3,2,1,0:T(8,128)(2,1)S(1)} %pad_maximum_fusion.2), channel_id=1, source_target_pairs={{0,1},{1,0},{8,9},{9,8},{16,17},{17,16},{24,25},{25,24},{2,3},{3,2... | collective-permute-start | bytes 196616 | tf_op jit(solution)/shard_map/ppermute | solution.py:381
  58.3 4.9 %collective-permute-start.14 = (bf16[2,16,8,128]{3,2,1,0:T(8,128)(2,1)S(1)}, bf16[2,16,8,128]{3,2,1,0:T(8,128)(2,1)S(1)}, u32[]{:S(2)}, u32[]{:S(2)}) collective-permute-start(bf16[2,16,8,128]{3,2,1,0:T(8,128)(2,1)S(1)} %pad_maximum_fusion.3), channel_id=1, source_target_pairs={{0,16},{1,17},{8,24},{9,25},{16,0},{17,1},{24,8},{25,9},{2,18},{3,... | collective-permute-start | bytes 196616 | tf_op jit(solution)/shard_map/ppermute | solution.py:381
  59.8 5.2 %collective-permute-start.15 = (bf16[2,16,8,128]{3,2,1,0:T(8,128)(2,1)S(1)}, bf16[2,16,8,128]{3,2,1,0:T(8,128)(2,1)S(1)}, u32[]{:S(2)}, u32[]{:S(2)}) collective-permute-start(bf16[2,16,8,128]{3,2,1,0:T(8,128)(2,1)S(1)} %pad_maximum_fusion.4), channel_id=1, source_target_pairs={{0,17},{1,16},{8,25},{9,24},{16,1},{17,0},{24,9},{25,8},{2,19},{3,... | collective-permute-start | bytes 196616 | tf_op jit(solution)/shard_map/ppermute | solution.py:381

commit v6 on v4

--- a/solution.py
+++ b/solution.py
@@ -149,6 +149,7 @@
 NEG = -1e30
 VMEM = pl.BlockSpec(memory_space=pltpu.VMEM)
 SMEM = pl.BlockSpec(memory_space=pltpu.SMEM)
+FAR = pl.BlockSpec(memory_space=pltpu.HBM)
 LIMIT = pltpu.CompilerParams(vmem_limit_bytes=8 * 1024 * 1024)
 SMALL = pltpu.CompilerParams(vmem_limit_bytes=4 * 1024 * 1024)
 
@@ -256,16 +257,16 @@
     window = Window(grid, tile, info_ref, query_ref, pairs_ref)
     size, count = window.size, grid[0] * grid[1]
     lane = lax.broadcasted_iota(jnp.int32, (size, HD), 1)
-    packed = jnp.zeros((size, HD), jnp.float32)
+    levels = jnp.zeros((size, HD), jnp.float32)
     for row in range(grid[0]):
         for col in range(grid[1]):
             index = row * grid[1] + col
             part, level = window.attend(row, first_col + col)
-            out_ref[window.slot(row, col)] = part.reshape(tile + (HD,)).astype(jnp.bfloat16)
-            high = level.astype(jnp.bfloat16).astype(jnp.float32)
-            middle = (level - high).astype(jnp.bfloat16).astype(jnp.float32)
-            for i, piece in enumerate((high, middle, level - high - middle)):
-                packed = jnp.where(lane == i * count + index, piece, packed)
+            out_ref[index] = part.reshape(tile + (HD,)).astype(jnp.bfloat16)
+            levels = jnp.where(lane == index, level, levels)
+    high = levels.astype(jnp.bfloat16).astype(jnp.float32)
+    middle = (levels - high).astype(jnp.bfloat16).astype(jnp.float32)
+    packed = high + pltpu.roll(middle, count, 1) + pltpu.roll(levels - high - middle, 2 * count, 1)
     out_ref[count] = packed.reshape(tile + (HD,)).astype(jnp.bfloat16)
 
 
@@ -290,7 +291,7 @@
         place = info_ref[2 + index]
         parts, levels = [part_ref[index]], [level_ref[index]]
         for ref, there, pack in zip(visits, present, packed):
-            parts.append(ref[place].reshape(size, HD).astype(jnp.float32))
+            parts.append(ref[index].reshape(size, HD).astype(jnp.float32))
             level = pack[:, index : index + 1]
             for i in (1, 2):
                 level = level + pack[:, i * count + index : i * count + index + 1]
@@ -314,28 +315,36 @@
 
 
 def pack_kernel(flips, side, me_ref, *refs):
-    sources, buffers = refs[: len(refs) - len(flips)], refs[len(refs) - len(flips) :]
-    for buffer, flip in zip(buffers, flips):
+    count = len(flips)
+    sources = refs[: -2 * count - 2]
+    query_buffers, pair_buffers = refs[-2 * count - 2 : -count - 2], refs[-count - 2 : -2]
+    held_ref, sems = refs[-2], refs[-1]
+    tile_rows, tile_cols, _ = sources[0].shape
+    copies = [pltpu.make_async_copy(x, held_ref.at[i], sems.at[i]) for i, x in enumerate(sources)]
+    for copy in copies:
+        copy.start()
+    heads = [[lanes(me_ref[0] ^ (flip ^ beside)) for beside in (0, side)] for flip in flips]
+    copies[0].wait()
+    for buffer, pair in zip(query_buffers, heads):
         for other in range(2):
-            head = me_ref[0] ^ (flip ^ (side if other else 0))
-            for member, source in enumerate(sources):
-                buffer[other, member] = source[:, :, lanes(head)]
-
-
-def query_kernel(flips, side, me_ref, query_ref, values_ref, *buffers):
-    tile_rows, tile_cols, _ = query_ref.shape
+            buffer[other, pl.ds(0, tile_rows)] = held_ref[0, :, :, pair[other]]
+    copies[1].wait()
     sub = lax.broadcasted_iota(jnp.int32, (tile_cols, HD), 0)
-    for buffer, flip in zip(buffers, flips):
+    for buffer, pair in zip(query_buffers, heads):
         for other in range(2):
-            head = me_ref[0] ^ (flip ^ (side if other else 0))
-            buffer[other, pl.ds(0, tile_rows)] = query_ref[:, :, lanes(head)]
             for start in range(0, tile_rows, tile_cols):
                 packed = jnp.zeros((tile_cols, HD), jnp.float32)
                 for line in range(tile_cols):
-                    values = values_ref[start + line, :, lanes(head)].astype(jnp.float32)
+                    values = held_ref[1, start + line, :, pair[other]].astype(jnp.float32)
                     edge = jnp.where(me_ref[1] == 0, values[:1], values[tile_cols - 1 :])
                     packed = jnp.where(sub == line, edge, packed)
                 buffer[other, tile_rows + start // tile_cols] = packed.astype(jnp.bfloat16)
+    for member, source in enumerate((*range(2, len(sources)), 1)):
+        if member < len(sources) - 2:
+            copies[source].wait()
+        for buffer, pair in zip(pair_buffers, heads):
+            for other in range(2):
+                buffer[other, member] = held_ref[source, :, :, pair[other]]
 
 
 def unpack_kernel(flips, side, me_ref, same_ref, beside_ref, *refs):
@@ -364,15 +373,19 @@
     def swap(x, flip):
         return lax.ppermute(x, axes, [(s, s ^ flip) for s in range(heads)])
 
-    def call(kernel, out_shape, params, cost, *operands):
+    def call(kernel, out_shape, params, cost, *operands, space=(VMEM, VMEM), scratch=()):
         return pl.pallas_call(
             kernel,
             out_shape=out_shape,
-            in_specs=[SMEM] + [VMEM] * (len(operands) - 1),
-            out_specs=jax.tree.map(lambda _: VMEM, out_shape),
+            in_specs=[SMEM] + [space[0]] * (len(operands) - 1),
+            out_specs=jax.tree.map(lambda _: space[1], out_shape),
+            scratch_shapes=scratch,
             compiler_params=params,
             cost_estimate=pl.CostEstimate(flops=cost << 30, bytes_accessed=1 << 20, transcendentals=0),
         )(*operands)
+
+    def stay(x):
+        return pltpu.with_memory_space_constraint(x, pltpu.HBM)
 
     def gather(buffers):
         got = [buffers[0]] + [swap(b, flip) for b, flip in zip(buffers[1:], flips[1:])]
@@ -383,15 +396,21 @@
     up = [(i, i + 1) for i in range(far - 1)]
     down = [(i + 1, i) for i in range(far - 1)]
     edges = -(-tile_rows // tile_cols)
-    buffer = jax.ShapeDtypeStruct((2, tile_rows + edges, tile_cols, HD), jnp.bfloat16)
-    packed_query = call(
-        functools.partial(query_kernel, flips, side), [buffer] * len(flips), SMALL, 0, me_ref, queries, values_new
-    )
-    query = gather(packed_query)
-    sources = (keys_cache[0], values_cache[0], keys_new, values_new)
-    buffer = jax.ShapeDtypeStruct((2, len(sources)) + block, jnp.bfloat16)
-    packed_pairs = call(functools.partial(pack_kernel, flips, side), [buffer] * len(flips), SMALL, 0, me_ref, *sources)
-    pairs = gather(packed_pairs)
+    sources = (queries, values_new, keys_cache[0], values_cache[0], keys_new)
+    query_buffer = jax.ShapeDtypeStruct((2, tile_rows + edges, tile_cols, HD), jnp.bfloat16)
+    pair_buffer = jax.ShapeDtypeStruct((2, len(sources) - 1) + block, jnp.bfloat16)
+    packed = call(
+        functools.partial(pack_kernel, flips, side),
+        [query_buffer] * len(flips) + [pair_buffer] * len(flips),
+        SMALL,
+        0,
+        me_ref,
+        *map(stay, sources),
+        space=(FAR, VMEM),
+        scratch=[pltpu.VMEM((len(sources),) + queries.shape, jnp.bfloat16), pltpu.SemaphoreType.DMA((len(sources),))],
+    )
+    query = gather(packed[: len(flips)])
+    pairs = gather(packed[len(flips) :])
     query_left = lax.ppermute(query, "far", up)
     query_right = lax.ppermute(query, "far", down)
     far_index = lax.axis_index("far")
@@ -422,7 +441,9 @@
     kernel = functools.partial(join_kernel, grid, tile)
     same, other = call(kernel, [half, half], LIMIT, 1, info, *own, from_left, from_right)
     received = swap(other, side)
-    got = [swap(jnp.stack([same[i], received[i]]), flips[i]) for i in range(1, len(flips))]
+    got = []
+    for i in range(1, len(flips)):
+        got.append(swap(jnp.stack([same[i], received[i]]), flips[i]))
     return call(
         functools.partial(unpack_kernel, flips, side),
         jax.ShapeDtypeStruct(queries.shape, jnp.bfloat16),

time: 68.2 us -> 65.4 us (0.959)
  local copies, waits for them, and re-layouts: 4.84 us -> 1.03 us
    unnamed x14 -> x2, local copies, waits for them, and re-layouts: 3.81 us -> 0.01 us
    pallas_call x7 -> x6, Pallas kernels: 13 us -> 13.6 us  [call(): pl.pallas_call(kernel, out_shape=out_shape, in_specs=[SMEM] + [space[0]]...]
  transfers between devices with their start and end apart: 16 -> 16, of which waited for: 8 -> 8; matrix products, arithmetic and copies ran while one was open for 2% -> 2% of each run, Pallas kernels for 14% -> 13%
where the time goes in v6:
time: 65.4 us; the launch traced here: 65.1 us
  waiting for transfers between devices  27.2 us (42%)
  starting transfers between devices  22.6 us (35%)
  Pallas kernels  13.6 us (21%)
  local copies, waits for them, and re-layouts  1.03 us (2%)
    ppermute x12, waiting for transfers between devices, swap(): return lax.ppermute(x, axes, [(s, s ^ flip) for s in range(heads)])  17 us
    pallas_call x6, Pallas kernels, call(): pl.pallas_call(kernel, out_shape=out_shape, in_specs=[SMEM] + [space[0]]...  13.6 us
    ppermute x12, starting transfers between devices, swap(): return lax.ppermute(x, axes, [(s, s ^ flip) for s in range(heads)])  12.1 us
    ppermute x1, waiting for transfers between devices, head_step(): from_right = lax.ppermute(left_part, 'far', down)  5.66 us
    ppermute x1, waiting for transfers between devices, head_step(): query_right = lax.ppermute(query, 'far', down)  4.58 us
    ppermute x1, starting transfers between devices, head_step(): query_left = lax.ppermute(query, 'far', up)  4.55 us
    ppermute x1, starting transfers between devices, head_step(): from_left = lax.ppermute(right_part, 'far', up)  3.43 us
  transfers between devices with their start and end apart: 16, of which 8 were waited for; matrix products, arithmetic and copies ran while one was open for 2% of the time, Pallas kernels for 13%

profile of v6, /device:TPU:0, one launch (start us, length us, event | category | flops | bytes accessed | tf_op | source)
XLA Modules:
  0.0 65.1 jit_solution(12981449715281482297)
XLA Ops:
  0.0 0.1 pad_add_fusion.me_ref
  0.1 2.0 %shard_map.73 = (bf16[2,18,8,128]{3,2,1,0:T(8,128)(2,1)S(1)}, bf16[2,18,8,128]{3,2,1,0:T(8,128)(2,1)S(1)}, bf16[2,18,8,128]{3,2,1,0:T(8,128)(2,1)S(1)}, bf16[2,1...) custom-call(s32[2]{0:T(128)S(1)} %pad_add_fusion.me_ref, ...), custom_call_target="tpu_custom_call" | custom-call | bytes 1048576 | tf_op jit(solution)/shard_map/pallas_call | solution.py:377
  2.1 4.0 %collective-permute-start.2 = (bf16[2,18,8,128]{3,2,1,0:T(8,128)(2,1)S(1)}, bf16[2,18,8,128]{3,2,1,0:T(8,128)(2,1)S(1)}, u32[]{:S(2)}, u32[]{:S(2)}) collective-permute-start(bf16[2,18,8,128]{3,2,1,0:T(8,128)(2,1)S(1)} %get-tuple-element.21), channel_id=1, source_target_pairs={{0,17},{1,16},{8,25},{9,24},{16,1},{17,0},{24,9},{25,8},{2,19},{3,... | collective-permute-start | bytes 221192 | tf_op jit(solution)/shard_map/ppermute | solution.py:374
  6.1 0.5 collective-permute-start.1
  6.6 0.1 collective-permute-start
  6.7 2.8 %collective-permute-start.6 = (bf16[2,4,16,8,128]{4,3,2,1,0:T(8,128)(2,1)S(1)}, bf16[2,4,16,8,128]{4,3,2,1,0:T(8,128)(2,1)S(1)}, u32[]{:S(2)}, u32[]{:S(2)}) collective-permute-start(bf16[2,4,16,8,128]{4,3,2,1,0:T(8,128)(2,1)S(1)} %get-tuple-element.25), channel_id=1, source_target_pairs={{0,17},{1,16},{8,25},{9,24},{16,1},{17,0},{24,9},{25,8},{2,19},{3,... | collective-permute-start | bytes 786440 | tf_op jit(solution)/shard_map/ppermute | solution.py:374
  9.5 0.5 collective-permute-start.5
  10.1 5.8 %collective-permute-done = bf16[2,18,8,128]{3,2,1,0:T(8,128)(2,1)S(1)} collective-permute-done((bf16[2,18,8,128]{3,2,1,0:T(8,128)(2,1)S(1)}, bf16[2,18,8,128]{3,2,1,0:T(8,128)(2,1)S(1)}, u32[]{:S(2)}, u32[]{:S(2)}) %collective-permute-start) | collective-permute-done | bytes 73760 | tf_op jit(solution)/shard_map/ppermute | solution.py:374
  16.0 0.1 collective-permute-start.3
  16.1 6.2 %collective-permute-done.4 = bf16[2,4,16,8,128]{4,3,2,1,0:T(8,128)(2,1)S(1)} collective-permute-done((bf16[2,4,16,8,128]{4,3,2,1,0:T(8,128)(2,1)S(1)}, bf16[2,4,16,8,128]{4,3,2,1,0:T(8,128)(2,1)S(1)}, u32[]{:S(2)}, u32[]{:S(2)}) %collective-permute-start.4) | collective-permute-done | bytes 262176 | tf_op jit(solution)/shard_map/ppermute | solution.py:374
  22.6 0.1 add_convert_fusion
  22.6 0.1 pad_add_fusion.1.info_ref
  22.7 1.3 %collective-permute-start.9 = (bf16[8,18,8,128]{3,2,1,0:T(8,128)(2,1)S(1)}, bf16[8,18,8,128]{3,2,1,0:T(8,128)(2,1)S(1)}, u32[]{:S(2)}, u32[]{:S(2)}) collective-permute-start(bf16[8,18,8,128]{3,2,1,0:T(8,128)(2,1)S(1)} %constant_dynamic-update-slice_fusion.query_ref), channel_id=1, source_target_pairs={{2,0},{4,2},{6,4},{3,1},{5,3},{7,5},{10,8},{12,10},{14,12},{11,9},... | collective-permute-start | bytes 884744 | tf_op jit(solution)/shard_map/ppermute | solution.py:415
  24.0 0.8 %dynamic-slice_bitcast_fusion.bias_ref = f32[1,128]{1,0:T(1,128)S(1)} fusion(f32[1024]{0:T(1024)} %param.13, s32[]{:T(128)S(6)} %select_n.27), kind=kLoop, calls=%fused_computation.33 | loop fusion | bytes 1028 | tf_op jit(solution)/shard_map/dynamic_slice | solution.py:427
  24.8 4.6 %collective-permute-start.8 = (bf16[8,18,8,128]{3,2,1,0:T(8,128)(2,1)S(1)}, bf16[8,18,8,128]{3,2,1,0:T(8,128)(2,1)S(1)}, u32[]{:S(2)}, u32[]{:S(2)}) collective-permute-start(bf16[8,18,8,128]{3,2,1,0:T(8,128)(2,1)S(1)} %constant_dynamic-update-slice_fusion.query_ref), channel_id=1, source_target_pairs={{0,2},{2,4},{4,6},{1,3},{3,5},{5,7},{8,10},{10,12},{12,14},{9,11},... | collective-permute-start | bytes 884744 | tf_op jit(solution)/shard_map/ppermute | solution.py:414
  29.4 0.1 constant_dynamic-update-slice_fusion.1.pairs_ref
  29.5 4.6 %collective-permute-done.9.after_ref.query_ref = bf16[8,18,8,128]{3,2,1,0:T(8,128)(2,1)S(1)} collective-permute-done((bf16[8,18,8,128]{3,2,1,0:T(8,128)(2,1)S(1)}, bf16[8,18,8,128]{3,2,1,0:T(8,128)(2,1)S(1)}, u32[]{:S(2)}, u32[]{:S(2)}) %collective-permute-start.9) | collective-permute-done | bytes 294944 | tf_op jit(solution)/shard_map/ppermute | solution.py:415
  34.0 2.6 %shard_map.75 = bf16[9,16,8,128]{3,2,1,0:T(8,128)(2,1)S(1)} custom-call(s32[10]{0:T(128)S(1)} %pad_add_fusion.1.info_ref, bf16[8,18,8,128]{3,2,1,0:T(8,128)(2,1)S(1)} %collective-permute-done.9.after_ref.query_ref, bf16[8,4,16,8,128]{4,3,2,1,0:T(8,128)(2,1)S(1)} %constant_dynamic-update-slice_fusion.1.pairs_ref), custom_call_target="tpu_custom_call" | custom-call | flops 4294967296 | bytes 1048576 | tf_op jit(solution)/shard_map/pallas_call | solution.py:377
  36.6 3.4 %collective-permute-start.10 = (bf16[9,16,8,128]{3,2,1,0:T(8,128)(2,1)S(1)}, bf16[9,16,8,128]{3,2,1,0:T(8,128)(2,1)S(1)}, u32[]{:S(2)}, u32[]{:S(2)}) collective-permute-start(bf16[9,16,8,128]{3,2,1,0:T(8,128)(2,1)S(1)} %shard_map.75), channel_id=1, source_target_pairs={{0,2},{2,4},{4,6},{1,3},{3,5},{5,7},{8,10},{10,12},{12,14},{9,11},... | collective-permute-start | bytes 884744 | tf_op jit(solution)/shard_map/ppermute | solution.py:436
  40.1 2.9 %shard_map.76 = bf16[9,16,8,128]{3,2,1,0:T(8,128)(2,1)S(1)} custom-call(s32[10]{0:T(128)S(1)} %pad_add_fusion.1.info_ref, bf16[8,18,8,128]{3,2,1,0:T(8,128)(2,1)S(1)} %collective-permute-done.8.before_ref.query_ref, bf16[8,4,16,8,128]{4,3,2,1,0:T(8,128)(2,1)S(1)} %constant_dynamic-update-slice_fusion.1.pairs_ref), custom_call_target="tpu_custom_call" | custom-call | flops 4294967296 | bytes 1048576 | tf_op jit(solution)/shard_map/pallas_call | solution.py:377
  42.9 1.3 %collective-permute-start.11 = (bf16[9,16,8,128]{3,2,1,0:T(8,128)(2,1)S(1)}, bf16[9,16,8,128]{3,2,1,0:T(8,128)(2,1)S(1)}, u32[]{:S(2)}, u32[]{:S(2)}) collective-permute-start(bf16[9,16,8,128]{3,2,1,0:T(8,128)(2,1)S(1)} %shard_map.76), channel_id=1, source_target_pairs={{2,0},{4,2},{6,4},{3,1},{5,3},{7,5},{10,8},{12,10},{14,12},{11,9},... | collective-permute-start | bytes 884744 | tf_op jit(solution)/shard_map/ppermute | solution.py:434
  44.2 3.2 %shard_map.74 = (f32[8,128,128]{2,1,0:T(8,128)S(1)}, f32[8,128,128]{2,1,0:T(8,128)S(1)}, f32[8,128,128]{2,1,0:T(8,128)S(1)}) custom-call(s32[10]{0:T(128)S(1)} %pad_add_fusion.1.info_ref, f32[3,3,128]{2,1,0:T(4,128)S(1)} %constant_dynamic-slice_fusion.weight_ref, f32[1,128]{1,0:T(1,128)S(1)} %dynamic-slice_bitcast_fusion.bias_ref, ...), custom_call_target="tpu_custom_call" | custom-call | flops 4294967296 | bytes 1048576 | tf_op jit(solution)/shard_map/pallas_call | solution.py:377
  47.4 5.7 %collective-permute-done.11.right_ref = bf16[9,16,8,128]{3,2,1,0:T(8,128)(2,1)S(1)} collective-permute-done((bf16[9,16,8,128]{3,2,1,0:T(8,128)(2,1)S(1)}, bf16[9,16,8,128]{3,2,1,0:T(8,128)(2,1)S(1)}, u32[]{:S(2)}, u32[]{:S(2)}) %collective-permute-start.11) | collective-permute-done | bytes 294944 | tf_op jit(solution)/shard_map/ppermute | solution.py:434
  53.1 1.7 %shard_map.77 = (bf16[4,16,8,128]{3,2,1,0:T(8,128)(2,1)S(1)}, bf16[4,16,8,128]{3,2,1,0:T(8,128)(2,1)S(1)}) custom-call(s32[10]{0:T(128)S(1)} %pad_add_fusion.1.info_ref, f32[8,128,128]{2,1,0:T(8,128)S(1)} %get-tuple-element.26.part_ref, f32[8,128,128]{2,1,0:T(8,128)S(1)} %get-tuple-element.27.level_ref, f32[8,128,128]{2,1,0:T(8,128)S(1)} %get-tuple-element.28.conv_ref, ...), custom_call_target="tpu_custom_call" | custom-call | flops 1073741824 | bytes 1048576 | tf_op jit(solution)/shard_map/pallas_call | solution.py:377
  54.9 1.3 %collective-permute-done.12.beside_ref = bf16[4,16,8,128]{3,2,1,0:T(8,128)(2,1)S(1)} collective-permute-done((bf16[4,16,8,128]{3,2,1,0:T(8,128)(2,1)S(1)}, bf16[4,16,8,128]{3,2,1,0:T(8,128)(2,1)S(1)}, u32[]{:S(2)}, u32[]{:S(2)}) %collective-permute-start.12) | collective-permute-done | bytes 131104 | tf_op jit(solution)/shard_map/ppermute | solution.py:374
  56.3 1.1 %collective-permute-start.13 = (bf16[2,16,8,128]{3,2,1,0:T(8,128)(2,1)S(1)}, bf16[2,16,8,128]{3,2,1,0:T(8,128)(2,1)S(1)}, u32[]{:S(2)}, u32[]{:S(2)}) collective-permute-start(bf16[2,16,8,128]{3,2,1,0:T(8,128)(2,1)S(1)} %pad_maximum_fusion.2), channel_id=1, source_target_pairs={{0,1},{1,0},{8,9},{9,8},{16,17},{17,16},{24,25},{25,24},{2,3},{3,2... | collective-permute-start | bytes 196616 | tf_op jit(solution)/shard_map/ppermute | solution.py:374
  57.3 1.2 %collective-permute-start.14 = (bf16[2,16,8,128]{3,2,1,0:T(8,128)(2,1)S(1)}, bf16[2,16,8,128]{3,2,1,0:T(8,128)(2,1)S(1)}, u32[]{:S(2)}, u32[]{:S(2)}) collective-permute-start(bf16[2,16,8,128]{3,2,1,0:T(8,128)(2,1)S(1)} %pad_maximum_fusion.3), channel_id=1, source_target_pairs={{0,16},{1,17},{8,24},{9,25},{16,0},{17,1},{24,8},{25,9},{2,18},{3,... | collective-permute-start | bytes 196616 | tf_op jit(solution)/shard_map/ppermute | solution.py:374
  58.6 1.5 %collective-permute-start.15 = (bf16[2,16,8,128]{3,2,1,0:T(8,128)(2,1)S(1)}, bf16[2,16,8,128]{3,2,1,0:T(8,128)(2,1)S(1)}, u32[]{:S(2)}, u32[]{:S(2)}) collective-permute-start(bf16[2,16,8,128]{3,2,1,0:T(8,128)(2,1)S(1)} %pad_maximum_fusion.4), channel_id=1, source_target_pairs={{0,17},{1,16},{8,25},{9,24},{16,1},{17,0},{24,9},{25,8},{2,19},{3,... | collective-permute-start | bytes 196616 | tf_op jit(solution)/shard_map/ppermute | solution.py:374
  60.1 0.5 collective-permute-done.13.refs_0_
  60.6 1.1 %collective-permute-done.14.refs_1_ = bf16[2,16,8,128]{3,2,1,0:T(8,128)(2,1)S(1)} collective-permute-done((bf16[2,16,8,128]{3,2,1,0:T(8,128)(2,1)S(1)}, bf16[2,16,8,128]{3,2,1,0:T(8,128)(2,1)S(1)}, u32[]{:S(2)}, u32[]{:S(2)}) %collective-permute-start.14) | collective-permute-done | bytes 65568 | tf_op jit(solution)/shard_map/ppermute | solution.py:374
  61.7 2.2 %collective-permute-done.15.refs_2_ = bf16[2,16,8,128]{3,2,1,0:T(8,128)(2,1)S(1)} collective-permute-done((bf16[2,16,8,128]{3,2,1,0:T(8,128)(2,1)S(1)}, bf16[2,16,8,128]{3,2,1,0:T(8,128)(2,1)S(1)}, u32[]{:S(2)}, u32[]{:S(2)}) %collective-permute-start.15) | collective-permute-done | bytes 65568 | tf_op jit(solution)/shard_map/ppermute | solution.py:374
  63.8 1.3 %shard_map.78 = bf16[16,8,1024]{2,1,0:T(8,128)(2,1)} custom-call(s32[2]{0:T(128)S(1)} %pad_add_fusion.me_ref, bf16[4,16,8,128]{3,2,1,0:T(8,128)(2,1)S(1)} %get-tuple-element.29.same_ref, bf16[4,16,8,128]{3,2,1,0:T(8,128)(2,1)S(1)} %collective-permute-done.12.beside_ref, bf16[2,16,8,128]{3,2,1,0:T(8,128)(2,1)S(1)} %collective-permute-done.13.refs_0_, ...), custom_call_target="tpu_custom_call" | custom-call | bytes 1048576 | tf_op jit(solution)/shard_map/pallas_call | solution.py:377
  (31 shorter events, 0.5 us)
Async XLA Ops:
  0.0 24.8 %copy-start = (f32[3,3,1024]{2,1,0:T(4,128)S(1)}, f32[3,3,1024]{2,1,0:T(4,128)}, u32[]{:S(2)}) copy-start(f32[3,3,1024]{2,1,0:T(4,128)} %param.12) | copy-start | bytes 110596
  2.1 13.9 %collective-permute-start.2 = (bf16[2,18,8,128]{3,2,1,0:T(8,128)(2,1)S(1)}, bf16[2,18,8,128]{3,2,1,0:T(8,128)(2,1)S(1)}, u32[]{:S(2)}, u32[]{:S(2)}) collective-permute-start(bf16[2,18,8,128]{3,2,1,0:T(8,128)(2,1)S(1)} %get-tuple-element.21), channel_id=1, source_target_pairs={{0,17},{1,16},{8,25},{9,24},{16,1},{17,0},{24,9},{25,8},{2,19},{3,... | collective-permute-start | bytes 221192 | tf_op jit(solution)/shard_map/ppermute | solution.py:374
  6.1 9.9 %collective-permute-start.1 = (bf16[2,18,8,128]{3,2,1,0:T(8,128)(2,1)S(1)}, bf16[2,18,8,128]{3,2,1,0:T(8,128)(2,1)S(1)}, u32[]{:S(2)}, u32[]{:S(2)}) collective-permute-start(bf16[2,18,8,128]{3,2,1,0:T(8,128)(2,1)S(1)} %get-tuple-element.20), channel_id=1, source_target_pairs={{0,16},{1,17},{8,24},{9,25},{16,0},{17,1},{24,8},{25,9},{2,18},{3,... | collective-permute-start | bytes 221192 | tf_op jit(solution)/shard_map/ppermute | solution.py:374
  6.6 9.3 %collective-permute-start = (bf16[2,18,8,128]{3,2,1,0:T(8,128)(2,1)S(1)}, bf16[2,18,8,128]{3,2,1,0:T(8,128)(2,1)S(1)}, u32[]{:S(2)}, u32[]{:S(2)}) collective-permute-start(bf16[2,18,8,128]{3,2,1,0:T(8,128)(2,1)S(1)} %get-tuple-element.19), channel_id=1, source_target_pairs={{0,1},{1,0},{8,9},{9,8},{16,17},{17,16},{24,25},{25,24},{2,3},{3,2... | collective-permute-start | bytes 221192 | tf_op jit(solution)/shard_map/ppermute | solution.py:374
  6.7 15.7 %collective-permute-start.6 = (bf16[2,4,16,8,128]{4,3,2,1,0:T(8,128)(2,1)S(1)}, bf16[2,4,16,8,128]{4,3,2,1,0:T(8,128)(2,1)S(1)}, u32[]{:S(2)}, u32[]{:S(2)}) collective-permute-start(bf16[2,4,16,8,128]{4,3,2,1,0:T(8,128)(2,1)S(1)} %get-tuple-element.25), channel_id=1, source_target_pairs={{0,17},{1,16},{8,25},{9,24},{16,1},{17,0},{24,9},{25,8},{2,19},{3,... | collective-permute-start | bytes 786440 | tf_op jit(solution)/shard_map/ppermute | solution.py:374
  9.5 12.8 %collective-permute-start.5 = (bf16[2,4,16,8,128]{4,3,2,1,0:T(8,128)(2,1)S(1)}, bf16[2,4,16,8,128]{4,3,2,1,0:T(8,128)(2,1)S(1)}, u32[]{:S(2)}, u32[]{:S(2)}) collective-permute-start(bf16[2,4,16,8,128]{4,3,2,1,0:T(8,128)(2,1)S(1)} %get-tuple-element.24), channel_id=1, source_target_pairs={{0,16},{1,17},{8,24},{9,25},{16,0},{17,1},{24,8},{25,9},{2,18},{3,... | collective-permute-start | bytes 786440 | tf_op jit(solution)/shard_map/ppermute | solution.py:374
  15.9 6.4 %collective-permute-start.4 = (bf16[2,4,16,8,128]{4,3,2,1,0:T(8,128)(2,1)S(1)}, bf16[2,4,16,8,128]{4,3,2,1,0:T(8,128)(2,1)S(1)}, u32[]{:S(2)}, u32[]{:S(2)}) collective-permute-start(bf16[2,4,16,8,128]{4,3,2,1,0:T(8,128)(2,1)S(1)} %get-tuple-element.23), channel_id=1, source_target_pairs={{0,1},{1,0},{8,9},{9,8},{16,17},{17,16},{24,25},{25,24},{2,3},{3,2... | collective-permute-start | bytes 786440 | tf_op jit(solution)/shard_map/ppermute | solution.py:374
  16.0 6.7 %collective-permute-start.3 = (bf16[4,18,8,128]{3,2,1,0:T(8,128)(2,1)S(1)}, bf16[4,18,8,128]{3,2,1,0:T(8,128)(2,1)S(1)}, u32[]{:S(2)}, u32[]{:S(2)}) collective-permute-start(bf16[4,18,8,128]{3,2,1,0:T(8,128)(2,1)S(1)} %pad_maximum_fusion.1), channel_id=1, source_target_pairs={{0,8},{1,9},{8,0},{9,1},{16,24},{17,25},{24,16},{25,17},{2,10},{3,... | collective-permute-start | bytes 442376 | tf_op jit(solution)/shard_map/ppermute | solution.py:374
  22.5 6.9 %collective-permute-start.7 = (bf16[4,4,16,8,128]{4,3,2,1,0:T(8,128)(2,1)S(1)}, bf16[4,4,16,8,128]{4,3,2,1,0:T(8,128)(2,1)S(1)}, u32[]{:S(2)}, u32[]{:S(2)}) collective-permute-start(bf16[4,4,16,8,128]{4,3,2,1,0:T(8,128)(2,1)S(1)} %pad_maximum_fusion), channel_id=1, source_target_pairs={{0,8},{1,9},{8,0},{9,1},{16,24},{17,25},{24,16},{25,17},{2,10},{3,... | collective-permute-start | bytes 1572872 | tf_op jit(solution)/shard_map/ppermute | solution.py:374
  22.7 11.3 %collective-permute-start.9 = (bf16[8,18,8,128]{3,2,1,0:T(8,128)(2,1)S(1)}, bf16[8,18,8,128]{3,2,1,0:T(8,128)(2,1)S(1)}, u32[]{:S(2)}, u32[]{:S(2)}) collective-permute-start(bf16[8,18,8,128]{3,2,1,0:T(8,128)(2,1)S(1)} %constant_dynamic-update-slice_fusion.query_ref), channel_id=1, source_target_pairs={{2,0},{4,2},{6,4},{3,1},{5,3},{7,5},{10,8},{12,10},{14,12},{11,9},... | collective-permute-start | bytes 884744 | tf_op jit(solution)/shard_map/ppermute | solution.py:415
  24.8 15.2 %collective-permute-start.8 = (bf16[8,18,8,128]{3,2,1,0:T(8,128)(2,1)S(1)}, bf16[8,18,8,128]{3,2,1,0:T(8,128)(2,1)S(1)}, u32[]{:S(2)}, u32[]{:S(2)}) collective-permute-start(bf16[8,18,8,128]{3,2,1,0:T(8,128)(2,1)S(1)} %constant_dynamic-update-slice_fusion.query_ref), channel_id=1, source_target_pairs={{0,2},{2,4},{4,6},{1,3},{3,5},{5,7},{8,10},{10,12},{12,14},{9,11},... | collective-permute-start | bytes 884744 | tf_op jit(solution)/shard_map/ppermute | solution.py:414
  36.6 10.8 %collective-permute-start.10 = (bf16[9,16,8,128]{3,2,1,0:T(8,128)(2,1)S(1)}, bf16[9,16,8,128]{3,2,1,0:T(8,128)(2,1)S(1)}, u32[]{:S(2)}, u32[]{:S(2)}) collective-permute-start(bf16[9,16,8,128]{3,2,1,0:T(8,128)(2,1)S(1)} %shard_map.75), channel_id=1, source_target_pairs={{0,2},{2,4},{4,6},{1,3},{3,5},{5,7},{8,10},{10,12},{12,14},{9,11},... | collective-permute-start | bytes 884744 | tf_op jit(solution)/shard_map/ppermute | solution.py:436
  42.9 10.2 %collective-permute-start.11 = (bf16[9,16,8,128]{3,2,1,0:T(8,128)(2,1)S(1)}, bf16[9,16,8,128]{3,2,1,0:T(8,128)(2,1)S(1)}, u32[]{:S(2)}, u32[]{:S(2)}) collective-permute-start(bf16[9,16,8,128]{3,2,1,0:T(8,128)(2,1)S(1)} %shard_map.76), channel_id=1, source_target_pairs={{2,0},{4,2},{6,4},{3,1},{5,3},{7,5},{10,8},{12,10},{14,12},{11,9},... | collective-permute-start | bytes 884744 | tf_op jit(solution)/shard_map/ppermute | solution.py:434
  54.8 1.4 %collective-permute-start.12 = (bf16[4,16,8,128]{3,2,1,0:T(8,128)(2,1)S(1)}, bf16[4,16,8,128]{3,2,1,0:T(8,128)(2,1)S(1)}, u32[]{:S(2)}, u32[]{:S(2)}) collective-permute-start(bf16[4,16,8,128]{3,2,1,0:T(8,128)(2,1)S(1)} %get-tuple-element.30), channel_id=1, source_target_pairs={{0,8},{1,9},{8,0},{9,1},{16,24},{17,25},{24,16},{25,17},{2,10},{3,... | collective-permute-start | bytes 393224 | tf_op jit(solution)/shard_map/ppermute | solution.py:374
  56.3 4.3 %collective-permute-start.13 = (bf16[2,16,8,128]{3,2,1,0:T(8,128)(2,1)S(1)}, bf16[2,16,8,128]{3,2,1,0:T(8,128)(2,1)S(1)}, u32[]{:S(2)}, u32[]{:S(2)}) collective-permute-start(bf16[2,16,8,128]{3,2,1,0:T(8,128)(2,1)S(1)} %pad_maximum_fusion.2), channel_id=1, source_target_pairs={{0,1},{1,0},{8,9},{9,8},{16,17},{17,16},{24,25},{25,24},{2,3},{3,2... | collective-permute-start | bytes 196616 | tf_op jit(solution)/shard_map/ppermute | solution.py:374
  57.3 4.3 %collective-permute-start.14 = (bf16[2,16,8,128]{3,2,1,0:T(8,128)(2,1)S(1)}, bf16[2,16,8,128]{3,2,1,0:T(8,128)(2,1)S(1)}, u32[]{:S(2)}, u32[]{:S(2)}) collective-permute-start(bf16[2,16,8,128]{3,2,1,0:T(8,128)(2,1)S(1)} %pad_maximum_fusion.3), channel_id=1, source_target_pairs={{0,16},{1,17},{8,24},{9,25},{16,0},{17,1},{24,8},{25,9},{2,18},{3,... | collective-permute-start | bytes 196616 | tf_op jit(solution)/shard_map/ppermute | solution.py:374
  58.6 5.2 %collective-permute-start.15 = (bf16[2,16,8,128]{3,2,1,0:T(8,128)(2,1)S(1)}, bf16[2,16,8,128]{3,2,1,0:T(8,128)(2,1)S(1)}, u32[]{:S(2)}, u32[]{:S(2)}) collective-permute-start(bf16[2,16,8,128]{3,2,1,0:T(8,128)(2,1)S(1)} %pad_maximum_fusion.4), channel_id=1, source_target_pairs={{0,17},{1,16},{8,25},{9,24},{16,1},{17,0},{24,9},{25,8},{2,19},{3,... | collective-permute-start | bytes 196616 | tf_op jit(solution)/shard_map/ppermute | solution.py:374

commit v7 on v6

--- a/solution.py
+++ b/solution.py
@@ -173,7 +173,7 @@
     def tile(self, member, row, col):
         return self.pairs[self.slot(row, col), member].reshape(self.size, HD)
 
-    def attend(self, row, col):
+    def scores(self, row, col):
         query = self.query[self.slot(row, col), pl.ds(0, self.tile_rows)].reshape(self.size, HD)
         frames = range(self.pairs.shape[1] // 2)
         cols = [c for c in range(self.grid_cols) if abs(c - col) <= 2]
@@ -199,11 +199,13 @@
         top = blocks[0][3]
         for entry in blocks[1:]:
             top = jnp.maximum(top, entry[3])
-        top = jnp.max(top, axis=1, keepdims=True)
+        return row, up and down, down, blocks, jnp.max(top, axis=1, keepdims=True)
+
+    def weigh(self, row, both, down, blocks, top):
         parts = []
         for f, off_row, c, block in blocks:
             weights = jnp.exp2((block - top) * self.scale).astype(jnp.bfloat16)
-            if off_row and up and down:
+            if off_row and both:
                 parts.append((f, row - 1, c, weights * self.upper_one))
                 parts.append((f, row + 1, c, weights * (1 - self.upper_one)))
             elif off_row:
@@ -215,6 +217,15 @@
         weights = jnp.concatenate([part for _, _, _, part in parts], axis=1)
         total = jnp.dot(weights, values, preferred_element_type=jnp.float32)
         return total[:, :HD] / total[:, HD:], top * self.scale + jnp.log2(total[:, HD:])
+
+    def attend_all(self, first_col):
+        places = [(row, col) for row in range(self.grid_rows) for col in range(self.grid_cols)]
+        held = None
+        for place in [*places, None]:
+            ready = self.scores(place[0], first_col + place[1]) if place else None
+            if held:
+                yield (*held[0], *self.weigh(*held[1]))
+            held = (place, ready)
 
     def enhanced(self, row, col, weight_ref, bias_ref, before_ref, after_ref):
         shape = (self.tile_cols, HD)
@@ -258,12 +269,10 @@
     size, count = window.size, grid[0] * grid[1]
     lane = lax.broadcasted_iota(jnp.int32, (size, HD), 1)
     levels = jnp.zeros((size, HD), jnp.float32)
-    for row in range(grid[0]):
-        for col in range(grid[1]):
-            index = row * grid[1] + col
-            part, level = window.attend(row, first_col + col)
-            out_ref[index] = part.reshape(tile + (HD,)).astype(jnp.bfloat16)
-            levels = jnp.where(lane == index, level, levels)
+    for row, col, part, level in window.attend_all(first_col):
+        index = row * grid[1] + col
+        out_ref[index] = part.reshape(tile + (HD,)).astype(jnp.bfloat16)
+        levels = jnp.where(lane == index, level, levels)
     high = levels.astype(jnp.bfloat16).astype(jnp.float32)
     middle = (levels - high).astype(jnp.bfloat16).astype(jnp.float32)
     packed = high + pltpu.roll(middle, count, 1) + pltpu.roll(levels - high - middle, 2 * count, 1)
@@ -274,40 +283,31 @@
     grid, tile, info_ref, weight_ref, bias_ref, query_ref, pairs_ref, before_ref, after_ref, part_ref, level_ref, conv_ref
 ):
     window = Window(grid, tile, info_ref, query_ref, pairs_ref)
-    for row in range(grid[0]):
-        for col in range(grid[1]):
-            index = row * grid[1] + col
-            part_ref[index], level_ref[index] = window.attend(row, col)
-            conv = window.enhanced(row, col, weight_ref, bias_ref, before_ref, after_ref)
-            conv_ref[index] = conv.reshape(window.size, HD)
-
-
-def join_kernel(grid, tile, info_ref, part_ref, level_ref, conv_ref, left_ref, right_ref, same_ref, beside_ref):
+    for row, col, part, level in window.attend_all(0):
+        index = row * grid[1] + col
+        part_ref[index], level_ref[index] = part, level
+        conv = window.enhanced(row, col, weight_ref, bias_ref, before_ref, after_ref)
+        conv_ref[index] = conv.reshape(window.size, HD)
+
+
+def join_kernel(grid, tile, info_ref, part_ref, level_ref, conv_ref, left_ref, right_ref, out_ref):
     size, count = tile[0] * tile[1], grid[0] * grid[1]
-    present = [info_ref[0] > 0, info_ref[1] > 0]
     visits = (left_ref, right_ref)
-    packed = [ref[count].reshape(size, HD).astype(jnp.float32) for ref in visits]
+    packed = []
+    for i, ref in enumerate(visits):
+        pack = ref[count].reshape(size, HD).astype(jnp.float32)
+        level = pack + pltpu.roll(pack, HD - count, 1) + pltpu.roll(pack, HD - 2 * count, 1)
+        packed.append(jnp.where(info_ref[i] > 0, level, NEG))
     for index in range(count):
-        place = info_ref[2 + index]
-        parts, levels = [part_ref[index]], [level_ref[index]]
-        for ref, there, pack in zip(visits, present, packed):
+        levels = [level_ref[index]]
+        parts = [part_ref[index]]
+        for ref, pack in zip(visits, packed):
             parts.append(ref[index].reshape(size, HD).astype(jnp.float32))
-            level = pack[:, index : index + 1]
-            for i in (1, 2):
-                level = level + pack[:, i * count + index : i * count + index + 1]
-            levels.append(jnp.broadcast_to(jnp.where(there, level, NEG), (size, HD)))
+            levels.append(jnp.broadcast_to(pack[:, index : index + 1], (size, HD)))
         top = jnp.maximum(jnp.maximum(levels[0], levels[1]), levels[2])
         shares = [jnp.exp2(level - top) for level in levels]
         mixed = sum(share * part for share, part in zip(shares, parts)) / sum(shares)
-        out = (mixed + conv_ref[index]).reshape(tile + (HD,)).astype(jnp.bfloat16)
-
-        @pl.when(place < count // 2)
-        def _():
-            same_ref[place] = out
-
-        @pl.when(place >= count // 2)
-        def _():
-            beside_ref[place - count // 2] = out
+        out_ref[info_ref[2 + index]] = (mixed + conv_ref[index]).reshape(tile + (HD,)).astype(jnp.bfloat16)
 
 
 def lanes(head):
@@ -437,9 +437,10 @@
     part = jax.ShapeDtypeStruct((heads, size, HD), jnp.float32)
     kernel = functools.partial(own_kernel, grid, tile)
     own = call(kernel, [part] * 3, LIMIT, 4, info, weight, bias, query, pairs, query_left, query_right)
-    half = jax.ShapeDtypeStruct((len(flips),) + block, jnp.bfloat16)
     kernel = functools.partial(join_kernel, grid, tile)
-    same, other = call(kernel, [half, half], LIMIT, 1, info, *own, from_left, from_right)
+    result = jax.ShapeDtypeStruct((heads,) + block, jnp.bfloat16)
+    result = call(kernel, result, LIMIT, 1, info, *own, from_left, from_right)
+    same, other = result[: len(flips)], result[len(flips) :]
     received = swap(other, side)
     got = []
     for i in range(1, len(flips)):

time: 65.4 us -> 64 us (0.979)
  Pallas kernels: 13.6 us -> 11.9 us
    pallas_call x6, Pallas kernels: 13.6 us -> 11.9 us  [call(): pl.pallas_call(kernel, out_shape=out_shape, in_specs=[SMEM] + [space[0]]...]
  transfers between devices with their start and end apart: 16 -> 16, of which waited for: 8 -> 8; matrix products, arithmetic and copies ran while one was open for 2% -> 2% of each run, Pallas kernels for 13% -> 12%
where the time goes in v7:
time: 64 us; the launch traced here: 63.8 us
  waiting for transfers between devices  27.5 us (43%)
  starting transfers between devices  22.6 us (35%)
  Pallas kernels  11.9 us (19%)
  local copies, waits for them, and re-layouts  1.05 us (2%)
    ppermute x12, waiting for transfers between devices, swap(): return lax.ppermute(x, axes, [(s, s ^ flip) for s in range(heads)])  17 us
    ppermute x12, starting transfers between devices, swap(): return lax.ppermute(x, axes, [(s, s ^ flip) for s in range(heads)])  12.1 us
    pallas_call x6, Pallas kernels, call(): pl.pallas_call(kernel, out_shape=out_shape, in_specs=[SMEM] + [space[0]]...  11.9 us
    ppermute x1, waiting for transfers between devices, head_step(): from_right = lax.ppermute(left_part, 'far', down)  5.94 us
    ppermute x1, waiting for transfers between devices, head_step(): query_right = lax.ppermute(query, 'far', down)  4.58 us
    ppermute x1, starting transfers between devices, head_step(): query_left = lax.ppermute(query, 'far', up)  4.55 us
    ppermute x1, starting transfers between devices, head_step(): from_left = lax.ppermute(right_part, 'far', up)  3.43 us
    ppermute x1, starting transfers between devices, head_step(): query_right = lax.ppermute(query, 'far', down)  1.29 us
  transfers between devices with their start and end apart: 16, of which 8 were waited for; matrix products, arithmetic and copies ran while one was open for 2% of the time, Pallas kernels for 12%

profile of v7, /device:TPU:0, one launch (start us, length us, event | category | flops | bytes accessed | tf_op | source)
XLA Modules:
  0.0 63.8 jit_solution(7324281689668502456)
XLA Ops:
  0.0 0.1 pad_add_fusion.me_ref
  0.1 2.0 %shard_map.73 = (bf16[2,18,8,128]{3,2,1,0:T(8,128)(2,1)S(1)}, bf16[2,18,8,128]{3,2,1,0:T(8,128)(2,1)S(1)}, bf16[2,18,8,128]{3,2,1,0:T(8,128)(2,1)S(1)}, bf16[2,1...) custom-call(s32[2]{0:T(128)S(1)} %pad_add_fusion.me_ref, ...), custom_call_target="tpu_custom_call" | custom-call | bytes 1048576 | tf_op jit(solution)/shard_map/pallas_call | solution.py:377
  2.1 4.0 %collective-permute-start.2 = (bf16[2,18,8,128]{3,2,1,0:T(8,128)(2,1)S(1)}, bf16[2,18,8,128]{3,2,1,0:T(8,128)(2,1)S(1)}, u32[]{:S(2)}, u32[]{:S(2)}) collective-permute-start(bf16[2,18,8,128]{3,2,1,0:T(8,128)(2,1)S(1)} %get-tuple-element.19), channel_id=1, source_target_pairs={{0,17},{1,16},{8,25},{9,24},{16,1},{17,0},{24,9},{25,8},{2,19},{3,... | collective-permute-start | bytes 221192 | tf_op jit(solution)/shard_map/ppermute | solution.py:374
  6.1 0.5 collective-permute-start.1
  6.6 0.1 collective-permute-start
  6.7 2.8 %collective-permute-start.6 = (bf16[2,4,16,8,128]{4,3,2,1,0:T(8,128)(2,1)S(1)}, bf16[2,4,16,8,128]{4,3,2,1,0:T(8,128)(2,1)S(1)}, u32[]{:S(2)}, u32[]{:S(2)}) collective-permute-start(bf16[2,4,16,8,128]{4,3,2,1,0:T(8,128)(2,1)S(1)} %get-tuple-element.23), channel_id=1, source_target_pairs={{0,17},{1,16},{8,25},{9,24},{16,1},{17,0},{24,9},{25,8},{2,19},{3,... | collective-permute-start | bytes 786440 | tf_op jit(solution)/shard_map/ppermute | solution.py:374
  9.5 0.5 collective-permute-start.5
  10.1 5.8 %collective-permute-done = bf16[2,18,8,128]{3,2,1,0:T(8,128)(2,1)S(1)} collective-permute-done((bf16[2,18,8,128]{3,2,1,0:T(8,128)(2,1)S(1)}, bf16[2,18,8,128]{3,2,1,0:T(8,128)(2,1)S(1)}, u32[]{:S(2)}, u32[]{:S(2)}) %collective-permute-start) | collective-permute-done | bytes 73760 | tf_op jit(solution)/shard_map/ppermute | solution.py:374
  16.1 6.2 %collective-permute-done.4 = bf16[2,4,16,8,128]{4,3,2,1,0:T(8,128)(2,1)S(1)} collective-permute-done((bf16[2,4,16,8,128]{4,3,2,1,0:T(8,128)(2,1)S(1)}, bf16[2,4,16,8,128]{4,3,2,1,0:T(8,128)(2,1)S(1)}, u32[]{:S(2)}, u32[]{:S(2)}) %collective-permute-start.4) | collective-permute-done | bytes 262176 | tf_op jit(solution)/shard_map/ppermute | solution.py:374
  22.6 0.1 add_convert_fusion
  22.6 0.1 pad_add_fusion.1.info_ref
  22.7 1.3 %collective-permute-start.9 = (bf16[8,18,8,128]{3,2,1,0:T(8,128)(2,1)S(1)}, bf16[8,18,8,128]{3,2,1,0:T(8,128)(2,1)S(1)}, u32[]{:S(2)}, u32[]{:S(2)}) collective-permute-start(bf16[8,18,8,128]{3,2,1,0:T(8,128)(2,1)S(1)} %constant_dynamic-update-slice_fusion.query_ref), channel_id=1, source_target_pairs={{2,0},{4,2},{6,4},{3,1},{5,3},{7,5},{10,8},{12,10},{14,12},{11,9},... | collective-permute-start | bytes 884744 | tf_op jit(solution)/shard_map/ppermute | solution.py:415
  24.0 0.8 %dynamic-slice_bitcast_fusion.bias_ref = f32[1,128]{1,0:T(1,128)S(1)} fusion(f32[1024]{0:T(1024)} %param.13, s32[]{:T(128)S(6)} %select_n.27), kind=kLoop, calls=%fused_computation.33 | loop fusion | bytes 1028 | tf_op jit(solution)/shard_map/dynamic_slice | solution.py:427
  24.8 4.6 %collective-permute-start.8 = (bf16[8,18,8,128]{3,2,1,0:T(8,128)(2,1)S(1)}, bf16[8,18,8,128]{3,2,1,0:T(8,128)(2,1)S(1)}, u32[]{:S(2)}, u32[]{:S(2)}) collective-permute-start(bf16[8,18,8,128]{3,2,1,0:T(8,128)(2,1)S(1)} %constant_dynamic-update-slice_fusion.query_ref), channel_id=1, source_target_pairs={{0,2},{2,4},{4,6},{1,3},{3,5},{5,7},{8,10},{10,12},{12,14},{9,11},... | collective-permute-start | bytes 884744 | tf_op jit(solution)/shard_map/ppermute | solution.py:414
  29.4 0.1 constant_dynamic-update-slice_fusion.1.pairs_ref
  29.5 4.6 %collective-permute-done.9.after_ref.query_ref = bf16[8,18,8,128]{3,2,1,0:T(8,128)(2,1)S(1)} collective-permute-done((bf16[8,18,8,128]{3,2,1,0:T(8,128)(2,1)S(1)}, bf16[8,18,8,128]{3,2,1,0:T(8,128)(2,1)S(1)}, u32[]{:S(2)}, u32[]{:S(2)}) %collective-permute-start.9) | collective-permute-done | bytes 294944 | tf_op jit(solution)/shard_map/ppermute | solution.py:415
  34.0 2.3 %shard_map.75 = bf16[9,16,8,128]{3,2,1,0:T(8,128)(2,1)S(1)} custom-call(s32[10]{0:T(128)S(1)} %pad_add_fusion.1.info_ref, bf16[8,18,8,128]{3,2,1,0:T(8,128)(2,1)S(1)} %collective-permute-done.9.after_ref.query_ref, bf16[8,4,16,8,128]{4,3,2,1,0:T(8,128)(2,1)S(1)} %constant_dynamic-update-slice_fusion.1.pairs_ref), custom_call_target="tpu_custom_call" | custom-call | flops 4294967296 | bytes 1048576 | tf_op jit(solution)/shard_map/pallas_call | solution.py:377
  36.4 3.4 %collective-permute-start.10 = (bf16[9,16,8,128]{3,2,1,0:T(8,128)(2,1)S(1)}, bf16[9,16,8,128]{3,2,1,0:T(8,128)(2,1)S(1)}, u32[]{:S(2)}, u32[]{:S(2)}) collective-permute-start(bf16[9,16,8,128]{3,2,1,0:T(8,128)(2,1)S(1)} %shard_map.75), channel_id=1, source_target_pairs={{0,2},{2,4},{4,6},{1,3},{3,5},{5,7},{8,10},{10,12},{12,14},{9,11},... | collective-permute-start | bytes 884744 | tf_op jit(solution)/shard_map/ppermute | solution.py:436
  39.8 2.3 %shard_map.76 = bf16[9,16,8,128]{3,2,1,0:T(8,128)(2,1)S(1)} custom-call(s32[10]{0:T(128)S(1)} %pad_add_fusion.1.info_ref, bf16[8,18,8,128]{3,2,1,0:T(8,128)(2,1)S(1)} %collective-permute-done.8.before_ref.query_ref, bf16[8,4,16,8,128]{4,3,2,1,0:T(8,128)(2,1)S(1)} %constant_dynamic-update-slice_fusion.1.pairs_ref), custom_call_target="tpu_custom_call" | custom-call | flops 4294967296 | bytes 1048576 | tf_op jit(solution)/shard_map/pallas_call | solution.py:377
  42.2 1.3 %collective-permute-start.11 = (bf16[9,16,8,128]{3,2,1,0:T(8,128)(2,1)S(1)}, bf16[9,16,8,128]{3,2,1,0:T(8,128)(2,1)S(1)}, u32[]{:S(2)}, u32[]{:S(2)}) collective-permute-start(bf16[9,16,8,128]{3,2,1,0:T(8,128)(2,1)S(1)} %shard_map.76), channel_id=1, source_target_pairs={{2,0},{4,2},{6,4},{3,1},{5,3},{7,5},{10,8},{12,10},{14,12},{11,9},... | collective-permute-start | bytes 884744 | tf_op jit(solution)/shard_map/ppermute | solution.py:434
  43.5 2.9 %shard_map.74 = (f32[8,128,128]{2,1,0:T(8,128)S(1)}, f32[8,128,128]{2,1,0:T(8,128)S(1)}, f32[8,128,128]{2,1,0:T(8,128)S(1)}) custom-call(s32[10]{0:T(128)S(1)} %pad_add_fusion.1.info_ref, f32[3,3,128]{2,1,0:T(4,128)S(1)} %constant_dynamic-slice_fusion.weight_ref, f32[1,128]{1,0:T(1,128)S(1)} %dynamic-slice_bitcast_fusion.bias_ref, ...), custom_call_target="tpu_custom_call" | custom-call | flops 4294967296 | bytes 1048576 | tf_op jit(solution)/shard_map/pallas_call | solution.py:377
  46.4 5.9 %collective-permute-done.11.right_ref = bf16[9,16,8,128]{3,2,1,0:T(8,128)(2,1)S(1)} collective-permute-done((bf16[9,16,8,128]{3,2,1,0:T(8,128)(2,1)S(1)}, bf16[9,16,8,128]{3,2,1,0:T(8,128)(2,1)S(1)}, u32[]{:S(2)}, u32[]{:S(2)}) %collective-permute-start.11) | collective-permute-done | bytes 294944 | tf_op jit(solution)/shard_map/ppermute | solution.py:434
  52.4 1.1 %shard_map.77 = bf16[8,16,8,128]{3,2,1,0:T(8,128)(2,1)S(1)} custom-call(s32[10]{0:T(128)S(1)} %pad_add_fusion.1.info_ref, f32[8,128,128]{2,1,0:T(8,128)S(1)} %get-tuple-element.24.part_ref, f32[8,128,128]{2,1,0:T(8,128)S(1)} %get-tuple-element.25.level_ref, f32[8,128,128]{2,1,0:T(8,128)S(1)} %get-tuple-element.26.conv_ref, ...), custom_call_target="tpu_custom_call" | custom-call | flops 1073741824 | bytes 1048576 | tf_op jit(solution)/shard_map/pallas_call | solution.py:377
  53.5 0.1 collective-permute-start.12
  53.6 1.3 %collective-permute-done.12.beside_ref = bf16[4,16,8,128]{3,2,1,0:T(8,128)(2,1)S(1)} collective-permute-done((bf16[4,16,8,128]{3,2,1,0:T(8,128)(2,1)S(1)}, bf16[4,16,8,128]{3,2,1,0:T(8,128)(2,1)S(1)}, u32[]{:S(2)}, u32[]{:S(2)}) %collective-permute-start.12) | collective-permute-done | bytes 131104 | tf_op jit(solution)/shard_map/ppermute | solution.py:374
  54.9 1.0 %collective-permute-start.13 = (bf16[2,16,8,128]{3,2,1,0:T(8,128)(2,1)S(1)}, bf16[2,16,8,128]{3,2,1,0:T(8,128)(2,1)S(1)}, u32[]{:S(2)}, u32[]{:S(2)}) collective-permute-start(bf16[2,16,8,128]{3,2,1,0:T(8,128)(2,1)S(1)} %pad_maximum_fusion.2), channel_id=1, source_target_pairs={{0,1},{1,0},{8,9},{9,8},{16,17},{17,16},{24,25},{25,24},{2,3},{3,2... | collective-permute-start | bytes 196616 | tf_op jit(solution)/shard_map/ppermute | solution.py:374
  56.0 1.3 %collective-permute-start.14 = (bf16[2,16,8,128]{3,2,1,0:T(8,128)(2,1)S(1)}, bf16[2,16,8,128]{3,2,1,0:T(8,128)(2,1)S(1)}, u32[]{:S(2)}, u32[]{:S(2)}) collective-permute-start(bf16[2,16,8,128]{3,2,1,0:T(8,128)(2,1)S(1)} %pad_maximum_fusion.3), channel_id=1, source_target_pairs={{0,16},{1,17},{8,24},{9,25},{16,0},{17,1},{24,8},{25,9},{2,18},{3,... | collective-permute-start | bytes 196616 | tf_op jit(solution)/shard_map/ppermute | solution.py:374
  57.2 1.5 %collective-permute-start.15 = (bf16[2,16,8,128]{3,2,1,0:T(8,128)(2,1)S(1)}, bf16[2,16,8,128]{3,2,1,0:T(8,128)(2,1)S(1)}, u32[]{:S(2)}, u32[]{:S(2)}) collective-permute-start(bf16[2,16,8,128]{3,2,1,0:T(8,128)(2,1)S(1)} %pad_maximum_fusion.4), channel_id=1, source_target_pairs={{0,17},{1,16},{8,25},{9,24},{16,1},{17,0},{24,9},{25,8},{2,19},{3,... | collective-permute-start | bytes 196616 | tf_op jit(solution)/shard_map/ppermute | solution.py:374
  58.7 0.5 collective-permute-done.13.refs_0_
  59.2 1.0 %collective-permute-done.14.refs_1_ = bf16[2,16,8,128]{3,2,1,0:T(8,128)(2,1)S(1)} collective-permute-done((bf16[2,16,8,128]{3,2,1,0:T(8,128)(2,1)S(1)}, bf16[2,16,8,128]{3,2,1,0:T(8,128)(2,1)S(1)}, u32[]{:S(2)}, u32[]{:S(2)}) %collective-permute-start.14) | collective-permute-done | bytes 65568 | tf_op jit(solution)/shard_map/ppermute | solution.py:374
  60.3 2.2 %collective-permute-done.15.refs_2_ = bf16[2,16,8,128]{3,2,1,0:T(8,128)(2,1)S(1)} collective-permute-done((bf16[2,16,8,128]{3,2,1,0:T(8,128)(2,1)S(1)}, bf16[2,16,8,128]{3,2,1,0:T(8,128)(2,1)S(1)}, u32[]{:S(2)}, u32[]{:S(2)}) %collective-permute-start.15) | collective-permute-done | bytes 65568 | tf_op jit(solution)/shard_map/ppermute | solution.py:374
  62.4 1.3 %shard_map.78 = bf16[16,8,1024]{2,1,0:T(8,128)(2,1)} custom-call(s32[2]{0:T(128)S(1)} %pad_add_fusion.me_ref, bf16[4,16,8,128]{3,2,1,0:T(8,128)(2,1)S(1)} %get-tuple-element.31.same_ref, bf16[4,16,8,128]{3,2,1,0:T(8,128)(2,1)S(1)} %collective-permute-done.12.beside_ref, bf16[2,16,8,128]{3,2,1,0:T(8,128)(2,1)S(1)} %collective-permute-done.13.refs_0_, ...), custom_call_target="tpu_custom_call" | custom-call | bytes 1048576 | tf_op jit(solution)/shard_map/pallas_call | solution.py:377
  (32 shorter events, 0.5 us)
Async XLA Ops:
  0.0 24.8 %copy-start = (f32[3,3,1024]{2,1,0:T(4,128)S(1)}, f32[3,3,1024]{2,1,0:T(4,128)}, u32[]{:S(2)}) copy-start(f32[3,3,1024]{2,1,0:T(4,128)} %param.12) | copy-start | bytes 110596
  2.1 13.9 %collective-permute-start.2 = (bf16[2,18,8,128]{3,2,1,0:T(8,128)(2,1)S(1)}, bf16[2,18,8,128]{3,2,1,0:T(8,128)(2,1)S(1)}, u32[]{:S(2)}, u32[]{:S(2)}) collective-permute-start(bf16[2,18,8,128]{3,2,1,0:T(8,128)(2,1)S(1)} %get-tuple-element.19), channel_id=1, source_target_pairs={{0,17},{1,16},{8,25},{9,24},{16,1},{17,0},{24,9},{25,8},{2,19},{3,... | collective-permute-start | bytes 221192 | tf_op jit(solution)/shard_map/ppermute | solution.py:374
  6.1 9.9 %collective-permute-start.1 = (bf16[2,18,8,128]{3,2,1,0:T(8,128)(2,1)S(1)}, bf16[2,18,8,128]{3,2,1,0:T(8,128)(2,1)S(1)}, u32[]{:S(2)}, u32[]{:S(2)}) collective-permute-start(bf16[2,18,8,128]{3,2,1,0:T(8,128)(2,1)S(1)} %get-tuple-element.18), channel_id=1, source_target_pairs={{0,16},{1,17},{8,24},{9,25},{16,0},{17,1},{24,8},{25,9},{2,18},{3,... | collective-permute-start | bytes 221192 | tf_op jit(solution)/shard_map/ppermute | solution.py:374
  6.6 9.3 %collective-permute-start = (bf16[2,18,8,128]{3,2,1,0:T(8,128)(2,1)S(1)}, bf16[2,18,8,128]{3,2,1,0:T(8,128)(2,1)S(1)}, u32[]{:S(2)}, u32[]{:S(2)}) collective-permute-start(bf16[2,18,8,128]{3,2,1,0:T(8,128)(2,1)S(1)} %get-tuple-element.17), channel_id=1, source_target_pairs={{0,1},{1,0},{8,9},{9,8},{16,17},{17,16},{24,25},{25,24},{2,3},{3,2... | collective-permute-start | bytes 221192 | tf_op jit(solution)/shard_map/ppermute | solution.py:374
  6.7 15.7 %collective-permute-start.6 = (bf16[2,4,16,8,128]{4,3,2,1,0:T(8,128)(2,1)S(1)}, bf16[2,4,16,8,128]{4,3,2,1,0:T(8,128)(2,1)S(1)}, u32[]{:S(2)}, u32[]{:S(2)}) collective-permute-start(bf16[2,4,16,8,128]{4,3,2,1,0:T(8,128)(2,1)S(1)} %get-tuple-element.23), channel_id=1, source_target_pairs={{0,17},{1,16},{8,25},{9,24},{16,1},{17,0},{24,9},{25,8},{2,19},{3,... | collective-permute-start | bytes 786440 | tf_op jit(solution)/shard_map/ppermute | solution.py:374
  9.5 12.8 %collective-permute-start.5 = (bf16[2,4,16,8,128]{4,3,2,1,0:T(8,128)(2,1)S(1)}, bf16[2,4,16,8,128]{4,3,2,1,0:T(8,128)(2,1)S(1)}, u32[]{:S(2)}, u32[]{:S(2)}) collective-permute-start(bf16[2,4,16,8,128]{4,3,2,1,0:T(8,128)(2,1)S(1)} %get-tuple-element.22), channel_id=1, source_target_pairs={{0,16},{1,17},{8,24},{9,25},{16,0},{17,1},{24,8},{25,9},{2,18},{3,... | collective-permute-start | bytes 786440 | tf_op jit(solution)/shard_map/ppermute | solution.py:374
  15.9 6.4 %collective-permute-start.4 = (bf16[2,4,16,8,128]{4,3,2,1,0:T(8,128)(2,1)S(1)}, bf16[2,4,16,8,128]{4,3,2,1,0:T(8,128)(2,1)S(1)}, u32[]{:S(2)}, u32[]{:S(2)}) collective-permute-start(bf16[2,4,16,8,128]{4,3,2,1,0:T(8,128)(2,1)S(1)} %get-tuple-element.21), channel_id=1, source_target_pairs={{0,1},{1,0},{8,9},{9,8},{16,17},{17,16},{24,25},{25,24},{2,3},{3,2... | collective-permute-start | bytes 786440 | tf_op jit(solution)/shard_map/ppermute | solution.py:374
  16.0 6.7 %collective-permute-start.3 = (bf16[4,18,8,128]{3,2,1,0:T(8,128)(2,1)S(1)}, bf16[4,18,8,128]{3,2,1,0:T(8,128)(2,1)S(1)}, u32[]{:S(2)}, u32[]{:S(2)}) collective-permute-start(bf16[4,18,8,128]{3,2,1,0:T(8,128)(2,1)S(1)} %pad_maximum_fusion.1), channel_id=1, source_target_pairs={{0,8},{1,9},{8,0},{9,1},{16,24},{17,25},{24,16},{25,17},{2,10},{3,... | collective-permute-start | bytes 442376 | tf_op jit(solution)/shard_map/ppermute | solution.py:374
  22.5 6.9 %collective-permute-start.7 = (bf16[4,4,16,8,128]{4,3,2,1,0:T(8,128)(2,1)S(1)}, bf16[4,4,16,8,128]{4,3,2,1,0:T(8,128)(2,1)S(1)}, u32[]{:S(2)}, u32[]{:S(2)}) collective-permute-start(bf16[4,4,16,8,128]{4,3,2,1,0:T(8,128)(2,1)S(1)} %pad_maximum_fusion), channel_id=1, source_target_pairs={{0,8},{1,9},{8,0},{9,1},{16,24},{17,25},{24,16},{25,17},{2,10},{3,... | collective-permute-start | bytes 1572872 | tf_op jit(solution)/shard_map/ppermute | solution.py:374
  22.7 11.3 %collective-permute-start.9 = (bf16[8,18,8,128]{3,2,1,0:T(8,128)(2,1)S(1)}, bf16[8,18,8,128]{3,2,1,0:T(8,128)(2,1)S(1)}, u32[]{:S(2)}, u32[]{:S(2)}) collective-permute-start(bf16[8,18,8,128]{3,2,1,0:T(8,128)(2,1)S(1)} %constant_dynamic-update-slice_fusion.query_ref), channel_id=1, source_target_pairs={{2,0},{4,2},{6,4},{3,1},{5,3},{7,5},{10,8},{12,10},{14,12},{11,9},... | collective-permute-start | bytes 884744 | tf_op jit(solution)/shard_map/ppermute | solution.py:415
  24.8 15.0 %collective-permute-start.8 = (bf16[8,18,8,128]{3,2,1,0:T(8,128)(2,1)S(1)}, bf16[8,18,8,128]{3,2,1,0:T(8,128)(2,1)S(1)}, u32[]{:S(2)}, u32[]{:S(2)}) collective-permute-start(bf16[8,18,8,128]{3,2,1,0:T(8,128)(2,1)S(1)} %constant_dynamic-update-slice_fusion.query_ref), channel_id=1, source_target_pairs={{0,2},{2,4},{4,6},{1,3},{3,5},{5,7},{8,10},{10,12},{12,14},{9,11},... | collective-permute-start | bytes 884744 | tf_op jit(solution)/shard_map/ppermute | solution.py:414
  36.4 10.0 %collective-permute-start.10 = (bf16[9,16,8,128]{3,2,1,0:T(8,128)(2,1)S(1)}, bf16[9,16,8,128]{3,2,1,0:T(8,128)(2,1)S(1)}, u32[]{:S(2)}, u32[]{:S(2)}) collective-permute-start(bf16[9,16,8,128]{3,2,1,0:T(8,128)(2,1)S(1)} %shard_map.75), channel_id=1, source_target_pairs={{0,2},{2,4},{4,6},{1,3},{3,5},{5,7},{8,10},{10,12},{12,14},{9,11},... | collective-permute-start | bytes 884744 | tf_op jit(solution)/shard_map/ppermute | solution.py:436
  42.2 10.2 %collective-permute-start.11 = (bf16[9,16,8,128]{3,2,1,0:T(8,128)(2,1)S(1)}, bf16[9,16,8,128]{3,2,1,0:T(8,128)(2,1)S(1)}, u32[]{:S(2)}, u32[]{:S(2)}) collective-permute-start(bf16[9,16,8,128]{3,2,1,0:T(8,128)(2,1)S(1)} %shard_map.76), channel_id=1, source_target_pairs={{2,0},{4,2},{6,4},{3,1},{5,3},{7,5},{10,8},{12,10},{14,12},{11,9},... | collective-permute-start | bytes 884744 | tf_op jit(solution)/shard_map/ppermute | solution.py:434
  53.5 1.4 %collective-permute-start.12 = (bf16[4,16,8,128]{3,2,1,0:T(8,128)(2,1)S(1)}, bf16[4,16,8,128]{3,2,1,0:T(8,128)(2,1)S(1)}, u32[]{:S(2)}, u32[]{:S(2)}) collective-permute-start(bf16[4,16,8,128]{3,2,1,0:T(8,128)(2,1)S(1)} %get-tuple-element.30), channel_id=1, source_target_pairs={{0,8},{1,9},{8,0},{9,1},{16,24},{17,25},{24,16},{25,17},{2,10},{3,... | collective-permute-start | bytes 393224 | tf_op jit(solution)/shard_map/ppermute | solution.py:374
  54.9 4.3 %collective-permute-start.13 = (bf16[2,16,8,128]{3,2,1,0:T(8,128)(2,1)S(1)}, bf16[2,16,8,128]{3,2,1,0:T(8,128)(2,1)S(1)}, u32[]{:S(2)}, u32[]{:S(2)}) collective-permute-start(bf16[2,16,8,128]{3,2,1,0:T(8,128)(2,1)S(1)} %pad_maximum_fusion.2), channel_id=1, source_target_pairs={{0,1},{1,0},{8,9},{9,8},{16,17},{17,16},{24,25},{25,24},{2,3},{3,2... | collective-permute-start | bytes 196616 | tf_op jit(solution)/shard_map/ppermute | solution.py:374
  56.0 4.3 %collective-permute-start.14 = (bf16[2,16,8,128]{3,2,1,0:T(8,128)(2,1)S(1)}, bf16[2,16,8,128]{3,2,1,0:T(8,128)(2,1)S(1)}, u32[]{:S(2)}, u32[]{:S(2)}) collective-permute-start(bf16[2,16,8,128]{3,2,1,0:T(8,128)(2,1)S(1)} %pad_maximum_fusion.3), channel_id=1, source_target_pairs={{0,16},{1,17},{8,24},{9,25},{16,0},{17,1},{24,8},{25,9},{2,18},{3,... | collective-permute-start | bytes 196616 | tf_op jit(solution)/shard_map/ppermute | solution.py:374
  57.2 5.2 %collective-permute-start.15 = (bf16[2,16,8,128]{3,2,1,0:T(8,128)(2,1)S(1)}, bf16[2,16,8,128]{3,2,1,0:T(8,128)(2,1)S(1)}, u32[]{:S(2)}, u32[]{:S(2)}) collective-permute-start(bf16[2,16,8,128]{3,2,1,0:T(8,128)(2,1)S(1)} %pad_maximum_fusion.4), channel_id=1, source_target_pairs={{0,17},{1,16},{8,25},{9,24},{16,1},{17,0},{24,9},{25,8},{2,19},{3,... | collective-permute-start | bytes 196616 | tf_op jit(solution)/shard_map/ppermute | solution.py:374

commit v8 on v7

--- a/solution.py
+++ b/solution.py
@@ -168,33 +168,30 @@
         self.upper_one = self.upper.astype(jnp.float32).astype(jnp.bfloat16)
 
     def slot(self, row, col):
-        return self.info[2 + row * self.grid_cols + col % self.grid_cols]
+        return self.info[3 + row * self.grid_cols + col]
 
     def tile(self, member, row, col):
         return self.pairs[self.slot(row, col), member].reshape(self.size, HD)
 
-    def scores(self, row, col):
+    def scores(self, row, col, cols):
         query = self.query[self.slot(row, col), pl.ds(0, self.tile_rows)].reshape(self.size, HD)
         frames = range(self.pairs.shape[1] // 2)
-        cols = [c for c in range(self.grid_cols) if abs(c - col) <= 2]
         up, down = row > 0, row + 1 < self.grid_rows
         rows = [r for r in (row - 1, row, row + 1) if 0 <= r < self.grid_rows]
-        needed = [(f, r, c) for f in frames for c in cols for r in rows]
-        keys = jnp.concatenate([self.tile(2 * f, r, c) for f, r, c in needed], axis=0)
+        needed = [(f, r, i) for f in frames for i in range(len(cols)) for r in rows]
+        keys = jnp.concatenate([self.tile(2 * f, r, cols[i][0]) for f, r, i in needed], axis=0)
         raw = lax.dot_general(query, keys, (((1,), (1,)), ((), ())), preferred_element_type=jnp.float32)
         scores = {key: raw[:, i * self.size : (i + 1) * self.size] for i, key in enumerate(needed)}
         blocks = []
         for f in frames:
-            for c in cols:
-                found = [(False, scores[f, row, c])]
+            for i, (c, allowed) in enumerate(cols):
+                found = [(False, scores[f, row, i])]
                 if up or down:
-                    above = scores[f, row - 1, c] if up else NEG
-                    found.append((True, jnp.where(self.upper, above, scores[f, row + 1, c] if down else NEG)))
+                    above = scores[f, row - 1, i] if up else NEG
+                    found.append((True, jnp.where(self.upper, above, scores[f, row + 1, i] if down else NEG)))
                 for off_row, block in found:
-                    if c - col == 2:
-                        block = jnp.where(self.left, NEG, block)
-                    elif c - col == -2:
-                        block = jnp.where(self.left, block, NEG)
+                    if allowed is not None:
+                        block = jnp.where(allowed, block, NEG)
                     blocks.append((f, off_row, c, block))
         top = blocks[0][3]
         for entry in blocks[1:]:
@@ -218,16 +215,15 @@
         total = jnp.dot(weights, values, preferred_element_type=jnp.float32)
         return total[:, :HD] / total[:, HD:], top * self.scale + jnp.log2(total[:, HD:])
 
-    def attend_all(self, first_col):
-        places = [(row, col) for row in range(self.grid_rows) for col in range(self.grid_cols)]
+    def attend(self, tiles):
         held = None
-        for place in [*places, None]:
-            ready = self.scores(place[0], first_col + place[1]) if place else None
+        for place in [*tiles, None]:
+            ready = self.scores(*place) if place else None
             if held:
-                yield (*held[0], *self.weigh(*held[1]))
+                yield (held[0][0] * self.grid_cols + held[0][1], *self.weigh(*held[1]))
             held = (place, ready)
 
-    def enhanced(self, row, col, weight_ref, bias_ref, before_ref, after_ref):
+    def enhanced(self, row, col, weight_ref, bias_ref, beyond):
         shape = (self.tile_cols, HD)
         sub = lax.broadcasted_iota(jnp.int32, shape, 0)
         taps = [[weight_ref[a, pl.ds(b, 1), :] for b in range(3)] for a in range(3)]
@@ -243,13 +239,15 @@
             def values(c):
                 return self.pairs[self.slot(tile_row, c), member, line].astype(jnp.float32)
 
-            def edge(ref, c):
-                packed = ref[self.slot(tile_row, c), self.tile_rows + line // self.tile_cols].astype(jnp.float32)
+            def edge(right, c):
+                place = self.slot(tile_row, c), self.tile_rows + line // self.tile_cols
+                first, second = (ref[place].astype(jnp.float32) for ref in beyond)
+                packed = jnp.where(self.info[2] == right, first, second)
                 return jnp.broadcast_to(packed[line % self.tile_cols : line % self.tile_cols + 1], shape)
 
             here = values(col)
-            before = pltpu.roll(values(col - 1), 1, 0) if col > 0 else edge(before_ref, self.grid_cols - 1)
-            after = pltpu.roll(values(col + 1), last, 0) if col + 1 < self.grid_cols else edge(after_ref, 0)
+            before = pltpu.roll(values(col - 1), 1, 0) if col > 0 else edge(0, self.grid_cols - 1)
+            after = pltpu.roll(values(col + 1), last, 0) if col + 1 < self.grid_cols else edge(1, 0)
             low = jnp.where(sub == 0, before, pltpu.roll(here, 1, 0))
             high = jnp.where(sub == last, after, pltpu.roll(here, last, 0))
             lines.append((low, here, high))
@@ -264,13 +262,18 @@
         return jnp.stack(sums, axis=0)
 
 
-def visit_kernel(grid, tile, first_col, info_ref, query_ref, pairs_ref, out_ref):
+def visit_kernel(grid, tile, first, info_ref, query_ref, pairs_ref, out_ref):
     window = Window(grid, tile, info_ref, query_ref, pairs_ref)
+    near = info_ref[2] if first else 1 - info_ref[2]
+    allowed = window.left.astype(jnp.int32) == near
+    tiles = []
+    for row in range(grid[0]):
+        tiles.append((row, 1 - near, [(near, None), (1 - near, allowed)]))
+        tiles.append((row, near, [(near, allowed)]))
     size, count = window.size, grid[0] * grid[1]
     lane = lax.broadcasted_iota(jnp.int32, (size, HD), 1)
     levels = jnp.zeros((size, HD), jnp.float32)
-    for row, col, part, level in window.attend_all(first_col):
-        index = row * grid[1] + col
+    for index, part, level in window.attend(tiles):
         out_ref[index] = part.reshape(tile + (HD,)).astype(jnp.bfloat16)
         levels = jnp.where(lane == index, level, levels)
     high = levels.astype(jnp.bfloat16).astype(jnp.float32)
@@ -280,19 +283,21 @@
 
 
 def own_kernel(
-    grid, tile, info_ref, weight_ref, bias_ref, query_ref, pairs_ref, before_ref, after_ref, part_ref, level_ref, conv_ref
+    grid, tile, info_ref, weight_ref, bias_ref, query_ref, pairs_ref, first_ref, second_ref, part_ref, level_ref, conv_ref
 ):
     window = Window(grid, tile, info_ref, query_ref, pairs_ref)
-    for row, col, part, level in window.attend_all(0):
-        index = row * grid[1] + col
+    cols = [(c, None) for c in range(grid[1])]
+    tiles = [(row, col, cols) for row in range(grid[0]) for col in range(grid[1])]
+    for index, part, level in window.attend(tiles):
         part_ref[index], level_ref[index] = part, level
-        conv = window.enhanced(row, col, weight_ref, bias_ref, before_ref, after_ref)
+        row, col = index // grid[1], index % grid[1]
+        conv = window.enhanced(row, col, weight_ref, bias_ref, (first_ref, second_ref))
         conv_ref[index] = conv.reshape(window.size, HD)
 
 
-def join_kernel(grid, tile, info_ref, part_ref, level_ref, conv_ref, left_ref, right_ref, out_ref):
+def join_kernel(grid, tile, info_ref, part_ref, level_ref, conv_ref, first_ref, second_ref, out_ref):
     size, count = tile[0] * tile[1], grid[0] * grid[1]
-    visits = (left_ref, right_ref)
+    visits = (first_ref, second_ref)
     packed = []
     for i, ref in enumerate(visits):
         pack = ref[count].reshape(size, HD).astype(jnp.float32)
@@ -307,44 +312,53 @@
         top = jnp.maximum(jnp.maximum(levels[0], levels[1]), levels[2])
         shares = [jnp.exp2(level - top) for level in levels]
         mixed = sum(share * part for share, part in zip(shares, parts)) / sum(shares)
-        out_ref[info_ref[2 + index]] = (mixed + conv_ref[index]).reshape(tile + (HD,)).astype(jnp.bfloat16)
+        out_ref[info_ref[3 + index]] = (mixed + conv_ref[index]).reshape(tile + (HD,)).astype(jnp.bfloat16)
 
 
 def lanes(head):
     return pl.ds(pl.multiple_of(head * HD, HD), HD)
 
 
-def pack_kernel(flips, side, me_ref, *refs):
-    count = len(flips)
-    sources = refs[: -2 * count - 2]
-    query_buffers, pair_buffers = refs[-2 * count - 2 : -count - 2], refs[-count - 2 : -2]
-    held_ref, sems = refs[-2], refs[-1]
-    tile_rows, tile_cols, _ = sources[0].shape
+def fetch(sources, held_ref, sems):
     copies = [pltpu.make_async_copy(x, held_ref.at[i], sems.at[i]) for i, x in enumerate(sources)]
     for copy in copies:
         copy.start()
-    heads = [[lanes(me_ref[0] ^ (flip ^ beside)) for beside in (0, side)] for flip in flips]
+    return copies
+
+
+def pack_kernel(flips, side, me_ref, *refs):
+    count = len(flips)
+    sources, buffers, held_ref, sems = refs[: -count - 2], refs[-count - 2 : -2], refs[-2], refs[-1]
+    for member, copy in enumerate(fetch(sources, held_ref, sems)):
+        copy.wait()
+        for buffer, flip in zip(buffers, flips):
+            for other in range(2):
+                head = lanes(me_ref[0] ^ (flip ^ (side if other else 0)))
+                buffer[other, member] = held_ref[member, :, :, head]
+
+
+def query_kernel(flips, side, me_ref, query_ref, values_ref, *refs):
+    buffers, held_ref, sems = refs[:-2], refs[-2], refs[-1]
+    tile_rows, tile_cols, _ = query_ref.shape
+    copies = fetch((query_ref, values_ref), held_ref, sems)
+    places = [
+        (buffer, other, lanes(me_ref[0] ^ (flip ^ (side if other else 0))))
+        for buffer, flip in zip(buffers, flips)
+        for other in range(2)
+    ]
     copies[0].wait()
-    for buffer, pair in zip(query_buffers, heads):
-        for other in range(2):
-            buffer[other, pl.ds(0, tile_rows)] = held_ref[0, :, :, pair[other]]
+    for buffer, other, head in places:
+        buffer[other, pl.ds(0, tile_rows)] = held_ref[0, :, :, head]
     copies[1].wait()
     sub = lax.broadcasted_iota(jnp.int32, (tile_cols, HD), 0)
-    for buffer, pair in zip(query_buffers, heads):
-        for other in range(2):
-            for start in range(0, tile_rows, tile_cols):
-                packed = jnp.zeros((tile_cols, HD), jnp.float32)
-                for line in range(tile_cols):
-                    values = held_ref[1, start + line, :, pair[other]].astype(jnp.float32)
-                    edge = jnp.where(me_ref[1] == 0, values[:1], values[tile_cols - 1 :])
-                    packed = jnp.where(sub == line, edge, packed)
-                buffer[other, tile_rows + start // tile_cols] = packed.astype(jnp.bfloat16)
-    for member, source in enumerate((*range(2, len(sources)), 1)):
-        if member < len(sources) - 2:
-            copies[source].wait()
-        for buffer, pair in zip(pair_buffers, heads):
-            for other in range(2):
-                buffer[other, member] = held_ref[source, :, :, pair[other]]
+    for buffer, other, head in places:
+        for start in range(0, tile_rows, tile_cols):
+            packed = jnp.zeros((tile_cols, HD), jnp.float32)
+            for line in range(tile_cols):
+                values = held_ref[1, start + line, :, head].astype(jnp.float32)
+                edge = jnp.where(me_ref[1] == 0, values[:1], values[tile_cols - 1 :])
+                packed = jnp.where(sub == line, edge, packed)
+            buffer[other, tile_rows + start // tile_cols] = packed.astype(jnp.bfloat16)
 
 
 def unpack_kernel(flips, side, me_ref, same_ref, beside_ref, *refs):
@@ -393,53 +407,62 @@
         beside = swap(forward, side)
         return jnp.concatenate([jnp.stack([b[0] for b in got]), beside], axis=0)
 
-    up = [(i, i + 1) for i in range(far - 1)]
-    down = [(i + 1, i) for i in range(far - 1)]
+    def rounds(start):
+        return [pair for i in range(start, far - 1, 2) for pair in ((i, i + 1), (i + 1, i))]
+
+    first, second = rounds(0), rounds(1)
     edges = -(-tile_rows // tile_cols)
-    sources = (queries, values_new, keys_cache[0], values_cache[0], keys_new)
-    query_buffer = jax.ShapeDtypeStruct((2, tile_rows + edges, tile_cols, HD), jnp.bfloat16)
-    pair_buffer = jax.ShapeDtypeStruct((2, len(sources) - 1) + block, jnp.bfloat16)
-    packed = call(
-        functools.partial(pack_kernel, flips, side),
-        [query_buffer] * len(flips) + [pair_buffer] * len(flips),
-        SMALL,
-        0,
-        me_ref,
-        *map(stay, sources),
-        space=(FAR, VMEM),
-        scratch=[pltpu.VMEM((len(sources),) + queries.shape, jnp.bfloat16), pltpu.SemaphoreType.DMA((len(sources),))],
-    )
-    query = gather(packed[: len(flips)])
-    pairs = gather(packed[len(flips) :])
-    query_left = lax.ppermute(query, "far", up)
-    query_right = lax.ppermute(query, "far", down)
+
+    def pack(kernel, buffer, *sources):
+        return call(
+            functools.partial(kernel, flips, side),
+            [jax.ShapeDtypeStruct(buffer, jnp.bfloat16)] * len(flips),
+            SMALL,
+            0,
+            me_ref,
+            *map(stay, sources),
+            space=(FAR, VMEM),
+            scratch=[
+                pltpu.VMEM((len(sources),) + queries.shape, jnp.bfloat16),
+                pltpu.SemaphoreType.DMA((len(sources),)),
+            ],
+        )
+
+    packed = pack(query_kernel, (2, tile_rows + edges, tile_cols, HD), queries, values_new)
+    query = gather(packed)
+    packed = pack(pack_kernel, (2, 4) + block, keys_cache[0], values_cache[0], keys_new, values_new)
+    pairs = gather(packed)
+    query_second = lax.ppermute(query, "far", second)
+    query_first = lax.ppermute(query, "far", first)
     far_index = lax.axis_index("far")
     flip = me ^ jnp.arange(heads, dtype=jnp.int32)
     beside = (flip // side) % 2
     order = flip % side + flip // (2 * side) * side
+    even = far_index % 2 == 0
+    below, above = far_index > 0, far_index < far - 1
     info = jnp.concatenate(
         [
-            jnp.stack([far_index > 0, far_index < far - 1]).astype(jnp.int32),
+            jnp.stack([~even | above, jnp.where(even, below, above), even]).astype(jnp.int32),
             beside * len(flips) + order,
         ]
     )
     weight = lax.dynamic_slice_in_dim(conv_weight, me * HD, HD, 2)
     bias = lax.dynamic_slice_in_dim(conv_bias.reshape(1, channels), me * HD, HD, 1)
 
-    def visit(queries, first_col):
-        kernel = functools.partial(visit_kernel, grid, tile, first_col)
+    def visit(queries, is_first):
+        kernel = functools.partial(visit_kernel, grid, tile, is_first)
         return call(kernel, jax.ShapeDtypeStruct((heads + 1,) + block, jnp.bfloat16), LIMIT, 4, info, queries, pairs)
 
-    left_part = visit(query_left, -group_cols)
-    from_right = lax.ppermute(left_part, "far", down)
-    right_part = visit(query_right, group_cols)
-    from_left = lax.ppermute(right_part, "far", up)
+    part = visit(query_second, False)
+    home_second = lax.ppermute(part, "far", second)
+    part = visit(query_first, True)
+    home_first = lax.ppermute(part, "far", first)
     part = jax.ShapeDtypeStruct((heads, size, HD), jnp.float32)
     kernel = functools.partial(own_kernel, grid, tile)
-    own = call(kernel, [part] * 3, LIMIT, 4, info, weight, bias, query, pairs, query_left, query_right)
+    own = call(kernel, [part] * 3, LIMIT, 4, info, weight, bias, query, pairs, query_first, query_second)
     kernel = functools.partial(join_kernel, grid, tile)
     result = jax.ShapeDtypeStruct((heads,) + block, jnp.bfloat16)
-    result = call(kernel, result, LIMIT, 1, info, *own, from_left, from_right)
+    result = call(kernel, result, LIMIT, 1, info, *own, home_first, home_second)
     same, other = result[: len(flips)], result[len(flips) :]
     received = swap(other, side)
     got = []

time: 64 us -> 59.9 us (0.936)
  the two profiles are of different devices: /device:TPU:0 before, /device:TPU:8 now
where the time goes in v8:
time: 59.9 us; the launch traced here: 59.7 us
  waiting for transfers between devices  24.2 us (40%)
  starting transfers between devices  20.4 us (34%)
  Pallas kernels  13.5 us (23%)
  local copies, waits for them, and re-layouts  1.04 us (2%)
    ppermute x12, waiting for transfers between devices, swap(): return lax.ppermute(x, axes, [(s, s ^ flip) for s in range(heads)])  16 us
    pallas_call x7, Pallas kernels, call(): pl.pallas_call(kernel, out_shape=out_shape, in_specs=[SMEM] + [space[0]]...  13.5 us
    ppermute x12, starting transfers between devices, swap(): return lax.ppermute(x, axes, [(s, s ^ flip) for s in range(heads)])  11.1 us
    ppermute x1, starting transfers between devices, head_step(): query_second = lax.ppermute(query, 'far', second)  4.6 us
    ppermute x1, waiting for transfers between devices, head_step(): home_second = lax.ppermute(part, 'far', second)  3.83 us
    ppermute x1, starting transfers between devices, head_step(): home_second = lax.ppermute(part, 'far', second)  3.67 us
    ppermute x1, waiting for transfers between devices, head_step(): query_first = lax.ppermute(query, 'far', first)  3.49 us
  transfers between devices with their start and end apart: 16, of which 9 were waited for; matrix products, arithmetic and copies ran while one was open for 2% of the time, Pallas kernels for 16%

profile of v8, /device:TPU:8, one launch (start us, length us, event | category | flops | bytes accessed | tf_op | source)
XLA Modules:
  0.0 59.7 jit_solution(16852467901186970442)
XLA Ops:
  0.0 0.1 pad_add_fusion.me_ref
  0.1 1.7 %shard_map.73 = (bf16[2,18,8,128]{3,2,1,0:T(8,128)(2,1)S(1)}, bf16[2,18,8,128]{3,2,1,0:T(8,128)(2,1)S(1)}, bf16[2,18,8,128]{3,2,1,0:T(8,128)(2,1)S(1)}, bf16[2,18,8,128]{3,2,1,0:T(8,128)(2,1)S(1)}) custom-call(s32[2]{0:T(128)S(1)} %pad_add_fusion.me_ref, bf16[16,8,1024]{2,1,0:T(8,128)(2,1)} %query_ref.1, bf16[16,8,1024]{2,1,0:T(8,128)(2,1)} %refs_3_.1), custom_call_target="tpu_custom_call" | custom-call | bytes 1048576 | tf_op jit(solution)/shard_map/pallas_call | solution.py:391
  1.8 2.5 %collective-permute-start.2 = (bf16[2,18,8,128]{3,2,1,0:T(8,128)(2,1)S(1)}, bf16[2,18,8,128]{3,2,1,0:T(8,128)(2,1)S(1)}, u32[]{:S(2)}, u32[]{:S(2)}) collective-permute-start(bf16[2,18,8,128]{3,2,1,0:T(8,128)(2,1)S(1)} %get-tuple-element.19), channel_id=1, source_target_pairs={{0,17},{1,16},{8,25},{9,24},{16,1},{17,0},{24,9},{25,8},{2,19},{3,... | collective-permute-start | bytes 221192 | tf_op jit(solution)/shard_map/ppermute | solution.py:388
  4.3 0.5 collective-permute-start.1
  4.8 0.5 collective-permute-start
  5.3 1.8 %shard_map.74 = (bf16[2,4,16,8,128]{4,3,2,1,0:T(8,128)(2,1)S(1)}, bf16[2,4,16,8,128]{4,3,2,1,0:T(8,128)(2,1)S(1)}, bf16[2,4,16,8,128]{4,3,2,1,0:T(8,128)(2,1)S(1)}, bf16[2,4,16,8,128]{4,3,2,1,0:T(8,128)(2,1)S(1)}) custom-call(s32[2]{0:T(128)S(1)} %pad_add_fusion.me_ref, bf16[16,8,1024]{2,1,0:T(8,128)(2,1)} %bitcast.9, bf16[16,8,1024]{2,1,0:T(8,128)(2,1)} %bitcast.10, ...), custom_call_target="tpu_custom_call" | custom-call | bytes 1048576 | tf_op jit(solution)/shard_map/pallas_call | solution.py:391
  7.2 2.5 %collective-permute-start.6 = (bf16[2,4,16,8,128]{4,3,2,1,0:T(8,128)(2,1)S(1)}, bf16[2,4,16,8,128]{4,3,2,1,0:T(8,128)(2,1)S(1)}, u32[]{:S(2)}, u32[]{:S(2)}) collective-permute-start(bf16[2,4,16,8,128]{4,3,2,1,0:T(8,128)(2,1)S(1)} %get-tuple-element.23), channel_id=1, source_target_pairs={{0,17},{1,16},{8,25},{9,24},{16,1},{17,0},{24,9},{25,8},{2,19},{3,... | collective-permute-start | bytes 786440 | tf_op jit(solution)/shard_map/ppermute | solution.py:388
  9.7 0.5 collective-permute-start.5
  10.3 0.6 collective-permute-start.4
  11.0 9.9 %collective-permute-done.4 = bf16[2,4,16,8,128]{4,3,2,1,0:T(8,128)(2,1)S(1)} collective-permute-done((bf16[2,4,16,8,128]{4,3,2,1,0:T(8,128)(2,1)S(1)}, bf16[2,4,16,8,128]{4,3,2,1,0:T(8,128)(2,1)S(1)}, u32[]{:S(2)}, u32[]{:S(2)}) %collective-permute-start.4) | collective-permute-done | bytes 262176 | tf_op jit(solution)/shard_map/ppermute | solution.py:388
  21.3 0.1 add_convert_fusion
  21.4 0.1 pad_add_fusion.1.info_ref
  21.5 0.5 collective-permute-start.8
  22.0 0.8 %dynamic-slice_bitcast_fusion.bias_ref = f32[1,128]{1,0:T(1,128)S(1)} fusion(f32[1024]{0:T(1024)} %param.13, s32[]{:T(128)S(6)} %select_n.39), kind=kLoop, calls=%fused_computation.33 | loop fusion | bytes 1028 | tf_op jit(solution)/shard_map/dynamic_slice | solution.py:450
  22.7 4.6 %collective-permute-start.9 = (bf16[8,18,8,128]{3,2,1,0:T(8,128)(2,1)S(1)}, bf16[8,18,8,128]{3,2,1,0:T(8,128)(2,1)S(1)}, u32[]{:S(2)}, u32[]{:S(2)}) collective-permute-start(bf16[8,18,8,128]{3,2,1,0:T(8,128)(2,1)S(1)} %constant_dynamic-update-slice_fusion.query_ref), channel_id=1, source_target_pairs={{2,4},{4,2},{3,5},{5,3},{10,12},{12,10},{11,13},{13,11},{18,20},{2... | collective-permute-start | bytes 884744 | tf_op jit(solution)/shard_map/ppermute | solution.py:435
  27.4 3.5 %collective-permute-done.8.first_ref.query_ref = bf16[8,18,8,128]{3,2,1,0:T(8,128)(2,1)S(1)} collective-permute-done((bf16[8,18,8,128]{3,2,1,0:T(8,128)(2,1)S(1)}, bf16[8,18,8,128]{3,2,1,0:T(8,128)(2,1)S(1)}, u32[]{:S(2)}, u32[]{:S(2)}) %collective-permute-start.8) | collective-permute-done | bytes 294944 | tf_op jit(solution)/shard_map/ppermute | solution.py:436
  30.9 2.3 %shard_map.76 = bf16[9,16,8,128]{3,2,1,0:T(8,128)(2,1)S(1)} custom-call(s32[11]{0:T(128)S(1)} %pad_add_fusion.1.info_ref, bf16[8,18,8,128]{3,2,1,0:T(8,128)(2,1)S(1)} %collective-permute-done.8.first_ref.query_ref, bf16[8,4,16,8,128]{4,3,2,1,0:T(8,128)(2,1)S(1)} %constant_dynamic-update-slice_fusion.1.pairs_ref), custom_call_target="tpu_custom_call" | custom-call | flops 4294967296 | bytes 1048576 | tf_op jit(solution)/shard_map/pallas_call | solution.py:391
  33.3 0.5 collective-permute-start.10
  33.8 0.9 %collective-permute-done.9.second_ref.query_ref = bf16[8,18,8,128]{3,2,1,0:T(8,128)(2,1)S(1)} collective-permute-done((bf16[8,18,8,128]{3,2,1,0:T(8,128)(2,1)S(1)}, bf16[8,18,8,128]{3,2,1,0:T(8,128)(2,1)S(1)}, u32[]{:S(2)}, u32[]{:S(2)}) %collective-permute-start.9) | collective-permute-done | bytes 294944 | tf_op jit(solution)/shard_map/ppermute | solution.py:435
  34.7 2.3 %shard_map.77 = bf16[9,16,8,128]{3,2,1,0:T(8,128)(2,1)S(1)} custom-call(s32[11]{0:T(128)S(1)} %pad_add_fusion.1.info_ref, bf16[8,18,8,128]{3,2,1,0:T(8,128)(2,1)S(1)} %collective-permute-done.9.second_ref.query_ref, bf16[8,4,16,8,128]{4,3,2,1,0:T(8,128)(2,1)S(1)} %constant_dynamic-update-slice_fusion.1.pairs_ref), custom_call_target="tpu_custom_call" | custom-call | flops 4294967296 | bytes 1048576 | tf_op jit(solution)/shard_map/pallas_call | solution.py:391
  37.1 3.7 %collective-permute-start.11 = (bf16[9,16,8,128]{3,2,1,0:T(8,128)(2,1)S(1)}, bf16[9,16,8,128]{3,2,1,0:T(8,128)(2,1)S(1)}, u32[]{:S(2)}, u32[]{:S(2)}) collective-permute-start(bf16[9,16,8,128]{3,2,1,0:T(8,128)(2,1)S(1)} %shard_map.77), channel_id=1, source_target_pairs={{2,4},{4,2},{3,5},{5,3},{10,12},{12,10},{11,13},{13,11},{18,20},{2... | collective-permute-start | bytes 884744 | tf_op jit(solution)/shard_map/ppermute | solution.py:457
  40.7 2.9 %shard_map.75 = (f32[8,128,128]{2,1,0:T(8,128)S(1)}, f32[8,128,128]{2,1,0:T(8,128)S(1)}, f32[8,128,128]{2,1,0:T(8,128)S(1)}) custom-call(s32[11]{0:T(128)S(1)} %pad_add_fusion.1.info_ref, f32[3,3,128]{2,1,0:T(4,128)S(1)} %constant_dynamic-slice_fusion.weight_ref, f32[1,128]{1,0:T(1,128)S(1)} %dynamic-slice_bitcast_fusion.bias_ref, ...), custom_call_target="tpu_custom_call" | custom-call | flops 4294967296 | bytes 1048576 | tf_op jit(solution)/shard_map/pallas_call | solution.py:391
  43.7 3.8 %collective-permute-done.11.second_ref = bf16[9,16,8,128]{3,2,1,0:T(8,128)(2,1)S(1)} collective-permute-done((bf16[9,16,8,128]{3,2,1,0:T(8,128)(2,1)S(1)}, bf16[9,16,8,128]{3,2,1,0:T(8,128)(2,1)S(1)}, u32[]{:S(2)}, u32[]{:S(2)}) %collective-permute-start.11) | collective-permute-done | bytes 294944 | tf_op jit(solution)/shard_map/ppermute | solution.py:457
  47.5 1.1 %shard_map.78 = bf16[8,16,8,128]{3,2,1,0:T(8,128)(2,1)S(1)} custom-call(s32[11]{0:T(128)S(1)} %pad_add_fusion.1.info_ref, f32[8,128,128]{2,1,0:T(8,128)S(1)} %get-tuple-element.24.part_ref, f32[8,128,128]{2,1,0:T(8,128)S(1)} %get-tuple-element.25.level_ref, f32[8,128,128]{2,1,0:T(8,128)S(1)} %get-tuple-element.26.conv_ref, ...), custom_call_target="tpu_custom_call" | custom-call | flops 1073741824 | bytes 1048576 | tf_op jit(solution)/shard_map/pallas_call | solution.py:391
  48.7 1.3 %collective-permute-done.12.beside_ref = bf16[4,16,8,128]{3,2,1,0:T(8,128)(2,1)S(1)} collective-permute-done((bf16[4,16,8,128]{3,2,1,0:T(8,128)(2,1)S(1)}, bf16[4,16,8,128]{3,2,1,0:T(8,128)(2,1)S(1)}, u32[]{:S(2)}, u32[]{:S(2)}) %collective-permute-start.12) | collective-permute-done | bytes 131104 | tf_op jit(solution)/shard_map/ppermute | solution.py:388
  50.1 1.5 %collective-permute-start.13 = (bf16[2,16,8,128]{3,2,1,0:T(8,128)(2,1)S(1)}, bf16[2,16,8,128]{3,2,1,0:T(8,128)(2,1)S(1)}, u32[]{:S(2)}, u32[]{:S(2)}) collective-permute-start(bf16[2,16,8,128]{3,2,1,0:T(8,128)(2,1)S(1)} %pad_maximum_fusion.2), channel_id=1, source_target_pairs={{0,1},{1,0},{8,9},{9,8},{16,17},{17,16},{24,25},{25,24},{2,3},{3,2... | collective-permute-start | bytes 196616 | tf_op jit(solution)/shard_map/ppermute | solution.py:388
  51.6 1.6 %collective-permute-start.14 = (bf16[2,16,8,128]{3,2,1,0:T(8,128)(2,1)S(1)}, bf16[2,16,8,128]{3,2,1,0:T(8,128)(2,1)S(1)}, u32[]{:S(2)}, u32[]{:S(2)}) collective-permute-start(bf16[2,16,8,128]{3,2,1,0:T(8,128)(2,1)S(1)} %pad_maximum_fusion.3), channel_id=1, source_target_pairs={{0,16},{1,17},{8,24},{9,25},{16,0},{17,1},{24,8},{25,9},{2,18},{3,... | collective-permute-start | bytes 196616 | tf_op jit(solution)/shard_map/ppermute | solution.py:388
  53.1 0.6 collective-permute-start.15
  53.7 0.6 %collective-permute-done.13.refs_0_ = bf16[2,16,8,128]{3,2,1,0:T(8,128)(2,1)S(1)} collective-permute-done((bf16[2,16,8,128]{3,2,1,0:T(8,128)(2,1)S(1)}, bf16[2,16,8,128]{3,2,1,0:T(8,128)(2,1)S(1)}, u32[]{:S(2)}, u32[]{:S(2)}) %collective-permute-start.13) | collective-permute-done | bytes 65568 | tf_op jit(solution)/shard_map/ppermute | solution.py:388
  54.4 2.0 %collective-permute-done.14.refs_1_ = bf16[2,16,8,128]{3,2,1,0:T(8,128)(2,1)S(1)} collective-permute-done((bf16[2,16,8,128]{3,2,1,0:T(8,128)(2,1)S(1)}, bf16[2,16,8,128]{3,2,1,0:T(8,128)(2,1)S(1)}, u32[]{:S(2)}, u32[]{:S(2)}) %collective-permute-start.14) | collective-permute-done | bytes 65568 | tf_op jit(solution)/shard_map/ppermute | solution.py:388
  56.4 1.9 %collective-permute-done.15.refs_2_ = bf16[2,16,8,128]{3,2,1,0:T(8,128)(2,1)S(1)} collective-permute-done((bf16[2,16,8,128]{3,2,1,0:T(8,128)(2,1)S(1)}, bf16[2,16,8,128]{3,2,1,0:T(8,128)(2,1)S(1)}, u32[]{:S(2)}, u32[]{:S(2)}) %collective-permute-start.15) | collective-permute-done | bytes 65568 | tf_op jit(solution)/shard_map/ppermute | solution.py:388
  58.4 1.3 %shard_map.79 = bf16[16,8,1024]{2,1,0:T(8,128)(2,1)} custom-call(s32[2]{0:T(128)S(1)} %pad_add_fusion.me_ref, bf16[4,16,8,128]{3,2,1,0:T(8,128)(2,1)S(1)} %get-tuple-element.31.same_ref, bf16[4,16,8,128]{3,2,1,0:T(8,128)(2,1)S(1)} %collective-permute-done.12.beside_ref, bf16[2,16,8,128]{3,2,1,0:T(8,128)(2,1)S(1)} %collective-permute-done.13.refs_0_, ...), custom_call_target="tpu_custom_call" | custom-call | bytes 1048576 | tf_op jit(solution)/shard_map/pallas_call | solution.py:391
  (33 shorter events, 0.7 us)
Async XLA Ops:
  0.0 22.7 %copy-start = (f32[3,3,1024]{2,1,0:T(4,128)S(1)}, f32[3,3,1024]{2,1,0:T(4,128)}, u32[]{:S(2)}) copy-start(f32[3,3,1024]{2,1,0:T(4,128)} %param.12) | copy-start | bytes 110596
  1.8 9.1 %collective-permute-start.2 = (bf16[2,18,8,128]{3,2,1,0:T(8,128)(2,1)S(1)}, bf16[2,18,8,128]{3,2,1,0:T(8,128)(2,1)S(1)}, u32[]{:S(2)}, u32[]{:S(2)}) collective-permute-start(bf16[2,18,8,128]{3,2,1,0:T(8,128)(2,1)S(1)} %get-tuple-element.19), channel_id=1, source_target_pairs={{0,17},{1,16},{8,25},{9,24},{16,1},{17,0},{24,9},{25,8},{2,19},{3,... | collective-permute-start | bytes 221192 | tf_op jit(solution)/shard_map/ppermute | solution.py:388
  4.3 6.6 %collective-permute-start.1 = (bf16[2,18,8,128]{3,2,1,0:T(8,128)(2,1)S(1)}, bf16[2,18,8,128]{3,2,1,0:T(8,128)(2,1)S(1)}, u32[]{:S(2)}, u32[]{:S(2)}) collective-permute-start(bf16[2,18,8,128]{3,2,1,0:T(8,128)(2,1)S(1)} %get-tuple-element.18), channel_id=1, source_target_pairs={{0,16},{1,17},{8,24},{9,25},{16,0},{17,1},{24,8},{25,9},{2,18},{3,... | collective-permute-start | bytes 221192 | tf_op jit(solution)/shard_map/ppermute | solution.py:388
  4.8 5.4 %collective-permute-start = (bf16[2,18,8,128]{3,2,1,0:T(8,128)(2,1)S(1)}, bf16[2,18,8,128]{3,2,1,0:T(8,128)(2,1)S(1)}, u32[]{:S(2)}, u32[]{:S(2)}) collective-permute-start(bf16[2,18,8,128]{3,2,1,0:T(8,128)(2,1)S(1)} %get-tuple-element.17), channel_id=1, source_target_pairs={{0,1},{1,0},{8,9},{9,8},{16,17},{17,16},{24,25},{25,24},{2,3},{3,2... | collective-permute-start | bytes 221192 | tf_op jit(solution)/shard_map/ppermute | solution.py:388
  7.2 13.9 %collective-permute-start.6 = (bf16[2,4,16,8,128]{4,3,2,1,0:T(8,128)(2,1)S(1)}, bf16[2,4,16,8,128]{4,3,2,1,0:T(8,128)(2,1)S(1)}, u32[]{:S(2)}, u32[]{:S(2)}) collective-permute-start(bf16[2,4,16,8,128]{4,3,2,1,0:T(8,128)(2,1)S(1)} %get-tuple-element.23), channel_id=1, source_target_pairs={{0,17},{1,16},{8,25},{9,24},{16,1},{17,0},{24,9},{25,8},{2,19},{3,... | collective-permute-start | bytes 786440 | tf_op jit(solution)/shard_map/ppermute | solution.py:388
  9.7 11.4 %collective-permute-start.5 = (bf16[2,4,16,8,128]{4,3,2,1,0:T(8,128)(2,1)S(1)}, bf16[2,4,16,8,128]{4,3,2,1,0:T(8,128)(2,1)S(1)}, u32[]{:S(2)}, u32[]{:S(2)}) collective-permute-start(bf16[2,4,16,8,128]{4,3,2,1,0:T(8,128)(2,1)S(1)} %get-tuple-element.22), channel_id=1, source_target_pairs={{0,16},{1,17},{8,24},{9,25},{16,0},{17,1},{24,8},{25,9},{2,18},{3,... | collective-permute-start | bytes 786440 | tf_op jit(solution)/shard_map/ppermute | solution.py:388
  10.3 10.7 %collective-permute-start.4 = (bf16[2,4,16,8,128]{4,3,2,1,0:T(8,128)(2,1)S(1)}, bf16[2,4,16,8,128]{4,3,2,1,0:T(8,128)(2,1)S(1)}, u32[]{:S(2)}, u32[]{:S(2)}) collective-permute-start(bf16[2,4,16,8,128]{4,3,2,1,0:T(8,128)(2,1)S(1)} %get-tuple-element.21), channel_id=1, source_target_pairs={{0,1},{1,0},{8,9},{9,8},{16,17},{17,16},{24,25},{25,24},{2,3},{3,2... | collective-permute-start | bytes 786440 | tf_op jit(solution)/shard_map/ppermute | solution.py:388
  10.9 10.5 %collective-permute-start.3 = (bf16[4,18,8,128]{3,2,1,0:T(8,128)(2,1)S(1)}, bf16[4,18,8,128]{3,2,1,0:T(8,128)(2,1)S(1)}, u32[]{:S(2)}, u32[]{:S(2)}) collective-permute-start(bf16[4,18,8,128]{3,2,1,0:T(8,128)(2,1)S(1)} %pad_maximum_fusion.1), channel_id=1, source_target_pairs={{0,8},{1,9},{8,0},{9,1},{16,24},{17,25},{24,16},{25,17},{2,10},{3,... | collective-permute-start | bytes 442376 | tf_op jit(solution)/shard_map/ppermute | solution.py:388
  21.2 6.2 %collective-permute-start.7 = (bf16[4,4,16,8,128]{4,3,2,1,0:T(8,128)(2,1)S(1)}, bf16[4,4,16,8,128]{4,3,2,1,0:T(8,128)(2,1)S(1)}, u32[]{:S(2)}, u32[]{:S(2)}) collective-permute-start(bf16[4,4,16,8,128]{4,3,2,1,0:T(8,128)(2,1)S(1)} %pad_maximum_fusion), channel_id=1, source_target_pairs={{0,8},{1,9},{8,0},{9,1},{16,24},{17,25},{24,16},{25,17},{2,10},{3,... | collective-permute-start | bytes 1572872 | tf_op jit(solution)/shard_map/ppermute | solution.py:388
  21.5 9.5 %collective-permute-start.8 = (bf16[8,18,8,128]{3,2,1,0:T(8,128)(2,1)S(1)}, bf16[8,18,8,128]{3,2,1,0:T(8,128)(2,1)S(1)}, u32[]{:S(2)}, u32[]{:S(2)}) collective-permute-start(bf16[8,18,8,128]{3,2,1,0:T(8,128)(2,1)S(1)} %constant_dynamic-update-slice_fusion.query_ref), channel_id=1, source_target_pairs={{0,2},{2,0},{4,6},{6,4},{1,3},{3,1},{5,7},{7,5},{8,10},{10,8},{12,... | collective-permute-start | bytes 884744 | tf_op jit(solution)/shard_map/ppermute | solution.py:436
  22.7 12.0 %collective-permute-start.9 = (bf16[8,18,8,128]{3,2,1,0:T(8,128)(2,1)S(1)}, bf16[8,18,8,128]{3,2,1,0:T(8,128)(2,1)S(1)}, u32[]{:S(2)}, u32[]{:S(2)}) collective-permute-start(bf16[8,18,8,128]{3,2,1,0:T(8,128)(2,1)S(1)} %constant_dynamic-update-slice_fusion.query_ref), channel_id=1, source_target_pairs={{2,4},{4,2},{3,5},{5,3},{10,12},{12,10},{11,13},{13,11},{18,20},{2... | collective-permute-start | bytes 884744 | tf_op jit(solution)/shard_map/ppermute | solution.py:435
  33.3 10.4 %collective-permute-start.10 = (bf16[9,16,8,128]{3,2,1,0:T(8,128)(2,1)S(1)}, bf16[9,16,8,128]{3,2,1,0:T(8,128)(2,1)S(1)}, u32[]{:S(2)}, u32[]{:S(2)}) collective-permute-start(bf16[9,16,8,128]{3,2,1,0:T(8,128)(2,1)S(1)} %shard_map.76), channel_id=1, source_target_pairs={{0,2},{2,0},{4,6},{6,4},{1,3},{3,1},{5,7},{7,5},{8,10},{10,8},{12,... | collective-permute-start | bytes 884744 | tf_op jit(solution)/shard_map/ppermute | solution.py:459
  37.1 10.4 %collective-permute-start.11 = (bf16[9,16,8,128]{3,2,1,0:T(8,128)(2,1)S(1)}, bf16[9,16,8,128]{3,2,1,0:T(8,128)(2,1)S(1)}, u32[]{:S(2)}, u32[]{:S(2)}) collective-permute-start(bf16[9,16,8,128]{3,2,1,0:T(8,128)(2,1)S(1)} %shard_map.77), channel_id=1, source_target_pairs={{2,4},{4,2},{3,5},{5,3},{10,12},{12,10},{11,13},{13,11},{18,20},{2... | collective-permute-start | bytes 884744 | tf_op jit(solution)/shard_map/ppermute | solution.py:457
  48.6 1.4 %collective-permute-start.12 = (bf16[4,16,8,128]{3,2,1,0:T(8,128)(2,1)S(1)}, bf16[4,16,8,128]{3,2,1,0:T(8,128)(2,1)S(1)}, u32[]{:S(2)}, u32[]{:S(2)}) collective-permute-start(bf16[4,16,8,128]{3,2,1,0:T(8,128)(2,1)S(1)} %get-tuple-element.30), channel_id=1, source_target_pairs={{0,8},{1,9},{8,0},{9,1},{16,24},{17,25},{24,16},{25,17},{2,10},{3,... | collective-permute-start | bytes 393224 | tf_op jit(solution)/shard_map/ppermute | solution.py:388
  50.1 4.3 %collective-permute-start.13 = (bf16[2,16,8,128]{3,2,1,0:T(8,128)(2,1)S(1)}, bf16[2,16,8,128]{3,2,1,0:T(8,128)(2,1)S(1)}, u32[]{:S(2)}, u32[]{:S(2)}) collective-permute-start(bf16[2,16,8,128]{3,2,1,0:T(8,128)(2,1)S(1)} %pad_maximum_fusion.2), channel_id=1, source_target_pairs={{0,1},{1,0},{8,9},{9,8},{16,17},{17,16},{24,25},{25,24},{2,3},{3,2... | collective-permute-start | bytes 196616 | tf_op jit(solution)/shard_map/ppermute | solution.py:388
  51.6 4.8 %collective-permute-start.14 = (bf16[2,16,8,128]{3,2,1,0:T(8,128)(2,1)S(1)}, bf16[2,16,8,128]{3,2,1,0:T(8,128)(2,1)S(1)}, u32[]{:S(2)}, u32[]{:S(2)}) collective-permute-start(bf16[2,16,8,128]{3,2,1,0:T(8,128)(2,1)S(1)} %pad_maximum_fusion.3), channel_id=1, source_target_pairs={{0,16},{1,17},{8,24},{9,25},{16,0},{17,1},{24,8},{25,9},{2,18},{3,... | collective-permute-start | bytes 196616 | tf_op jit(solution)/shard_map/ppermute | solution.py:388
  53.1 5.2 %collective-permute-start.15 = (bf16[2,16,8,128]{3,2,1,0:T(8,128)(2,1)S(1)}, bf16[2,16,8,128]{3,2,1,0:T(8,128)(2,1)S(1)}, u32[]{:S(2)}, u32[]{:S(2)}) collective-permute-start(bf16[2,16,8,128]{3,2,1,0:T(8,128)(2,1)S(1)} %pad_maximum_fusion.4), channel_id=1, source_target_pairs={{0,17},{1,16},{8,25},{9,24},{16,1},{17,0},{24,9},{25,8},{2,19},{3,... | collective-permute-start | bytes 196616 | tf_op jit(solution)/shard_map/ppermute | solution.py:388

commit v9 on v8

--- a/solution.py
+++ b/solution.py
@@ -320,17 +320,27 @@
 
 
 def fetch(sources, held_ref, sems):
-    copies = [pltpu.make_async_copy(x, held_ref.at[i], sems.at[i]) for i, x in enumerate(sources)]
+    groups = sems.shape[1]
+    rows = held_ref.shape[1] // groups
+    copies = []
+    for i, source in enumerate(sources):
+        parts = [pl.ds(j * rows, rows) for j in range(groups)]
+        copies.append([pltpu.make_async_copy(source.at[p], held_ref.at[i, p], sems.at[i, j]) for j, p in enumerate(parts)])
+        for copy in copies[-1]:
+            copy.start()
+    return copies
+
+
+def finish(copies):
     for copy in copies:
-        copy.start()
-    return copies
+        copy.wait()
 
 
 def pack_kernel(flips, side, me_ref, *refs):
     count = len(flips)
     sources, buffers, held_ref, sems = refs[: -count - 2], refs[-count - 2 : -2], refs[-2], refs[-1]
-    for member, copy in enumerate(fetch(sources, held_ref, sems)):
-        copy.wait()
+    for member, copies in enumerate(fetch(sources, held_ref, sems)):
+        finish(copies)
         for buffer, flip in zip(buffers, flips):
             for other in range(2):
                 head = lanes(me_ref[0] ^ (flip ^ (side if other else 0)))
@@ -346,10 +356,10 @@
         for buffer, flip in zip(buffers, flips)
         for other in range(2)
     ]
-    copies[0].wait()
+    finish(copies[0])
     for buffer, other, head in places:
         buffer[other, pl.ds(0, tile_rows)] = held_ref[0, :, :, head]
-    copies[1].wait()
+    finish(copies[1])
     sub = lax.broadcasted_iota(jnp.int32, (tile_cols, HD), 0)
     for buffer, other, head in places:
         for start in range(0, tile_rows, tile_cols):
@@ -361,13 +371,10 @@
             buffer[other, tile_rows + start // tile_cols] = packed.astype(jnp.bfloat16)
 
 
-def unpack_kernel(flips, side, me_ref, same_ref, beside_ref, *refs):
+def unpack_kernel(flips, me_ref, *refs):
     out_ref = refs[-1]
-    out_ref[:, :, lanes(me_ref[0])] = same_ref[0]
-    out_ref[:, :, lanes(me_ref[0] ^ side)] = beside_ref[0]
-    for i, flip in enumerate(flips[1:]):
-        out_ref[:, :, lanes(me_ref[0] ^ flip)] = refs[i][0]
-        out_ref[:, :, lanes(me_ref[0] ^ (flip ^ side))] = refs[i][1]
+    for flip, ref in zip(flips, refs):
+        out_ref[:, :, lanes(me_ref[0] ^ flip)] = ref[...]
 
 
 def head_step(shape, queries, keys_new, values_new, keys_cache, values_cache, conv_weight, conv_bias):
@@ -403,9 +410,9 @@
 
     def gather(buffers):
         got = [buffers[0]] + [swap(b, flip) for b, flip in zip(buffers[1:], flips[1:])]
-        forward = jnp.stack([b[1] for b in got])
-        beside = swap(forward, side)
-        return jnp.concatenate([jnp.stack([b[0] for b in got]), beside], axis=0)
+        forward = [b[1] for b in got]
+        beside = [swap(b, side) for b in forward]
+        return jnp.stack([b[0] for b in got] + beside)
 
     def rounds(start):
         return [pair for i in range(start, far - 1, 2) for pair in ((i, i + 1), (i + 1, i))]
@@ -424,7 +431,7 @@
             space=(FAR, VMEM),
             scratch=[
                 pltpu.VMEM((len(sources),) + queries.shape, jnp.bfloat16),
-                pltpu.SemaphoreType.DMA((len(sources),)),
+                pltpu.SemaphoreType.DMA((len(sources), 4)),
             ],
         )
 
@@ -463,20 +470,17 @@
     kernel = functools.partial(join_kernel, grid, tile)
     result = jax.ShapeDtypeStruct((heads,) + block, jnp.bfloat16)
     result = call(kernel, result, LIMIT, 1, info, *own, home_first, home_second)
-    same, other = result[: len(flips)], result[len(flips) :]
-    received = swap(other, side)
-    got = []
-    for i in range(1, len(flips)):
-        got.append(swap(jnp.stack([same[i], received[i]]), flips[i]))
+    places = [*flips, *(flip ^ side for flip in flips)]
+    got = {0: result[0]}
+    for flip in sorted(places[1:], key=lambda flip: (-flip.bit_count(), -flip)):
+        got[flip] = swap(result[places.index(flip)], flip)
     return call(
-        functools.partial(unpack_kernel, flips, side),
+        functools.partial(unpack_kernel, list(got)),
         jax.ShapeDtypeStruct(queries.shape, jnp.bfloat16),
         SMALL,
         0,
         me_ref,
-        same,
-        received,
-        *got,
+        *got.values(),
     )
 
 

time: 59.9 us -> 58.6 us (0.978)
  the two profiles are of different devices: /device:TPU:8 before, /device:TPU:10 now
where the time goes in v9:
time: 58.6 us; the launch traced here: 58.3 us
  starting transfers between devices  23.3 us (40%)
  waiting for transfers between devices  19.6 us (33%)
  Pallas kernels  13.7 us (23%)
  local copies, waits for them, and re-layouts  1.06 us (2%)
    ppermute x21, starting transfers between devices, swap(): return lax.ppermute(x, axes, [(s, s ^ flip) for s in range(heads)])  15.8 us
    pallas_call x7, Pallas kernels, call(): pl.pallas_call(kernel, out_shape=out_shape, in_specs=[SMEM] + [space[0]]...  13.7 us
    ppermute x21, waiting for transfers between devices, swap(): return lax.ppermute(x, axes, [(s, s ^ flip) for s in range(heads)])  13.4 us
    ppermute x1, waiting for transfers between devices, head_step(): home_second = lax.ppermute(part, 'far', second)  3.53 us
    ppermute x1, starting transfers between devices, head_step(): home_second = lax.ppermute(part, 'far', second)  3.49 us
    ppermute x1, starting transfers between devices, head_step(): query_second = lax.ppermute(query, 'far', second)  3.47 us
    ppermute x1, waiting for transfers between devices, head_step(): query_second = lax.ppermute(query, 'far', second)  2.7 us
  transfers between devices with their start and end apart: 25, of which 12 were waited for; matrix products, arithmetic and copies ran while one was open for 2% of the time, Pallas kernels for 16%

profile of v9, /device:TPU:10, one launch (start us, length us, event | category | flops | bytes accessed | tf_op | source)
XLA Modules:
  0.0 58.3 jit_solution(14401042124872365708)
XLA Ops:
  0.1 1.8 %shard_map.73 = (bf16[2,18,8,128]{3,2,1,0:T(8,128)(2,1)S(1)}, bf16[2,18,8,128]{3,2,1,0:T(8,128)(2,1)S(1)}, bf16[2,18,8,128]{3,2,1,0:T(8,128)(2,1)S(1)}, bf16[2,18,8,128]{3,2,1,0:T(8,128)(2,1)S(1)}) custom-call(s32[2]{0:T(128)S(1)} %pad_add_fusion.me_ref, bf16[16,8,1024]{2,1,0:T(8,128)(2,1)} %query_ref.1, bf16[16,8,1024]{2,1,0:T(8,128)(2,1)} %refs_3_.1), custom_call_target="tpu_custom_call" | custom-call | bytes 1048576 | tf_op jit(solution)/shard_map/pallas_call | solution.py:398
  1.8 1.6 %collective-permute-start.2 = (bf16[2,18,8,128]{3,2,1,0:T(8,128)(2,1)S(1)}, bf16[2,18,8,128]{3,2,1,0:T(8,128)(2,1)S(1)}, u32[]{:S(2)}, u32[]{:S(2)}) collective-permute-start(bf16[2,18,8,128]{3,2,1,0:T(8,128)(2,1)S(1)} %get-tuple-element.19), channel_id=1, source_target_pairs={{0,17},{1,16},{8,25},{9,24},{16,1},{17,0},{24,9},{25,8},{2,19},{3,... | collective-permute-start | bytes 221192 | tf_op jit(solution)/shard_map/ppermute | solution.py:395
  3.4 1.5 %collective-permute-start.1 = (bf16[2,18,8,128]{3,2,1,0:T(8,128)(2,1)S(1)}, bf16[2,18,8,128]{3,2,1,0:T(8,128)(2,1)S(1)}, u32[]{:S(2)}, u32[]{:S(2)}) collective-permute-start(bf16[2,18,8,128]{3,2,1,0:T(8,128)(2,1)S(1)} %get-tuple-element.18), channel_id=1, source_target_pairs={{0,16},{1,17},{8,24},{9,25},{16,0},{17,1},{24,8},{25,9},{2,18},{3,... | collective-permute-start | bytes 221192 | tf_op jit(solution)/shard_map/ppermute | solution.py:395
  4.9 0.5 collective-permute-start
  5.4 2.0 %shard_map.74 = (bf16[2,4,16,8,128]{4,3,2,1,0:T(8,128)(2,1)S(1)}, bf16[2,4,16,8,128]{4,3,2,1,0:T(8,128)(2,1)S(1)}, bf16[2,4,16,8,128]{4,3,2,1,0:T(8,128)(2,1)S(1)}, bf16[2,4,16,8,128]{4,3,2,1,0:T(8,128)(2,1)S(1)}) custom-call(s32[2]{0:T(128)S(1)} %pad_add_fusion.me_ref, bf16[16,8,1024]{2,1,0:T(8,128)(2,1)} %bitcast.57, bf16[16,8,1024]{2,1,0:T(8,128)(2,1)} %bitcast.58, ...), custom_call_target="tpu_custom_call" | custom-call | bytes 1048576 | tf_op jit(solution)/shard_map/pallas_call | solution.py:398
  7.4 1.6 %collective-permute-start.9 = (bf16[2,4,16,8,128]{4,3,2,1,0:T(8,128)(2,1)S(1)}, bf16[2,4,16,8,128]{4,3,2,1,0:T(8,128)(2,1)S(1)}, u32[]{:S(2)}, u32[]{:S(2)}) collective-permute-start(bf16[2,4,16,8,128]{4,3,2,1,0:T(8,128)(2,1)S(1)} %get-tuple-element.23), channel_id=1, source_target_pairs={{0,17},{1,16},{8,25},{9,24},{16,1},{17,0},{24,9},{25,8},{2,19},{3,... | collective-permute-start | bytes 786440 | tf_op jit(solution)/shard_map/ppermute | solution.py:395
  9.0 0.8 %dynamic-slice_bitcast_fusion.bias_ref = f32[1,128]{1,0:T(1,128)S(1)} fusion(f32[1024]{0:T(1024)} %param.13, s32[]{:T(128)S(6)} %select_n.39), kind=kLoop, calls=%fused_computation.50 | loop fusion | bytes 1028 | tf_op jit(solution)/shard_map/dynamic_slice | solution.py:457
  10.0 1.5 %collective-permute-start.8 = (bf16[2,4,16,8,128]{4,3,2,1,0:T(8,128)(2,1)S(1)}, bf16[2,4,16,8,128]{4,3,2,1,0:T(8,128)(2,1)S(1)}, u32[]{:S(2)}, u32[]{:S(2)}) collective-permute-start(bf16[2,4,16,8,128]{4,3,2,1,0:T(8,128)(2,1)S(1)} %get-tuple-element.22), channel_id=1, source_target_pairs={{0,16},{1,17},{8,24},{9,25},{16,0},{17,1},{24,8},{25,9},{2,18},{3,... | collective-permute-start | bytes 786440 | tf_op jit(solution)/shard_map/ppermute | solution.py:395
  11.5 0.6 collective-permute-start.7
  12.2 0.6 collective-permute-start.4
  12.8 0.9 %collective-permute-done.4 = bf16[18,8,128]{2,1,0:T(8,128)(2,1)S(1)} collective-permute-done((bf16[18,8,128]{2,1,0:T(8,128)(2,1)S(1)}, bf16[18,8,128]{2,1,0:T(8,128)(2,1)S(1)}, u32[]{:S(2)}, u32[]{:S(2)}) %collective-permute-start.4) | collective-permute-done | bytes 36896 | tf_op jit(solution)/shard_map/ppermute | solution.py:395
  14.0 0.9 %collective-permute-done.5 = bf16[18,8,128]{2,1,0:T(8,128)(2,1)S(1)} collective-permute-done((bf16[18,8,128]{2,1,0:T(8,128)(2,1)S(1)}, bf16[18,8,128]{2,1,0:T(8,128)(2,1)S(1)}, u32[]{:S(2)}, u32[]{:S(2)}) %collective-permute-start.5) | collective-permute-done | bytes 36896 | tf_op jit(solution)/shard_map/ppermute | solution.py:395
  15.2 0.9 %collective-permute-done.6 = bf16[18,8,128]{2,1,0:T(8,128)(2,1)S(1)} collective-permute-done((bf16[18,8,128]{2,1,0:T(8,128)(2,1)S(1)}, bf16[18,8,128]{2,1,0:T(8,128)(2,1)S(1)}, u32[]{:S(2)}, u32[]{:S(2)}) %collective-permute-start.6) | collective-permute-done | bytes 36896 | tf_op jit(solution)/shard_map/ppermute | solution.py:395
  16.1 0.5 collective-permute-start.14
  16.6 6.1 %collective-permute-done.7 = bf16[2,4,16,8,128]{4,3,2,1,0:T(8,128)(2,1)S(1)} collective-permute-done((bf16[2,4,16,8,128]{4,3,2,1,0:T(8,128)(2,1)S(1)}, bf16[2,4,16,8,128]{4,3,2,1,0:T(8,128)(2,1)S(1)}, u32[]{:S(2)}, u32[]{:S(2)}) %collective-permute-start.7) | collective-permute-done | bytes 262176 | tf_op jit(solution)/shard_map/ppermute | solution.py:395
  22.7 3.5 %collective-permute-start.15 = (bf16[8,18,8,128]{3,2,1,0:T(8,128)(2,1)S(1)}, bf16[8,18,8,128]{3,2,1,0:T(8,128)(2,1)S(1)}, u32[]{:S(2)}, u32[]{:S(2)}) collective-permute-start(bf16[8,18,8,128]{3,2,1,0:T(8,128)(2,1)S(1)} %bitcast_dynamic-update-slice_fusion.4.query_ref), channel_id=1, source_target_pairs={{2,4},{4,2},{3,5},{5,3},{10,12},{12,10},{11,13},{13,11},{18,20},{2... | collective-permute-start | bytes 884744 | tf_op jit(solution)/shard_map/ppermute | solution.py:442
  26.4 0.6 collective-permute-start.12
  27.1 0.6 %collective-permute-done.11 = bf16[4,16,8,128]{3,2,1,0:T(8,128)(2,1)S(1)} collective-permute-done((bf16[4,16,8,128]{3,2,1,0:T(8,128)(2,1)S(1)}, bf16[4,16,8,128]{3,2,1,0:T(8,128)(2,1)S(1)}, u32[]{:S(2)}, u32[]{:S(2)}) %collective-permute-start.11) | collective-permute-done | bytes 131104 | tf_op jit(solution)/shard_map/ppermute | solution.py:395
  28.4 2.3 %shard_map.76 = bf16[9,16,8,128]{3,2,1,0:T(8,128)(2,1)S(1)} custom-call(s32[11]{0:T(128)S(1)} %pad_add_fusion.1.info_ref, bf16[8,18,8,128]{3,2,1,0:T(8,128)(2,1)S(1)} %collective-permute-done.14.first_ref.query_ref, bf16[8,4,16,8,128]{4,3,2,1,0:T(8,128)(2,1)S(1)} %bitcast_dynamic-update-slice_fusion.pairs_ref), custom_call_target="tpu_custom_call" | custom-call | flops 4294967296 | bytes 1048576 | tf_op jit(solution)/shard_map/pallas_call | solution.py:398
  30.8 2.7 %collective-permute-done.15.second_ref.query_ref = bf16[8,18,8,128]{3,2,1,0:T(8,128)(2,1)S(1)} collective-permute-done((bf16[8,18,8,128]{3,2,1,0:T(8,128)(2,1)S(1)}, bf16[8,18,8,128]{3,2,1,0:T(8,128)(2,1)S(1)}, u32[]{:S(2)}, u32[]{:S(2)}) %collective-permute-start.15) | collective-permute-done | bytes 294944 | tf_op jit(solution)/shard_map/ppermute | solution.py:442
  33.5 2.3 %shard_map.77 = bf16[9,16,8,128]{3,2,1,0:T(8,128)(2,1)S(1)} custom-call(s32[11]{0:T(128)S(1)} %pad_add_fusion.1.info_ref, bf16[8,18,8,128]{3,2,1,0:T(8,128)(2,1)S(1)} %collective-permute-done.15.second_ref.query_ref, bf16[8,4,16,8,128]{4,3,2,1,0:T(8,128)(2,1)S(1)} %bitcast_dynamic-update-slice_fusion.pairs_ref), custom_call_target="tpu_custom_call" | custom-call | flops 4294967296 | bytes 1048576 | tf_op jit(solution)/shard_map/pallas_call | solution.py:398
  35.9 3.5 %collective-permute-start.17 = (bf16[9,16,8,128]{3,2,1,0:T(8,128)(2,1)S(1)}, bf16[9,16,8,128]{3,2,1,0:T(8,128)(2,1)S(1)}, u32[]{:S(2)}, u32[]{:S(2)}) collective-permute-start(bf16[9,16,8,128]{3,2,1,0:T(8,128)(2,1)S(1)} %shard_map.77), channel_id=1, source_target_pairs={{2,4},{4,2},{3,5},{5,3},{10,12},{12,10},{11,13},{13,11},{18,20},{2... | collective-permute-start | bytes 884744 | tf_op jit(solution)/shard_map/ppermute | solution.py:464
  39.4 2.9 %shard_map.75 = (f32[8,128,128]{2,1,0:T(8,128)S(1)}, f32[8,128,128]{2,1,0:T(8,128)S(1)}, f32[8,128,128]{2,1,0:T(8,128)S(1)}) custom-call(s32[11]{0:T(128)S(1)} %pad_add_fusion.1.info_ref, f32[3,3,128]{2,1,0:T(4,128)S(1)} %constant_dynamic-slice_fusion.weight_ref, f32[1,128]{1,0:T(1,128)S(1)} %dynamic-slice_bitcast_fusion.bias_ref, ...), custom_call_target="tpu_custom_call" | custom-call | flops 4294967296 | bytes 1048576 | tf_op jit(solution)/shard_map/pallas_call | solution.py:398
  42.3 3.5 %collective-permute-done.17.second_ref = bf16[9,16,8,128]{3,2,1,0:T(8,128)(2,1)S(1)} collective-permute-done((bf16[9,16,8,128]{3,2,1,0:T(8,128)(2,1)S(1)}, bf16[9,16,8,128]{3,2,1,0:T(8,128)(2,1)S(1)}, u32[]{:S(2)}, u32[]{:S(2)}) %collective-permute-start.17) | collective-permute-done | bytes 294944 | tf_op jit(solution)/shard_map/ppermute | solution.py:464
  45.8 1.1 %shard_map.78 = bf16[8,16,8,128]{3,2,1,0:T(8,128)(2,1)S(1)} custom-call(s32[11]{0:T(128)S(1)} %pad_add_fusion.1.info_ref, f32[8,128,128]{2,1,0:T(8,128)S(1)} %get-tuple-element.24.part_ref, f32[8,128,128]{2,1,0:T(8,128)S(1)} %get-tuple-element.25.level_ref, f32[8,128,128]{2,1,0:T(8,128)S(1)} %get-tuple-element.26.conv_ref, ...), custom_call_target="tpu_custom_call" | custom-call | flops 1073741824 | bytes 1048576 | tf_op jit(solution)/shard_map/pallas_call | solution.py:398
  47.0 2.7 %collective-permute-start.19 = (bf16[16,8,128]{2,1,0:T(8,128)(2,1)S(1)}, bf16[16,8,128]{2,1,0:T(8,128)(2,1)S(1)}, u32[]{:S(2)}, u32[]{:S(2)}) collective-permute-start(bf16[16,8,128]{2,1,0:T(8,128)(2,1)S(1)} %get-tuple-element.32), channel_id=1, source_target_pairs={{0,24},{1,25},{8,16},{9,17},{16,8},{17,9},{24,0},{25,1},{2,26},{3,... | collective-permute-start | bytes 98312 | tf_op jit(solution)/shard_map/ppermute | solution.py:395
  50.2 0.7 %collective-permute-start.21 = (bf16[16,8,128]{2,1,0:T(8,128)(2,1)S(1)}, bf16[16,8,128]{2,1,0:T(8,128)(2,1)S(1)}, u32[]{:S(2)}, u32[]{:S(2)}) collective-permute-start(bf16[16,8,128]{2,1,0:T(8,128)(2,1)S(1)} %get-tuple-element.30), channel_id=1, source_target_pairs={{0,9},{1,8},{8,1},{9,0},{16,25},{17,24},{24,17},{25,16},{2,11},{3,... | collective-permute-start | bytes 98312 | tf_op jit(solution)/shard_map/ppermute | solution.py:395
  50.9 0.8 %collective-permute-start.22 = (bf16[16,8,128]{2,1,0:T(8,128)(2,1)S(1)}, bf16[16,8,128]{2,1,0:T(8,128)(2,1)S(1)}, u32[]{:S(2)}, u32[]{:S(2)}) collective-permute-start(bf16[16,8,128]{2,1,0:T(8,128)(2,1)S(1)} %get-tuple-element.29), channel_id=1, source_target_pairs={{0,16},{1,17},{8,24},{9,25},{16,0},{17,1},{24,8},{25,9},{2,18},{3,... | collective-permute-start | bytes 98312 | tf_op jit(solution)/shard_map/ppermute | solution.py:395
  51.7 1.4 %collective-permute-start.23 = (bf16[16,8,128]{2,1,0:T(8,128)(2,1)S(1)}, bf16[16,8,128]{2,1,0:T(8,128)(2,1)S(1)}, u32[]{:S(2)}, u32[]{:S(2)}) collective-permute-start(bf16[16,8,128]{2,1,0:T(8,128)(2,1)S(1)} %get-tuple-element.28), channel_id=1, source_target_pairs={{0,8},{1,9},{8,0},{9,1},{16,24},{17,25},{24,16},{25,17},{2,10},{3,... | collective-permute-start | bytes 98312 | tf_op jit(solution)/shard_map/ppermute | solution.py:395
  53.6 1.1 %collective-permute-done.20.refs_3_ = bf16[16,8,128]{2,1,0:T(8,128)(2,1)S(1)} collective-permute-done((bf16[16,8,128]{2,1,0:T(8,128)(2,1)S(1)}, bf16[16,8,128]{2,1,0:T(8,128)(2,1)S(1)}, u32[]{:S(2)}, u32[]{:S(2)}) %collective-permute-start.20) | collective-permute-done | bytes 32800 | tf_op jit(solution)/shard_map/ppermute | solution.py:395
  55.1 1.8 %collective-permute-done.24.refs_7_ = bf16[16,8,128]{2,1,0:T(8,128)(2,1)S(1)} collective-permute-done((bf16[16,8,128]{2,1,0:T(8,128)(2,1)S(1)}, bf16[16,8,128]{2,1,0:T(8,128)(2,1)S(1)}, u32[]{:S(2)}, u32[]{:S(2)}) %collective-permute-start.24) | collective-permute-done | bytes 32800 | tf_op jit(solution)/shard_map/ppermute | solution.py:395
  57.0 1.3 %shard_map.79 = bf16[16,8,1024]{2,1,0:T(8,128)(2,1)} custom-call(s32[2]{0:T(128)S(1)} %pad_add_fusion.me_ref, bf16[16,8,128]{2,1,0:T(8,128)(2,1)S(1)} %get-tuple-element.34.refs_0_, bf16[16,8,128]{2,1,0:T(8,128)(2,1)S(1)} %collective-permute-done.18.refs_1_, bf16[16,8,128]{2,1,0:T(8,128)(2,1)S(1)} %collective-permute-done.19.refs_2_, ...), custom_call_target="tpu_custom_call" | custom-call | bytes 1048576 | tf_op jit(solution)/shard_map/pallas_call | solution.py:398
  (50 shorter events, 3.7 us)
Async XLA Ops:
  0.0 9.0 %copy-start = (f32[3,3,1024]{2,1,0:T(4,128)S(1)}, f32[3,3,1024]{2,1,0:T(4,128)}, u32[]{:S(2)}) copy-start(f32[3,3,1024]{2,1,0:T(4,128)} %param.12) | copy-start | bytes 110596
  1.8 10.2 %collective-permute-start.2 = (bf16[2,18,8,128]{3,2,1,0:T(8,128)(2,1)S(1)}, bf16[2,18,8,128]{3,2,1,0:T(8,128)(2,1)S(1)}, u32[]{:S(2)}, u32[]{:S(2)}) collective-permute-start(bf16[2,18,8,128]{3,2,1,0:T(8,128)(2,1)S(1)} %get-tuple-element.19), channel_id=1, source_target_pairs={{0,17},{1,16},{8,25},{9,24},{16,1},{17,0},{24,9},{25,8},{2,19},{3,... | collective-permute-start | bytes 221192 | tf_op jit(solution)/shard_map/ppermute | solution.py:395
  3.4 8.1 %collective-permute-start.1 = (bf16[2,18,8,128]{3,2,1,0:T(8,128)(2,1)S(1)}, bf16[2,18,8,128]{3,2,1,0:T(8,128)(2,1)S(1)}, u32[]{:S(2)}, u32[]{:S(2)}) collective-permute-start(bf16[2,18,8,128]{3,2,1,0:T(8,128)(2,1)S(1)} %get-tuple-element.18), channel_id=1, source_target_pairs={{0,16},{1,17},{8,24},{9,25},{16,0},{17,1},{24,8},{25,9},{2,18},{3,... | collective-permute-start | bytes 221192 | tf_op jit(solution)/shard_map/ppermute | solution.py:395
  4.9 5.1 %collective-permute-start = (bf16[2,18,8,128]{3,2,1,0:T(8,128)(2,1)S(1)}, bf16[2,18,8,128]{3,2,1,0:T(8,128)(2,1)S(1)}, u32[]{:S(2)}, u32[]{:S(2)}) collective-permute-start(bf16[2,18,8,128]{3,2,1,0:T(8,128)(2,1)S(1)} %get-tuple-element.17), channel_id=1, source_target_pairs={{0,1},{1,0},{8,9},{9,8},{16,17},{17,16},{24,25},{25,24},{2,3},{3,2... | collective-permute-start | bytes 221192 | tf_op jit(solution)/shard_map/ppermute | solution.py:395
  5.4 6.8 %collective-permute-start.3 = (bf16[18,8,128]{2,1,0:T(8,128)(2,1)S(1)}, bf16[18,8,128]{2,1,0:T(8,128)(2,1)S(1)}, u32[]{:S(2)}, u32[]{:S(2)}) collective-permute-start(bf16[18,8,128]{2,1,0:T(8,128)(2,1)S(1)} %get-tuple-element.49), channel_id=1, source_target_pairs={{0,8},{1,9},{8,0},{9,1},{16,24},{17,25},{24,16},{25,17},{2,10},{3,... | collective-permute-start | bytes 110600 | tf_op jit(solution)/shard_map/ppermute | solution.py:395
  7.4 18.9 %collective-permute-start.9 = (bf16[2,4,16,8,128]{4,3,2,1,0:T(8,128)(2,1)S(1)}, bf16[2,4,16,8,128]{4,3,2,1,0:T(8,128)(2,1)S(1)}, u32[]{:S(2)}, u32[]{:S(2)}) collective-permute-start(bf16[2,4,16,8,128]{4,3,2,1,0:T(8,128)(2,1)S(1)} %get-tuple-element.23), channel_id=1, source_target_pairs={{0,17},{1,16},{8,25},{9,24},{16,1},{17,0},{24,9},{25,8},{2,19},{3,... | collective-permute-start | bytes 786440 | tf_op jit(solution)/shard_map/ppermute | solution.py:395
  10.0 16.2 %collective-permute-start.8 = (bf16[2,4,16,8,128]{4,3,2,1,0:T(8,128)(2,1)S(1)}, bf16[2,4,16,8,128]{4,3,2,1,0:T(8,128)(2,1)S(1)}, u32[]{:S(2)}, u32[]{:S(2)}) collective-permute-start(bf16[2,4,16,8,128]{4,3,2,1,0:T(8,128)(2,1)S(1)} %get-tuple-element.22), channel_id=1, source_target_pairs={{0,16},{1,17},{8,24},{9,25},{16,0},{17,1},{24,8},{25,9},{2,18},{3,... | collective-permute-start | bytes 786440 | tf_op jit(solution)/shard_map/ppermute | solution.py:395
  11.5 11.2 %collective-permute-start.7 = (bf16[2,4,16,8,128]{4,3,2,1,0:T(8,128)(2,1)S(1)}, bf16[2,4,16,8,128]{4,3,2,1,0:T(8,128)(2,1)S(1)}, u32[]{:S(2)}, u32[]{:S(2)}) collective-permute-start(bf16[2,4,16,8,128]{4,3,2,1,0:T(8,128)(2,1)S(1)} %get-tuple-element.21), channel_id=1, source_target_pairs={{0,1},{1,0},{8,9},{9,8},{16,17},{17,16},{24,25},{25,24},{2,3},{3,2... | collective-permute-start | bytes 786440 | tf_op jit(solution)/shard_map/ppermute | solution.py:395
  12.1 14.8 %collective-permute-start.10 = (bf16[4,16,8,128]{3,2,1,0:T(8,128)(2,1)S(1)}, bf16[4,16,8,128]{3,2,1,0:T(8,128)(2,1)S(1)}, u32[]{:S(2)}, u32[]{:S(2)}) collective-permute-start(bf16[4,16,8,128]{3,2,1,0:T(8,128)(2,1)S(1)} %get-tuple-element.41), channel_id=1, source_target_pairs={{0,8},{1,9},{8,0},{9,1},{16,24},{17,25},{24,16},{25,17},{2,10},{3,... | collective-permute-start | bytes 393224 | tf_op jit(solution)/shard_map/ppermute | solution.py:395
  12.2 1.4 %collective-permute-start.4 = (bf16[18,8,128]{2,1,0:T(8,128)(2,1)S(1)}, bf16[18,8,128]{2,1,0:T(8,128)(2,1)S(1)}, u32[]{:S(2)}, u32[]{:S(2)}) collective-permute-start(bf16[18,8,128]{2,1,0:T(8,128)(2,1)S(1)} %get-tuple-element.47), channel_id=1, source_target_pairs={{0,8},{1,9},{8,0},{9,1},{16,24},{17,25},{24,16},{25,17},{2,10},{3,... | collective-permute-start | bytes 110600 | tf_op jit(solution)/shard_map/ppermute | solution.py:395
  13.6 1.2 %collective-permute-start.5 = (bf16[18,8,128]{2,1,0:T(8,128)(2,1)S(1)}, bf16[18,8,128]{2,1,0:T(8,128)(2,1)S(1)}, u32[]{:S(2)}, u32[]{:S(2)}) collective-permute-start(bf16[18,8,128]{2,1,0:T(8,128)(2,1)S(1)} %get-tuple-element.45), channel_id=1, source_target_pairs={{0,8},{1,9},{8,0},{9,1},{16,24},{17,25},{24,16},{25,17},{2,10},{3,... | collective-permute-start | bytes 110600 | tf_op jit(solution)/shard_map/ppermute | solution.py:395
  14.8 1.2 %collective-permute-start.6 = (bf16[18,8,128]{2,1,0:T(8,128)(2,1)S(1)}, bf16[18,8,128]{2,1,0:T(8,128)(2,1)S(1)}, u32[]{:S(2)}, u32[]{:S(2)}) collective-permute-start(bf16[18,8,128]{2,1,0:T(8,128)(2,1)S(1)} %get-tuple-element.43), channel_id=1, source_target_pairs={{0,8},{1,9},{8,0},{9,1},{16,24},{17,25},{24,16},{25,17},{2,10},{3,... | collective-permute-start | bytes 110600 | tf_op jit(solution)/shard_map/ppermute | solution.py:395
  16.1 12.3 %collective-permute-start.14 = (bf16[8,18,8,128]{3,2,1,0:T(8,128)(2,1)S(1)}, bf16[8,18,8,128]{3,2,1,0:T(8,128)(2,1)S(1)}, u32[]{:S(2)}, u32[]{:S(2)}) collective-permute-start(bf16[8,18,8,128]{3,2,1,0:T(8,128)(2,1)S(1)} %bitcast_dynamic-update-slice_fusion.4.query_ref), channel_id=1, source_target_pairs={{0,2},{2,0},{4,6},{6,4},{1,3},{3,1},{5,7},{7,5},{8,10},{10,8},{12,... | collective-permute-start | bytes 884744 | tf_op jit(solution)/shard_map/ppermute | solution.py:443
  22.7 10.8 %collective-permute-start.15 = (bf16[8,18,8,128]{3,2,1,0:T(8,128)(2,1)S(1)}, bf16[8,18,8,128]{3,2,1,0:T(8,128)(2,1)S(1)}, u32[]{:S(2)}, u32[]{:S(2)}) collective-permute-start(bf16[8,18,8,128]{3,2,1,0:T(8,128)(2,1)S(1)} %bitcast_dynamic-update-slice_fusion.4.query_ref), channel_id=1, source_target_pairs={{2,4},{4,2},{3,5},{5,3},{10,12},{12,10},{11,13},{13,11},{18,20},{2... | collective-permute-start | bytes 884744 | tf_op jit(solution)/shard_map/ppermute | solution.py:442
  26.2 1.4 %collective-permute-start.11 = (bf16[4,16,8,128]{3,2,1,0:T(8,128)(2,1)S(1)}, bf16[4,16,8,128]{3,2,1,0:T(8,128)(2,1)S(1)}, u32[]{:S(2)}, u32[]{:S(2)}) collective-permute-start(bf16[4,16,8,128]{3,2,1,0:T(8,128)(2,1)S(1)} %get-tuple-element.39), channel_id=1, source_target_pairs={{0,8},{1,9},{8,0},{9,1},{16,24},{17,25},{24,16},{25,17},{2,10},{3,... | collective-permute-start | bytes 393224 | tf_op jit(solution)/shard_map/ppermute | solution.py:395
  26.4 1.5 %collective-permute-start.12 = (bf16[4,16,8,128]{3,2,1,0:T(8,128)(2,1)S(1)}, bf16[4,16,8,128]{3,2,1,0:T(8,128)(2,1)S(1)}, u32[]{:S(2)}, u32[]{:S(2)}) collective-permute-start(bf16[4,16,8,128]{3,2,1,0:T(8,128)(2,1)S(1)} %get-tuple-element.37), channel_id=1, source_target_pairs={{0,8},{1,9},{8,0},{9,1},{16,24},{17,25},{24,16},{25,17},{2,10},{3,... | collective-permute-start | bytes 393224 | tf_op jit(solution)/shard_map/ppermute | solution.py:395
  27.0 1.4 %collective-permute-start.13 = (bf16[4,16,8,128]{3,2,1,0:T(8,128)(2,1)S(1)}, bf16[4,16,8,128]{3,2,1,0:T(8,128)(2,1)S(1)}, u32[]{:S(2)}, u32[]{:S(2)}) collective-permute-start(bf16[4,16,8,128]{3,2,1,0:T(8,128)(2,1)S(1)} %get-tuple-element.35), channel_id=1, source_target_pairs={{0,8},{1,9},{8,0},{9,1},{16,24},{17,25},{24,16},{25,17},{2,10},{3,... | collective-permute-start | bytes 393224 | tf_op jit(solution)/shard_map/ppermute | solution.py:395
  30.7 11.5 %collective-permute-start.16 = (bf16[9,16,8,128]{3,2,1,0:T(8,128)(2,1)S(1)}, bf16[9,16,8,128]{3,2,1,0:T(8,128)(2,1)S(1)}, u32[]{:S(2)}, u32[]{:S(2)}) collective-permute-start(bf16[9,16,8,128]{3,2,1,0:T(8,128)(2,1)S(1)} %shard_map.76), channel_id=1, source_target_pairs={{0,2},{2,0},{4,6},{6,4},{1,3},{3,1},{5,7},{7,5},{8,10},{10,8},{12,... | collective-permute-start | bytes 884744 | tf_op jit(solution)/shard_map/ppermute | solution.py:466
  35.9 10.0 %collective-permute-start.17 = (bf16[9,16,8,128]{3,2,1,0:T(8,128)(2,1)S(1)}, bf16[9,16,8,128]{3,2,1,0:T(8,128)(2,1)S(1)}, u32[]{:S(2)}, u32[]{:S(2)}) collective-permute-start(bf16[9,16,8,128]{3,2,1,0:T(8,128)(2,1)S(1)} %shard_map.77), channel_id=1, source_target_pairs={{2,4},{4,2},{3,5},{5,3},{10,12},{12,10},{11,13},{13,11},{18,20},{2... | collective-permute-start | bytes 884744 | tf_op jit(solution)/shard_map/ppermute | solution.py:464
  46.9 4.7 %collective-permute-start.18 = (bf16[16,8,128]{2,1,0:T(8,128)(2,1)S(1)}, bf16[16,8,128]{2,1,0:T(8,128)(2,1)S(1)}, u32[]{:S(2)}, u32[]{:S(2)}) collective-permute-start(bf16[16,8,128]{2,1,0:T(8,128)(2,1)S(1)} %get-tuple-element.33), channel_id=1, source_target_pairs={{0,25},{1,24},{8,17},{9,16},{16,9},{17,8},{24,1},{25,0},{2,27},{3,... | collective-permute-start | bytes 98312 | tf_op jit(solution)/shard_map/ppermute | solution.py:395
  47.0 6.0 %collective-permute-start.19 = (bf16[16,8,128]{2,1,0:T(8,128)(2,1)S(1)}, bf16[16,8,128]{2,1,0:T(8,128)(2,1)S(1)}, u32[]{:S(2)}, u32[]{:S(2)}) collective-permute-start(bf16[16,8,128]{2,1,0:T(8,128)(2,1)S(1)} %get-tuple-element.32), channel_id=1, source_target_pairs={{0,24},{1,25},{8,16},{9,17},{16,8},{17,9},{24,0},{25,1},{2,26},{3,... | collective-permute-start | bytes 98312 | tf_op jit(solution)/shard_map/ppermute | solution.py:395
  49.7 5.0 %collective-permute-start.20 = (bf16[16,8,128]{2,1,0:T(8,128)(2,1)S(1)}, bf16[16,8,128]{2,1,0:T(8,128)(2,1)S(1)}, u32[]{:S(2)}, u32[]{:S(2)}) collective-permute-start(bf16[16,8,128]{2,1,0:T(8,128)(2,1)S(1)} %get-tuple-element.31), channel_id=1, source_target_pairs={{0,17},{1,16},{8,25},{9,24},{16,1},{17,0},{24,9},{25,8},{2,19},{3,... | collective-permute-start | bytes 98312 | tf_op jit(solution)/shard_map/ppermute | solution.py:395
  50.2 4.5 %collective-permute-start.21 = (bf16[16,8,128]{2,1,0:T(8,128)(2,1)S(1)}, bf16[16,8,128]{2,1,0:T(8,128)(2,1)S(1)}, u32[]{:S(2)}, u32[]{:S(2)}) collective-permute-start(bf16[16,8,128]{2,1,0:T(8,128)(2,1)S(1)} %get-tuple-element.30), channel_id=1, source_target_pairs={{0,9},{1,8},{8,1},{9,0},{16,25},{17,24},{24,17},{25,16},{2,11},{3,... | collective-permute-start | bytes 98312 | tf_op jit(solution)/shard_map/ppermute | solution.py:395
  50.9 4.2 %collective-permute-start.22 = (bf16[16,8,128]{2,1,0:T(8,128)(2,1)S(1)}, bf16[16,8,128]{2,1,0:T(8,128)(2,1)S(1)}, u32[]{:S(2)}, u32[]{:S(2)}) collective-permute-start(bf16[16,8,128]{2,1,0:T(8,128)(2,1)S(1)} %get-tuple-element.29), channel_id=1, source_target_pairs={{0,16},{1,17},{8,24},{9,25},{16,0},{17,1},{24,8},{25,9},{2,18},{3,... | collective-permute-start | bytes 98312 | tf_op jit(solution)/shard_map/ppermute | solution.py:395
  51.7 3.4 %collective-permute-start.23 = (bf16[16,8,128]{2,1,0:T(8,128)(2,1)S(1)}, bf16[16,8,128]{2,1,0:T(8,128)(2,1)S(1)}, u32[]{:S(2)}, u32[]{:S(2)}) collective-permute-start(bf16[16,8,128]{2,1,0:T(8,128)(2,1)S(1)} %get-tuple-element.28), channel_id=1, source_target_pairs={{0,8},{1,9},{8,0},{9,1},{16,24},{17,25},{24,16},{25,17},{2,10},{3,... | collective-permute-start | bytes 98312 | tf_op jit(solution)/shard_map/ppermute | solution.py:395
  53.1 3.9 %collective-permute-start.24 = (bf16[16,8,128]{2,1,0:T(8,128)(2,1)S(1)}, bf16[16,8,128]{2,1,0:T(8,128)(2,1)S(1)}, u32[]{:S(2)}, u32[]{:S(2)}) collective-permute-start(bf16[16,8,128]{2,1,0:T(8,128)(2,1)S(1)} %get-tuple-element.27), channel_id=1, source_target_pairs={{0,1},{1,0},{8,9},{9,8},{16,17},{17,16},{24,25},{25,24},{2,3},{3,2... | collective-permute-start | bytes 98312 | tf_op jit(solution)/shard_map/ppermute | solution.py:395

commit v10 on v8

--- a/solution.py
+++ b/solution.py
@@ -148,18 +148,32 @@
 LOG2E = 1.4426950408889634
 NEG = -1e30
 VMEM = pl.BlockSpec(memory_space=pltpu.VMEM)
-SMEM = pl.BlockSpec(memory_space=pltpu.SMEM)
 FAR = pl.BlockSpec(memory_space=pltpu.HBM)
 LIMIT = pltpu.CompilerParams(vmem_limit_bytes=8 * 1024 * 1024)
 SMALL = pltpu.CompilerParams(vmem_limit_bytes=4 * 1024 * 1024)
 
 
+def position(group_cols):
+    return lax.axis_index("ht") * group_cols + lax.axis_index("near")
+
+
+def slot_of(group_cols, tile):
+    side = group_cols
+    flip = position(group_cols) ^ tile
+    order = lax.rem(flip, side) + flip // (2 * side) * side
+    return lax.rem(flip // side, 2) * (lax.axis_size("ht") * group_cols // 2) + order
+
+
+def first_is_right():
+    return 1 - lax.rem(lax.axis_index("far"), 2)
+
+
 class Window:
-    def __init__(self, grid, tile, info_ref, query_ref, pairs_ref):
+    def __init__(self, grid, tile, query_ref, pairs_ref):
         self.grid_rows, self.grid_cols = grid
         self.tile_rows, self.tile_cols = tile
         self.size = self.tile_rows * self.tile_cols
-        self.info, self.query, self.pairs = info_ref, query_ref, pairs_ref
+        self.query, self.pairs = query_ref, pairs_ref
         self.scale = HD ** (-0.5) * LOG2E
         query = lax.broadcasted_iota(jnp.int32, (self.size, self.size), 0)
         key = lax.broadcasted_iota(jnp.int32, (self.size, self.size), 1)
@@ -168,7 +182,7 @@
         self.upper_one = self.upper.astype(jnp.float32).astype(jnp.bfloat16)
 
     def slot(self, row, col):
-        return self.info[3 + row * self.grid_cols + col]
+        return slot_of(self.grid_cols, row * self.grid_cols + col)
 
     def tile(self, member, row, col):
         return self.pairs[self.slot(row, col), member].reshape(self.size, HD)
@@ -242,7 +256,7 @@
             def edge(right, c):
                 place = self.slot(tile_row, c), self.tile_rows + line // self.tile_cols
                 first, second = (ref[place].astype(jnp.float32) for ref in beyond)
-                packed = jnp.where(self.info[2] == right, first, second)
+                packed = jnp.where(first_is_right() == right, first, second)
                 return jnp.broadcast_to(packed[line % self.tile_cols : line % self.tile_cols + 1], shape)
 
             here = values(col)
@@ -262,9 +276,9 @@
         return jnp.stack(sums, axis=0)
 
 
-def visit_kernel(grid, tile, first, info_ref, query_ref, pairs_ref, out_ref):
-    window = Window(grid, tile, info_ref, query_ref, pairs_ref)
-    near = info_ref[2] if first else 1 - info_ref[2]
+def visit_kernel(grid, tile, first, query_ref, pairs_ref, out_ref):
+    window = Window(grid, tile, query_ref, pairs_ref)
+    near = first_is_right() if first else 1 - first_is_right()
     allowed = window.left.astype(jnp.int32) == near
     tiles = []
     for row in range(grid[0]):
@@ -283,9 +297,9 @@
 
 
 def own_kernel(
-    grid, tile, info_ref, weight_ref, bias_ref, query_ref, pairs_ref, first_ref, second_ref, part_ref, level_ref, conv_ref
+    grid, tile, weight_ref, bias_ref, query_ref, pairs_ref, first_ref, second_ref, part_ref, level_ref, conv_ref
 ):
-    window = Window(grid, tile, info_ref, query_ref, pairs_ref)
+    window = Window(grid, tile, query_ref, pairs_ref)
     cols = [(c, None) for c in range(grid[1])]
     tiles = [(row, col, cols) for row in range(grid[0]) for col in range(grid[1])]
     for index, part, level in window.attend(tiles):
@@ -295,14 +309,17 @@
         conv_ref[index] = conv.reshape(window.size, HD)
 
 
-def join_kernel(grid, tile, info_ref, part_ref, level_ref, conv_ref, first_ref, second_ref, out_ref):
+def join_kernel(grid, tile, far, part_ref, level_ref, conv_ref, first_ref, second_ref, out_ref):
     size, count = tile[0] * tile[1], grid[0] * grid[1]
     visits = (first_ref, second_ref)
+    place = lax.axis_index("far")
+    even = lax.rem(place, 2) == 0
+    present = [~even | (place < far - 1), jnp.where(even, place > 0, place < far - 1)]
     packed = []
-    for i, ref in enumerate(visits):
+    for there, ref in zip(present, visits):
         pack = ref[count].reshape(size, HD).astype(jnp.float32)
         level = pack + pltpu.roll(pack, HD - count, 1) + pltpu.roll(pack, HD - 2 * count, 1)
-        packed.append(jnp.where(info_ref[i] > 0, level, NEG))
+        packed.append(jnp.where(there, level, NEG))
     for index in range(count):
         levels = [level_ref[index]]
         parts = [part_ref[index]]
@@ -312,7 +329,7 @@
         top = jnp.maximum(jnp.maximum(levels[0], levels[1]), levels[2])
         shares = [jnp.exp2(level - top) for level in levels]
         mixed = sum(share * part for share, part in zip(shares, parts)) / sum(shares)
-        out_ref[info_ref[3 + index]] = (mixed + conv_ref[index]).reshape(tile + (HD,)).astype(jnp.bfloat16)
+        out_ref[slot_of(grid[1], index)] = (mixed + conv_ref[index]).reshape(tile + (HD,)).astype(jnp.bfloat16)
 
 
 def lanes(head):
@@ -326,23 +343,23 @@
     return copies
 
 
-def pack_kernel(flips, side, me_ref, *refs):
+def pack_kernel(flips, side, *refs):
     count = len(flips)
     sources, buffers, held_ref, sems = refs[: -count - 2], refs[-count - 2 : -2], refs[-2], refs[-1]
     for member, copy in enumerate(fetch(sources, held_ref, sems)):
         copy.wait()
         for buffer, flip in zip(buffers, flips):
             for other in range(2):
-                head = lanes(me_ref[0] ^ (flip ^ (side if other else 0)))
+                head = lanes(position(side) ^ (flip ^ (side if other else 0)))
                 buffer[other, member] = held_ref[member, :, :, head]
 
 
-def query_kernel(flips, side, me_ref, query_ref, values_ref, *refs):
+def query_kernel(flips, side, query_ref, values_ref, *refs):
     buffers, held_ref, sems = refs[:-2], refs[-2], refs[-1]
     tile_rows, tile_cols, _ = query_ref.shape
     copies = fetch((query_ref, values_ref), held_ref, sems)
     places = [
-        (buffer, other, lanes(me_ref[0] ^ (flip ^ (side if other else 0))))
+        (buffer, other, lanes(position(side) ^ (flip ^ (side if other else 0))))
         for buffer, flip in zip(buffers, flips)
         for other in range(2)
     ]
@@ -356,18 +373,18 @@
             packed = jnp.zeros((tile_cols, HD), jnp.float32)
             for line in range(tile_cols):
                 values = held_ref[1, start + line, :, head].astype(jnp.float32)
-                edge = jnp.where(me_ref[1] == 0, values[:1], values[tile_cols - 1 :])
+                edge = jnp.where(lax.axis_index("near") == 0, values[:1], values[tile_cols - 1 :])
                 packed = jnp.where(sub == line, edge, packed)
             buffer[other, tile_rows + start // tile_cols] = packed.astype(jnp.bfloat16)
 
 
-def unpack_kernel(flips, side, me_ref, same_ref, beside_ref, *refs):
+def unpack_kernel(flips, side, same_ref, beside_ref, *refs):
     out_ref = refs[-1]
-    out_ref[:, :, lanes(me_ref[0])] = same_ref[0]
-    out_ref[:, :, lanes(me_ref[0] ^ side)] = beside_ref[0]
+    out_ref[:, :, lanes(position(side))] = same_ref[0]
+    out_ref[:, :, lanes(position(side) ^ side)] = beside_ref[0]
     for i, flip in enumerate(flips[1:]):
-        out_ref[:, :, lanes(me_ref[0] ^ flip)] = refs[i][0]
-        out_ref[:, :, lanes(me_ref[0] ^ (flip ^ side))] = refs[i][1]
+        out_ref[:, :, lanes(position(side) ^ flip)] = refs[i][0]
+        out_ref[:, :, lanes(position(side) ^ (flip ^ side))] = refs[i][1]
 
 
 def head_step(shape, queries, keys_new, values_new, keys_cache, values_cache, conv_weight, conv_bias):
@@ -382,7 +399,6 @@
     flips = [flip for flip in range(heads) if not flip & side]
     near = lax.axis_index("near").astype(jnp.int32)
     me = lax.axis_index("ht").astype(jnp.int32) * group_cols + near
-    me_ref = jnp.stack([me, near])
 
     def swap(x, flip):
         return lax.ppermute(x, axes, [(s, s ^ flip) for s in range(heads)])
@@ -391,7 +407,7 @@
         return pl.pallas_call(
             kernel,
             out_shape=out_shape,
-            in_specs=[SMEM] + [space[0]] * (len(operands) - 1),
+            in_specs=[space[0]] * len(operands),
             out_specs=jax.tree.map(lambda _: space[1], out_shape),
             scratch_shapes=scratch,
             compiler_params=params,
@@ -419,7 +435,6 @@
             [jax.ShapeDtypeStruct(buffer, jnp.bfloat16)] * len(flips),
             SMALL,
             0,
-            me_ref,
             *map(stay, sources),
             space=(FAR, VMEM),
             scratch=[
@@ -434,24 +449,12 @@
     pairs = gather(packed)
     query_second = lax.ppermute(query, "far", second)
     query_first = lax.ppermute(query, "far", first)
-    far_index = lax.axis_index("far")
-    flip = me ^ jnp.arange(heads, dtype=jnp.int32)
-    beside = (flip // side) % 2
-    order = flip % side + flip // (2 * side) * side
-    even = far_index % 2 == 0
-    below, above = far_index > 0, far_index < far - 1
-    info = jnp.concatenate(
-        [
-            jnp.stack([~even | above, jnp.where(even, below, above), even]).astype(jnp.int32),
-            beside * len(flips) + order,
-        ]
-    )
     weight = lax.dynamic_slice_in_dim(conv_weight, me * HD, HD, 2)
     bias = lax.dynamic_slice_in_dim(conv_bias.reshape(1, channels), me * HD, HD, 1)
 
     def visit(queries, is_first):
         kernel = functools.partial(visit_kernel, grid, tile, is_first)
-        return call(kernel, jax.ShapeDtypeStruct((heads + 1,) + block, jnp.bfloat16), LIMIT, 4, info, queries, pairs)
+        return call(kernel, jax.ShapeDtypeStruct((heads + 1,) + block, jnp.bfloat16), LIMIT, 4, queries, pairs)
 
     part = visit(query_second, False)
     home_second = lax.ppermute(part, "far", second)
@@ -459,10 +462,10 @@
     home_first = lax.ppermute(part, "far", first)
     part = jax.ShapeDtypeStruct((heads, size, HD), jnp.float32)
     kernel = functools.partial(own_kernel, grid, tile)
-    own = call(kernel, [part] * 3, LIMIT, 4, info, weight, bias, query, pairs, query_first, query_second)
-    kernel = functools.partial(join_kernel, grid, tile)
+    own = call(kernel, [part] * 3, LIMIT, 4, weight, bias, query, pairs, query_first, query_second)
+    kernel = functools.partial(join_kernel, grid, tile, far)
     result = jax.ShapeDtypeStruct((heads,) + block, jnp.bfloat16)
-    result = call(kernel, result, LIMIT, 1, info, *own, home_first, home_second)
+    result = call(kernel, result, LIMIT, 1, *own, home_first, home_second)
     same, other = result[: len(flips)], result[len(flips) :]
     received = swap(other, side)
     got = []
@@ -473,7 +476,6 @@
         jax.ShapeDtypeStruct(queries.shape, jnp.bfloat16),
         SMALL,
         0,
-        me_ref,
         same,
         received,
         *got,

time: 59.9 us -> 58.4 us (0.975)
  Pallas kernels: 13.5 us -> 9.58 us
  waiting for transfers between devices: 24.2 us -> 26.4 us
    pallas_call x7, Pallas kernels: 13.5 us -> 9.58 us  [call(): pl.pallas_call(kernel, out_shape=out_shape, in_specs=[space[0]] * len(ope...]
    ppermute x12, waiting for transfers between devices: 16 us -> 17.6 us  [swap(): return lax.ppermute(x, axes, [(s, s ^ flip) for s in range(heads)])]
  transfers between devices with their start and end apart: 16 -> 16, of which waited for: 9 -> 10; matrix products, arithmetic and copies ran while one was open for 2% -> 2% of each run, Pallas kernels for 16% -> 12%
where the time goes in v10:
time: 58.4 us; the launch traced here: 58.2 us
  waiting for transfers between devices  26.4 us (45%)
  starting transfers between devices  20.8 us (36%)
  Pallas kernels  9.58 us (16%)
  local copies, waits for them, and re-layouts  1.05 us (2%)
    ppermute x12, waiting for transfers between devices, swap(): return lax.ppermute(x, axes, [(s, s ^ flip) for s in range(heads)])  17.6 us
    ppermute x12, starting transfers between devices, swap(): return lax.ppermute(x, axes, [(s, s ^ flip) for s in range(heads)])  11.5 us
    pallas_call x7, Pallas kernels, call(): pl.pallas_call(kernel, out_shape=out_shape, in_specs=[space[0]] * len(ope...  9.58 us
    ppermute x1, starting transfers between devices, head_step(): query_second = lax.ppermute(query, 'far', second)  4.6 us
    ppermute x1, waiting for transfers between devices, head_step(): home_second = lax.ppermute(part, 'far', second)  4.19 us
    ppermute x1, starting transfers between devices, head_step(): home_second = lax.ppermute(part, 'far', second)  3.64 us
    ppermute x1, waiting for transfers between devices, head_step(): query_first = lax.ppermute(query, 'far', first)  3.13 us
    ppermute x1, waiting for transfers between devices, head_step(): query_second = lax.ppermute(query, 'far', second)  1.46 us
  transfers between devices with their start and end apart: 16, of which 10 were waited for; matrix products, arithmetic and copies ran while one was open for 2% of the time, Pallas kernels for 12%

profile of v10, /device:TPU:8, one launch (start us, length us, event | category | flops | bytes accessed | tf_op | source)
XLA Modules:
  0.0 58.2 jit_solution(2039035268490869098)
XLA Ops:
  0.0 1.1 %shard_map.73 = (bf16[2,18,8,128]{3,2,1,0:T(8,128)(2,1)S(1)}, bf16[2,18,8,128]{3,2,1,0:T(8,128)(2,1)S(1)}, bf16[2,18,8,128]{3,2,1,0:T(8,128)(2,1)S(1)}, bf16[2,18,8,128]{3,2,1,0:T(8,128)(2,1)S(1)}) custom-call(bf16[16,8,1024]{2,1,0:T(8,128)(2,1)} %query_ref.1, bf16[16,8,1024]{2,1,0:T(8,128)(2,1)} %refs_3_.1), custom_call_target="tpu_custom_call" | custom-call | bytes 1048576 | tf_op jit(solution)/shard_map/pallas_call | solution.py:407
  1.2 2.5 %collective-permute-start.2 = (bf16[2,18,8,128]{3,2,1,0:T(8,128)(2,1)S(1)}, bf16[2,18,8,128]{3,2,1,0:T(8,128)(2,1)S(1)}, u32[]{:S(2)}, u32[]{:S(2)}) collective-permute-start(bf16[2,18,8,128]{3,2,1,0:T(8,128)(2,1)S(1)} %get-tuple-element.19), channel_id=1, source_target_pairs={{0,17},{1,16},{8,25},{9,24},{16,1},{17,0},{24,9},{25,8},{2,19},{3,... | collective-permute-start | bytes 221192 | tf_op jit(solution)/shard_map/ppermute | solution.py:404
  3.7 0.5 collective-permute-start.1
  4.2 0.5 collective-permute-start
  4.7 1.3 %shard_map.74 = (bf16[2,4,16,8,128]{4,3,2,1,0:T(8,128)(2,1)S(1)}, bf16[2,4,16,8,128]{4,3,2,1,0:T(8,128)(2,1)S(1)}, bf16[2,4,16,8,128]{4,3,2,1,0:T(8,128)(2,1)S(1)}, bf16[2,4,16,8,128]{4,3,2,1,0:T(8,128)(2,1)S(1)}) custom-call(bf16[16,8,1024]{2,1,0:T(8,128)(2,1)} %bitcast.4, bf16[16,8,1024]{2,1,0:T(8,128)(2,1)} %bitcast.5, bf16[16,8,1024]{2,1,0:T(8,128)(2,1)} %refs_2_.1, ...), custom_call_target="tpu_custom_call" | custom-call | bytes 1048576 | tf_op jit(solution)/shard_map/pallas_call | solution.py:407
  6.0 2.5 %collective-permute-start.6 = (bf16[2,4,16,8,128]{4,3,2,1,0:T(8,128)(2,1)S(1)}, bf16[2,4,16,8,128]{4,3,2,1,0:T(8,128)(2,1)S(1)}, u32[]{:S(2)}, u32[]{:S(2)}) collective-permute-start(bf16[2,4,16,8,128]{4,3,2,1,0:T(8,128)(2,1)S(1)} %get-tuple-element.23), channel_id=1, source_target_pairs={{0,17},{1,16},{8,25},{9,24},{16,1},{17,0},{24,9},{25,8},{2,19},{3,... | collective-permute-start | bytes 786440 | tf_op jit(solution)/shard_map/ppermute | solution.py:404
  8.5 0.5 collective-permute-start.5
  9.1 0.6 collective-permute-start.4
  9.7 10.0 %collective-permute-done.4 = bf16[2,4,16,8,128]{4,3,2,1,0:T(8,128)(2,1)S(1)} collective-permute-done((bf16[2,4,16,8,128]{4,3,2,1,0:T(8,128)(2,1)S(1)}, bf16[2,4,16,8,128]{4,3,2,1,0:T(8,128)(2,1)S(1)}, u32[]{:S(2)}, u32[]{:S(2)}) %collective-permute-start.4) | collective-permute-done | bytes 262176 | tf_op jit(solution)/shard_map/ppermute | solution.py:404
  20.2 0.6 collective-permute-start.3
  20.7 1.5 %collective-permute-done.3 = bf16[4,18,8,128]{3,2,1,0:T(8,128)(2,1)S(1)} collective-permute-done((bf16[4,18,8,128]{3,2,1,0:T(8,128)(2,1)S(1)}, bf16[4,18,8,128]{3,2,1,0:T(8,128)(2,1)S(1)}, u32[]{:S(2)}, u32[]{:S(2)}) %collective-permute-start.3) | collective-permute-done | bytes 147488 | tf_op jit(solution)/shard_map/ppermute | solution.py:404
  22.3 0.5 collective-permute-start.8
  22.8 0.8 %dynamic-slice_bitcast_fusion.bias_ref = f32[1,128]{1,0:T(1,128)S(1)} fusion(f32[1024]{0:T(1024)} %param.13, s32[]{:T(128)S(6)} %select_n.4), kind=kLoop, calls=%fused_computation.15 | loop fusion | bytes 1028 | tf_op jit(solution)/shard_map/dynamic_slice | solution.py:453
  23.5 4.6 %collective-permute-start.9 = (bf16[8,18,8,128]{3,2,1,0:T(8,128)(2,1)S(1)}, bf16[8,18,8,128]{3,2,1,0:T(8,128)(2,1)S(1)}, u32[]{:S(2)}, u32[]{:S(2)}) collective-permute-start(bf16[8,18,8,128]{3,2,1,0:T(8,128)(2,1)S(1)} %constant_dynamic-update-slice_fusion.query_ref), channel_id=1, source_target_pairs={{2,4},{4,2},{3,5},{5,3},{10,12},{12,10},{11,13},{13,11},{18,20},{2... | collective-permute-start | bytes 884744 | tf_op jit(solution)/shard_map/ppermute | solution.py:450
  28.2 0.1 constant_dynamic-update-slice_fusion.1.pairs_ref
  28.2 3.1 %collective-permute-done.8.first_ref.query_ref = bf16[8,18,8,128]{3,2,1,0:T(8,128)(2,1)S(1)} collective-permute-done((bf16[8,18,8,128]{3,2,1,0:T(8,128)(2,1)S(1)}, bf16[8,18,8,128]{3,2,1,0:T(8,128)(2,1)S(1)}, u32[]{:S(2)}, u32[]{:S(2)}) %collective-permute-start.8) | collective-permute-done | bytes 294944 | tf_op jit(solution)/shard_map/ppermute | solution.py:451
  31.4 1.8 %shard_map.76 = bf16[9,16,8,128]{3,2,1,0:T(8,128)(2,1)S(1)} custom-call(bf16[8,18,8,128]{3,2,1,0:T(8,128)(2,1)S(1)} %collective-permute-done.8.first_ref.query_ref, bf16[8,4,16,8,128]{4,3,2,1,0:T(8,128)(2,1)S(1)} %constant_dynamic-update-slice_fusion.1.pairs_ref), custom_call_target="tpu_custom_call" | custom-call | flops 4294967296 | bytes 1048576 | tf_op jit(solution)/shard_map/pallas_call | solution.py:407
  33.2 0.5 collective-permute-start.10
  33.7 1.5 %collective-permute-done.9.second_ref.query_ref = bf16[8,18,8,128]{3,2,1,0:T(8,128)(2,1)S(1)} collective-permute-done((bf16[8,18,8,128]{3,2,1,0:T(8,128)(2,1)S(1)}, bf16[8,18,8,128]{3,2,1,0:T(8,128)(2,1)S(1)}, u32[]{:S(2)}, u32[]{:S(2)}) %collective-permute-start.9) | collective-permute-done | bytes 294944 | tf_op jit(solution)/shard_map/ppermute | solution.py:450
  35.2 1.8 %shard_map.77 = bf16[9,16,8,128]{3,2,1,0:T(8,128)(2,1)S(1)} custom-call(bf16[8,18,8,128]{3,2,1,0:T(8,128)(2,1)S(1)} %collective-permute-done.9.second_ref.query_ref, bf16[8,4,16,8,128]{4,3,2,1,0:T(8,128)(2,1)S(1)} %constant_dynamic-update-slice_fusion.1.pairs_ref), custom_call_target="tpu_custom_call" | custom-call | flops 4294967296 | bytes 1048576 | tf_op jit(solution)/shard_map/pallas_call | solution.py:407
  37.0 3.6 %collective-permute-start.11 = (bf16[9,16,8,128]{3,2,1,0:T(8,128)(2,1)S(1)}, bf16[9,16,8,128]{3,2,1,0:T(8,128)(2,1)S(1)}, u32[]{:S(2)}, u32[]{:S(2)}) collective-permute-start(bf16[9,16,8,128]{3,2,1,0:T(8,128)(2,1)S(1)} %shard_map.77), channel_id=1, source_target_pairs={{2,4},{4,2},{3,5},{5,3},{10,12},{12,10},{11,13},{13,11},{18,20},{2... | collective-permute-start | bytes 884744 | tf_op jit(solution)/shard_map/ppermute | solution.py:460
  40.6 2.2 %shard_map.75 = (f32[8,128,128]{2,1,0:T(8,128)S(1)}, f32[8,128,128]{2,1,0:T(8,128)S(1)}, f32[8,128,128]{2,1,0:T(8,128)S(1)}) custom-call(f32[3,3,128]{2,1,0:T(4,128)S(1)} %constant_dynamic-slice_fusion.weight_ref, f32[1,128]{1,0:T(1,128)S(1)} %dynamic-slice_bitcast_fusion.bias_ref, bf16[8,18,8,128]{3,2,1,0:T(8,128)(2,1)S(1)} %constant_dynamic-update-slice_fusion.query_ref, ...), custom_call_target="tpu_custom_call" | custom-call | flops 4294967296 | bytes 1048576 | tf_op jit(solution)/shard_map/pallas_call | solution.py:407
  42.9 4.2 %collective-permute-done.11.second_ref = bf16[9,16,8,128]{3,2,1,0:T(8,128)(2,1)S(1)} collective-permute-done((bf16[9,16,8,128]{3,2,1,0:T(8,128)(2,1)S(1)}, bf16[9,16,8,128]{3,2,1,0:T(8,128)(2,1)S(1)}, u32[]{:S(2)}, u32[]{:S(2)}) %collective-permute-start.11) | collective-permute-done | bytes 294944 | tf_op jit(solution)/shard_map/ppermute | solution.py:460
  47.0 0.5 shard_map.78
  47.7 1.3 %collective-permute-done.12.beside_ref = bf16[4,16,8,128]{3,2,1,0:T(8,128)(2,1)S(1)} collective-permute-done((bf16[4,16,8,128]{3,2,1,0:T(8,128)(2,1)S(1)}, bf16[4,16,8,128]{3,2,1,0:T(8,128)(2,1)S(1)}, u32[]{:S(2)}, u32[]{:S(2)}) %collective-permute-start.12) | collective-permute-done | bytes 131104 | tf_op jit(solution)/shard_map/ppermute | solution.py:404
  49.1 1.5 %collective-permute-start.13 = (bf16[2,16,8,128]{3,2,1,0:T(8,128)(2,1)S(1)}, bf16[2,16,8,128]{3,2,1,0:T(8,128)(2,1)S(1)}, u32[]{:S(2)}, u32[]{:S(2)}) collective-permute-start(bf16[2,16,8,128]{3,2,1,0:T(8,128)(2,1)S(1)} %pad_maximum_fusion.2), channel_id=1, source_target_pairs={{0,1},{1,0},{8,9},{9,8},{16,17},{17,16},{24,25},{25,24},{2,3},{3,2... | collective-permute-start | bytes 196616 | tf_op jit(solution)/shard_map/ppermute | solution.py:404
  50.6 1.5 %collective-permute-start.14 = (bf16[2,16,8,128]{3,2,1,0:T(8,128)(2,1)S(1)}, bf16[2,16,8,128]{3,2,1,0:T(8,128)(2,1)S(1)}, u32[]{:S(2)}, u32[]{:S(2)}) collective-permute-start(bf16[2,16,8,128]{3,2,1,0:T(8,128)(2,1)S(1)} %pad_maximum_fusion.3), channel_id=1, source_target_pairs={{0,16},{1,17},{8,24},{9,25},{16,0},{17,1},{24,8},{25,9},{2,18},{3,... | collective-permute-start | bytes 196616 | tf_op jit(solution)/shard_map/ppermute | solution.py:404
  52.2 0.6 %collective-permute-start.15 = (bf16[2,16,8,128]{3,2,1,0:T(8,128)(2,1)S(1)}, bf16[2,16,8,128]{3,2,1,0:T(8,128)(2,1)S(1)}, u32[]{:S(2)}, u32[]{:S(2)}) collective-permute-start(bf16[2,16,8,128]{3,2,1,0:T(8,128)(2,1)S(1)} %pad_maximum_fusion.4), channel_id=1, source_target_pairs={{0,17},{1,16},{8,25},{9,24},{16,1},{17,0},{24,9},{25,8},{2,19},{3,... | collective-permute-start | bytes 196616 | tf_op jit(solution)/shard_map/ppermute | solution.py:404
  52.8 0.6 %collective-permute-done.13.refs_0_ = bf16[2,16,8,128]{3,2,1,0:T(8,128)(2,1)S(1)} collective-permute-done((bf16[2,16,8,128]{3,2,1,0:T(8,128)(2,1)S(1)}, bf16[2,16,8,128]{3,2,1,0:T(8,128)(2,1)S(1)}, u32[]{:S(2)}, u32[]{:S(2)}) %collective-permute-start.13) | collective-permute-done | bytes 65568 | tf_op jit(solution)/shard_map/ppermute | solution.py:404
  53.4 2.1 %collective-permute-done.14.refs_1_ = bf16[2,16,8,128]{3,2,1,0:T(8,128)(2,1)S(1)} collective-permute-done((bf16[2,16,8,128]{3,2,1,0:T(8,128)(2,1)S(1)}, bf16[2,16,8,128]{3,2,1,0:T(8,128)(2,1)S(1)}, u32[]{:S(2)}, u32[]{:S(2)}) %collective-permute-start.14) | collective-permute-done | bytes 65568 | tf_op jit(solution)/shard_map/ppermute | solution.py:404
  55.5 1.9 %collective-permute-done.15.refs_2_ = bf16[2,16,8,128]{3,2,1,0:T(8,128)(2,1)S(1)} collective-permute-done((bf16[2,16,8,128]{3,2,1,0:T(8,128)(2,1)S(1)}, bf16[2,16,8,128]{3,2,1,0:T(8,128)(2,1)S(1)}, u32[]{:S(2)}, u32[]{:S(2)}) %collective-permute-start.15) | collective-permute-done | bytes 65568 | tf_op jit(solution)/shard_map/ppermute | solution.py:404
  57.4 0.8 %shard_map.79 = bf16[16,8,1024]{2,1,0:T(8,128)(2,1)} custom-call(bf16[4,16,8,128]{3,2,1,0:T(8,128)(2,1)S(1)} %get-tuple-element.31.same_ref, bf16[4,16,8,128]{3,2,1,0:T(8,128)(2,1)S(1)} %collective-permute-done.12.beside_ref, bf16[2,16,8,128]{3,2,1,0:T(8,128)(2,1)S(1)} %collective-permute-done.13.refs_0_, ...), custom_call_target="tpu_custom_call" | custom-call | bytes 1048576 | tf_op jit(solution)/shard_map/pallas_call | solution.py:407
  (29 shorter events, 0.6 us)
Async XLA Ops:
  0.0 23.5 %copy-start = (f32[3,3,1024]{2,1,0:T(4,128)S(1)}, f32[3,3,1024]{2,1,0:T(4,128)}, u32[]{:S(2)}) copy-start(f32[3,3,1024]{2,1,0:T(4,128)} %param.12) | copy-start | bytes 110596
  1.2 8.6 %collective-permute-start.2 = (bf16[2,18,8,128]{3,2,1,0:T(8,128)(2,1)S(1)}, bf16[2,18,8,128]{3,2,1,0:T(8,128)(2,1)S(1)}, u32[]{:S(2)}, u32[]{:S(2)}) collective-permute-start(bf16[2,18,8,128]{3,2,1,0:T(8,128)(2,1)S(1)} %get-tuple-element.19), channel_id=1, source_target_pairs={{0,17},{1,16},{8,25},{9,24},{16,1},{17,0},{24,9},{25,8},{2,19},{3,... | collective-permute-start | bytes 221192 | tf_op jit(solution)/shard_map/ppermute | solution.py:404
  3.7 6.0 %collective-permute-start.1 = (bf16[2,18,8,128]{3,2,1,0:T(8,128)(2,1)S(1)}, bf16[2,18,8,128]{3,2,1,0:T(8,128)(2,1)S(1)}, u32[]{:S(2)}, u32[]{:S(2)}) collective-permute-start(bf16[2,18,8,128]{3,2,1,0:T(8,128)(2,1)S(1)} %get-tuple-element.18), channel_id=1, source_target_pairs={{0,16},{1,17},{8,24},{9,25},{16,0},{17,1},{24,8},{25,9},{2,18},{3,... | collective-permute-start | bytes 221192 | tf_op jit(solution)/shard_map/ppermute | solution.py:404
  4.2 4.9 %collective-permute-start = (bf16[2,18,8,128]{3,2,1,0:T(8,128)(2,1)S(1)}, bf16[2,18,8,128]{3,2,1,0:T(8,128)(2,1)S(1)}, u32[]{:S(2)}, u32[]{:S(2)}) collective-permute-start(bf16[2,18,8,128]{3,2,1,0:T(8,128)(2,1)S(1)} %get-tuple-element.17), channel_id=1, source_target_pairs={{0,1},{1,0},{8,9},{9,8},{16,17},{17,16},{24,25},{25,24},{2,3},{3,2... | collective-permute-start | bytes 221192 | tf_op jit(solution)/shard_map/ppermute | solution.py:404
  6.0 13.9 %collective-permute-start.6 = (bf16[2,4,16,8,128]{4,3,2,1,0:T(8,128)(2,1)S(1)}, bf16[2,4,16,8,128]{4,3,2,1,0:T(8,128)(2,1)S(1)}, u32[]{:S(2)}, u32[]{:S(2)}) collective-permute-start(bf16[2,4,16,8,128]{4,3,2,1,0:T(8,128)(2,1)S(1)} %get-tuple-element.23), channel_id=1, source_target_pairs={{0,17},{1,16},{8,25},{9,24},{16,1},{17,0},{24,9},{25,8},{2,19},{3,... | collective-permute-start | bytes 786440 | tf_op jit(solution)/shard_map/ppermute | solution.py:404
  8.5 11.4 %collective-permute-start.5 = (bf16[2,4,16,8,128]{4,3,2,1,0:T(8,128)(2,1)S(1)}, bf16[2,4,16,8,128]{4,3,2,1,0:T(8,128)(2,1)S(1)}, u32[]{:S(2)}, u32[]{:S(2)}) collective-permute-start(bf16[2,4,16,8,128]{4,3,2,1,0:T(8,128)(2,1)S(1)} %get-tuple-element.22), channel_id=1, source_target_pairs={{0,16},{1,17},{8,24},{9,25},{16,0},{17,1},{24,8},{25,9},{2,18},{3,... | collective-permute-start | bytes 786440 | tf_op jit(solution)/shard_map/ppermute | solution.py:404
  9.1 10.7 %collective-permute-start.4 = (bf16[2,4,16,8,128]{4,3,2,1,0:T(8,128)(2,1)S(1)}, bf16[2,4,16,8,128]{4,3,2,1,0:T(8,128)(2,1)S(1)}, u32[]{:S(2)}, u32[]{:S(2)}) collective-permute-start(bf16[2,4,16,8,128]{4,3,2,1,0:T(8,128)(2,1)S(1)} %get-tuple-element.21), channel_id=1, source_target_pairs={{0,1},{1,0},{8,9},{9,8},{16,17},{17,16},{24,25},{25,24},{2,3},{3,2... | collective-permute-start | bytes 786440 | tf_op jit(solution)/shard_map/ppermute | solution.py:404
  20.0 8.1 %collective-permute-start.7 = (bf16[4,4,16,8,128]{4,3,2,1,0:T(8,128)(2,1)S(1)}, bf16[4,4,16,8,128]{4,3,2,1,0:T(8,128)(2,1)S(1)}, u32[]{:S(2)}, u32[]{:S(2)}) collective-permute-start(bf16[4,4,16,8,128]{4,3,2,1,0:T(8,128)(2,1)S(1)} %pad_maximum_fusion), channel_id=1, source_target_pairs={{0,8},{1,9},{8,0},{9,1},{16,24},{17,25},{24,16},{25,17},{2,10},{3,... | collective-permute-start | bytes 1572872 | tf_op jit(solution)/shard_map/ppermute | solution.py:404
  20.2 2.1 %collective-permute-start.3 = (bf16[4,18,8,128]{3,2,1,0:T(8,128)(2,1)S(1)}, bf16[4,18,8,128]{3,2,1,0:T(8,128)(2,1)S(1)}, u32[]{:S(2)}, u32[]{:S(2)}) collective-permute-start(bf16[4,18,8,128]{3,2,1,0:T(8,128)(2,1)S(1)} %pad_maximum_fusion.1), channel_id=1, source_target_pairs={{0,8},{1,9},{8,0},{9,1},{16,24},{17,25},{24,16},{25,17},{2,10},{3,... | collective-permute-start | bytes 442376 | tf_op jit(solution)/shard_map/ppermute | solution.py:404
  22.3 9.1 %collective-permute-start.8 = (bf16[8,18,8,128]{3,2,1,0:T(8,128)(2,1)S(1)}, bf16[8,18,8,128]{3,2,1,0:T(8,128)(2,1)S(1)}, u32[]{:S(2)}, u32[]{:S(2)}) collective-permute-start(bf16[8,18,8,128]{3,2,1,0:T(8,128)(2,1)S(1)} %constant_dynamic-update-slice_fusion.query_ref), channel_id=1, source_target_pairs={{0,2},{2,0},{4,6},{6,4},{1,3},{3,1},{5,7},{7,5},{8,10},{10,8},{12,... | collective-permute-start | bytes 884744 | tf_op jit(solution)/shard_map/ppermute | solution.py:451
  23.5 11.6 %collective-permute-start.9 = (bf16[8,18,8,128]{3,2,1,0:T(8,128)(2,1)S(1)}, bf16[8,18,8,128]{3,2,1,0:T(8,128)(2,1)S(1)}, u32[]{:S(2)}, u32[]{:S(2)}) collective-permute-start(bf16[8,18,8,128]{3,2,1,0:T(8,128)(2,1)S(1)} %constant_dynamic-update-slice_fusion.query_ref), channel_id=1, source_target_pairs={{2,4},{4,2},{3,5},{5,3},{10,12},{12,10},{11,13},{13,11},{18,20},{2... | collective-permute-start | bytes 884744 | tf_op jit(solution)/shard_map/ppermute | solution.py:450
  33.2 9.7 %collective-permute-start.10 = (bf16[9,16,8,128]{3,2,1,0:T(8,128)(2,1)S(1)}, bf16[9,16,8,128]{3,2,1,0:T(8,128)(2,1)S(1)}, u32[]{:S(2)}, u32[]{:S(2)}) collective-permute-start(bf16[9,16,8,128]{3,2,1,0:T(8,128)(2,1)S(1)} %shard_map.76), channel_id=1, source_target_pairs={{0,2},{2,0},{4,6},{6,4},{1,3},{3,1},{5,7},{7,5},{8,10},{10,8},{12,... | collective-permute-start | bytes 884744 | tf_op jit(solution)/shard_map/ppermute | solution.py:462
  37.0 10.1 %collective-permute-start.11 = (bf16[9,16,8,128]{3,2,1,0:T(8,128)(2,1)S(1)}, bf16[9,16,8,128]{3,2,1,0:T(8,128)(2,1)S(1)}, u32[]{:S(2)}, u32[]{:S(2)}) collective-permute-start(bf16[9,16,8,128]{3,2,1,0:T(8,128)(2,1)S(1)} %shard_map.77), channel_id=1, source_target_pairs={{2,4},{4,2},{3,5},{5,3},{10,12},{12,10},{11,13},{13,11},{18,20},{2... | collective-permute-start | bytes 884744 | tf_op jit(solution)/shard_map/ppermute | solution.py:460
  47.6 1.4 %collective-permute-start.12 = (bf16[4,16,8,128]{3,2,1,0:T(8,128)(2,1)S(1)}, bf16[4,16,8,128]{3,2,1,0:T(8,128)(2,1)S(1)}, u32[]{:S(2)}, u32[]{:S(2)}) collective-permute-start(bf16[4,16,8,128]{3,2,1,0:T(8,128)(2,1)S(1)} %get-tuple-element.30), channel_id=1, source_target_pairs={{0,8},{1,9},{8,0},{9,1},{16,24},{17,25},{24,16},{25,17},{2,10},{3,... | collective-permute-start | bytes 393224 | tf_op jit(solution)/shard_map/ppermute | solution.py:404
  49.1 4.3 %collective-permute-start.13 = (bf16[2,16,8,128]{3,2,1,0:T(8,128)(2,1)S(1)}, bf16[2,16,8,128]{3,2,1,0:T(8,128)(2,1)S(1)}, u32[]{:S(2)}, u32[]{:S(2)}) collective-permute-start(bf16[2,16,8,128]{3,2,1,0:T(8,128)(2,1)S(1)} %pad_maximum_fusion.2), channel_id=1, source_target_pairs={{0,1},{1,0},{8,9},{9,8},{16,17},{17,16},{24,25},{25,24},{2,3},{3,2... | collective-permute-start | bytes 196616 | tf_op jit(solution)/shard_map/ppermute | solution.py:404
  50.6 4.9 %collective-permute-start.14 = (bf16[2,16,8,128]{3,2,1,0:T(8,128)(2,1)S(1)}, bf16[2,16,8,128]{3,2,1,0:T(8,128)(2,1)S(1)}, u32[]{:S(2)}, u32[]{:S(2)}) collective-permute-start(bf16[2,16,8,128]{3,2,1,0:T(8,128)(2,1)S(1)} %pad_maximum_fusion.3), channel_id=1, source_target_pairs={{0,16},{1,17},{8,24},{9,25},{16,0},{17,1},{24,8},{25,9},{2,18},{3,... | collective-permute-start | bytes 196616 | tf_op jit(solution)/shard_map/ppermute | solution.py:404
  52.2 5.2 %collective-permute-start.15 = (bf16[2,16,8,128]{3,2,1,0:T(8,128)(2,1)S(1)}, bf16[2,16,8,128]{3,2,1,0:T(8,128)(2,1)S(1)}, u32[]{:S(2)}, u32[]{:S(2)}) collective-permute-start(bf16[2,16,8,128]{3,2,1,0:T(8,128)(2,1)S(1)} %pad_maximum_fusion.4), channel_id=1, source_target_pairs={{0,17},{1,16},{8,25},{9,24},{16,1},{17,0},{24,9},{25,8},{2,19},{3,... | collective-permute-start | bytes 196616 | tf_op jit(solution)/shard_map/ppermute | solution.py:404

commit v11 on v10

--- a/solution.py
+++ b/solution.py
@@ -157,11 +157,20 @@
     return lax.axis_index("ht") * group_cols + lax.axis_index("near")
 
 
-def slot_of(group_cols, tile):
+def place_of(group_cols, tile):
     side = group_cols
     flip = position(group_cols) ^ tile
-    order = lax.rem(flip, side) + flip // (2 * side) * side
-    return lax.rem(flip // side, 2) * (lax.axis_size("ht") * group_cols // 2) + order
+    return lax.rem(flip // side, 2), lax.rem(flip, side) + flip // (2 * side) * side
+
+
+def slot_of(group_cols, tile):
+    beside, order = place_of(group_cols, tile)
+    return beside * (lax.axis_size("ht") * group_cols // 2) + order
+
+
+def pair_slot_of(group_cols, tile):
+    beside, order = place_of(group_cols, tile)
+    return order * 2 + beside
 
 
 def first_is_right():
@@ -184,8 +193,11 @@
     def slot(self, row, col):
         return slot_of(self.grid_cols, row * self.grid_cols + col)
 
+    def pair_slot(self, row, col):
+        return pair_slot_of(self.grid_cols, row * self.grid_cols + col)
+
     def tile(self, member, row, col):
-        return self.pairs[self.slot(row, col), member].reshape(self.size, HD)
+        return self.pairs[self.pair_slot(row, col), member].reshape(self.size, HD)
 
     def scores(self, row, col, cols):
         query = self.query[self.slot(row, col), pl.ds(0, self.tile_rows)].reshape(self.size, HD)
@@ -251,7 +263,7 @@
                 continue
 
             def values(c):
-                return self.pairs[self.slot(tile_row, c), member, line].astype(jnp.float32)
+                return self.pairs[self.pair_slot(tile_row, c), member, line].astype(jnp.float32)
 
             def edge(right, c):
                 place = self.slot(tile_row, c), self.tile_rows + line // self.tile_cols
@@ -336,46 +348,36 @@
     return pl.ds(pl.multiple_of(head * HD, HD), HD)
 
 
-def fetch(sources, held_ref, sems):
+def pack_kernel(flips, side, *refs):
+    count = len(flips)
+    sources, buffers = refs[: -count - 4], refs[-count - 4 : -4]
+    same_ref, beside_ref, held_ref, sems = refs[-4:]
+    tile_rows, tile_cols, _ = sources[0].shape
     copies = [pltpu.make_async_copy(x, held_ref.at[i], sems.at[i]) for i, x in enumerate(sources)]
     for copy in copies:
         copy.start()
-    return copies
-
-
-def pack_kernel(flips, side, *refs):
-    count = len(flips)
-    sources, buffers, held_ref, sems = refs[: -count - 2], refs[-count - 2 : -2], refs[-2], refs[-1]
-    for member, copy in enumerate(fetch(sources, held_ref, sems)):
-        copy.wait()
-        for buffer, flip in zip(buffers, flips):
-            for other in range(2):
-                head = lanes(position(side) ^ (flip ^ (side if other else 0)))
-                buffer[other, member] = held_ref[member, :, :, head]
-
-
-def query_kernel(flips, side, query_ref, values_ref, *refs):
-    buffers, held_ref, sems = refs[:-2], refs[-2], refs[-1]
-    tile_rows, tile_cols, _ = query_ref.shape
-    copies = fetch((query_ref, values_ref), held_ref, sems)
-    places = [
-        (buffer, other, lanes(position(side) ^ (flip ^ (side if other else 0))))
-        for buffer, flip in zip(buffers, flips)
-        for other in range(2)
-    ]
+    heads = [[lanes(position(side) ^ (flip ^ beside)) for beside in (0, side)] for flip in flips]
     copies[0].wait()
-    for buffer, other, head in places:
-        buffer[other, pl.ds(0, tile_rows)] = held_ref[0, :, :, head]
+    for buffer, pair in zip(buffers, heads):
+        for other in range(2):
+            buffer[other, pl.ds(0, tile_rows)] = held_ref[0, :, :, pair[other]]
     copies[1].wait()
     sub = lax.broadcasted_iota(jnp.int32, (tile_cols, HD), 0)
-    for buffer, other, head in places:
-        for start in range(0, tile_rows, tile_cols):
-            packed = jnp.zeros((tile_cols, HD), jnp.float32)
-            for line in range(tile_cols):
-                values = held_ref[1, start + line, :, head].astype(jnp.float32)
-                edge = jnp.where(lax.axis_index("near") == 0, values[:1], values[tile_cols - 1 :])
-                packed = jnp.where(sub == line, edge, packed)
-            buffer[other, tile_rows + start // tile_cols] = packed.astype(jnp.bfloat16)
+    for buffer, pair in zip(buffers, heads):
+        for other in range(2):
+            for start in range(0, tile_rows, tile_cols):
+                packed = jnp.zeros((tile_cols, HD), jnp.float32)
+                for line in range(tile_cols):
+                    values = held_ref[1, start + line, :, pair[other]].astype(jnp.float32)
+                    edge = jnp.where(lax.axis_index("near") == 0, values[:1], values[tile_cols - 1 :])
+                    packed = jnp.where(sub == line, edge, packed)
+                buffer[other, tile_rows + start // tile_cols] = packed.astype(jnp.bfloat16)
+    for member, source in enumerate((*range(2, len(sources)), 1)):
+        if source != 1:
+            copies[source].wait()
+        for i, pair in enumerate(heads):
+            same_ref[i, member] = held_ref[source, :, :, pair[0]]
+            beside_ref[i, member] = held_ref[source, :, :, pair[1]]
 
 
 def unpack_kernel(flips, side, same_ref, beside_ref, *refs):
@@ -417,11 +419,11 @@
     def stay(x):
         return pltpu.with_memory_space_constraint(x, pltpu.HBM)
 
-    def gather(buffers):
-        got = [buffers[0]] + [swap(b, flip) for b, flip in zip(buffers[1:], flips[1:])]
-        forward = jnp.stack([b[1] for b in got])
-        beside = swap(forward, side)
-        return jnp.concatenate([jnp.stack([b[0] for b in got]), beside], axis=0)
+    def send(buffers):
+        got = [buffers[0]]
+        for i in range(1, len(flips)):
+            got.append(swap(buffers[i], flips[i]))
+        return got
 
     def rounds(start):
         return [pair for i in range(start, far - 1, 2) for pair in ((i, i + 1), (i + 1, i))]
@@ -429,24 +431,27 @@
     first, second = rounds(0), rounds(1)
     edges = -(-tile_rows // tile_cols)
 
-    def pack(kernel, buffer, *sources):
-        return call(
-            functools.partial(kernel, flips, side),
-            [jax.ShapeDtypeStruct(buffer, jnp.bfloat16)] * len(flips),
-            SMALL,
-            0,
-            *map(stay, sources),
-            space=(FAR, VMEM),
-            scratch=[
-                pltpu.VMEM((len(sources),) + queries.shape, jnp.bfloat16),
-                pltpu.SemaphoreType.DMA((len(sources),)),
-            ],
-        )
-
-    packed = pack(query_kernel, (2, tile_rows + edges, tile_cols, HD), queries, values_new)
-    query = gather(packed)
-    packed = pack(pack_kernel, (2, 4) + block, keys_cache[0], values_cache[0], keys_new, values_new)
-    pairs = gather(packed)
+    sources = (queries, values_new, keys_cache[0], values_cache[0], keys_new)
+    query_buffer = jax.ShapeDtypeStruct((2, tile_rows + edges, tile_cols, HD), jnp.bfloat16)
+    pair_buffer = jax.ShapeDtypeStruct((len(flips), len(sources) - 1) + block, jnp.bfloat16)
+    packed = call(
+        functools.partial(pack_kernel, flips, side),
+        [query_buffer] * len(flips) + [pair_buffer] * 2,
+        SMALL,
+        0,
+        *map(stay, sources),
+        space=(FAR, VMEM),
+        scratch=[pltpu.VMEM((len(sources),) + queries.shape, jnp.bfloat16), pltpu.SemaphoreType.DMA((len(sources),))],
+    )
+    same, beside = packed[len(flips) :]
+    beside = swap(beside, side)
+    got = send(packed[: len(flips)])
+    both = [jnp.stack([same[i], beside[i]]) for i in range(len(flips))]
+    pairs = send(both)
+    pairs = jnp.concatenate(pairs, axis=0)
+    forward = jnp.stack([b[1] for b in got])
+    forward = swap(forward, side)
+    query = jnp.concatenate([jnp.stack([b[0] for b in got]), forward], axis=0)
     query_second = lax.ppermute(query, "far", second)
     query_first = lax.ppermute(query, "far", first)
     weight = lax.dynamic_slice_in_dim(conv_weight, me * HD, HD, 2)

time: 58.4 us -> 54 us (0.925)
  the two profiles are of different devices: /device:TPU:8 before, /device:TPU:16 now
where the time goes in v11:
time: 54 us; the launch traced here: 53.7 us
  waiting for transfers between devices  21.6 us (40%)
  starting transfers between devices  18.2 us (34%)
  Pallas kernels  8.62 us (16%)
  local copies, waits for them, and re-layouts  4.92 us (9%)
    ppermute x12, waiting for transfers between devices, swap(): return lax.ppermute(x, axes, [(s, s ^ flip) for s in range(heads)])  15.9 us
    ppermute x12, starting transfers between devices, swap(): return lax.ppermute(x, axes, [(s, s ^ flip) for s in range(heads)])  11.1 us
    pallas_call x6, Pallas kernels, call(): pl.pallas_call(kernel, out_shape=out_shape, in_specs=[space[0]] * len(ope...  8.62 us
    ppermute x1, waiting for transfers between devices, head_step(): home_second = lax.ppermute(part, 'far', second)  5 us
    slice x4, local copies, waits for them, and re-layouts, head_step(): forward = jnp.stack([b[1] for b in got])  2.41 us
    ppermute x1, starting transfers between devices, head_step(): home_second = lax.ppermute(part, 'far', second)  1.92 us
    ppermute x1, starting transfers between devices, head_step(): query_second = lax.ppermute(query, 'far', second)  1.91 us
    ppermute x1, starting transfers between devices, head_step(): home_first = lax.ppermute(part, 'far', first)  1.65 us
  transfers between devices with their start and end apart: 16, of which 10 were waited for; matrix products, arithmetic and copies ran while one was open for 8% of the time, Pallas kernels for 11%

profile of v11, /device:TPU:16, one launch (start us, length us, event | category | flops | bytes accessed | tf_op | source)
XLA Modules:
  0.0 53.7 jit_solution(13591451263838395691)
XLA Ops:
  0.0 1.4 %shard_map.73 = (bf16[2,18,8,128]{3,2,1,0:T(8,128)(2,1)S(1)}, bf16[2,18,8,128]{3,2,1,0:T(8,128)(2,1)S(1)}, bf16[2,18,8,128]{3,2,1,0:T(8,128)(2,1)S(1)}, bf16[2,1...) custom-call(bf16[16,8,1024]{2,1,0:T(8,128)(2,1)} %refs_0_.1, ...), custom_call_target="tpu_custom_call" | custom-call | bytes 1048576 | tf_op jit(solution)/shard_map/pallas_call | solution.py:409
  1.5 2.5 %collective-permute-start.2 = (bf16[2,18,8,128]{3,2,1,0:T(8,128)(2,1)S(1)}, bf16[2,18,8,128]{3,2,1,0:T(8,128)(2,1)}, u32[]{:S(2)}, u32[]{:S(2)}) collective-permute-start(bf16[2,18,8,128]{3,2,1,0:T(8,128)(2,1)S(1)} %get-tuple-element.17), channel_id=1, source_target_pairs={{0,17},{1,16},{8,25},{9,24},{16,1},{17,0},{24,9},{25,8},{2,19},{3,... | collective-permute-start | bytes 221192 | tf_op jit(solution)/shard_map/ppermute | solution.py:406
  5.0 0.7 %fusion = (bf16[1,4,16,8,128]{4,3,2,1,0:T(8,128)(2,1)S(1)}, bf16[1,4,16,8,128]{4,3,2,1,0:T(8,128)(2,1)S(1)}, bf16[1,4,16,8,128]{4,3,2,1,0:T(8,128)(2,1)}, bf16[8,4,16,8,128]{4,3,2,1,0:T(8,128)(2,1)S(1)}) fusion(bf16[4,4,16,8,128]{4,3,2,1,0:T(8,128)(2,1)S(1)} %get-tuple-element.18), kind=kLoop, calls=%fused_computation.19 | loop fusion | bytes 1048576 | tf_op jit(solution)/shard_map/slice | solution.py:449
  5.7 0.8 %dynamic-slice_bitcast_fusion.bias_ref = f32[1,128]{1,0:T(1,128)S(1)} fusion(f32[1024]{0:T(1024)} %param.13, s32[]{:T(128)S(6)} %select_n.4), kind=kLoop, calls=%fused_computation.17 | loop fusion | bytes 1028 | tf_op jit(solution)/shard_map/dynamic_slice | solution.py:458
  6.5 2.5 %collective-permute-done = bf16[2,18,8,128]{3,2,1,0:T(8,128)(2,1)} collective-permute-done((bf16[2,18,8,128]{3,2,1,0:T(8,128)(2,1)S(1)}, bf16[2,18,8,128]{3,2,1,0:T(8,128)(2,1)}, u32[]{:S(2)}, u32[]{:S(2)}) %collective-permute-start) | collective-permute-done | bytes 73760 | tf_op jit(solution)/shard_map/ppermute | solution.py:406
  9.0 0.8 %fusion.6 = (bf16[1,18,8,128]{3,2,1,0:T(8,128)(2,1)S(1)}, bf16[8,18,8,128]{3,2,1,0:T(8,128)(2,1)S(1)}) fusion(bf16[2,18,8,128]{3,2,1,0:T(8,128)(2,1)} %collective-permute-done, bf16[8,18,8,128]{3,2,1,0:T(8,128)(2,1)S(1)} %get-tuple-element.40), kind=kLoop, calls=%fused_computation.25 | loop fusion | bytes 147456 | tf_op jit(solution)/shard_map/slice | solution.py:452
  9.8 0.8 %fusion.7 = (bf16[1,18,8,128]{3,2,1,0:T(8,128)(2,1)S(1)}, bf16[8,18,8,128]{3,2,1,0:T(8,128)(2,1)S(1)}) fusion(bf16[2,18,8,128]{3,2,1,0:T(8,128)(2,1)} %collective-permute-done.1, bf16[8,18,8,128]{3,2,1,0:T(8,128)(2,1)S(1)} %get-tuple-element.42), kind=kLoop, calls=%fused_computation.26 | loop fusion | bytes 147456 | tf_op jit(solution)/shard_map/slice | solution.py:452
  10.6 0.8 %fusion.8 = (bf16[1,18,8,128]{3,2,1,0:T(8,128)(2,1)S(1)}, bf16[8,18,8,128]{3,2,1,0:T(8,128)(2,1)S(1)}) fusion(bf16[2,18,8,128]{3,2,1,0:T(8,128)(2,1)} %collective-permute-done.2, bf16[8,18,8,128]{3,2,1,0:T(8,128)(2,1)S(1)} %get-tuple-element.44), kind=kLoop, calls=%fused_computation.27 | loop fusion | bytes 147456 | tf_op jit(solution)/shard_map/slice | solution.py:452
  11.6 0.8 %copy-done.1 = bf16[1,4,16,8,128]{4,3,2,1,0:T(8,128)(2,1)S(1)} copy-done((bf16[1,4,16,8,128]{4,3,2,1,0:T(8,128)(2,1)S(1)}, bf16[1,4,16,8,128]{4,3,2,1,0:T(8,128)(2,1)}, u32[]{:S(2)}) %copy-start.1) | copy-done | bytes 131096
  12.4 0.8 %collective-permute-start.5 = (bf16[2,4,16,8,128]{4,3,2,1,0:T(8,128)(2,1)S(1)}, bf16[2,4,16,8,128]{4,3,2,1,0:T(8,128)(2,1)S(1)}, u32[]{:S(2)}, u32[]{:S(2)}) collective-permute-start(bf16[2,4,16,8,128]{4,3,2,1,0:T(8,128)(2,1)S(1)} %pad_maximum_fusion), channel_id=1, source_target_pairs={{0,1},{1,0},{8,9},{9,8},{16,17},{17,16},{24,25},{25,24},{2,3},{3,2... | collective-permute-start | bytes 786440 | tf_op jit(solution)/shard_map/ppermute | solution.py:406
  13.3 1.5 %collective-permute-start.6 = (bf16[2,4,16,8,128]{4,3,2,1,0:T(8,128)(2,1)S(1)}, bf16[2,4,16,8,128]{4,3,2,1,0:T(8,128)(2,1)S(1)}, u32[]{:S(2)}, u32[]{:S(2)}) collective-permute-start(bf16[2,4,16,8,128]{4,3,2,1,0:T(8,128)(2,1)S(1)} %pad_maximum_fusion.1), channel_id=1, source_target_pairs={{0,16},{1,17},{8,24},{9,25},{16,0},{17,1},{24,8},{25,9},{2,18},{3,... | collective-permute-start | bytes 786440 | tf_op jit(solution)/shard_map/ppermute | solution.py:406
  14.8 1.4 %collective-permute-start.7 = (bf16[2,4,16,8,128]{4,3,2,1,0:T(8,128)(2,1)S(1)}, bf16[2,4,16,8,128]{4,3,2,1,0:T(8,128)(2,1)S(1)}, u32[]{:S(2)}, u32[]{:S(2)}) collective-permute-start(bf16[2,4,16,8,128]{4,3,2,1,0:T(8,128)(2,1)S(1)} %pad_maximum_fusion.2), channel_id=1, source_target_pairs={{0,17},{1,16},{8,25},{9,24},{16,1},{17,0},{24,9},{25,8},{2,19},{3,... | collective-permute-start | bytes 786440 | tf_op jit(solution)/shard_map/ppermute | solution.py:406
  16.2 1.6 %collective-permute-start.8 = (bf16[8,18,8,128]{3,2,1,0:T(8,128)(2,1)S(1)}, bf16[8,18,8,128]{3,2,1,0:T(8,128)(2,1)S(1)}, u32[]{:S(2)}, u32[]{:S(2)}) collective-permute-start(bf16[8,18,8,128]{3,2,1,0:T(8,128)(2,1)S(1)} %constant_dynamic-update-slice_fusion.query_ref), channel_id=1, source_target_pairs={{0,2},{2,0},{4,6},{6,4},{1,3},{3,1},{5,7},{7,5},{8,10},{10,8},{12,... | collective-permute-start | bytes 884744 | tf_op jit(solution)/shard_map/ppermute | solution.py:456
  17.9 1.9 %collective-permute-start.9 = (bf16[8,18,8,128]{3,2,1,0:T(8,128)(2,1)S(1)}, bf16[8,18,8,128]{3,2,1,0:T(8,128)(2,1)S(1)}, u32[]{:S(2)}, u32[]{:S(2)}) collective-permute-start(bf16[8,18,8,128]{3,2,1,0:T(8,128)(2,1)S(1)} %constant_dynamic-update-slice_fusion.query_ref), channel_id=1, source_target_pairs={{2,4},{4,2},{3,5},{5,3},{10,12},{12,10},{11,13},{13,11},{18,20},{2... | collective-permute-start | bytes 884744 | tf_op jit(solution)/shard_map/ppermute | solution.py:455
  19.8 1.4 %collective-permute-done.5 = bf16[2,4,16,8,128]{4,3,2,1,0:T(8,128)(2,1)S(1)} collective-permute-done((bf16[2,4,16,8,128]{4,3,2,1,0:T(8,128)(2,1)S(1)}, bf16[2,4,16,8,128]{4,3,2,1,0:T(8,128)(2,1)S(1)}, u32[]{:S(2)}, u32[]{:S(2)}) %collective-permute-start.5) | collective-permute-done | bytes 262176 | tf_op jit(solution)/shard_map/ppermute | solution.py:406
  21.2 1.3 %collective-permute-done.6 = bf16[2,4,16,8,128]{4,3,2,1,0:T(8,128)(2,1)S(1)} collective-permute-done((bf16[2,4,16,8,128]{4,3,2,1,0:T(8,128)(2,1)S(1)}, bf16[2,4,16,8,128]{4,3,2,1,0:T(8,128)(2,1)S(1)}, u32[]{:S(2)}, u32[]{:S(2)}) %collective-permute-start.6) | collective-permute-done | bytes 262176 | tf_op jit(solution)/shard_map/ppermute | solution.py:406
  22.5 5.6 %collective-permute-done.7 = bf16[2,4,16,8,128]{4,3,2,1,0:T(8,128)(2,1)S(1)} collective-permute-done((bf16[2,4,16,8,128]{4,3,2,1,0:T(8,128)(2,1)S(1)}, bf16[2,4,16,8,128]{4,3,2,1,0:T(8,128)(2,1)S(1)}, u32[]{:S(2)}, u32[]{:S(2)}) %collective-permute-start.7) | collective-permute-done | bytes 262176 | tf_op jit(solution)/shard_map/ppermute | solution.py:406
  28.1 1.8 %shard_map.75 = bf16[9,16,8,128]{3,2,1,0:T(8,128)(2,1)S(1)} custom-call(bf16[8,18,8,128]{3,2,1,0:T(8,128)(2,1)S(1)} %collective-permute-done.8.first_ref.query_ref, bf16[8,4,16,8,128]{4,3,2,1,0:T(8,128)(2,1)S(1)} %constant_dynamic-update-slice_fusion.1.pairs_ref), custom_call_target="tpu_custom_call" | custom-call | flops 4294967296 | bytes 1048576 | tf_op jit(solution)/shard_map/pallas_call | solution.py:409
  30.0 1.6 %collective-permute-start.10 = (bf16[9,16,8,128]{3,2,1,0:T(8,128)(2,1)S(1)}, bf16[9,16,8,128]{3,2,1,0:T(8,128)(2,1)S(1)}, u32[]{:S(2)}, u32[]{:S(2)}) collective-permute-start(bf16[9,16,8,128]{3,2,1,0:T(8,128)(2,1)S(1)} %shard_map.75), channel_id=1, source_target_pairs={{0,2},{2,0},{4,6},{6,4},{1,3},{3,1},{5,7},{7,5},{8,10},{10,8},{12,... | collective-permute-start | bytes 884744 | tf_op jit(solution)/shard_map/ppermute | solution.py:467
  31.6 1.8 %shard_map.76 = bf16[9,16,8,128]{3,2,1,0:T(8,128)(2,1)S(1)} custom-call(bf16[8,18,8,128]{3,2,1,0:T(8,128)(2,1)S(1)} %collective-permute-done.9.second_ref.query_ref, bf16[8,4,16,8,128]{4,3,2,1,0:T(8,128)(2,1)S(1)} %constant_dynamic-update-slice_fusion.1.pairs_ref), custom_call_target="tpu_custom_call" | custom-call | flops 4294967296 | bytes 1048576 | tf_op jit(solution)/shard_map/pallas_call | solution.py:409
  33.4 1.9 %collective-permute-start.11 = (bf16[9,16,8,128]{3,2,1,0:T(8,128)(2,1)S(1)}, bf16[9,16,8,128]{3,2,1,0:T(8,128)(2,1)S(1)}, u32[]{:S(2)}, u32[]{:S(2)}) collective-permute-start(bf16[9,16,8,128]{3,2,1,0:T(8,128)(2,1)S(1)} %shard_map.76), channel_id=1, source_target_pairs={{2,4},{4,2},{3,5},{5,3},{10,12},{12,10},{11,13},{13,11},{18,20},{2... | collective-permute-start | bytes 884744 | tf_op jit(solution)/shard_map/ppermute | solution.py:465
  35.4 2.2 %shard_map.74 = (f32[8,128,128]{2,1,0:T(8,128)S(1)}, f32[8,128,128]{2,1,0:T(8,128)S(1)}, f32[8,128,128]{2,1,0:T(8,128)S(1)}) custom-call(f32[3,3,128]{2,1,0:T(4,128)S(1)} %constant_dynamic-slice_fusion.weight_ref, f32[1,128]{1,0:T(1,128)S(1)} %dynamic-slice_bitcast_fusion.bias_ref, bf16[8,18,8,128]{3,2,1,0:T(8,128)(2,1)S(1)} %constant_dynamic-update-slice_fusion.query_ref, ...), custom_call_target="tpu_custom_call" | custom-call | flops 4294967296 | bytes 1048576 | tf_op jit(solution)/shard_map/pallas_call | solution.py:409
  37.6 0.7 %collective-permute-done.10.first_ref = bf16[9,16,8,128]{3,2,1,0:T(8,128)(2,1)S(1)} collective-permute-done((bf16[9,16,8,128]{3,2,1,0:T(8,128)(2,1)S(1)}, bf16[9,16,8,128]{3,2,1,0:T(8,128)(2,1)S(1)}, u32[]{:S(2)}, u32[]{:S(2)}) %collective-permute-start.10) | collective-permute-done | bytes 294944 | tf_op jit(solution)/shard_map/ppermute | solution.py:467
  38.3 5.0 %collective-permute-done.11.second_ref = bf16[9,16,8,128]{3,2,1,0:T(8,128)(2,1)S(1)} collective-permute-done((bf16[9,16,8,128]{3,2,1,0:T(8,128)(2,1)S(1)}, bf16[9,16,8,128]{3,2,1,0:T(8,128)(2,1)S(1)}, u32[]{:S(2)}, u32[]{:S(2)}) %collective-permute-start.11) | collective-permute-done | bytes 294944 | tf_op jit(solution)/shard_map/ppermute | solution.py:465
  44.0 1.3 %collective-permute-done.12.beside_ref = bf16[4,16,8,128]{3,2,1,0:T(8,128)(2,1)S(1)} collective-permute-done((bf16[4,16,8,128]{3,2,1,0:T(8,128)(2,1)S(1)}, bf16[4,16,8,128]{3,2,1,0:T(8,128)(2,1)S(1)}, u32[]{:S(2)}, u32[]{:S(2)}) %collective-permute-start.12) | collective-permute-done | bytes 131104 | tf_op jit(solution)/shard_map/ppermute | solution.py:406
  45.3 0.8 %collective-permute-start.13 = (bf16[2,16,8,128]{3,2,1,0:T(8,128)(2,1)S(1)}, bf16[2,16,8,128]{3,2,1,0:T(8,128)(2,1)S(1)}, u32[]{:S(2)}, u32[]{:S(2)}) collective-permute-start(bf16[2,16,8,128]{3,2,1,0:T(8,128)(2,1)S(1)} %pad_maximum_fusion.4), channel_id=1, source_target_pairs={{0,1},{1,0},{8,9},{9,8},{16,17},{17,16},{24,25},{25,24},{2,3},{3,2... | collective-permute-start | bytes 196616 | tf_op jit(solution)/shard_map/ppermute | solution.py:406
  46.1 1.5 %collective-permute-start.14 = (bf16[2,16,8,128]{3,2,1,0:T(8,128)(2,1)S(1)}, bf16[2,16,8,128]{3,2,1,0:T(8,128)(2,1)S(1)}, u32[]{:S(2)}, u32[]{:S(2)}) collective-permute-start(bf16[2,16,8,128]{3,2,1,0:T(8,128)(2,1)S(1)} %pad_maximum_fusion.5), channel_id=1, source_target_pairs={{0,16},{1,17},{8,24},{9,25},{16,0},{17,1},{24,8},{25,9},{2,18},{3,... | collective-permute-start | bytes 196616 | tf_op jit(solution)/shard_map/ppermute | solution.py:406
  47.6 1.4 %collective-permute-start.15 = (bf16[2,16,8,128]{3,2,1,0:T(8,128)(2,1)S(1)}, bf16[2,16,8,128]{3,2,1,0:T(8,128)(2,1)S(1)}, u32[]{:S(2)}, u32[]{:S(2)}) collective-permute-start(bf16[2,16,8,128]{3,2,1,0:T(8,128)(2,1)S(1)} %pad_maximum_fusion.6), channel_id=1, source_target_pairs={{0,17},{1,16},{8,25},{9,24},{16,1},{17,0},{24,9},{25,8},{2,19},{3,... | collective-permute-start | bytes 196616 | tf_op jit(solution)/shard_map/ppermute | solution.py:406
  49.0 0.6 %collective-permute-done.13.refs_0_ = bf16[2,16,8,128]{3,2,1,0:T(8,128)(2,1)S(1)} collective-permute-done((bf16[2,16,8,128]{3,2,1,0:T(8,128)(2,1)S(1)}, bf16[2,16,8,128]{3,2,1,0:T(8,128)(2,1)S(1)}, u32[]{:S(2)}, u32[]{:S(2)}) %collective-permute-start.13) | collective-permute-done | bytes 65568 | tf_op jit(solution)/shard_map/ppermute | solution.py:406
  49.7 0.8 %collective-permute-done.14.refs_1_ = bf16[2,16,8,128]{3,2,1,0:T(8,128)(2,1)S(1)} collective-permute-done((bf16[2,16,8,128]{3,2,1,0:T(8,128)(2,1)S(1)}, bf16[2,16,8,128]{3,2,1,0:T(8,128)(2,1)S(1)}, u32[]{:S(2)}, u32[]{:S(2)}) %collective-permute-start.14) | collective-permute-done | bytes 65568 | tf_op jit(solution)/shard_map/ppermute | solution.py:406
  50.5 2.4 %collective-permute-done.15.refs_2_ = bf16[2,16,8,128]{3,2,1,0:T(8,128)(2,1)S(1)} collective-permute-done((bf16[2,16,8,128]{3,2,1,0:T(8,128)(2,1)S(1)}, bf16[2,16,8,128]{3,2,1,0:T(8,128)(2,1)S(1)}, u32[]{:S(2)}, u32[]{:S(2)}) %collective-permute-start.15) | collective-permute-done | bytes 65568 | tf_op jit(solution)/shard_map/ppermute | solution.py:406
  52.9 0.8 %shard_map.78 = bf16[16,8,1024]{2,1,0:T(8,128)(2,1)} custom-call(bf16[4,16,8,128]{3,2,1,0:T(8,128)(2,1)S(1)} %get-tuple-element.35.same_ref, bf16[4,16,8,128]{3,2,1,0:T(8,128)(2,1)S(1)} %collective-permute-done.12.beside_ref, bf16[2,16,8,128]{3,2,1,0:T(8,128)(2,1)S(1)} %collective-permute-done.13.refs_0_, ...), custom_call_target="tpu_custom_call" | custom-call | bytes 1048576 | tf_op jit(solution)/shard_map/pallas_call | solution.py:409
  (32 shorter events, 2.1 us)
Async XLA Ops:
  0.0 5.7 %copy-start = (f32[3,3,1024]{2,1,0:T(4,128)S(1)}, f32[3,3,1024]{2,1,0:T(4,128)}, u32[]{:S(2)}) copy-start(f32[3,3,1024]{2,1,0:T(4,128)} %param.12) | copy-start | bytes 110596
  1.5 9.1 %collective-permute-start.2 = (bf16[2,18,8,128]{3,2,1,0:T(8,128)(2,1)S(1)}, bf16[2,18,8,128]{3,2,1,0:T(8,128)(2,1)}, u32[]{:S(2)}, u32[]{:S(2)}) collective-permute-start(bf16[2,18,8,128]{3,2,1,0:T(8,128)(2,1)S(1)} %get-tuple-element.17), channel_id=1, source_target_pairs={{0,17},{1,16},{8,25},{9,24},{16,1},{17,0},{24,9},{25,8},{2,19},{3,... | collective-permute-start | bytes 221192 | tf_op jit(solution)/shard_map/ppermute | solution.py:406
  4.0 5.8 %collective-permute-start.1 = (bf16[2,18,8,128]{3,2,1,0:T(8,128)(2,1)S(1)}, bf16[2,18,8,128]{3,2,1,0:T(8,128)(2,1)}, u32[]{:S(2)}, u32[]{:S(2)}) collective-permute-start(bf16[2,18,8,128]{3,2,1,0:T(8,128)(2,1)S(1)} %get-tuple-element.16), channel_id=1, source_target_pairs={{0,16},{1,17},{8,24},{9,25},{16,0},{17,1},{24,8},{25,9},{2,18},{3,... | collective-permute-start | bytes 221192 | tf_op jit(solution)/shard_map/ppermute | solution.py:406
  4.5 4.5 %collective-permute-start = (bf16[2,18,8,128]{3,2,1,0:T(8,128)(2,1)S(1)}, bf16[2,18,8,128]{3,2,1,0:T(8,128)(2,1)}, u32[]{:S(2)}, u32[]{:S(2)}) collective-permute-start(bf16[2,18,8,128]{3,2,1,0:T(8,128)(2,1)S(1)} %get-tuple-element.15), channel_id=1, source_target_pairs={{0,1},{1,0},{8,9},{9,8},{16,17},{17,16},{24,25},{25,24},{2,3},{3,2... | collective-permute-start | bytes 221192 | tf_op jit(solution)/shard_map/ppermute | solution.py:406
  5.0 6.5 %collective-permute-start.4 = (bf16[4,4,16,8,128]{4,3,2,1,0:T(8,128)(2,1)S(1)}, bf16[4,4,16,8,128]{4,3,2,1,0:T(8,128)(2,1)S(1)}, u32[]{:S(2)}, u32[]{:S(2)}) collective-permute-start(bf16[4,4,16,8,128]{4,3,2,1,0:T(8,128)(2,1)S(1)} %get-tuple-element.19), channel_id=1, source_target_pairs={{0,8},{1,9},{8,0},{9,1},{16,24},{17,25},{24,16},{25,17},{2,10},{3,... | collective-permute-start | bytes 1572872 | tf_op jit(solution)/shard_map/ppermute | solution.py:406
  11.4 4.8 %collective-permute-start.3 = (bf16[4,18,8,128]{3,2,1,0:T(8,128)(2,1)S(1)}, bf16[4,18,8,128]{3,2,1,0:T(8,128)(2,1)S(1)}, u32[]{:S(2)}, u32[]{:S(2)}) collective-permute-start(bf16[4,18,8,128]{3,2,1,0:T(8,128)(2,1)S(1)} %pad_maximum_fusion.3), channel_id=1, source_target_pairs={{0,8},{1,9},{8,0},{9,1},{16,24},{17,25},{24,16},{25,17},{2,10},{3,... | collective-permute-start | bytes 442376 | tf_op jit(solution)/shard_map/ppermute | solution.py:406
  11.5 0.9 %copy-start.1 = (bf16[1,4,16,8,128]{4,3,2,1,0:T(8,128)(2,1)S(1)}, bf16[1,4,16,8,128]{4,3,2,1,0:T(8,128)(2,1)}, u32[]{:S(2)}) copy-start(bf16[1,4,16,8,128]{4,3,2,1,0:T(8,128)(2,1)} %get-tuple-element.25) | copy-start | bytes 393220
  12.4 8.8 %collective-permute-start.5 = (bf16[2,4,16,8,128]{4,3,2,1,0:T(8,128)(2,1)S(1)}, bf16[2,4,16,8,128]{4,3,2,1,0:T(8,128)(2,1)S(1)}, u32[]{:S(2)}, u32[]{:S(2)}) collective-permute-start(bf16[2,4,16,8,128]{4,3,2,1,0:T(8,128)(2,1)S(1)} %pad_maximum_fusion), channel_id=1, source_target_pairs={{0,1},{1,0},{8,9},{9,8},{16,17},{17,16},{24,25},{25,24},{2,3},{3,2... | collective-permute-start | bytes 786440 | tf_op jit(solution)/shard_map/ppermute | solution.py:406
  13.3 9.2 %collective-permute-start.6 = (bf16[2,4,16,8,128]{4,3,2,1,0:T(8,128)(2,1)S(1)}, bf16[2,4,16,8,128]{4,3,2,1,0:T(8,128)(2,1)S(1)}, u32[]{:S(2)}, u32[]{:S(2)}) collective-permute-start(bf16[2,4,16,8,128]{4,3,2,1,0:T(8,128)(2,1)S(1)} %pad_maximum_fusion.1), channel_id=1, source_target_pairs={{0,16},{1,17},{8,24},{9,25},{16,0},{17,1},{24,8},{25,9},{2,18},{3,... | collective-permute-start | bytes 786440 | tf_op jit(solution)/shard_map/ppermute | solution.py:406
  14.8 13.3 %collective-permute-start.7 = (bf16[2,4,16,8,128]{4,3,2,1,0:T(8,128)(2,1)S(1)}, bf16[2,4,16,8,128]{4,3,2,1,0:T(8,128)(2,1)S(1)}, u32[]{:S(2)}, u32[]{:S(2)}) collective-permute-start(bf16[2,4,16,8,128]{4,3,2,1,0:T(8,128)(2,1)S(1)} %pad_maximum_fusion.2), channel_id=1, source_target_pairs={{0,17},{1,16},{8,25},{9,24},{16,1},{17,0},{24,9},{25,8},{2,19},{3,... | collective-permute-start | bytes 786440 | tf_op jit(solution)/shard_map/ppermute | solution.py:406
  16.2 11.9 %collective-permute-start.8 = (bf16[8,18,8,128]{3,2,1,0:T(8,128)(2,1)S(1)}, bf16[8,18,8,128]{3,2,1,0:T(8,128)(2,1)S(1)}, u32[]{:S(2)}, u32[]{:S(2)}) collective-permute-start(bf16[8,18,8,128]{3,2,1,0:T(8,128)(2,1)S(1)} %constant_dynamic-update-slice_fusion.query_ref), channel_id=1, source_target_pairs={{0,2},{2,0},{4,6},{6,4},{1,3},{3,1},{5,7},{7,5},{8,10},{10,8},{12,... | collective-permute-start | bytes 884744 | tf_op jit(solution)/shard_map/ppermute | solution.py:456
  17.9 13.8 %collective-permute-start.9 = (bf16[8,18,8,128]{3,2,1,0:T(8,128)(2,1)S(1)}, bf16[8,18,8,128]{3,2,1,0:T(8,128)(2,1)S(1)}, u32[]{:S(2)}, u32[]{:S(2)}) collective-permute-start(bf16[8,18,8,128]{3,2,1,0:T(8,128)(2,1)S(1)} %constant_dynamic-update-slice_fusion.query_ref), channel_id=1, source_target_pairs={{2,4},{4,2},{3,5},{5,3},{10,12},{12,10},{11,13},{13,11},{18,20},{2... | collective-permute-start | bytes 884744 | tf_op jit(solution)/shard_map/ppermute | solution.py:455
  30.0 8.3 %collective-permute-start.10 = (bf16[9,16,8,128]{3,2,1,0:T(8,128)(2,1)S(1)}, bf16[9,16,8,128]{3,2,1,0:T(8,128)(2,1)S(1)}, u32[]{:S(2)}, u32[]{:S(2)}) collective-permute-start(bf16[9,16,8,128]{3,2,1,0:T(8,128)(2,1)S(1)} %shard_map.75), channel_id=1, source_target_pairs={{0,2},{2,0},{4,6},{6,4},{1,3},{3,1},{5,7},{7,5},{8,10},{10,8},{12,... | collective-permute-start | bytes 884744 | tf_op jit(solution)/shard_map/ppermute | solution.py:467
  33.4 9.9 %collective-permute-start.11 = (bf16[9,16,8,128]{3,2,1,0:T(8,128)(2,1)S(1)}, bf16[9,16,8,128]{3,2,1,0:T(8,128)(2,1)S(1)}, u32[]{:S(2)}, u32[]{:S(2)}) collective-permute-start(bf16[9,16,8,128]{3,2,1,0:T(8,128)(2,1)S(1)} %shard_map.76), channel_id=1, source_target_pairs={{2,4},{4,2},{3,5},{5,3},{10,12},{12,10},{11,13},{13,11},{18,20},{2... | collective-permute-start | bytes 884744 | tf_op jit(solution)/shard_map/ppermute | solution.py:465
  43.9 1.4 %collective-permute-start.12 = (bf16[4,16,8,128]{3,2,1,0:T(8,128)(2,1)S(1)}, bf16[4,16,8,128]{3,2,1,0:T(8,128)(2,1)S(1)}, u32[]{:S(2)}, u32[]{:S(2)}) collective-permute-start(bf16[4,16,8,128]{3,2,1,0:T(8,128)(2,1)S(1)} %get-tuple-element.34), channel_id=1, source_target_pairs={{0,8},{1,9},{8,0},{9,1},{16,24},{17,25},{24,16},{25,17},{2,10},{3,... | collective-permute-start | bytes 393224 | tf_op jit(solution)/shard_map/ppermute | solution.py:406
  45.3 4.3 %collective-permute-start.13 = (bf16[2,16,8,128]{3,2,1,0:T(8,128)(2,1)S(1)}, bf16[2,16,8,128]{3,2,1,0:T(8,128)(2,1)S(1)}, u32[]{:S(2)}, u32[]{:S(2)}) collective-permute-start(bf16[2,16,8,128]{3,2,1,0:T(8,128)(2,1)S(1)} %pad_maximum_fusion.4), channel_id=1, source_target_pairs={{0,1},{1,0},{8,9},{9,8},{16,17},{17,16},{24,25},{25,24},{2,3},{3,2... | collective-permute-start | bytes 196616 | tf_op jit(solution)/shard_map/ppermute | solution.py:406
  46.1 4.3 %collective-permute-start.14 = (bf16[2,16,8,128]{3,2,1,0:T(8,128)(2,1)S(1)}, bf16[2,16,8,128]{3,2,1,0:T(8,128)(2,1)S(1)}, u32[]{:S(2)}, u32[]{:S(2)}) collective-permute-start(bf16[2,16,8,128]{3,2,1,0:T(8,128)(2,1)S(1)} %pad_maximum_fusion.5), channel_id=1, source_target_pairs={{0,16},{1,17},{8,24},{9,25},{16,0},{17,1},{24,8},{25,9},{2,18},{3,... | collective-permute-start | bytes 196616 | tf_op jit(solution)/shard_map/ppermute | solution.py:406
  47.6 5.2 %collective-permute-start.15 = (bf16[2,16,8,128]{3,2,1,0:T(8,128)(2,1)S(1)}, bf16[2,16,8,128]{3,2,1,0:T(8,128)(2,1)S(1)}, u32[]{:S(2)}, u32[]{:S(2)}) collective-permute-start(bf16[2,16,8,128]{3,2,1,0:T(8,128)(2,1)S(1)} %pad_maximum_fusion.6), channel_id=1, source_target_pairs={{0,17},{1,16},{8,25},{9,24},{16,1},{17,0},{24,9},{25,8},{2,19},{3,... | collective-permute-start | bytes 196616 | tf_op jit(solution)/shard_map/ppermute | solution.py:406

commit v12 on v11

--- a/solution.py
+++ b/solution.py
@@ -350,8 +350,8 @@
 
 def pack_kernel(flips, side, *refs):
     count = len(flips)
-    sources, buffers = refs[: -count - 4], refs[-count - 4 : -4]
-    same_ref, beside_ref, held_ref, sems = refs[-4:]
+    sources, buffers = refs[: -2 * count - 3], refs[-2 * count - 3 : -count - 3]
+    messages, (beside_ref, held_ref, sems) = refs[-count - 3 : -3], refs[-3:]
     tile_rows, tile_cols, _ = sources[0].shape
     copies = [pltpu.make_async_copy(x, held_ref.at[i], sems.at[i]) for i, x in enumerate(sources)]
     for copy in copies:
@@ -376,8 +376,15 @@
         if source != 1:
             copies[source].wait()
         for i, pair in enumerate(heads):
-            same_ref[i, member] = held_ref[source, :, :, pair[0]]
+            messages[i][0, member] = held_ref[source, :, :, pair[0]]
             beside_ref[i, member] = held_ref[source, :, :, pair[1]]
+
+
+def split_kernel(*refs):
+    mine_ref, other_ref = refs[-2:]
+    for i, ref in enumerate(refs[:-2]):
+        mine_ref[i] = ref[0]
+        other_ref[i] = ref[1]
 
 
 def unpack_kernel(flips, side, same_ref, beside_ref, *refs):
@@ -433,25 +440,27 @@
 
     sources = (queries, values_new, keys_cache[0], values_cache[0], keys_new)
     query_buffer = jax.ShapeDtypeStruct((2, tile_rows + edges, tile_cols, HD), jnp.bfloat16)
-    pair_buffer = jax.ShapeDtypeStruct((len(flips), len(sources) - 1) + block, jnp.bfloat16)
+    message = jax.ShapeDtypeStruct((2, len(sources) - 1) + block, jnp.bfloat16)
+    beside = jax.ShapeDtypeStruct((len(flips), len(sources) - 1) + block, jnp.bfloat16)
     packed = call(
         functools.partial(pack_kernel, flips, side),
-        [query_buffer] * len(flips) + [pair_buffer] * 2,
+        [query_buffer] * len(flips) + [message] * len(flips) + [beside],
         SMALL,
         0,
         *map(stay, sources),
         space=(FAR, VMEM),
         scratch=[pltpu.VMEM((len(sources),) + queries.shape, jnp.bfloat16), pltpu.SemaphoreType.DMA((len(sources),))],
     )
-    same, beside = packed[len(flips) :]
-    beside = swap(beside, side)
+    beside = swap(packed[-1], side)
     got = send(packed[: len(flips)])
-    both = [jnp.stack([same[i], beside[i]]) for i in range(len(flips))]
+    messages = packed[len(flips) : -1]
+    both = [lax.dynamic_update_slice_in_dim(m, beside[i : i + 1], 1, 0) for i, m in enumerate(messages)]
     pairs = send(both)
     pairs = jnp.concatenate(pairs, axis=0)
-    forward = jnp.stack([b[1] for b in got])
+    half = jax.ShapeDtypeStruct((len(flips),) + query_buffer.shape[1:], jnp.bfloat16)
+    mine, forward = call(split_kernel, [half, half], SMALL, 0, *got)
     forward = swap(forward, side)
-    query = jnp.concatenate([jnp.stack([b[0] for b in got]), forward], axis=0)
+    query = jnp.concatenate([mine, forward], axis=0)
     query_second = lax.ppermute(query, "far", second)
     query_first = lax.ppermute(query, "far", first)
     weight = lax.dynamic_slice_in_dim(conv_weight, me * HD, HD, 2)

time: 54 us -> 52 us (0.963)
  local copies, waits for them, and re-layouts: 4.92 us -> 0.91 us
  waiting for transfers between devices: 21.6 us -> 23.5 us
    slice x6 -> x0, local copies, waits for them, and re-layouts: 3.14 us -> none  [the longest x4 2.41 us: head_step(): forward = jnp.stack([b[1] for b in got])]
    ppermute x12, waiting for transfers between devices: 15.9 us -> 17.3 us  [swap(): return lax.ppermute(x, axes, [(s, s ^ flip) for s in range(heads)])]
    unnamed x6 -> x3, local copies, waits for them, and re-layouts: 0.92 us -> 0.02 us
    pallas_call x6 -> x7, Pallas kernels: 8.62 us -> 8.91 us  [call(): pl.pallas_call(kernel, out_shape=out_shape, in_specs=[space[0]] * len(ope...]
  transfers between devices with their start and end apart: 16 -> 16, of which waited for: 10 -> 12; matrix products, arithmetic and copies ran while one was open for 8% -> 2% of each run, Pallas kernels for 11% -> 12%
where the time goes in v12:
time: 52 us; the launch traced here: 51.8 us
  waiting for transfers between devices  23.5 us (45%)
  starting transfers between devices  18.1 us (35%)
  Pallas kernels  8.91 us (17%)
  local copies, waits for them, and re-layouts  0.91 us (2%)
    ppermute x12, waiting for transfers between devices, swap(): return lax.ppermute(x, axes, [(s, s ^ flip) for s in range(heads)])  17.3 us
    ppermute x12, starting transfers between devices, swap(): return lax.ppermute(x, axes, [(s, s ^ flip) for s in range(heads)])  11 us
    pallas_call x7, Pallas kernels, call(): pl.pallas_call(kernel, out_shape=out_shape, in_specs=[space[0]] * len(ope...  8.91 us
    ppermute x1, waiting for transfers between devices, head_step(): home_second = lax.ppermute(part, 'far', second)  5.07 us
    ppermute x1, starting transfers between devices, head_step(): home_second = lax.ppermute(part, 'far', second)  1.92 us
    ppermute x1, starting transfers between devices, head_step(): query_second = lax.ppermute(query, 'far', second)  1.91 us
    ppermute x1, starting transfers between devices, head_step(): query_first = lax.ppermute(query, 'far', first)  1.64 us
    ppermute x1, starting transfers between devices, head_step(): home_first = lax.ppermute(part, 'far', first)  1.64 us
  transfers between devices with their start and end apart: 16, of which 12 were waited for; matrix products, arithmetic and copies ran while one was open for 2% of the time, Pallas kernels for 12%

profile of v12, /device:TPU:16, one launch (start us, length us, event | category | flops | bytes accessed | tf_op | source)
XLA Modules:
  0.0 51.8 jit_solution(3262691981485370398)
XLA Ops:
  0.0 1.4 %shard_map.73 = (bf16[2,18,8,128]{3,2,1,0:T(8,128)(2,1)S(1)}, bf16[2,18,8,128]{3,2,1,0:T(8,128)(2,1)S(1)}, bf16[2,18,8,128]{3,2,1,0:T(8,128)(2,1)S(1)}, bf16[2,1...) custom-call(bf16[16,8,1024]{2,1,0:T(8,128)(2,1)} %refs_0_.1, ...), custom_call_target="tpu_custom_call" | custom-call | bytes 1048576 | tf_op jit(solution)/shard_map/pallas_call | solution.py:416
  1.5 1.6 %collective-permute-start = (bf16[2,18,8,128]{3,2,1,0:T(8,128)(2,1)S(1)}, bf16[2,18,8,128]{3,2,1,0:T(8,128)(2,1)S(1)}, u32[]{:S(2)}, u32[]{:S(2)}) collective-permute-start(bf16[2,18,8,128]{3,2,1,0:T(8,128)(2,1)S(1)} %get-tuple-element.20), channel_id=1, source_target_pairs={{0,1},{1,0},{8,9},{9,8},{16,17},{17,16},{24,25},{25,24},{2,3},{3,2... | collective-permute-start | bytes 221192 | tf_op jit(solution)/shard_map/ppermute | solution.py:413
  3.1 1.5 %collective-permute-start.1 = (bf16[2,18,8,128]{3,2,1,0:T(8,128)(2,1)S(1)}, bf16[2,18,8,128]{3,2,1,0:T(8,128)(2,1)S(1)}, u32[]{:S(2)}, u32[]{:S(2)}) collective-permute-start(bf16[2,18,8,128]{3,2,1,0:T(8,128)(2,1)S(1)} %get-tuple-element.21), channel_id=1, source_target_pairs={{0,16},{1,17},{8,24},{9,25},{16,0},{17,1},{24,8},{25,9},{2,18},{3,... | collective-permute-start | bytes 221192 | tf_op jit(solution)/shard_map/ppermute | solution.py:413
  4.6 0.5 collective-permute-start.2
  5.1 1.1 %collective-permute-done.refs_1_ = bf16[2,18,8,128]{3,2,1,0:T(8,128)(2,1)S(1)} collective-permute-done((bf16[2,18,8,128]{3,2,1,0:T(8,128)(2,1)S(1)}, bf16[2,18,8,128]{3,2,1,0:T(8,128)(2,1)S(1)}, u32[]{:S(2)}, u32[]{:S(2)}) %collective-permute-start) | collective-permute-done | bytes 73760 | tf_op jit(solution)/shard_map/ppermute | solution.py:413
  6.2 1.7 %collective-permute-done.1.refs_2_ = bf16[2,18,8,128]{3,2,1,0:T(8,128)(2,1)S(1)} collective-permute-done((bf16[2,18,8,128]{3,2,1,0:T(8,128)(2,1)S(1)}, bf16[2,18,8,128]{3,2,1,0:T(8,128)(2,1)S(1)}, u32[]{:S(2)}, u32[]{:S(2)}) %collective-permute-start.1) | collective-permute-done | bytes 73760 | tf_op jit(solution)/shard_map/ppermute | solution.py:413
  7.9 1.9 %collective-permute-done.2.refs_3_ = bf16[2,18,8,128]{3,2,1,0:T(8,128)(2,1)S(1)} collective-permute-done((bf16[2,18,8,128]{3,2,1,0:T(8,128)(2,1)S(1)}, bf16[2,18,8,128]{3,2,1,0:T(8,128)(2,1)S(1)}, u32[]{:S(2)}, u32[]{:S(2)}) %collective-permute-start.2) | collective-permute-done | bytes 73760 | tf_op jit(solution)/shard_map/ppermute | solution.py:413
  10.1 1.6 %collective-permute-start.7 = (bf16[2,4,16,8,128]{4,3,2,1,0:T(8,128)(2,1)S(1)}, bf16[2,4,16,8,128]{4,3,2,1,0:T(8,128)(2,1)S(1)}, u32[]{:S(2)}, u32[]{:S(2)}) collective-permute-start(bf16[2,4,16,8,128]{4,3,2,1,0:T(8,128)(2,1)S(1)} %get-tuple-element.34), channel_id=1, source_target_pairs={{0,17},{1,16},{8,25},{9,24},{16,1},{17,0},{24,9},{25,8},{2,19},{3,... | collective-permute-start | bytes 786440 | tf_op jit(solution)/shard_map/ppermute | solution.py:413
  11.7 0.6 %collective-permute-start.6 = (bf16[2,4,16,8,128]{4,3,2,1,0:T(8,128)(2,1)S(1)}, bf16[2,4,16,8,128]{4,3,2,1,0:T(8,128)(2,1)S(1)}, u32[]{:S(2)}, u32[]{:S(2)}) collective-permute-start(bf16[2,4,16,8,128]{4,3,2,1,0:T(8,128)(2,1)S(1)} %get-tuple-element.35), channel_id=1, source_target_pairs={{0,16},{1,17},{8,24},{9,25},{16,0},{17,1},{24,8},{25,9},{2,18},{3,... | collective-permute-start | bytes 786440 | tf_op jit(solution)/shard_map/ppermute | solution.py:413
  12.3 1.4 %collective-permute-start.5 = (bf16[2,4,16,8,128]{4,3,2,1,0:T(8,128)(2,1)S(1)}, bf16[2,4,16,8,128]{4,3,2,1,0:T(8,128)(2,1)S(1)}, u32[]{:S(2)}, u32[]{:S(2)}) collective-permute-start(bf16[2,4,16,8,128]{4,3,2,1,0:T(8,128)(2,1)S(1)} %get-tuple-element.36), channel_id=1, source_target_pairs={{0,1},{1,0},{8,9},{9,8},{16,17},{17,16},{24,25},{25,24},{2,3},{3,2... | collective-permute-start | bytes 786440 | tf_op jit(solution)/shard_map/ppermute | solution.py:413
  13.7 1.6 %collective-permute-start.8 = (bf16[8,18,8,128]{3,2,1,0:T(8,128)(2,1)S(1)}, bf16[8,18,8,128]{3,2,1,0:T(8,128)(2,1)S(1)}, u32[]{:S(2)}, u32[]{:S(2)}) collective-permute-start(bf16[8,18,8,128]{3,2,1,0:T(8,128)(2,1)S(1)} %constant_dynamic-update-slice_fusion.query_ref), channel_id=1, source_target_pairs={{0,2},{2,0},{4,6},{6,4},{1,3},{3,1},{5,7},{7,5},{8,10},{10,8},{12,... | collective-permute-start | bytes 884744 | tf_op jit(solution)/shard_map/ppermute | solution.py:465
  15.3 0.8 %dynamic-slice_bitcast_fusion.bias_ref = f32[1,128]{1,0:T(1,128)S(1)} fusion(f32[1024]{0:T(1024)} %param.13, s32[]{:T(128)S(6)} %select_n.4), kind=kLoop, calls=%fused_computation.11 | loop fusion | bytes 1028 | tf_op jit(solution)/shard_map/dynamic_slice | solution.py:467
  16.1 1.9 %collective-permute-start.9 = (bf16[8,18,8,128]{3,2,1,0:T(8,128)(2,1)S(1)}, bf16[8,18,8,128]{3,2,1,0:T(8,128)(2,1)S(1)}, u32[]{:S(2)}, u32[]{:S(2)}) collective-permute-start(bf16[8,18,8,128]{3,2,1,0:T(8,128)(2,1)S(1)} %constant_dynamic-update-slice_fusion.query_ref), channel_id=1, source_target_pairs={{2,4},{4,2},{3,5},{5,3},{10,12},{12,10},{11,13},{13,11},{18,20},{2... | collective-permute-start | bytes 884744 | tf_op jit(solution)/shard_map/ppermute | solution.py:464
  18.0 2.3 %collective-permute-done.7 = bf16[2,4,16,8,128]{4,3,2,1,0:T(8,128)(2,1)S(1)} collective-permute-done((bf16[2,4,16,8,128]{4,3,2,1,0:T(8,128)(2,1)S(1)}, bf16[2,4,16,8,128]{4,3,2,1,0:T(8,128)(2,1)S(1)}, u32[]{:S(2)}, u32[]{:S(2)}) %collective-permute-start.7) | collective-permute-done | bytes 262176 | tf_op jit(solution)/shard_map/ppermute | solution.py:413
  20.3 4.3 %collective-permute-done.6 = bf16[2,4,16,8,128]{4,3,2,1,0:T(8,128)(2,1)S(1)} collective-permute-done((bf16[2,4,16,8,128]{4,3,2,1,0:T(8,128)(2,1)S(1)}, bf16[2,4,16,8,128]{4,3,2,1,0:T(8,128)(2,1)S(1)}, u32[]{:S(2)}, u32[]{:S(2)}) %collective-permute-start.6) | collective-permute-done | bytes 262176 | tf_op jit(solution)/shard_map/ppermute | solution.py:413
  24.6 0.8 %collective-permute-done.5 = bf16[2,4,16,8,128]{4,3,2,1,0:T(8,128)(2,1)S(1)} collective-permute-done((bf16[2,4,16,8,128]{4,3,2,1,0:T(8,128)(2,1)S(1)}, bf16[2,4,16,8,128]{4,3,2,1,0:T(8,128)(2,1)S(1)}, u32[]{:S(2)}, u32[]{:S(2)}) %collective-permute-start.5) | collective-permute-done | bytes 262176 | tf_op jit(solution)/shard_map/ppermute | solution.py:413
  25.5 1.9 %shard_map.76 = bf16[9,16,8,128]{3,2,1,0:T(8,128)(2,1)S(1)} custom-call(bf16[8,18,8,128]{3,2,1,0:T(8,128)(2,1)S(1)} %collective-permute-done.8.first_ref.query_ref, bf16[8,4,16,8,128]{4,3,2,1,0:T(8,128)(2,1)S(1)} %pad_maximum_fusion.pairs_ref), custom_call_target="tpu_custom_call" | custom-call | flops 4294967296 | bytes 1048576 | tf_op jit(solution)/shard_map/pallas_call | solution.py:416
  27.4 1.6 %collective-permute-start.10 = (bf16[9,16,8,128]{3,2,1,0:T(8,128)(2,1)S(1)}, bf16[9,16,8,128]{3,2,1,0:T(8,128)(2,1)S(1)}, u32[]{:S(2)}, u32[]{:S(2)}) collective-permute-start(bf16[9,16,8,128]{3,2,1,0:T(8,128)(2,1)S(1)} %shard_map.76), channel_id=1, source_target_pairs={{0,2},{2,0},{4,6},{6,4},{1,3},{3,1},{5,7},{7,5},{8,10},{10,8},{12,... | collective-permute-start | bytes 884744 | tf_op jit(solution)/shard_map/ppermute | solution.py:476
  29.1 1.9 %shard_map.77 = bf16[9,16,8,128]{3,2,1,0:T(8,128)(2,1)S(1)} custom-call(bf16[8,18,8,128]{3,2,1,0:T(8,128)(2,1)S(1)} %collective-permute-done.9.second_ref.query_ref, bf16[8,4,16,8,128]{4,3,2,1,0:T(8,128)(2,1)S(1)} %pad_maximum_fusion.pairs_ref), custom_call_target="tpu_custom_call" | custom-call | flops 4294967296 | bytes 1048576 | tf_op jit(solution)/shard_map/pallas_call | solution.py:416
  31.0 1.9 %collective-permute-start.11 = (bf16[9,16,8,128]{3,2,1,0:T(8,128)(2,1)S(1)}, bf16[9,16,8,128]{3,2,1,0:T(8,128)(2,1)S(1)}, u32[]{:S(2)}, u32[]{:S(2)}) collective-permute-start(bf16[9,16,8,128]{3,2,1,0:T(8,128)(2,1)S(1)} %shard_map.77), channel_id=1, source_target_pairs={{2,4},{4,2},{3,5},{5,3},{10,12},{12,10},{11,13},{13,11},{18,20},{2... | collective-permute-start | bytes 884744 | tf_op jit(solution)/shard_map/ppermute | solution.py:474
  32.9 2.3 %shard_map.75 = (f32[8,128,128]{2,1,0:T(8,128)S(1)}, f32[8,128,128]{2,1,0:T(8,128)S(1)}, f32[8,128,128]{2,1,0:T(8,128)S(1)}) custom-call(f32[3,3,128]{2,1,0:T(4,128)S(1)} %constant_dynamic-slice_fusion.weight_ref, f32[1,128]{1,0:T(1,128)S(1)} %dynamic-slice_bitcast_fusion.bias_ref, bf16[8,18,8,128]{3,2,1,0:T(8,128)(2,1)S(1)} %constant_dynamic-update-slice_fusion.query_ref, ...), custom_call_target="tpu_custom_call" | custom-call | flops 4294967296 | bytes 1048576 | tf_op jit(solution)/shard_map/pallas_call | solution.py:416
  35.2 1.2 %collective-permute-done.10.first_ref = bf16[9,16,8,128]{3,2,1,0:T(8,128)(2,1)S(1)} collective-permute-done((bf16[9,16,8,128]{3,2,1,0:T(8,128)(2,1)S(1)}, bf16[9,16,8,128]{3,2,1,0:T(8,128)(2,1)S(1)}, u32[]{:S(2)}, u32[]{:S(2)}) %collective-permute-start.10) | collective-permute-done | bytes 294944 | tf_op jit(solution)/shard_map/ppermute | solution.py:476
  36.4 5.1 %collective-permute-done.11.second_ref = bf16[9,16,8,128]{3,2,1,0:T(8,128)(2,1)S(1)} collective-permute-done((bf16[9,16,8,128]{3,2,1,0:T(8,128)(2,1)S(1)}, bf16[9,16,8,128]{3,2,1,0:T(8,128)(2,1)S(1)}, u32[]{:S(2)}, u32[]{:S(2)}) %collective-permute-start.11) | collective-permute-done | bytes 294944 | tf_op jit(solution)/shard_map/ppermute | solution.py:474
  41.5 0.6 %shard_map.78 = bf16[8,16,8,128]{3,2,1,0:T(8,128)(2,1)S(1)} custom-call(f32[8,128,128]{2,1,0:T(8,128)S(1)} %get-tuple-element.30.part_ref, f32[8,128,128]{2,1,0:T(8,128)S(1)} %get-tuple-element.31.level_ref, f32[8,128,128]{2,1,0:T(8,128)S(1)} %get-tuple-element.32.conv_ref, bf16[9,16,8,128]{3,2,1,0:T(8,128)(2,1)S(1)} %collective-permute-done.10.first_ref, ...), custom_call_target="tpu_custom_call" | custom-call | flops 1073741824 | bytes 1048576 | tf_op jit(solution)/shard_map/pallas_call | solution.py:416
  42.2 1.3 %collective-permute-done.12.beside_ref = bf16[4,16,8,128]{3,2,1,0:T(8,128)(2,1)S(1)} collective-permute-done((bf16[4,16,8,128]{3,2,1,0:T(8,128)(2,1)S(1)}, bf16[4,16,8,128]{3,2,1,0:T(8,128)(2,1)S(1)}, u32[]{:S(2)}, u32[]{:S(2)}) %collective-permute-start.12) | collective-permute-done | bytes 131104 | tf_op jit(solution)/shard_map/ppermute | solution.py:413
  43.5 0.7 %collective-permute-start.13 = (bf16[2,16,8,128]{3,2,1,0:T(8,128)(2,1)S(1)}, bf16[2,16,8,128]{3,2,1,0:T(8,128)(2,1)S(1)}, u32[]{:S(2)}, u32[]{:S(2)}) collective-permute-start(bf16[2,16,8,128]{3,2,1,0:T(8,128)(2,1)S(1)} %pad_maximum_fusion.1), channel_id=1, source_target_pairs={{0,1},{1,0},{8,9},{9,8},{16,17},{17,16},{24,25},{25,24},{2,3},{3,2... | collective-permute-start | bytes 196616 | tf_op jit(solution)/shard_map/ppermute | solution.py:413
  44.2 1.5 %collective-permute-start.14 = (bf16[2,16,8,128]{3,2,1,0:T(8,128)(2,1)S(1)}, bf16[2,16,8,128]{3,2,1,0:T(8,128)(2,1)S(1)}, u32[]{:S(2)}, u32[]{:S(2)}) collective-permute-start(bf16[2,16,8,128]{3,2,1,0:T(8,128)(2,1)S(1)} %pad_maximum_fusion.2), channel_id=1, source_target_pairs={{0,16},{1,17},{8,24},{9,25},{16,0},{17,1},{24,8},{25,9},{2,18},{3,... | collective-permute-start | bytes 196616 | tf_op jit(solution)/shard_map/ppermute | solution.py:413
  45.8 1.4 %collective-permute-start.15 = (bf16[2,16,8,128]{3,2,1,0:T(8,128)(2,1)S(1)}, bf16[2,16,8,128]{3,2,1,0:T(8,128)(2,1)S(1)}, u32[]{:S(2)}, u32[]{:S(2)}) collective-permute-start(bf16[2,16,8,128]{3,2,1,0:T(8,128)(2,1)S(1)} %pad_maximum_fusion.3), channel_id=1, source_target_pairs={{0,17},{1,16},{8,25},{9,24},{16,1},{17,0},{24,9},{25,8},{2,19},{3,... | collective-permute-start | bytes 196616 | tf_op jit(solution)/shard_map/ppermute | solution.py:413
  47.2 0.6 %collective-permute-done.13.refs_0_ = bf16[2,16,8,128]{3,2,1,0:T(8,128)(2,1)S(1)} collective-permute-done((bf16[2,16,8,128]{3,2,1,0:T(8,128)(2,1)S(1)}, bf16[2,16,8,128]{3,2,1,0:T(8,128)(2,1)S(1)}, u32[]{:S(2)}, u32[]{:S(2)}) %collective-permute-start.13) | collective-permute-done | bytes 65568 | tf_op jit(solution)/shard_map/ppermute | solution.py:413
  47.9 1.3 %collective-permute-done.14.refs_1_ = bf16[2,16,8,128]{3,2,1,0:T(8,128)(2,1)S(1)} collective-permute-done((bf16[2,16,8,128]{3,2,1,0:T(8,128)(2,1)S(1)}, bf16[2,16,8,128]{3,2,1,0:T(8,128)(2,1)S(1)}, u32[]{:S(2)}, u32[]{:S(2)}) %collective-permute-start.14) | collective-permute-done | bytes 65568 | tf_op jit(solution)/shard_map/ppermute | solution.py:413
  49.2 1.9 %collective-permute-done.15.refs_2_ = bf16[2,16,8,128]{3,2,1,0:T(8,128)(2,1)S(1)} collective-permute-done((bf16[2,16,8,128]{3,2,1,0:T(8,128)(2,1)S(1)}, bf16[2,16,8,128]{3,2,1,0:T(8,128)(2,1)S(1)}, u32[]{:S(2)}, u32[]{:S(2)}) %collective-permute-start.15) | collective-permute-done | bytes 65568 | tf_op jit(solution)/shard_map/ppermute | solution.py:413
  51.0 0.8 %shard_map.79 = bf16[16,8,1024]{2,1,0:T(8,128)(2,1)} custom-call(bf16[4,16,8,128]{3,2,1,0:T(8,128)(2,1)S(1)} %get-tuple-element.41.same_ref, bf16[4,16,8,128]{3,2,1,0:T(8,128)(2,1)S(1)} %collective-permute-done.12.beside_ref, bf16[2,16,8,128]{3,2,1,0:T(8,128)(2,1)S(1)} %collective-permute-done.13.refs_0_, ...), custom_call_target="tpu_custom_call" | custom-call | bytes 1048576 | tf_op jit(solution)/shard_map/pallas_call | solution.py:416
  (21 shorter events, 0.5 us)
Async XLA Ops:
  0.0 16.1 %copy-start = (f32[3,3,1024]{2,1,0:T(4,128)S(1)}, f32[3,3,1024]{2,1,0:T(4,128)}, u32[]{:S(2)}) copy-start(f32[3,3,1024]{2,1,0:T(4,128)} %param.12) | copy-start | bytes 110596
  1.5 8.5 %collective-permute-start.4 = (bf16[4,4,16,8,128]{4,3,2,1,0:T(8,128)(2,1)S(1)}, bf16[4,4,16,8,128]{4,3,2,1,0:T(8,128)(2,1)S(1)}, u32[]{:S(2)}, u32[]{:S(2)}) collective-permute-start(bf16[4,4,16,8,128]{4,3,2,1,0:T(8,128)(2,1)S(1)} %get-tuple-element.26), channel_id=1, source_target_pairs={{0,8},{1,9},{8,0},{9,1},{16,24},{17,25},{24,16},{25,17},{2,10},{3,... | collective-permute-start | bytes 1572872 | tf_op jit(solution)/shard_map/ppermute | solution.py:413
  1.5 4.7 %collective-permute-start = (bf16[2,18,8,128]{3,2,1,0:T(8,128)(2,1)S(1)}, bf16[2,18,8,128]{3,2,1,0:T(8,128)(2,1)S(1)}, u32[]{:S(2)}, u32[]{:S(2)}) collective-permute-start(bf16[2,18,8,128]{3,2,1,0:T(8,128)(2,1)S(1)} %get-tuple-element.20), channel_id=1, source_target_pairs={{0,1},{1,0},{8,9},{9,8},{16,17},{17,16},{24,25},{25,24},{2,3},{3,2... | collective-permute-start | bytes 221192 | tf_op jit(solution)/shard_map/ppermute | solution.py:413
  3.1 4.8 %collective-permute-start.1 = (bf16[2,18,8,128]{3,2,1,0:T(8,128)(2,1)S(1)}, bf16[2,18,8,128]{3,2,1,0:T(8,128)(2,1)S(1)}, u32[]{:S(2)}, u32[]{:S(2)}) collective-permute-start(bf16[2,18,8,128]{3,2,1,0:T(8,128)(2,1)S(1)} %get-tuple-element.21), channel_id=1, source_target_pairs={{0,16},{1,17},{8,24},{9,25},{16,0},{17,1},{24,8},{25,9},{2,18},{3,... | collective-permute-start | bytes 221192 | tf_op jit(solution)/shard_map/ppermute | solution.py:413
  4.6 5.3 %collective-permute-start.2 = (bf16[2,18,8,128]{3,2,1,0:T(8,128)(2,1)S(1)}, bf16[2,18,8,128]{3,2,1,0:T(8,128)(2,1)S(1)}, u32[]{:S(2)}, u32[]{:S(2)}) collective-permute-start(bf16[2,18,8,128]{3,2,1,0:T(8,128)(2,1)S(1)} %get-tuple-element.22), channel_id=1, source_target_pairs={{0,17},{1,16},{8,25},{9,24},{16,1},{17,0},{24,9},{25,8},{2,19},{3,... | collective-permute-start | bytes 221192 | tf_op jit(solution)/shard_map/ppermute | solution.py:413
  9.9 3.7 %collective-permute-start.3 = (bf16[4,18,8,128]{3,2,1,0:T(8,128)(2,1)S(1)}, bf16[4,18,8,128]{3,2,1,0:T(8,128)(2,1)S(1)}, u32[]{:S(2)}, u32[]{:S(2)}) collective-permute-start(bf16[4,18,8,128]{3,2,1,0:T(8,128)(2,1)S(1)} %get-tuple-element.24), channel_id=1, source_target_pairs={{0,8},{1,9},{8,0},{9,1},{16,24},{17,25},{24,16},{25,17},{2,10},{3,... | collective-permute-start | bytes 442376 | tf_op jit(solution)/shard_map/ppermute | solution.py:413
  10.1 10.2 %collective-permute-start.7 = (bf16[2,4,16,8,128]{4,3,2,1,0:T(8,128)(2,1)S(1)}, bf16[2,4,16,8,128]{4,3,2,1,0:T(8,128)(2,1)S(1)}, u32[]{:S(2)}, u32[]{:S(2)}) collective-permute-start(bf16[2,4,16,8,128]{4,3,2,1,0:T(8,128)(2,1)S(1)} %get-tuple-element.34), channel_id=1, source_target_pairs={{0,17},{1,16},{8,25},{9,24},{16,1},{17,0},{24,9},{25,8},{2,19},{3,... | collective-permute-start | bytes 786440 | tf_op jit(solution)/shard_map/ppermute | solution.py:413
  11.7 12.9 %collective-permute-start.6 = (bf16[2,4,16,8,128]{4,3,2,1,0:T(8,128)(2,1)S(1)}, bf16[2,4,16,8,128]{4,3,2,1,0:T(8,128)(2,1)S(1)}, u32[]{:S(2)}, u32[]{:S(2)}) collective-permute-start(bf16[2,4,16,8,128]{4,3,2,1,0:T(8,128)(2,1)S(1)} %get-tuple-element.35), channel_id=1, source_target_pairs={{0,16},{1,17},{8,24},{9,25},{16,0},{17,1},{24,8},{25,9},{2,18},{3,... | collective-permute-start | bytes 786440 | tf_op jit(solution)/shard_map/ppermute | solution.py:413
  12.3 13.1 %collective-permute-start.5 = (bf16[2,4,16,8,128]{4,3,2,1,0:T(8,128)(2,1)S(1)}, bf16[2,4,16,8,128]{4,3,2,1,0:T(8,128)(2,1)S(1)}, u32[]{:S(2)}, u32[]{:S(2)}) collective-permute-start(bf16[2,4,16,8,128]{4,3,2,1,0:T(8,128)(2,1)S(1)} %get-tuple-element.36), channel_id=1, source_target_pairs={{0,1},{1,0},{8,9},{9,8},{16,17},{17,16},{24,25},{25,24},{2,3},{3,2... | collective-permute-start | bytes 786440 | tf_op jit(solution)/shard_map/ppermute | solution.py:413
  13.7 11.8 %collective-permute-start.8 = (bf16[8,18,8,128]{3,2,1,0:T(8,128)(2,1)S(1)}, bf16[8,18,8,128]{3,2,1,0:T(8,128)(2,1)S(1)}, u32[]{:S(2)}, u32[]{:S(2)}) collective-permute-start(bf16[8,18,8,128]{3,2,1,0:T(8,128)(2,1)S(1)} %constant_dynamic-update-slice_fusion.query_ref), channel_id=1, source_target_pairs={{0,2},{2,0},{4,6},{6,4},{1,3},{3,1},{5,7},{7,5},{8,10},{10,8},{12,... | collective-permute-start | bytes 884744 | tf_op jit(solution)/shard_map/ppermute | solution.py:465
  16.1 13.0 %collective-permute-start.9 = (bf16[8,18,8,128]{3,2,1,0:T(8,128)(2,1)S(1)}, bf16[8,18,8,128]{3,2,1,0:T(8,128)(2,1)S(1)}, u32[]{:S(2)}, u32[]{:S(2)}) collective-permute-start(bf16[8,18,8,128]{3,2,1,0:T(8,128)(2,1)S(1)} %constant_dynamic-update-slice_fusion.query_ref), channel_id=1, source_target_pairs={{2,4},{4,2},{3,5},{5,3},{10,12},{12,10},{11,13},{13,11},{18,20},{2... | collective-permute-start | bytes 884744 | tf_op jit(solution)/shard_map/ppermute | solution.py:464
  27.4 9.0 %collective-permute-start.10 = (bf16[9,16,8,128]{3,2,1,0:T(8,128)(2,1)S(1)}, bf16[9,16,8,128]{3,2,1,0:T(8,128)(2,1)S(1)}, u32[]{:S(2)}, u32[]{:S(2)}) collective-permute-start(bf16[9,16,8,128]{3,2,1,0:T(8,128)(2,1)S(1)} %shard_map.76), channel_id=1, source_target_pairs={{0,2},{2,0},{4,6},{6,4},{1,3},{3,1},{5,7},{7,5},{8,10},{10,8},{12,... | collective-permute-start | bytes 884744 | tf_op jit(solution)/shard_map/ppermute | solution.py:476
  31.0 10.5 %collective-permute-start.11 = (bf16[9,16,8,128]{3,2,1,0:T(8,128)(2,1)S(1)}, bf16[9,16,8,128]{3,2,1,0:T(8,128)(2,1)S(1)}, u32[]{:S(2)}, u32[]{:S(2)}) collective-permute-start(bf16[9,16,8,128]{3,2,1,0:T(8,128)(2,1)S(1)} %shard_map.77), channel_id=1, source_target_pairs={{2,4},{4,2},{3,5},{5,3},{10,12},{12,10},{11,13},{13,11},{18,20},{2... | collective-permute-start | bytes 884744 | tf_op jit(solution)/shard_map/ppermute | solution.py:474
  42.1 1.4 %collective-permute-start.12 = (bf16[4,16,8,128]{3,2,1,0:T(8,128)(2,1)S(1)}, bf16[4,16,8,128]{3,2,1,0:T(8,128)(2,1)S(1)}, u32[]{:S(2)}, u32[]{:S(2)}) collective-permute-start(bf16[4,16,8,128]{3,2,1,0:T(8,128)(2,1)S(1)} %get-tuple-element.40), channel_id=1, source_target_pairs={{0,8},{1,9},{8,0},{9,1},{16,24},{17,25},{24,16},{25,17},{2,10},{3,... | collective-permute-start | bytes 393224 | tf_op jit(solution)/shard_map/ppermute | solution.py:413
  43.5 4.3 %collective-permute-start.13 = (bf16[2,16,8,128]{3,2,1,0:T(8,128)(2,1)S(1)}, bf16[2,16,8,128]{3,2,1,0:T(8,128)(2,1)S(1)}, u32[]{:S(2)}, u32[]{:S(2)}) collective-permute-start(bf16[2,16,8,128]{3,2,1,0:T(8,128)(2,1)S(1)} %pad_maximum_fusion.1), channel_id=1, source_target_pairs={{0,1},{1,0},{8,9},{9,8},{16,17},{17,16},{24,25},{25,24},{2,3},{3,2... | collective-permute-start | bytes 196616 | tf_op jit(solution)/shard_map/ppermute | solution.py:413
  44.2 4.9 %collective-permute-start.14 = (bf16[2,16,8,128]{3,2,1,0:T(8,128)(2,1)S(1)}, bf16[2,16,8,128]{3,2,1,0:T(8,128)(2,1)S(1)}, u32[]{:S(2)}, u32[]{:S(2)}) collective-permute-start(bf16[2,16,8,128]{3,2,1,0:T(8,128)(2,1)S(1)} %pad_maximum_fusion.2), channel_id=1, source_target_pairs={{0,16},{1,17},{8,24},{9,25},{16,0},{17,1},{24,8},{25,9},{2,18},{3,... | collective-permute-start | bytes 196616 | tf_op jit(solution)/shard_map/ppermute | solution.py:413
  45.8 5.2 %collective-permute-start.15 = (bf16[2,16,8,128]{3,2,1,0:T(8,128)(2,1)S(1)}, bf16[2,16,8,128]{3,2,1,0:T(8,128)(2,1)S(1)}, u32[]{:S(2)}, u32[]{:S(2)}) collective-permute-start(bf16[2,16,8,128]{3,2,1,0:T(8,128)(2,1)S(1)} %pad_maximum_fusion.3), channel_id=1, source_target_pairs={{0,17},{1,16},{8,25},{9,24},{16,1},{17,0},{24,9},{25,8},{2,19},{3,... | collective-permute-start | bytes 196616 | tf_op jit(solution)/shard_map/ppermute | solution.py:413

commit v13 on v12

--- a/solution.py
+++ b/solution.py
@@ -297,15 +297,18 @@
         tiles.append((row, 1 - near, [(near, None), (1 - near, allowed)]))
         tiles.append((row, near, [(near, allowed)]))
     size, count = window.size, grid[0] * grid[1]
+    half = count // 2
     lane = lax.broadcasted_iota(jnp.int32, (size, HD), 1)
     levels = jnp.zeros((size, HD), jnp.float32)
     for index, part, level in window.attend(tiles):
-        out_ref[index] = part.reshape(tile + (HD,)).astype(jnp.bfloat16)
-        levels = jnp.where(lane == index, level, levels)
+        beside, order = place_of(grid[1], index)
+        place = (1 - beside) * (half + 1) + order
+        out_ref[place] = part.reshape(tile + (HD,)).astype(jnp.bfloat16)
+        levels = jnp.where(lane == beside * half + order, level, levels)
     high = levels.astype(jnp.bfloat16).astype(jnp.float32)
     middle = (levels - high).astype(jnp.bfloat16).astype(jnp.float32)
     packed = high + pltpu.roll(middle, count, 1) + pltpu.roll(levels - high - middle, 2 * count, 1)
-    out_ref[count] = packed.reshape(tile + (HD,)).astype(jnp.bfloat16)
+    out_ref[half] = packed.reshape(tile + (HD,)).astype(jnp.bfloat16)
 
 
 def own_kernel(
@@ -321,27 +324,30 @@
         conv_ref[index] = conv.reshape(window.size, HD)
 
 
-def join_kernel(grid, tile, far, part_ref, level_ref, conv_ref, first_ref, second_ref, out_ref):
-    size, count = tile[0] * tile[1], grid[0] * grid[1]
-    visits = (first_ref, second_ref)
+def join_kernel(grid, tile, far, flips, beside, part_ref, level_ref, conv_ref, first_ref, level_first_ref, second_ref, out_ref):
+    size, count, side = tile[0] * tile[1], grid[0] * grid[1], grid[1]
+    half = count // 2
     place = lax.axis_index("far")
     even = lax.rem(place, 2) == 0
     present = [~even | (place < far - 1), jnp.where(even, place > 0, place < far - 1)]
     packed = []
-    for there, ref in zip(present, visits):
-        pack = ref[count].reshape(size, HD).astype(jnp.float32)
+    for there, ref in zip(present, (level_first_ref, second_ref)):
+        pack = ref[half].reshape(size, HD).astype(jnp.float32)
         level = pack + pltpu.roll(pack, HD - count, 1) + pltpu.roll(pack, HD - 2 * count, 1)
         packed.append(jnp.where(there, level, NEG))
-    for index in range(count):
+    for order, flip in enumerate(flips):
+        index = position(side) ^ (flip ^ (side if beside else 0))
+        lane = order + (half if beside else 0)
+        visits = [first_ref[order], second_ref[order + (0 if beside else half + 1)]]
         levels = [level_ref[index]]
         parts = [part_ref[index]]
-        for ref, pack in zip(visits, packed):
-            parts.append(ref[index].reshape(size, HD).astype(jnp.float32))
-            levels.append(jnp.broadcast_to(pack[:, index : index + 1], (size, HD)))
+        for visit, pack in zip(visits, packed):
+            parts.append(visit.reshape(size, HD).astype(jnp.float32))
+            levels.append(jnp.broadcast_to(pack[:, lane : lane + 1], (size, HD)))
         top = jnp.maximum(jnp.maximum(levels[0], levels[1]), levels[2])
         shares = [jnp.exp2(level - top) for level in levels]
         mixed = sum(share * part for share, part in zip(shares, parts)) / sum(shares)
-        out_ref[slot_of(grid[1], index)] = (mixed + conv_ref[index]).reshape(tile + (HD,)).astype(jnp.bfloat16)
+        out_ref[order] = (mixed + conv_ref[index]).reshape(tile + (HD,)).astype(jnp.bfloat16)
 
 
 def lanes(head):
@@ -460,8 +466,10 @@
     half = jax.ShapeDtypeStruct((len(flips),) + query_buffer.shape[1:], jnp.bfloat16)
     mine, forward = call(split_kernel, [half, half], SMALL, 0, *got)
     forward = swap(forward, side)
+    second_a = lax.ppermute(mine, "far", second)
+    second_b = lax.ppermute(forward, "far", second)
     query = jnp.concatenate([mine, forward], axis=0)
-    query_second = lax.ppermute(query, "far", second)
+    query_second = jnp.concatenate([second_a, second_b], axis=0)
     query_first = lax.ppermute(query, "far", first)
     weight = lax.dynamic_slice_in_dim(conv_weight, me * HD, HD, 2)
     bias = lax.dynamic_slice_in_dim(conv_bias.reshape(1, channels), me * HD, HD, 1)
@@ -473,15 +481,21 @@
     part = visit(query_second, False)
     home_second = lax.ppermute(part, "far", second)
     part = visit(query_first, True)
-    home_first = lax.ppermute(part, "far", first)
+    half = len(flips) + 1
+    home_first_a = lax.ppermute(part[:half], "far", first)
+    home_first_b = lax.ppermute(part[half:], "far", first)
     part = jax.ShapeDtypeStruct((heads, size, HD), jnp.float32)
     kernel = functools.partial(own_kernel, grid, tile)
     own = call(kernel, [part] * 3, LIMIT, 4, weight, bias, query, pairs, query_first, query_second)
-    kernel = functools.partial(join_kernel, grid, tile, far)
-    result = jax.ShapeDtypeStruct((heads,) + block, jnp.bfloat16)
-    result = call(kernel, result, LIMIT, 1, *own, home_first, home_second)
-    same, other = result[: len(flips)], result[len(flips) :]
+    result = jax.ShapeDtypeStruct((len(flips),) + block, jnp.bfloat16)
+
+    def join(beside, tiles):
+        kernel = functools.partial(join_kernel, grid, tile, far, flips, beside)
+        return call(kernel, result, LIMIT, 1, *own, tiles, home_first_a, home_second)
+
+    other = join(True, home_first_a)
     received = swap(other, side)
+    same = join(False, home_first_b)
     got = []
     for i in range(1, len(flips)):
         got.append(swap(jnp.stack([same[i], received[i]]), flips[i]))

time: 52 us -> 58 us (1.12)
  starting transfers between devices: 18.1 us -> 21.3 us
  waiting for transfers between devices: 23.5 us -> 26.1 us
    ppermute x2 -> x4, starting transfers between devices: 3.54 us -> 7.91 us  [the longest x1 3.48 us: head_step(): second_b = lax.ppermute(forward, 'far', second)]
    ppermute x12, waiting for transfers between devices: 17.3 us -> 18.9 us  [swap(): return lax.ppermute(x, axes, [(s, s ^ flip) for s in range(heads)])]
    ppermute x1, starting transfers between devices: 1.64 us -> 0.07 us  [head_step(): query_first = lax.ppermute(query, 'far', first)]
    ppermute x2 -> x4, waiting for transfers between devices: 1.21 us -> 1.96 us  [the longest x1 1.63 us: head_step(): second_b = lax.ppermute(forward, 'far', second)]
    pallas_call x7 -> x8, Pallas kernels: 8.91 us -> 9.07 us  [call(): pl.pallas_call(kernel, out_shape=out_shape, in_specs=[space[0]] * len(ope...]
  transfers between devices with their start and end apart: 16 -> 18, of which waited for: 12 -> 13; matrix products, arithmetic and copies ran while one was open for 2% -> 2% of each run, Pallas kernels for 12% -> 9%
where the time goes in v13:
time: 58 us; the launch traced here: 57.8 us
  waiting for transfers between devices  26.1 us (45%)
  starting transfers between devices  21.3 us (37%)
  Pallas kernels  9.07 us (16%)
  local copies, waits for them, and re-layouts  0.95 us (2%)
    ppermute x12, waiting for transfers between devices, swap(): return lax.ppermute(x, axes, [(s, s ^ flip) for s in range(heads)])  18.9 us
    ppermute x12, starting transfers between devices, swap(): return lax.ppermute(x, axes, [(s, s ^ flip) for s in range(heads)])  11 us
    pallas_call x8, Pallas kernels, call(): pl.pallas_call(kernel, out_shape=out_shape, in_specs=[space[0]] * len(ope...  9.07 us
    ppermute x1, waiting for transfers between devices, head_step(): home_second = lax.ppermute(part, 'far', second)  5.24 us
    ppermute x1, starting transfers between devices, head_step(): second_b = lax.ppermute(forward, 'far', second)  3.48 us
    ppermute x1, starting transfers between devices, head_step(): home_second = lax.ppermute(part, 'far', second)  2.35 us
    ppermute x1, starting transfers between devices, head_step(): second_a = lax.ppermute(mine, 'far', second)  2.35 us
    ppermute x1, starting transfers between devices, head_step(): home_first_a = lax.ppermute(part[:half], 'far', first)  2.01 us
  transfers between devices with their start and end apart: 18, of which 13 were waited for; matrix products, arithmetic and copies ran while one was open for 2% of the time, Pallas kernels for 9%

profile of v13, /device:TPU:16, one launch (start us, length us, event | category | flops | bytes accessed | tf_op | source)
XLA Modules:
  0.0 57.8 jit_solution(15830549936520011773)
XLA Ops:
  0.0 1.4 %shard_map.73 = (bf16[2,18,8,128]{3,2,1,0:T(8,128)(2,1)S(1)}, bf16[2,18,8,128]{3,2,1,0:T(8,128)(2,1)S(1)}, bf16[2,18,8,128]{3,2,1,0:T(8,128)(2,1)S(1)}, bf16[2,1...) custom-call(bf16[16,8,1024]{2,1,0:T(8,128)(2,1)} %refs_0_.1, ...), custom_call_target="tpu_custom_call" | custom-call | bytes 1048576 | tf_op jit(solution)/shard_map/pallas_call | solution.py:422
  1.5 1.6 %collective-permute-start = (bf16[2,18,8,128]{3,2,1,0:T(8,128)(2,1)S(1)}, bf16[2,18,8,128]{3,2,1,0:T(8,128)(2,1)S(1)}, u32[]{:S(2)}, u32[]{:S(2)}) collective-permute-start(bf16[2,18,8,128]{3,2,1,0:T(8,128)(2,1)S(1)} %get-tuple-element.20), channel_id=1, source_target_pairs={{0,1},{1,0},{8,9},{9,8},{16,17},{17,16},{24,25},{25,24},{2,3},{3,2... | collective-permute-start | bytes 221192 | tf_op jit(solution)/shard_map/ppermute | solution.py:419
  3.1 1.5 %collective-permute-start.1 = (bf16[2,18,8,128]{3,2,1,0:T(8,128)(2,1)S(1)}, bf16[2,18,8,128]{3,2,1,0:T(8,128)(2,1)S(1)}, u32[]{:S(2)}, u32[]{:S(2)}) collective-permute-start(bf16[2,18,8,128]{3,2,1,0:T(8,128)(2,1)S(1)} %get-tuple-element.21), channel_id=1, source_target_pairs={{0,16},{1,17},{8,24},{9,25},{16,0},{17,1},{24,8},{25,9},{2,18},{3,... | collective-permute-start | bytes 221192 | tf_op jit(solution)/shard_map/ppermute | solution.py:419
  4.6 0.5 collective-permute-start.2
  5.1 1.1 %collective-permute-done.refs_1_ = bf16[2,18,8,128]{3,2,1,0:T(8,128)(2,1)S(1)} collective-permute-done((bf16[2,18,8,128]{3,2,1,0:T(8,128)(2,1)S(1)}, bf16[2,18,8,128]{3,2,1,0:T(8,128)(2,1)S(1)}, u32[]{:S(2)}, u32[]{:S(2)}) %collective-permute-start) | collective-permute-done | bytes 73760 | tf_op jit(solution)/shard_map/ppermute | solution.py:419
  6.2 1.7 %collective-permute-done.1.refs_2_ = bf16[2,18,8,128]{3,2,1,0:T(8,128)(2,1)S(1)} collective-permute-done((bf16[2,18,8,128]{3,2,1,0:T(8,128)(2,1)S(1)}, bf16[2,18,8,128]{3,2,1,0:T(8,128)(2,1)S(1)}, u32[]{:S(2)}, u32[]{:S(2)}) %collective-permute-start.1) | collective-permute-done | bytes 73760 | tf_op jit(solution)/shard_map/ppermute | solution.py:419
  7.9 1.9 %collective-permute-done.2.refs_3_ = bf16[2,18,8,128]{3,2,1,0:T(8,128)(2,1)S(1)} collective-permute-done((bf16[2,18,8,128]{3,2,1,0:T(8,128)(2,1)S(1)}, bf16[2,18,8,128]{3,2,1,0:T(8,128)(2,1)S(1)}, u32[]{:S(2)}, u32[]{:S(2)}) %collective-permute-start.2) | collective-permute-done | bytes 73760 | tf_op jit(solution)/shard_map/ppermute | solution.py:419
  10.0 0.8 %dynamic-slice_bitcast_fusion.bias_ref = f32[1,128]{1,0:T(1,128)S(1)} fusion(f32[1024]{0:T(1024)} %param.13, s32[]{:T(128)S(6)} %select_n.4), kind=kLoop, calls=%fused_computation.13 | loop fusion | bytes 1028 | tf_op jit(solution)/shard_map/dynamic_slice | solution.py:475
  10.7 2.3 %collective-permute-start.9 = (bf16[4,18,8,128]{3,2,1,0:T(8,128)(2,1)S(1)}, bf16[4,18,8,128]{3,2,1,0:T(8,128)(2,1)S(1)}, u32[]{:S(2)}, u32[]{:S(2)}) collective-permute-start(bf16[4,18,8,128]{3,2,1,0:T(8,128)(2,1)S(1)} %get-tuple-element.23), channel_id=1, source_target_pairs={{2,4},{4,2},{3,5},{5,3},{10,12},{12,10},{11,13},{13,11},{18,20},{2... | collective-permute-start | bytes 442376 | tf_op jit(solution)/shard_map/ppermute | solution.py:469
  13.1 3.5 %collective-permute-start.10 = (bf16[4,18,8,128]{3,2,1,0:T(8,128)(2,1)S(1)}, bf16[4,18,8,128]{3,2,1,0:T(8,128)(2,1)S(1)}, u32[]{:S(2)}, u32[]{:S(2)}) collective-permute-start(bf16[4,18,8,128]{3,2,1,0:T(8,128)(2,1)S(1)} %collective-permute-done.3), channel_id=1, source_target_pairs={{2,4},{4,2},{3,5},{5,3},{10,12},{12,10},{11,13},{13,11},{18,20},{2... | collective-permute-start | bytes 442376 | tf_op jit(solution)/shard_map/ppermute | solution.py:470
  16.7 1.6 %collective-permute-start.7 = (bf16[2,4,16,8,128]{4,3,2,1,0:T(8,128)(2,1)S(1)}, bf16[2,4,16,8,128]{4,3,2,1,0:T(8,128)(2,1)S(1)}, u32[]{:S(2)}, u32[]{:S(2)}) collective-permute-start(bf16[2,4,16,8,128]{4,3,2,1,0:T(8,128)(2,1)S(1)} %get-tuple-element.34), channel_id=1, source_target_pairs={{0,17},{1,16},{8,25},{9,24},{16,1},{17,0},{24,9},{25,8},{2,19},{3,... | collective-permute-start | bytes 786440 | tf_op jit(solution)/shard_map/ppermute | solution.py:419
  18.3 0.6 collective-permute-start.6
  18.9 1.4 %collective-permute-start.5 = (bf16[2,4,16,8,128]{4,3,2,1,0:T(8,128)(2,1)S(1)}, bf16[2,4,16,8,128]{4,3,2,1,0:T(8,128)(2,1)S(1)}, u32[]{:S(2)}, u32[]{:S(2)}) collective-permute-start(bf16[2,4,16,8,128]{4,3,2,1,0:T(8,128)(2,1)S(1)} %get-tuple-element.36), channel_id=1, source_target_pairs={{0,1},{1,0},{8,9},{9,8},{16,17},{17,16},{24,25},{25,24},{2,3},{3,2... | collective-permute-start | bytes 786440 | tf_op jit(solution)/shard_map/ppermute | solution.py:419
  20.4 1.6 %collective-permute-done.10 = bf16[4,18,8,128]{3,2,1,0:T(8,128)(2,1)S(1)} collective-permute-done((bf16[4,18,8,128]{3,2,1,0:T(8,128)(2,1)S(1)}, bf16[4,18,8,128]{3,2,1,0:T(8,128)(2,1)S(1)}, u32[]{:S(2)}, u32[]{:S(2)}) %collective-permute-start.10) | collective-permute-done | bytes 147488 | tf_op jit(solution)/shard_map/ppermute | solution.py:470
  22.0 4.8 %collective-permute-done.7 = bf16[2,4,16,8,128]{4,3,2,1,0:T(8,128)(2,1)S(1)} collective-permute-done((bf16[2,4,16,8,128]{4,3,2,1,0:T(8,128)(2,1)S(1)}, bf16[2,4,16,8,128]{4,3,2,1,0:T(8,128)(2,1)S(1)}, u32[]{:S(2)}, u32[]{:S(2)}) %collective-permute-start.7) | collective-permute-done | bytes 262176 | tf_op jit(solution)/shard_map/ppermute | solution.py:419
  26.9 3.8 %collective-permute-done.6 = bf16[2,4,16,8,128]{4,3,2,1,0:T(8,128)(2,1)S(1)} collective-permute-done((bf16[2,4,16,8,128]{4,3,2,1,0:T(8,128)(2,1)S(1)}, bf16[2,4,16,8,128]{4,3,2,1,0:T(8,128)(2,1)S(1)}, u32[]{:S(2)}, u32[]{:S(2)}) %collective-permute-start.6) | collective-permute-done | bytes 262176 | tf_op jit(solution)/shard_map/ppermute | solution.py:419
  30.7 0.8 %collective-permute-done.5 = bf16[2,4,16,8,128]{4,3,2,1,0:T(8,128)(2,1)S(1)} collective-permute-done((bf16[2,4,16,8,128]{4,3,2,1,0:T(8,128)(2,1)S(1)}, bf16[2,4,16,8,128]{4,3,2,1,0:T(8,128)(2,1)S(1)}, u32[]{:S(2)}, u32[]{:S(2)}) %collective-permute-start.5) | collective-permute-done | bytes 262176 | tf_op jit(solution)/shard_map/ppermute | solution.py:419
  31.6 1.9 %shard_map.76 = bf16[9,16,8,128]{3,2,1,0:T(8,128)(2,1)S(1)} custom-call(bf16[8,18,8,128]{3,2,1,0:T(8,128)(2,1)S(1)} %collective-permute-done.8.first_ref.query_ref, bf16[8,4,16,8,128]{4,3,2,1,0:T(8,128)(2,1)S(1)} %pad_maximum_fusion.pairs_ref), custom_call_target="tpu_custom_call" | custom-call | flops 4294967296 | bytes 1048576 | tf_op jit(solution)/shard_map/pallas_call | solution.py:422
  33.6 2.0 %collective-permute-start.12 = (bf16[5,16,8,128]{3,2,1,0:T(8,128)(2,1)S(1)}, bf16[5,16,8,128]{3,2,1,0:T(8,128)(2,1)S(1)}, u32[]{:S(2)}, u32[]{:S(2)}) collective-permute-start(bf16[5,16,8,128]{3,2,1,0:T(8,128)(2,1)S(1)} %slice.53), channel_id=1, source_target_pairs={{0,2},{2,0},{4,6},{6,4},{1,3},{3,1},{5,7},{7,5},{8,10},{10,8},{12,... | collective-permute-start | bytes 491528 | tf_op jit(solution)/shard_map/ppermute | solution.py:485
  35.6 1.9 %shard_map.77 = bf16[9,16,8,128]{3,2,1,0:T(8,128)(2,1)S(1)} custom-call(bf16[8,18,8,128]{3,2,1,0:T(8,128)(2,1)S(1)} %constant_dynamic-update-slice_fusion.2.second_ref.query_ref, bf16[8,4,16,8,128]{4,3,2,1,0:T(8,128)(2,1)S(1)} %pad_maximum_fusion.pairs_ref), custom_call_target="tpu_custom_call" | custom-call | flops 4294967296 | bytes 1048576 | tf_op jit(solution)/shard_map/pallas_call | solution.py:422
  37.5 2.3 %collective-permute-start.13 = (bf16[9,16,8,128]{3,2,1,0:T(8,128)(2,1)S(1)}, bf16[9,16,8,128]{3,2,1,0:T(8,128)(2,1)S(1)}, u32[]{:S(2)}, u32[]{:S(2)}) collective-permute-start(bf16[9,16,8,128]{3,2,1,0:T(8,128)(2,1)S(1)} %shard_map.77), channel_id=1, source_target_pairs={{2,4},{4,2},{3,5},{5,3},{10,12},{12,10},{11,13},{13,11},{18,20},{2... | collective-permute-start | bytes 884744 | tf_op jit(solution)/shard_map/ppermute | solution.py:482
  39.9 2.3 %shard_map.75 = (f32[8,128,128]{2,1,0:T(8,128)S(1)}, f32[8,128,128]{2,1,0:T(8,128)S(1)}, f32[8,128,128]{2,1,0:T(8,128)S(1)}) custom-call(f32[3,3,128]{2,1,0:T(4,128)S(1)} %constant_dynamic-slice_fusion.weight_ref, f32[1,128]{1,0:T(1,128)S(1)} %dynamic-slice_bitcast_fusion.bias_ref, bf16[8,18,8,128]{3,2,1,0:T(8,128)(2,1)S(1)} %constant_dynamic-update-slice_fusion.query_ref, ...), custom_call_target="tpu_custom_call" | custom-call | flops 4294967296 | bytes 1048576 | tf_op jit(solution)/shard_map/pallas_call | solution.py:422
  42.5 5.2 %collective-permute-done.13.second_ref = bf16[9,16,8,128]{3,2,1,0:T(8,128)(2,1)S(1)} collective-permute-done((bf16[9,16,8,128]{3,2,1,0:T(8,128)(2,1)S(1)}, bf16[9,16,8,128]{3,2,1,0:T(8,128)(2,1)S(1)}, u32[]{:S(2)}, u32[]{:S(2)}) %collective-permute-start.13) | collective-permute-done | bytes 294944 | tf_op jit(solution)/shard_map/ppermute | solution.py:482
  48.2 0.4 shard_map.78.same_ref
  48.6 1.0 %collective-permute-done.14.beside_ref = bf16[4,16,8,128]{3,2,1,0:T(8,128)(2,1)S(1)} collective-permute-done((bf16[4,16,8,128]{3,2,1,0:T(8,128)(2,1)S(1)}, bf16[4,16,8,128]{3,2,1,0:T(8,128)(2,1)S(1)}, u32[]{:S(2)}, u32[]{:S(2)}) %collective-permute-start.14) | collective-permute-done | bytes 131104 | tf_op jit(solution)/shard_map/ppermute | solution.py:419
  49.6 0.7 %collective-permute-start.15 = (bf16[2,16,8,128]{3,2,1,0:T(8,128)(2,1)S(1)}, bf16[2,16,8,128]{3,2,1,0:T(8,128)(2,1)S(1)}, u32[]{:S(2)}, u32[]{:S(2)}) collective-permute-start(bf16[2,16,8,128]{3,2,1,0:T(8,128)(2,1)S(1)} %pad_maximum_fusion.1), channel_id=1, source_target_pairs={{0,1},{1,0},{8,9},{9,8},{16,17},{17,16},{24,25},{25,24},{2,3},{3,2... | collective-permute-start | bytes 196616 | tf_op jit(solution)/shard_map/ppermute | solution.py:419
  50.3 1.5 %collective-permute-start.16 = (bf16[2,16,8,128]{3,2,1,0:T(8,128)(2,1)S(1)}, bf16[2,16,8,128]{3,2,1,0:T(8,128)(2,1)S(1)}, u32[]{:S(2)}, u32[]{:S(2)}) collective-permute-start(bf16[2,16,8,128]{3,2,1,0:T(8,128)(2,1)S(1)} %pad_maximum_fusion.2), channel_id=1, source_target_pairs={{0,16},{1,17},{8,24},{9,25},{16,0},{17,1},{24,8},{25,9},{2,18},{3,... | collective-permute-start | bytes 196616 | tf_op jit(solution)/shard_map/ppermute | solution.py:419
  51.8 1.4 %collective-permute-start.17 = (bf16[2,16,8,128]{3,2,1,0:T(8,128)(2,1)S(1)}, bf16[2,16,8,128]{3,2,1,0:T(8,128)(2,1)S(1)}, u32[]{:S(2)}, u32[]{:S(2)}) collective-permute-start(bf16[2,16,8,128]{3,2,1,0:T(8,128)(2,1)S(1)} %pad_maximum_fusion.3), channel_id=1, source_target_pairs={{0,17},{1,16},{8,25},{9,24},{16,1},{17,0},{24,9},{25,8},{2,19},{3,... | collective-permute-start | bytes 196616 | tf_op jit(solution)/shard_map/ppermute | solution.py:419
  53.3 0.6 %collective-permute-done.15.refs_0_ = bf16[2,16,8,128]{3,2,1,0:T(8,128)(2,1)S(1)} collective-permute-done((bf16[2,16,8,128]{3,2,1,0:T(8,128)(2,1)S(1)}, bf16[2,16,8,128]{3,2,1,0:T(8,128)(2,1)S(1)}, u32[]{:S(2)}, u32[]{:S(2)}) %collective-permute-start.15) | collective-permute-done | bytes 65568 | tf_op jit(solution)/shard_map/ppermute | solution.py:419
  53.9 1.3 %collective-permute-done.16.refs_1_ = bf16[2,16,8,128]{3,2,1,0:T(8,128)(2,1)S(1)} collective-permute-done((bf16[2,16,8,128]{3,2,1,0:T(8,128)(2,1)S(1)}, bf16[2,16,8,128]{3,2,1,0:T(8,128)(2,1)S(1)}, u32[]{:S(2)}, u32[]{:S(2)}) %collective-permute-start.16) | collective-permute-done | bytes 65568 | tf_op jit(solution)/shard_map/ppermute | solution.py:419
  55.2 1.9 %collective-permute-done.17.refs_2_ = bf16[2,16,8,128]{3,2,1,0:T(8,128)(2,1)S(1)} collective-permute-done((bf16[2,16,8,128]{3,2,1,0:T(8,128)(2,1)S(1)}, bf16[2,16,8,128]{3,2,1,0:T(8,128)(2,1)S(1)}, u32[]{:S(2)}, u32[]{:S(2)}) %collective-permute-start.17) | collective-permute-done | bytes 65568 | tf_op jit(solution)/shard_map/ppermute | solution.py:419
  57.0 0.8 %shard_map.80 = bf16[16,8,1024]{2,1,0:T(8,128)(2,1)} custom-call(bf16[4,16,8,128]{3,2,1,0:T(8,128)(2,1)S(1)} %shard_map.78.same_ref, bf16[4,16,8,128]{3,2,1,0:T(8,128)(2,1)S(1)} %collective-permute-done.14.beside_ref, bf16[2,16,8,128]{3,2,1,0:T(8,128)(2,1)S(1)} %collective-permute-done.15.refs_0_, ...), custom_call_target="tpu_custom_call" | custom-call | bytes 1048576 | tf_op jit(solution)/shard_map/pallas_call | solution.py:422
  (29 shorter events, 1.4 us)
Async XLA Ops:
  0.0 5.1 %copy-start = (f32[3,3,1024]{2,1,0:T(4,128)S(1)}, f32[3,3,1024]{2,1,0:T(4,128)}, u32[]{:S(2)}) copy-start(f32[3,3,1024]{2,1,0:T(4,128)} %param.12) | copy-start | bytes 110596
  1.5 15.2 %collective-permute-start.4 = (bf16[4,4,16,8,128]{4,3,2,1,0:T(8,128)(2,1)S(1)}, bf16[4,4,16,8,128]{4,3,2,1,0:T(8,128)(2,1)S(1)}, u32[]{:S(2)}, u32[]{:S(2)}) collective-permute-start(bf16[4,4,16,8,128]{4,3,2,1,0:T(8,128)(2,1)S(1)} %get-tuple-element.26), channel_id=1, source_target_pairs={{0,8},{1,9},{8,0},{9,1},{16,24},{17,25},{24,16},{25,17},{2,10},{3,... | collective-permute-start | bytes 1572872 | tf_op jit(solution)/shard_map/ppermute | solution.py:419
  1.5 4.7 %collective-permute-start = (bf16[2,18,8,128]{3,2,1,0:T(8,128)(2,1)S(1)}, bf16[2,18,8,128]{3,2,1,0:T(8,128)(2,1)S(1)}, u32[]{:S(2)}, u32[]{:S(2)}) collective-permute-start(bf16[2,18,8,128]{3,2,1,0:T(8,128)(2,1)S(1)} %get-tuple-element.20), channel_id=1, source_target_pairs={{0,1},{1,0},{8,9},{9,8},{16,17},{17,16},{24,25},{25,24},{2,3},{3,2... | collective-permute-start | bytes 221192 | tf_op jit(solution)/shard_map/ppermute | solution.py:419
  3.1 4.8 %collective-permute-start.1 = (bf16[2,18,8,128]{3,2,1,0:T(8,128)(2,1)S(1)}, bf16[2,18,8,128]{3,2,1,0:T(8,128)(2,1)S(1)}, u32[]{:S(2)}, u32[]{:S(2)}) collective-permute-start(bf16[2,18,8,128]{3,2,1,0:T(8,128)(2,1)S(1)} %get-tuple-element.21), channel_id=1, source_target_pairs={{0,16},{1,17},{8,24},{9,25},{16,0},{17,1},{24,8},{25,9},{2,18},{3,... | collective-permute-start | bytes 221192 | tf_op jit(solution)/shard_map/ppermute | solution.py:419
  4.6 5.3 %collective-permute-start.2 = (bf16[2,18,8,128]{3,2,1,0:T(8,128)(2,1)S(1)}, bf16[2,18,8,128]{3,2,1,0:T(8,128)(2,1)S(1)}, u32[]{:S(2)}, u32[]{:S(2)}) collective-permute-start(bf16[2,18,8,128]{3,2,1,0:T(8,128)(2,1)S(1)} %get-tuple-element.22), channel_id=1, source_target_pairs={{0,17},{1,16},{8,25},{9,24},{16,1},{17,0},{24,9},{25,8},{2,19},{3,... | collective-permute-start | bytes 221192 | tf_op jit(solution)/shard_map/ppermute | solution.py:419
  9.9 3.2 %collective-permute-start.3 = (bf16[4,18,8,128]{3,2,1,0:T(8,128)(2,1)S(1)}, bf16[4,18,8,128]{3,2,1,0:T(8,128)(2,1)S(1)}, u32[]{:S(2)}, u32[]{:S(2)}) collective-permute-start(bf16[4,18,8,128]{3,2,1,0:T(8,128)(2,1)S(1)} %get-tuple-element.24), channel_id=1, source_target_pairs={{0,8},{1,9},{8,0},{9,1},{16,24},{17,25},{24,16},{25,17},{2,10},{3,... | collective-permute-start | bytes 442376 | tf_op jit(solution)/shard_map/ppermute | solution.py:419
  10.7 9.5 %collective-permute-start.9 = (bf16[4,18,8,128]{3,2,1,0:T(8,128)(2,1)S(1)}, bf16[4,18,8,128]{3,2,1,0:T(8,128)(2,1)S(1)}, u32[]{:S(2)}, u32[]{:S(2)}) collective-permute-start(bf16[4,18,8,128]{3,2,1,0:T(8,128)(2,1)S(1)} %get-tuple-element.23), channel_id=1, source_target_pairs={{2,4},{4,2},{3,5},{5,3},{10,12},{12,10},{11,13},{13,11},{18,20},{2... | collective-permute-start | bytes 442376 | tf_op jit(solution)/shard_map/ppermute | solution.py:469
  13.1 8.9 %collective-permute-start.10 = (bf16[4,18,8,128]{3,2,1,0:T(8,128)(2,1)S(1)}, bf16[4,18,8,128]{3,2,1,0:T(8,128)(2,1)S(1)}, u32[]{:S(2)}, u32[]{:S(2)}) collective-permute-start(bf16[4,18,8,128]{3,2,1,0:T(8,128)(2,1)S(1)} %collective-permute-done.3), channel_id=1, source_target_pairs={{2,4},{4,2},{3,5},{5,3},{10,12},{12,10},{11,13},{13,11},{18,20},{2... | collective-permute-start | bytes 442376 | tf_op jit(solution)/shard_map/ppermute | solution.py:470
  16.7 10.2 %collective-permute-start.7 = (bf16[2,4,16,8,128]{4,3,2,1,0:T(8,128)(2,1)S(1)}, bf16[2,4,16,8,128]{4,3,2,1,0:T(8,128)(2,1)S(1)}, u32[]{:S(2)}, u32[]{:S(2)}) collective-permute-start(bf16[2,4,16,8,128]{4,3,2,1,0:T(8,128)(2,1)S(1)} %get-tuple-element.34), channel_id=1, source_target_pairs={{0,17},{1,16},{8,25},{9,24},{16,1},{17,0},{24,9},{25,8},{2,19},{3,... | collective-permute-start | bytes 786440 | tf_op jit(solution)/shard_map/ppermute | solution.py:419
  18.3 12.3 %collective-permute-start.6 = (bf16[2,4,16,8,128]{4,3,2,1,0:T(8,128)(2,1)S(1)}, bf16[2,4,16,8,128]{4,3,2,1,0:T(8,128)(2,1)S(1)}, u32[]{:S(2)}, u32[]{:S(2)}) collective-permute-start(bf16[2,4,16,8,128]{4,3,2,1,0:T(8,128)(2,1)S(1)} %get-tuple-element.35), channel_id=1, source_target_pairs={{0,16},{1,17},{8,24},{9,25},{16,0},{17,1},{24,8},{25,9},{2,18},{3,... | collective-permute-start | bytes 786440 | tf_op jit(solution)/shard_map/ppermute | solution.py:419
  18.9 12.5 %collective-permute-start.5 = (bf16[2,4,16,8,128]{4,3,2,1,0:T(8,128)(2,1)S(1)}, bf16[2,4,16,8,128]{4,3,2,1,0:T(8,128)(2,1)S(1)}, u32[]{:S(2)}, u32[]{:S(2)}) collective-permute-start(bf16[2,4,16,8,128]{4,3,2,1,0:T(8,128)(2,1)S(1)} %get-tuple-element.36), channel_id=1, source_target_pairs={{0,1},{1,0},{8,9},{9,8},{16,17},{17,16},{24,25},{25,24},{2,3},{3,2... | collective-permute-start | bytes 786440 | tf_op jit(solution)/shard_map/ppermute | solution.py:419
  20.3 11.3 %collective-permute-start.8 = (bf16[8,18,8,128]{3,2,1,0:T(8,128)(2,1)S(1)}, bf16[8,18,8,128]{3,2,1,0:T(8,128)(2,1)S(1)}, u32[]{:S(2)}, u32[]{:S(2)}) collective-permute-start(bf16[8,18,8,128]{3,2,1,0:T(8,128)(2,1)S(1)} %constant_dynamic-update-slice_fusion.query_ref), channel_id=1, source_target_pairs={{0,2},{2,0},{4,6},{6,4},{1,3},{3,1},{5,7},{7,5},{8,10},{10,8},{12,... | collective-permute-start | bytes 884744 | tf_op jit(solution)/shard_map/ppermute | solution.py:473
  33.5 14.7 %collective-permute-start.11 = (bf16[4,16,8,128]{3,2,1,0:T(8,128)(2,1)S(1)}, bf16[4,16,8,128]{3,2,1,0:T(8,128)(2,1)S(1)}, u32[]{:S(2)}, u32[]{:S(2)}) collective-permute-start(bf16[4,16,8,128]{3,2,1,0:T(8,128)(2,1)S(1)} %slice.52), channel_id=1, source_target_pairs={{0,2},{2,0},{4,6},{6,4},{1,3},{3,1},{5,7},{7,5},{8,10},{10,8},{12,... | collective-permute-start | bytes 393224 | tf_op jit(solution)/shard_map/ppermute | solution.py:486
  33.6 8.9 %collective-permute-start.12 = (bf16[5,16,8,128]{3,2,1,0:T(8,128)(2,1)S(1)}, bf16[5,16,8,128]{3,2,1,0:T(8,128)(2,1)S(1)}, u32[]{:S(2)}, u32[]{:S(2)}) collective-permute-start(bf16[5,16,8,128]{3,2,1,0:T(8,128)(2,1)S(1)} %slice.53), channel_id=1, source_target_pairs={{0,2},{2,0},{4,6},{6,4},{1,3},{3,1},{5,7},{7,5},{8,10},{10,8},{12,... | collective-permute-start | bytes 491528 | tf_op jit(solution)/shard_map/ppermute | solution.py:485
  37.5 10.3 %collective-permute-start.13 = (bf16[9,16,8,128]{3,2,1,0:T(8,128)(2,1)S(1)}, bf16[9,16,8,128]{3,2,1,0:T(8,128)(2,1)S(1)}, u32[]{:S(2)}, u32[]{:S(2)}) collective-permute-start(bf16[9,16,8,128]{3,2,1,0:T(8,128)(2,1)S(1)} %shard_map.77), channel_id=1, source_target_pairs={{2,4},{4,2},{3,5},{5,3},{10,12},{12,10},{11,13},{13,11},{18,20},{2... | collective-permute-start | bytes 884744 | tf_op jit(solution)/shard_map/ppermute | solution.py:482
  48.1 1.4 %collective-permute-start.14 = (bf16[4,16,8,128]{3,2,1,0:T(8,128)(2,1)S(1)}, bf16[4,16,8,128]{3,2,1,0:T(8,128)(2,1)S(1)}, u32[]{:S(2)}, u32[]{:S(2)}) collective-permute-start(bf16[4,16,8,128]{3,2,1,0:T(8,128)(2,1)S(1)} %shard_map.79), channel_id=1, source_target_pairs={{0,8},{1,9},{8,0},{9,1},{16,24},{17,25},{24,16},{25,17},{2,10},{3,... | collective-permute-start | bytes 393224 | tf_op jit(solution)/shard_map/ppermute | solution.py:419
  49.6 4.3 %collective-permute-start.15 = (bf16[2,16,8,128]{3,2,1,0:T(8,128)(2,1)S(1)}, bf16[2,16,8,128]{3,2,1,0:T(8,128)(2,1)S(1)}, u32[]{:S(2)}, u32[]{:S(2)}) collective-permute-start(bf16[2,16,8,128]{3,2,1,0:T(8,128)(2,1)S(1)} %pad_maximum_fusion.1), channel_id=1, source_target_pairs={{0,1},{1,0},{8,9},{9,8},{16,17},{17,16},{24,25},{25,24},{2,3},{3,2... | collective-permute-start | bytes 196616 | tf_op jit(solution)/shard_map/ppermute | solution.py:419
  50.3 4.9 %collective-permute-start.16 = (bf16[2,16,8,128]{3,2,1,0:T(8,128)(2,1)S(1)}, bf16[2,16,8,128]{3,2,1,0:T(8,128)(2,1)S(1)}, u32[]{:S(2)}, u32[]{:S(2)}) collective-permute-start(bf16[2,16,8,128]{3,2,1,0:T(8,128)(2,1)S(1)} %pad_maximum_fusion.2), channel_id=1, source_target_pairs={{0,16},{1,17},{8,24},{9,25},{16,0},{17,1},{24,8},{25,9},{2,18},{3,... | collective-permute-start | bytes 196616 | tf_op jit(solution)/shard_map/ppermute | solution.py:419
  51.8 5.2 %collective-permute-start.17 = (bf16[2,16,8,128]{3,2,1,0:T(8,128)(2,1)S(1)}, bf16[2,16,8,128]{3,2,1,0:T(8,128)(2,1)S(1)}, u32[]{:S(2)}, u32[]{:S(2)}) collective-permute-start(bf16[2,16,8,128]{3,2,1,0:T(8,128)(2,1)S(1)} %pad_maximum_fusion.3), channel_id=1, source_target_pairs={{0,17},{1,16},{8,25},{9,24},{16,1},{17,0},{24,9},{25,8},{2,19},{3,... | collective-permute-start | bytes 196616 | tf_op jit(solution)/shard_map/ppermute | solution.py:419

commit v14 on v13

--- a/solution.py
+++ b/solution.py
@@ -266,8 +266,8 @@
                 return self.pairs[self.pair_slot(tile_row, c), member, line].astype(jnp.float32)
 
             def edge(right, c):
-                place = self.slot(tile_row, c), self.tile_rows + line // self.tile_cols
-                first, second = (ref[place].astype(jnp.float32) for ref in beyond)
+                back = self.tile_rows // self.tile_cols - line // self.tile_cols
+                first, second = (ref[self.slot(tile_row, c), ref.shape[1] - back].astype(jnp.float32) for ref in beyond)
                 packed = jnp.where(first_is_right() == right, first, second)
                 return jnp.broadcast_to(packed[line % self.tile_cols : line % self.tile_cols + 1], shape)
 
@@ -466,9 +466,10 @@
     half = jax.ShapeDtypeStruct((len(flips),) + query_buffer.shape[1:], jnp.bfloat16)
     mine, forward = call(split_kernel, [half, half], SMALL, 0, *got)
     forward = swap(forward, side)
-    second_a = lax.ppermute(mine, "far", second)
-    second_b = lax.ppermute(forward, "far", second)
+    second_a = lax.ppermute(mine[:, :tile_rows], "far", second)
+    second_b = lax.ppermute(forward[:, :tile_rows], "far", second)
     query = jnp.concatenate([mine, forward], axis=0)
+    edges_second = lax.ppermute(query[:, tile_rows:], "far", second)
     query_second = jnp.concatenate([second_a, second_b], axis=0)
     query_first = lax.ppermute(query, "far", first)
     weight = lax.dynamic_slice_in_dim(conv_weight, me * HD, HD, 2)
@@ -486,7 +487,7 @@
     home_first_b = lax.ppermute(part[half:], "far", first)
     part = jax.ShapeDtypeStruct((heads, size, HD), jnp.float32)
     kernel = functools.partial(own_kernel, grid, tile)
-    own = call(kernel, [part] * 3, LIMIT, 4, weight, bias, query, pairs, query_first, query_second)
+    own = call(kernel, [part] * 3, LIMIT, 4, weight, bias, query, pairs, query_first, edges_second)
     result = jax.ShapeDtypeStruct((len(flips),) + block, jnp.bfloat16)
 
     def join(beside, tiles):

time: 58 us -> 57.3 us (0.988)
  waiting for transfers between devices: 26.1 us -> 22.5 us
  starting transfers between devices: 21.3 us -> 24.1 us
    ppermute x2 -> x3, starting transfers between devices: 5.83 us -> 8.64 us  [the longest x1 3.48 us: head_step(): second_b = lax.ppermute(forward[:, :tile_rows], 'far', second)]
    ppermute x12, waiting for transfers between devices: 18.9 us -> 16.8 us  [swap(): return lax.ppermute(x, axes, [(s, s ^ flip) for s in range(heads)])]
    ppermute x2 -> x3, waiting for transfers between devices: 1.63 us -> 0.14 us  [the longest x1 0.14 us: head_step(): second_b = lax.ppermute(forward[:, :tile_rows], 'far', second)]
  transfers between devices with their start and end apart: 18 -> 19, of which waited for: 13 -> 13; matrix products, arithmetic and copies ran while one was open for 2% -> 2% of each run, Pallas kernels for 9% -> 12%
where the time goes in v14:
time: 57.3 us; the launch traced here: 57.1 us
  starting transfers between devices  24.1 us (42%)
  waiting for transfers between devices  22.5 us (39%)
  Pallas kernels  9.09 us (16%)
  local copies, waits for them, and re-layouts  0.95 us (2%)
    ppermute x12, waiting for transfers between devices, swap(): return lax.ppermute(x, axes, [(s, s ^ flip) for s in range(heads)])  16.8 us
    ppermute x12, starting transfers between devices, swap(): return lax.ppermute(x, axes, [(s, s ^ flip) for s in range(heads)])  11 us
    pallas_call x8, Pallas kernels, call(): pl.pallas_call(kernel, out_shape=out_shape, in_specs=[space[0]] * len(ope...  9.09 us
    ppermute x1, waiting for transfers between devices, head_step(): home_second = lax.ppermute(part, 'far', second)  5.24 us
    ppermute x1, starting transfers between devices, head_step(): second_b = lax.ppermute(forward[:, :tile_rows], 'far', second)  3.48 us
    ppermute x1, starting transfers between devices, head_step(): edges_second = lax.ppermute(query[:, tile_rows:], 'far', second)  2.8 us
    ppermute x1, starting transfers between devices, head_step(): second_a = lax.ppermute(mine[:, :tile_rows], 'far', second)  2.36 us
    ppermute x1, starting transfers between devices, head_step(): home_second = lax.ppermute(part, 'far', second)  2.35 us
  transfers between devices with their start and end apart: 19, of which 13 were waited for; matrix products, arithmetic and copies ran while one was open for 2% of the time, Pallas kernels for 12%

profile of v14, /device:TPU:16, one launch (start us, length us, event | category | flops | bytes accessed | tf_op | source)
XLA Modules:
  0.0 57.1 jit_solution(17230163825335087902)
XLA Ops:
  0.0 1.4 %shard_map.73 = (bf16[2,18,8,128]{3,2,1,0:T(8,128)(2,1)S(1)}, bf16[2,18,8,128]{3,2,1,0:T(8,128)(2,1)S(1)}, bf16[2,18,8,128]{3,2,1,0:T(8,128)(2,1)S(1)}, bf16[2,1...) custom-call(bf16[16,8,1024]{2,1,0:T(8,128)(2,1)} %refs_0_.1, ...), custom_call_target="tpu_custom_call" | custom-call | bytes 1048576 | tf_op jit(solution)/shard_map/pallas_call | solution.py:422
  1.5 1.6 %collective-permute-start = (bf16[2,18,8,128]{3,2,1,0:T(8,128)(2,1)S(1)}, bf16[2,18,8,128]{3,2,1,0:T(8,128)(2,1)S(1)}, u32[]{:S(2)}, u32[]{:S(2)}) collective-permute-start(bf16[2,18,8,128]{3,2,1,0:T(8,128)(2,1)S(1)} %get-tuple-element.20), channel_id=1, source_target_pairs={{0,1},{1,0},{8,9},{9,8},{16,17},{17,16},{24,25},{25,24},{2,3},{3,2... | collective-permute-start | bytes 221192 | tf_op jit(solution)/shard_map/ppermute | solution.py:419
  3.1 1.5 %collective-permute-start.1 = (bf16[2,18,8,128]{3,2,1,0:T(8,128)(2,1)S(1)}, bf16[2,18,8,128]{3,2,1,0:T(8,128)(2,1)S(1)}, u32[]{:S(2)}, u32[]{:S(2)}) collective-permute-start(bf16[2,18,8,128]{3,2,1,0:T(8,128)(2,1)S(1)} %get-tuple-element.21), channel_id=1, source_target_pairs={{0,16},{1,17},{8,24},{9,25},{16,0},{17,1},{24,8},{25,9},{2,18},{3,... | collective-permute-start | bytes 221192 | tf_op jit(solution)/shard_map/ppermute | solution.py:419
  4.6 0.5 collective-permute-start.2
  5.1 1.1 %collective-permute-done.refs_1_ = bf16[2,18,8,128]{3,2,1,0:T(8,128)(2,1)S(1)} collective-permute-done((bf16[2,18,8,128]{3,2,1,0:T(8,128)(2,1)S(1)}, bf16[2,18,8,128]{3,2,1,0:T(8,128)(2,1)S(1)}, u32[]{:S(2)}, u32[]{:S(2)}) %collective-permute-start) | collective-permute-done | bytes 73760 | tf_op jit(solution)/shard_map/ppermute | solution.py:419
  6.2 1.7 %collective-permute-done.1.refs_2_ = bf16[2,18,8,128]{3,2,1,0:T(8,128)(2,1)S(1)} collective-permute-done((bf16[2,18,8,128]{3,2,1,0:T(8,128)(2,1)S(1)}, bf16[2,18,8,128]{3,2,1,0:T(8,128)(2,1)S(1)}, u32[]{:S(2)}, u32[]{:S(2)}) %collective-permute-start.1) | collective-permute-done | bytes 73760 | tf_op jit(solution)/shard_map/ppermute | solution.py:419
  7.9 1.9 %collective-permute-done.2.refs_3_ = bf16[2,18,8,128]{3,2,1,0:T(8,128)(2,1)S(1)} collective-permute-done((bf16[2,18,8,128]{3,2,1,0:T(8,128)(2,1)S(1)}, bf16[2,18,8,128]{3,2,1,0:T(8,128)(2,1)S(1)}, u32[]{:S(2)}, u32[]{:S(2)}) %collective-permute-start.2) | collective-permute-done | bytes 73760 | tf_op jit(solution)/shard_map/ppermute | solution.py:419
  10.0 2.4 %collective-permute-start.12 = (bf16[4,16,8,128]{3,2,1,0:T(8,128)(2,1)S(1)}, bf16[4,16,8,128]{3,2,1,0:T(8,128)(2,1)S(1)}, u32[]{:S(2)}, u32[]{:S(2)}) collective-permute-start(bf16[4,16,8,128]{3,2,1,0:T(8,128)(2,1)S(1)} %slice.52), channel_id=1, source_target_pairs={{2,4},{4,2},{3,5},{5,3},{10,12},{12,10},{11,13},{13,11},{18,20},{2... | collective-permute-start | bytes 393224 | tf_op jit(solution)/shard_map/ppermute | solution.py:469
  12.4 3.5 %collective-permute-start.13 = (bf16[4,16,8,128]{3,2,1,0:T(8,128)(2,1)S(1)}, bf16[4,16,8,128]{3,2,1,0:T(8,128)(2,1)S(1)}, u32[]{:S(2)}, u32[]{:S(2)}) collective-permute-start(bf16[4,16,8,128]{3,2,1,0:T(8,128)(2,1)S(1)} %slice.67), channel_id=1, source_target_pairs={{2,4},{4,2},{3,5},{5,3},{10,12},{12,10},{11,13},{13,11},{18,20},{2... | collective-permute-start | bytes 393224 | tf_op jit(solution)/shard_map/ppermute | solution.py:470
  16.0 1.6 %collective-permute-start.7 = (bf16[2,4,16,8,128]{4,3,2,1,0:T(8,128)(2,1)S(1)}, bf16[2,4,16,8,128]{4,3,2,1,0:T(8,128)(2,1)S(1)}, u32[]{:S(2)}, u32[]{:S(2)}) collective-permute-start(bf16[2,4,16,8,128]{4,3,2,1,0:T(8,128)(2,1)S(1)} %get-tuple-element.34), channel_id=1, source_target_pairs={{0,17},{1,16},{8,25},{9,24},{16,1},{17,0},{24,9},{25,8},{2,19},{3,... | collective-permute-start | bytes 786440 | tf_op jit(solution)/shard_map/ppermute | solution.py:419
  17.6 0.6 collective-permute-start.6
  18.2 1.4 %collective-permute-start.5 = (bf16[2,4,16,8,128]{4,3,2,1,0:T(8,128)(2,1)S(1)}, bf16[2,4,16,8,128]{4,3,2,1,0:T(8,128)(2,1)S(1)}, u32[]{:S(2)}, u32[]{:S(2)}) collective-permute-start(bf16[2,4,16,8,128]{4,3,2,1,0:T(8,128)(2,1)S(1)} %get-tuple-element.36), channel_id=1, source_target_pairs={{0,1},{1,0},{8,9},{9,8},{16,17},{17,16},{24,25},{25,24},{2,3},{3,2... | collective-permute-start | bytes 786440 | tf_op jit(solution)/shard_map/ppermute | solution.py:419
  19.7 0.8 %dynamic-slice_bitcast_fusion.bias_ref = f32[1,128]{1,0:T(1,128)S(1)} fusion(f32[1024]{0:T(1024)} %param.13, s32[]{:T(128)S(6)} %select_n.4), kind=kLoop, calls=%fused_computation.12 | loop fusion | bytes 1028 | tf_op jit(solution)/shard_map/dynamic_slice | solution.py:476
  20.6 2.8 %collective-permute-start.9 = (bf16[8,2,8,128]{3,2,1,0:T(8,128)(2,1)S(1)}, bf16[8,2,8,128]{3,2,1,0:T(8,128)(2,1)S(1)}, u32[]{:S(2)}, u32[]{:S(2)}) collective-permute-start(bf16[8,2,8,128]{3,2,1,0:T(8,128)(2,1)S(1)} %slice.64), channel_id=1, source_target_pairs={{2,4},{4,2},{3,5},{5,3},{10,12},{12,10},{11,13},{13,11},{18,20},{2... | collective-permute-start | bytes 98312 | tf_op jit(solution)/shard_map/ppermute | solution.py:472
  23.4 2.8 %collective-permute-done.7 = bf16[2,4,16,8,128]{4,3,2,1,0:T(8,128)(2,1)S(1)} collective-permute-done((bf16[2,4,16,8,128]{4,3,2,1,0:T(8,128)(2,1)S(1)}, bf16[2,4,16,8,128]{4,3,2,1,0:T(8,128)(2,1)S(1)}, u32[]{:S(2)}, u32[]{:S(2)}) %collective-permute-start.7) | collective-permute-done | bytes 262176 | tf_op jit(solution)/shard_map/ppermute | solution.py:419
  26.2 3.7 %collective-permute-done.6 = bf16[2,4,16,8,128]{4,3,2,1,0:T(8,128)(2,1)S(1)} collective-permute-done((bf16[2,4,16,8,128]{4,3,2,1,0:T(8,128)(2,1)S(1)}, bf16[2,4,16,8,128]{4,3,2,1,0:T(8,128)(2,1)S(1)}, u32[]{:S(2)}, u32[]{:S(2)}) %collective-permute-start.6) | collective-permute-done | bytes 262176 | tf_op jit(solution)/shard_map/ppermute | solution.py:419
  29.9 0.8 %collective-permute-done.5 = bf16[2,4,16,8,128]{4,3,2,1,0:T(8,128)(2,1)S(1)} collective-permute-done((bf16[2,4,16,8,128]{4,3,2,1,0:T(8,128)(2,1)S(1)}, bf16[2,4,16,8,128]{4,3,2,1,0:T(8,128)(2,1)S(1)}, u32[]{:S(2)}, u32[]{:S(2)}) %collective-permute-start.5) | collective-permute-done | bytes 262176 | tf_op jit(solution)/shard_map/ppermute | solution.py:419
  30.9 1.9 %shard_map.76 = bf16[9,16,8,128]{3,2,1,0:T(8,128)(2,1)S(1)} custom-call(bf16[8,18,8,128]{3,2,1,0:T(8,128)(2,1)S(1)} %collective-permute-done.8.first_ref.query_ref, bf16[8,4,16,8,128]{4,3,2,1,0:T(8,128)(2,1)S(1)} %pad_maximum_fusion.pairs_ref), custom_call_target="tpu_custom_call" | custom-call | flops 4294967296 | bytes 1048576 | tf_op jit(solution)/shard_map/pallas_call | solution.py:422
  32.9 2.0 %collective-permute-start.11 = (bf16[5,16,8,128]{3,2,1,0:T(8,128)(2,1)S(1)}, bf16[5,16,8,128]{3,2,1,0:T(8,128)(2,1)S(1)}, u32[]{:S(2)}, u32[]{:S(2)}) collective-permute-start(bf16[5,16,8,128]{3,2,1,0:T(8,128)(2,1)S(1)} %slice.66), channel_id=1, source_target_pairs={{0,2},{2,0},{4,6},{6,4},{1,3},{3,1},{5,7},{7,5},{8,10},{10,8},{12,... | collective-permute-start | bytes 491528 | tf_op jit(solution)/shard_map/ppermute | solution.py:486
  34.9 1.9 %shard_map.77 = bf16[9,16,8,128]{3,2,1,0:T(8,128)(2,1)S(1)} custom-call(bf16[8,16,8,128]{3,2,1,0:T(8,128)(2,1)S(1)} %pad_maximum_fusion.1.query_ref, bf16[8,4,16,8,128]{4,3,2,1,0:T(8,128)(2,1)S(1)} %pad_maximum_fusion.pairs_ref), custom_call_target="tpu_custom_call" | custom-call | flops 4294967296 | bytes 1048576 | tf_op jit(solution)/shard_map/pallas_call | solution.py:422
  36.8 2.4 %collective-permute-start.14 = (bf16[9,16,8,128]{3,2,1,0:T(8,128)(2,1)S(1)}, bf16[9,16,8,128]{3,2,1,0:T(8,128)(2,1)S(1)}, u32[]{:S(2)}, u32[]{:S(2)}) collective-permute-start(bf16[9,16,8,128]{3,2,1,0:T(8,128)(2,1)S(1)} %shard_map.77), channel_id=1, source_target_pairs={{2,4},{4,2},{3,5},{5,3},{10,12},{12,10},{11,13},{13,11},{18,20},{2... | collective-permute-start | bytes 884744 | tf_op jit(solution)/shard_map/ppermute | solution.py:483
  39.2 2.3 %shard_map.75 = (f32[8,128,128]{2,1,0:T(8,128)S(1)}, f32[8,128,128]{2,1,0:T(8,128)S(1)}, f32[8,128,128]{2,1,0:T(8,128)S(1)}) custom-call(f32[3,3,128]{2,1,0:T(4,128)S(1)} %constant_dynamic-slice_fusion.weight_ref, f32[1,128]{1,0:T(1,128)S(1)} %dynamic-slice_bitcast_fusion.bias_ref, bf16[8,18,8,128]{3,2,1,0:T(8,128)(2,1)S(1)} %constant_dynamic-update-slice_fusion.query_ref, ...), custom_call_target="tpu_custom_call" | custom-call | flops 4294967296 | bytes 1048576 | tf_op jit(solution)/shard_map/pallas_call | solution.py:422
  41.8 5.2 %collective-permute-done.14.second_ref = bf16[9,16,8,128]{3,2,1,0:T(8,128)(2,1)S(1)} collective-permute-done((bf16[9,16,8,128]{3,2,1,0:T(8,128)(2,1)S(1)}, bf16[9,16,8,128]{3,2,1,0:T(8,128)(2,1)S(1)}, u32[]{:S(2)}, u32[]{:S(2)}) %collective-permute-start.14) | collective-permute-done | bytes 294944 | tf_op jit(solution)/shard_map/ppermute | solution.py:483
  47.5 0.4 shard_map.78.same_ref
  47.9 0.9 %collective-permute-done.15.beside_ref = bf16[4,16,8,128]{3,2,1,0:T(8,128)(2,1)S(1)} collective-permute-done((bf16[4,16,8,128]{3,2,1,0:T(8,128)(2,1)S(1)}, bf16[4,16,8,128]{3,2,1,0:T(8,128)(2,1)S(1)}, u32[]{:S(2)}, u32[]{:S(2)}) %collective-permute-start.15) | collective-permute-done | bytes 131104 | tf_op jit(solution)/shard_map/ppermute | solution.py:419
  48.9 0.7 %collective-permute-start.16 = (bf16[2,16,8,128]{3,2,1,0:T(8,128)(2,1)S(1)}, bf16[2,16,8,128]{3,2,1,0:T(8,128)(2,1)S(1)}, u32[]{:S(2)}, u32[]{:S(2)}) collective-permute-start(bf16[2,16,8,128]{3,2,1,0:T(8,128)(2,1)S(1)} %pad_maximum_fusion.2), channel_id=1, source_target_pairs={{0,1},{1,0},{8,9},{9,8},{16,17},{17,16},{24,25},{25,24},{2,3},{3,2... | collective-permute-start | bytes 196616 | tf_op jit(solution)/shard_map/ppermute | solution.py:419
  49.6 1.5 %collective-permute-start.17 = (bf16[2,16,8,128]{3,2,1,0:T(8,128)(2,1)S(1)}, bf16[2,16,8,128]{3,2,1,0:T(8,128)(2,1)S(1)}, u32[]{:S(2)}, u32[]{:S(2)}) collective-permute-start(bf16[2,16,8,128]{3,2,1,0:T(8,128)(2,1)S(1)} %pad_maximum_fusion.3), channel_id=1, source_target_pairs={{0,16},{1,17},{8,24},{9,25},{16,0},{17,1},{24,8},{25,9},{2,18},{3,... | collective-permute-start | bytes 196616 | tf_op jit(solution)/shard_map/ppermute | solution.py:419
  51.1 1.4 %collective-permute-start.18 = (bf16[2,16,8,128]{3,2,1,0:T(8,128)(2,1)S(1)}, bf16[2,16,8,128]{3,2,1,0:T(8,128)(2,1)S(1)}, u32[]{:S(2)}, u32[]{:S(2)}) collective-permute-start(bf16[2,16,8,128]{3,2,1,0:T(8,128)(2,1)S(1)} %pad_maximum_fusion.4), channel_id=1, source_target_pairs={{0,17},{1,16},{8,25},{9,24},{16,1},{17,0},{24,9},{25,8},{2,19},{3,... | collective-permute-start | bytes 196616 | tf_op jit(solution)/shard_map/ppermute | solution.py:419
  52.6 0.6 %collective-permute-done.16.refs_0_ = bf16[2,16,8,128]{3,2,1,0:T(8,128)(2,1)S(1)} collective-permute-done((bf16[2,16,8,128]{3,2,1,0:T(8,128)(2,1)S(1)}, bf16[2,16,8,128]{3,2,1,0:T(8,128)(2,1)S(1)}, u32[]{:S(2)}, u32[]{:S(2)}) %collective-permute-start.16) | collective-permute-done | bytes 65568 | tf_op jit(solution)/shard_map/ppermute | solution.py:419
  53.2 1.3 %collective-permute-done.17.refs_1_ = bf16[2,16,8,128]{3,2,1,0:T(8,128)(2,1)S(1)} collective-permute-done((bf16[2,16,8,128]{3,2,1,0:T(8,128)(2,1)S(1)}, bf16[2,16,8,128]{3,2,1,0:T(8,128)(2,1)S(1)}, u32[]{:S(2)}, u32[]{:S(2)}) %collective-permute-start.17) | collective-permute-done | bytes 65568 | tf_op jit(solution)/shard_map/ppermute | solution.py:419
  54.5 1.8 %collective-permute-done.18.refs_2_ = bf16[2,16,8,128]{3,2,1,0:T(8,128)(2,1)S(1)} collective-permute-done((bf16[2,16,8,128]{3,2,1,0:T(8,128)(2,1)S(1)}, bf16[2,16,8,128]{3,2,1,0:T(8,128)(2,1)S(1)}, u32[]{:S(2)}, u32[]{:S(2)}) %collective-permute-start.18) | collective-permute-done | bytes 65568 | tf_op jit(solution)/shard_map/ppermute | solution.py:419
  56.3 0.8 %shard_map.80 = bf16[16,8,1024]{2,1,0:T(8,128)(2,1)} custom-call(bf16[4,16,8,128]{3,2,1,0:T(8,128)(2,1)S(1)} %shard_map.78.same_ref, bf16[4,16,8,128]{3,2,1,0:T(8,128)(2,1)S(1)} %collective-permute-done.15.beside_ref, bf16[2,16,8,128]{3,2,1,0:T(8,128)(2,1)S(1)} %collective-permute-done.16.refs_0_, ...), custom_call_target="tpu_custom_call" | custom-call | bytes 1048576 | tf_op jit(solution)/shard_map/pallas_call | solution.py:422
  (33 shorter events, 1.5 us)
Async XLA Ops:
  0.0 10.0 %copy-start = (f32[3,3,1024]{2,1,0:T(4,128)S(1)}, f32[3,3,1024]{2,1,0:T(4,128)}, u32[]{:S(2)}) copy-start(f32[3,3,1024]{2,1,0:T(4,128)} %param.12) | copy-start | bytes 110596
  1.5 14.5 %collective-permute-start.4 = (bf16[4,4,16,8,128]{4,3,2,1,0:T(8,128)(2,1)S(1)}, bf16[4,4,16,8,128]{4,3,2,1,0:T(8,128)(2,1)S(1)}, u32[]{:S(2)}, u32[]{:S(2)}) collective-permute-start(bf16[4,4,16,8,128]{4,3,2,1,0:T(8,128)(2,1)S(1)} %get-tuple-element.26), channel_id=1, source_target_pairs={{0,8},{1,9},{8,0},{9,1},{16,24},{17,25},{24,16},{25,17},{2,10},{3,... | collective-permute-start | bytes 1572872 | tf_op jit(solution)/shard_map/ppermute | solution.py:419
  1.5 4.7 %collective-permute-start = (bf16[2,18,8,128]{3,2,1,0:T(8,128)(2,1)S(1)}, bf16[2,18,8,128]{3,2,1,0:T(8,128)(2,1)S(1)}, u32[]{:S(2)}, u32[]{:S(2)}) collective-permute-start(bf16[2,18,8,128]{3,2,1,0:T(8,128)(2,1)S(1)} %get-tuple-element.20), channel_id=1, source_target_pairs={{0,1},{1,0},{8,9},{9,8},{16,17},{17,16},{24,25},{25,24},{2,3},{3,2... | collective-permute-start | bytes 221192 | tf_op jit(solution)/shard_map/ppermute | solution.py:419
  3.1 4.8 %collective-permute-start.1 = (bf16[2,18,8,128]{3,2,1,0:T(8,128)(2,1)S(1)}, bf16[2,18,8,128]{3,2,1,0:T(8,128)(2,1)S(1)}, u32[]{:S(2)}, u32[]{:S(2)}) collective-permute-start(bf16[2,18,8,128]{3,2,1,0:T(8,128)(2,1)S(1)} %get-tuple-element.21), channel_id=1, source_target_pairs={{0,16},{1,17},{8,24},{9,25},{16,0},{17,1},{24,8},{25,9},{2,18},{3,... | collective-permute-start | bytes 221192 | tf_op jit(solution)/shard_map/ppermute | solution.py:419
  4.6 5.3 %collective-permute-start.2 = (bf16[2,18,8,128]{3,2,1,0:T(8,128)(2,1)S(1)}, bf16[2,18,8,128]{3,2,1,0:T(8,128)(2,1)S(1)}, u32[]{:S(2)}, u32[]{:S(2)}) collective-permute-start(bf16[2,18,8,128]{3,2,1,0:T(8,128)(2,1)S(1)} %get-tuple-element.22), channel_id=1, source_target_pairs={{0,17},{1,16},{8,25},{9,24},{16,1},{17,0},{24,9},{25,8},{2,19},{3,... | collective-permute-start | bytes 221192 | tf_op jit(solution)/shard_map/ppermute | solution.py:419
  9.9 2.5 %collective-permute-start.3 = (bf16[4,18,8,128]{3,2,1,0:T(8,128)(2,1)S(1)}, bf16[4,18,8,128]{3,2,1,0:T(8,128)(2,1)S(1)}, u32[]{:S(2)}, u32[]{:S(2)}) collective-permute-start(bf16[4,18,8,128]{3,2,1,0:T(8,128)(2,1)S(1)} %get-tuple-element.24), channel_id=1, source_target_pairs={{0,8},{1,9},{8,0},{9,1},{16,24},{17,25},{24,16},{25,17},{2,10},{3,... | collective-permute-start | bytes 442376 | tf_op jit(solution)/shard_map/ppermute | solution.py:419
  10.0 9.6 %collective-permute-start.12 = (bf16[4,16,8,128]{3,2,1,0:T(8,128)(2,1)S(1)}, bf16[4,16,8,128]{3,2,1,0:T(8,128)(2,1)S(1)}, u32[]{:S(2)}, u32[]{:S(2)}) collective-permute-start(bf16[4,16,8,128]{3,2,1,0:T(8,128)(2,1)S(1)} %slice.52), channel_id=1, source_target_pairs={{2,4},{4,2},{3,5},{5,3},{10,12},{12,10},{11,13},{13,11},{18,20},{2... | collective-permute-start | bytes 393224 | tf_op jit(solution)/shard_map/ppermute | solution.py:469
  12.4 8.2 %collective-permute-start.13 = (bf16[4,16,8,128]{3,2,1,0:T(8,128)(2,1)S(1)}, bf16[4,16,8,128]{3,2,1,0:T(8,128)(2,1)S(1)}, u32[]{:S(2)}, u32[]{:S(2)}) collective-permute-start(bf16[4,16,8,128]{3,2,1,0:T(8,128)(2,1)S(1)} %slice.67), channel_id=1, source_target_pairs={{2,4},{4,2},{3,5},{5,3},{10,12},{12,10},{11,13},{13,11},{18,20},{2... | collective-permute-start | bytes 393224 | tf_op jit(solution)/shard_map/ppermute | solution.py:470
  16.0 10.2 %collective-permute-start.7 = (bf16[2,4,16,8,128]{4,3,2,1,0:T(8,128)(2,1)S(1)}, bf16[2,4,16,8,128]{4,3,2,1,0:T(8,128)(2,1)S(1)}, u32[]{:S(2)}, u32[]{:S(2)}) collective-permute-start(bf16[2,4,16,8,128]{4,3,2,1,0:T(8,128)(2,1)S(1)} %get-tuple-element.34), channel_id=1, source_target_pairs={{0,17},{1,16},{8,25},{9,24},{16,1},{17,0},{24,9},{25,8},{2,19},{3,... | collective-permute-start | bytes 786440 | tf_op jit(solution)/shard_map/ppermute | solution.py:419
  17.6 12.3 %collective-permute-start.6 = (bf16[2,4,16,8,128]{4,3,2,1,0:T(8,128)(2,1)S(1)}, bf16[2,4,16,8,128]{4,3,2,1,0:T(8,128)(2,1)S(1)}, u32[]{:S(2)}, u32[]{:S(2)}) collective-permute-start(bf16[2,4,16,8,128]{4,3,2,1,0:T(8,128)(2,1)S(1)} %get-tuple-element.35), channel_id=1, source_target_pairs={{0,16},{1,17},{8,24},{9,25},{16,0},{17,1},{24,8},{25,9},{2,18},{3,... | collective-permute-start | bytes 786440 | tf_op jit(solution)/shard_map/ppermute | solution.py:419
  18.2 12.5 %collective-permute-start.5 = (bf16[2,4,16,8,128]{4,3,2,1,0:T(8,128)(2,1)S(1)}, bf16[2,4,16,8,128]{4,3,2,1,0:T(8,128)(2,1)S(1)}, u32[]{:S(2)}, u32[]{:S(2)}) collective-permute-start(bf16[2,4,16,8,128]{4,3,2,1,0:T(8,128)(2,1)S(1)} %get-tuple-element.36), channel_id=1, source_target_pairs={{0,1},{1,0},{8,9},{9,8},{16,17},{17,16},{24,25},{25,24},{2,3},{3,2... | collective-permute-start | bytes 786440 | tf_op jit(solution)/shard_map/ppermute | solution.py:419
  19.6 11.3 %collective-permute-start.8 = (bf16[8,18,8,128]{3,2,1,0:T(8,128)(2,1)S(1)}, bf16[8,18,8,128]{3,2,1,0:T(8,128)(2,1)S(1)}, u32[]{:S(2)}, u32[]{:S(2)}) collective-permute-start(bf16[8,18,8,128]{3,2,1,0:T(8,128)(2,1)S(1)} %constant_dynamic-update-slice_fusion.query_ref), channel_id=1, source_target_pairs={{0,2},{2,0},{4,6},{6,4},{1,3},{3,1},{5,7},{7,5},{8,10},{10,8},{12,... | collective-permute-start | bytes 884744 | tf_op jit(solution)/shard_map/ppermute | solution.py:474
  20.6 18.6 %collective-permute-start.9 = (bf16[8,2,8,128]{3,2,1,0:T(8,128)(2,1)S(1)}, bf16[8,2,8,128]{3,2,1,0:T(8,128)(2,1)S(1)}, u32[]{:S(2)}, u32[]{:S(2)}) collective-permute-start(bf16[8,2,8,128]{3,2,1,0:T(8,128)(2,1)S(1)} %slice.64), channel_id=1, source_target_pairs={{2,4},{4,2},{3,5},{5,3},{10,12},{12,10},{11,13},{13,11},{18,20},{2... | collective-permute-start | bytes 98312 | tf_op jit(solution)/shard_map/ppermute | solution.py:472
  32.8 14.7 %collective-permute-start.10 = (bf16[4,16,8,128]{3,2,1,0:T(8,128)(2,1)S(1)}, bf16[4,16,8,128]{3,2,1,0:T(8,128)(2,1)S(1)}, u32[]{:S(2)}, u32[]{:S(2)}) collective-permute-start(bf16[4,16,8,128]{3,2,1,0:T(8,128)(2,1)S(1)} %slice.65), channel_id=1, source_target_pairs={{0,2},{2,0},{4,6},{6,4},{1,3},{3,1},{5,7},{7,5},{8,10},{10,8},{12,... | collective-permute-start | bytes 393224 | tf_op jit(solution)/shard_map/ppermute | solution.py:487
  32.9 8.9 %collective-permute-start.11 = (bf16[5,16,8,128]{3,2,1,0:T(8,128)(2,1)S(1)}, bf16[5,16,8,128]{3,2,1,0:T(8,128)(2,1)S(1)}, u32[]{:S(2)}, u32[]{:S(2)}) collective-permute-start(bf16[5,16,8,128]{3,2,1,0:T(8,128)(2,1)S(1)} %slice.66), channel_id=1, source_target_pairs={{0,2},{2,0},{4,6},{6,4},{1,3},{3,1},{5,7},{7,5},{8,10},{10,8},{12,... | collective-permute-start | bytes 491528 | tf_op jit(solution)/shard_map/ppermute | solution.py:486
  36.8 10.3 %collective-permute-start.14 = (bf16[9,16,8,128]{3,2,1,0:T(8,128)(2,1)S(1)}, bf16[9,16,8,128]{3,2,1,0:T(8,128)(2,1)S(1)}, u32[]{:S(2)}, u32[]{:S(2)}) collective-permute-start(bf16[9,16,8,128]{3,2,1,0:T(8,128)(2,1)S(1)} %shard_map.77), channel_id=1, source_target_pairs={{2,4},{4,2},{3,5},{5,3},{10,12},{12,10},{11,13},{13,11},{18,20},{2... | collective-permute-start | bytes 884744 | tf_op jit(solution)/shard_map/ppermute | solution.py:483
  47.4 1.4 %collective-permute-start.15 = (bf16[4,16,8,128]{3,2,1,0:T(8,128)(2,1)S(1)}, bf16[4,16,8,128]{3,2,1,0:T(8,128)(2,1)S(1)}, u32[]{:S(2)}, u32[]{:S(2)}) collective-permute-start(bf16[4,16,8,128]{3,2,1,0:T(8,128)(2,1)S(1)} %shard_map.79), channel_id=1, source_target_pairs={{0,8},{1,9},{8,0},{9,1},{16,24},{17,25},{24,16},{25,17},{2,10},{3,... | collective-permute-start | bytes 393224 | tf_op jit(solution)/shard_map/ppermute | solution.py:419
  48.9 4.3 %collective-permute-start.16 = (bf16[2,16,8,128]{3,2,1,0:T(8,128)(2,1)S(1)}, bf16[2,16,8,128]{3,2,1,0:T(8,128)(2,1)S(1)}, u32[]{:S(2)}, u32[]{:S(2)}) collective-permute-start(bf16[2,16,8,128]{3,2,1,0:T(8,128)(2,1)S(1)} %pad_maximum_fusion.2), channel_id=1, source_target_pairs={{0,1},{1,0},{8,9},{9,8},{16,17},{17,16},{24,25},{25,24},{2,3},{3,2... | collective-permute-start | bytes 196616 | tf_op jit(solution)/shard_map/ppermute | solution.py:419
  49.6 4.9 %collective-permute-start.17 = (bf16[2,16,8,128]{3,2,1,0:T(8,128)(2,1)S(1)}, bf16[2,16,8,128]{3,2,1,0:T(8,128)(2,1)S(1)}, u32[]{:S(2)}, u32[]{:S(2)}) collective-permute-start(bf16[2,16,8,128]{3,2,1,0:T(8,128)(2,1)S(1)} %pad_maximum_fusion.3), channel_id=1, source_target_pairs={{0,16},{1,17},{8,24},{9,25},{16,0},{17,1},{24,8},{25,9},{2,18},{3,... | collective-permute-start | bytes 196616 | tf_op jit(solution)/shard_map/ppermute | solution.py:419
  51.1 5.2 %collective-permute-start.18 = (bf16[2,16,8,128]{3,2,1,0:T(8,128)(2,1)S(1)}, bf16[2,16,8,128]{3,2,1,0:T(8,128)(2,1)S(1)}, u32[]{:S(2)}, u32[]{:S(2)}) collective-permute-start(bf16[2,16,8,128]{3,2,1,0:T(8,128)(2,1)S(1)} %pad_maximum_fusion.4), channel_id=1, source_target_pairs={{0,17},{1,16},{8,25},{9,24},{16,1},{17,0},{24,9},{25,8},{2,19},{3,... | collective-permute-start | bytes 196616 | tf_op jit(solution)/shard_map/ppermute | solution.py:419
